TPU v7x, 32 devices: a whole 2x2x4 slice. The times are simulated.
32 devices in a mesh: energy: 8 (over z, y), mom: 4 (over x, core).
Axes of the slice: x: 2, y: 2, z: 4, core: 2. Of those that a mesh axis runs over, the one named last changes fastest.
Arguments:
- green_ret: bfloat16 [16, 16, 2, 512, 512], P('mom', 'energy'), may hold values from -0.25 to 0.25
- broadening: float32 [16, 16, 512], P('mom', 'energy'), may hold values from 0.2 to 2
- coupling: bfloat16 [16, 512, 512], P(None, 'mom'), may hold values from -1.5 to 1.5
- shift_steps: int32 [4], replicated, may hold values from 1 to 2, as said below
- mode_weight: float32 [4], replicated, may hold values from 0.05 to 0.25
- occupation: float32 [4], replicated, may hold values from 0.1 to 2
- momentum_map: int32 [16, 16], replicated, may hold values from 0 to 15, as said below
Outputs:
- self_energy: bfloat16 [16, 16, 2, 512, 512], P(None, 'energy', None, 'mom')
- density: float32 [512, 16, 2, 512], P('energy', 'mom')
Inputs may be any that keep to these rules, and one draw needn't show every extreme that they name: `shift_steps`: some entry equals 2. `momentum_map`: every row and every column holds each of the 16 momentum indices once.
All inputs are finite; a program needn't handle non-finite values.
Results may differ from a plain program's by a relative error of at most 0.02.
Values may be sent and summed in bfloat16 or wider, within the bound.
No kernel may reach another device: no remote copies, remote signals or barrier semaphores. Data moves between devices by JAX's collectives and lax.ppermute only.
A program may use at most 192 MiB of HBM per device.

v0:
```python
import functools

import jax
import jax.numpy as jnp
from jax import lax
from jax.experimental import pallas as pl
from jax.experimental.pallas import tpu as pltpu
from jax.sharding import PartitionSpec as P


SHIFT_MAX = 2
F32 = jnp.float32
BF16 = jnp.bfloat16


def params(**kw):
    return pltpu.CompilerParams(vmem_limit_bytes=56 * 1024 * 1024, **kw)


def cost(flops, nbytes):
    return pl.CostEstimate(flops=int(flops), bytes_accessed=int(nbytes), transcendentals=0)


def dot_nt(a, b):
    return lax.dot_general(a, b, (((1,), (1,)), ((), ())), preferred_element_type=F32)


def dot_nn(a, b):
    return lax.dot_general(a, b, (((1,), (0,)), ((), ())), preferred_element_type=F32)


def row_col(rows, cols):
    return lax.broadcasted_iota(jnp.int32, (rows, cols), 0), lax.broadcasted_iota(jnp.int32, (rows, cols), 1)


def lesser_kernel(sel, g_ref, gamma_ref, out_ref):
    n = g_ref.shape[-1]
    half = n // 2
    e = pl.program_id(0)
    gamma = gamma_ref[0, pl.ds(e, 1), :]
    g_re, g_im = g_ref[0, 0, 0], g_ref[0, 0, 1]
    s_re = (g_re.astype(F32) * gamma).astype(BF16)
    s_im = (g_im.astype(F32) * gamma).astype(BF16)
    row, col = row_col(half, half)

    def real(i, j):
        i, j = slice(i * half, (i + 1) * half), slice(j * half, (j + 1) * half)
        return dot_nt(s_re[i], g_re[j]) + dot_nt(s_im[i], g_im[j])

    def imag(i, j):
        i, j = slice(i * half, (i + 1) * half), slice(j * half, (j + 1) * half)
        return dot_nt(s_im[i], g_re[j]) - dot_nt(s_re[i], g_im[j])

    for d in range(2):
        out_ref[0, d * half:(d + 1) * half, d * half:(d + 1) * half] = jnp.where(
            col >= row, real(d, d), imag(d, d)).astype(BF16)
    out_ref[0, :half, half:] = real(0, 1).astype(BF16)
    out_ref[0, half:, :half] = imag(1, 0).astype(BF16)


def lesser_packed(which, green, broadening):
    _, le, _, n, _ = green.shape
    return pl.pallas_call(
        lesser_kernel,
        out_shape=jax.ShapeDtypeStruct((le, n, n), BF16),
        grid_spec=pltpu.PrefetchScalarGridSpec(
            num_scalar_prefetch=1,
            grid=(le,),
            in_specs=[
                pl.BlockSpec((1, 1, 2, n, n), lambda e, sel: (sel[0], e, 0, 0, 0)),
                pl.BlockSpec((1, le, n), lambda e, sel: (sel[0], 0, 0)),
            ],
            out_specs=pl.BlockSpec((1, n, n), lambda e, sel: (e, 0, 0)),
        ),
        compiler_params=params(),
        cost_estimate=cost(le * 6 * n**3, le * n * n * 6),
        name="lesser",
    )(which[None], green, broadening)


def place_kernel(where, c_ref, *refs):
    full_ref, turned_ref = refs[-2:]
    full_ref[...] = c_ref[...]
    for q in range(c_ref.shape[0]):
        turned_ref[q] = c_ref[q].T


def place_coupling(where, piece, held):
    nk, rows, n = piece.shape
    each = 4
    alias = [] if held is None else list(held)
    return pl.pallas_call(
        place_kernel,
        out_shape=[jax.ShapeDtypeStruct((nk, n, n), BF16)] * 2,
        grid_spec=pltpu.PrefetchScalarGridSpec(
            num_scalar_prefetch=1,
            grid=(nk // each,),
            in_specs=[pl.BlockSpec((each, rows, n), lambda q, w: (q, 0, 0))]
            + [pl.BlockSpec(memory_space=pl.ANY)] * len(alias),
            out_specs=[
                pl.BlockSpec((each, rows, n), lambda q, w: (q, w[0], 0)),
                pl.BlockSpec((each, n, rows), lambda q, w: (q, 0, w[0])),
            ],
        ),
        input_output_aliases={2: 0, 3: 1} if alias else {},
        compiler_params=params(),
        cost_estimate=cost(nk * rows * n * 4, nk * rows * n * 6),
        name="place",
    )(where[None], piece, *alias)


def source_kernel(odd, w_ref, keep, recv, kz, rz, *refs):
    le = keep.shape[0]
    outs = refs[-2 * le:]

    def emit(order):
        line = [(ref, e) for ref in order for e in range(le)]
        for e in range(le):
            for ref, target in ((keep, outs[e]), (recv, outs[le + e])):
                at = [i for i, held in enumerate(order) if held is ref][0] * le + e
                total = None
                for s in range(1, SHIFT_MAX + 1):
                    for j, sign in ((0, s), (1, -s)):
                        source, index = line[at + sign]
                        term = w_ref[2 * (s - 1) + j] * source[index].astype(F32)
                        total = term if total is None else total + term
                target[0] = total.astype(BF16)

    @pl.when(odd[0] == 0)
    def _():
        emit((rz, keep, recv, kz))

    @pl.when(odd[0] == 1)
    def _():
        emit((kz, recv, keep, rz))


def sources(odd, weights, j, hk, keep, recv, kz, rz, held):
    le, n, _ = keep.shape
    rows = n // 4
    big = pl.BlockSpec((le, rows, n), lambda r, *_: (0, r, 0))
    first = pl.BlockSpec((1, rows, n), lambda r, *_: (0, r, 0))
    later = pl.BlockSpec((1, rows, n), lambda r, *_: (j, r, 0))
    shapes = [(1 if e == 0 else hk, n, n) for e in range(le)] * 2
    specs = [first if e == 0 else later for e in range(le)] * 2
    alias = {}
    extra = []
    if held is not None:
        for at, value in enumerate(held):
            if at % le:
                alias[6 + len(extra)] = at
                extra.append(value)
    return pl.pallas_call(
        source_kernel,
        out_shape=[jax.ShapeDtypeStruct(shape, BF16) for shape in shapes],
        grid_spec=pltpu.PrefetchScalarGridSpec(
            num_scalar_prefetch=2,
            grid=(n // rows,),
            in_specs=[big] * 4 + [pl.BlockSpec(memory_space=pl.ANY)] * len(extra),
            out_specs=specs,
        ),
        input_output_aliases=alias,
        compiler_params=params(),
        cost_estimate=cost(le * n * n * 16, le * n * n * 12),
        name="source",
    )(odd[None], weights, keep, recv, kz, rz, *extra)


def home_kernel(lk, pieces, slots, *refs):
    ins, (c_ref, ct_ref, x_ref, y_ref, q_ref) = refs[:pieces], refs[pieces:]
    each, rows, n = ins[0].shape
    count = pieces * each
    for s in range(pieces):
        for j in range(each):
            q_ref[s * each + j] = ins[s][j]
    tr, tc = 16, 256

    def tile(index, _):
        r = pl.ds(pl.multiple_of((index // (n // tc)) * tr, tr), tr)
        m = pl.ds(pl.multiple_of((index % (n // tc)) * tc, tc), tc)
        xs, ys = [None] * lk, [None] * lk
        for q in range(0, count, 4):
            px, py = [None] * lk, [None] * lk
            for p in (q, q + 2):
                c, ct = [c_ref[p + i, r, m] for i in range(2)], [ct_ref[p + i, r, m] for i in range(2)]
                for k in range(lk):
                    v = [q_ref[slots[k * count + p + i], r, m] for i in range(2)]
                    x, y = c[0] * v[0] + c[1] * v[1], ct[0] * v[0] + ct[1] * v[1]
                    px[k] = x if p == q else px[k] + x
                    py[k] = y if p == q else py[k] + y
            for k in range(lk):
                xs[k] = px[k] if q == 0 else xs[k] + px[k]
                ys[k] = py[k] if q == 0 else ys[k] + py[k]
        for k in range(lk):
            x_ref[k, r, m] = xs[k]
            y_ref[k, r, m] = ys[k]
        return 0

    lax.fori_loop(0, (rows // tr) * (n // tc), tile, 0)


def home_blocks(slots, pieces, full, turned, lk):
    each, n, _ = pieces[0].shape
    count = each * len(pieces)
    rows = n // 8
    block = lambda lead: pl.BlockSpec((lead, rows, n), lambda g, s: (0, g, 0))
    return pl.pallas_call(
        functools.partial(home_kernel, lk, len(pieces)),
        out_shape=[jax.ShapeDtypeStruct((lk, n, n), BF16)] * 2,
        grid_spec=pltpu.PrefetchScalarGridSpec(
            num_scalar_prefetch=1,
            grid=(n // rows,),
            in_specs=[block(each)] * len(pieces) + [block(count), block(count)],
            out_specs=[block(lk), block(lk)],
            scratch_shapes=[pltpu.VMEM((count, rows, n), BF16)],
        ),
        compiler_params=params(),
        cost_estimate=cost(4 * lk * count * n * n, n * n * (6 * count + 4 * lk)),
        name="home",
    )(slots, *pieces, full, turned)


def rows_kernel(pieces, mine, slots, *refs):
    a_refs, b_refs, refs = refs[:pieces], refs[pieces:2 * pieces], refs[2 * pieces:]
    c_ref, out_ref, re_ref, im_ref = (refs[0],) + refs[-3:]
    each, rows, cols = a_refs[0].shape
    count = pieces * each
    row, col = row_col(rows, cols)
    above = (col - row) + (pl.program_id(0) * cols - mine[0] * rows)
    for s in range(pieces):
        for j in range(each):
            a, b = a_refs[s][j].astype(F32), b_refs[s][j].astype(F32).T
            re_ref[s * each + j] = jnp.where(above >= 0, a, b).astype(BF16)
            im_ref[s * each + j] = jnp.where(above < 0, a, jnp.where(above > 0, -b, 0.0)).astype(BF16)
    tr, kg, tc = 16, 4, 256
    wide = cols // tc

    def tile(index, _):
        r = pl.ds(pl.multiple_of(((index // wide) % (rows // tr)) * tr, tr), tr)
        m = pl.ds(pl.multiple_of((index % wide) * tc, tc), tc)
        k0 = (index // (wide * (rows // tr))) * kg
        us, vs = [None] * kg, [None] * kg
        for q in range(0, count, 4):
            pu, pv = [None] * kg, [None] * kg
            for p in (q, q + 2):
                c = [c_ref[p + i, r, m] for i in range(2)]
                for k in range(kg):
                    slot = [slots[(k0 + k) * count + p + i] for i in range(2)]
                    u = c[0] * re_ref[slot[0], r, m] + c[1] * re_ref[slot[1], r, m]
                    v = c[0] * im_ref[slot[0], r, m] + c[1] * im_ref[slot[1], r, m]
                    pu[k] = u if p == q else pu[k] + u
                    pv[k] = v if p == q else pv[k] + v
            for k in range(kg):
                us[k] = pu[k] if q == 0 else us[k] + pu[k]
                vs[k] = pv[k] if q == 0 else vs[k] + pv[k]
        for k in range(kg):
            out_ref[k0 + k, 0, 0, r, m] = us[k]
            out_ref[k0 + k, 0, 1, r, m] = vs[k]
        return 0

    lax.fori_loop(0, wide * (rows // tr) * (count // kg), tile, 0)


def own_rows(mine, slots, pieces, coupling, energy, le, held):
    each, n, _ = pieces[0].shape
    count, rows, _ = coupling.shape
    cols = n // 2
    alias = [] if held is None else [held]
    in_specs = (
        [pl.BlockSpec((each, rows, cols), lambda t, mine, slots: (0, mine[0], t))] * len(pieces)
        + [pl.BlockSpec((each, cols, rows), lambda t, mine, slots: (0, t, mine[0]))] * len(pieces)
        + [pl.BlockSpec((count, rows, cols), lambda t, mine, slots: (0, 0, t))]
        + [pl.BlockSpec(memory_space=pl.ANY)] * len(alias)
    )
    return pl.pallas_call(
        functools.partial(rows_kernel, len(pieces)),
        out_shape=jax.ShapeDtypeStruct((count, le, 2, rows, n), BF16),
        grid_spec=pltpu.PrefetchScalarGridSpec(
            num_scalar_prefetch=2,
            grid=(n // cols,),
            in_specs=in_specs,
            out_specs=pl.BlockSpec((count, 1, 2, rows, cols), lambda t, mine, slots: (0, energy, 0, 0, t)),
            scratch_shapes=[pltpu.VMEM((count, rows, cols), BF16)] * 2,
        ),
        input_output_aliases={2 + len(in_specs) - 1: 0} if alias else {},
        compiler_params=params(),
        cost_estimate=cost(4 * count * count * rows * n, rows * n * count * 10),
        name="rows",
    )(mine[None], slots, *pieces, *pieces, coupling, *alias)


def density_terms(energy, g_ref, gamma_ref, x_ref, y_ref):
    n = g_ref.shape[-1]
    gamma = gamma_ref[0, energy:energy + 1, :]
    g_re, g_im = g_ref[0, 0, 0], g_ref[0, 0, 1]
    row, col = row_col(n, n)
    x, yt = x_ref[0].astype(F32), y_ref[0].astype(F32).T
    s_re = jnp.where(col >= row, x, yt).astype(BF16)
    s_im = jnp.where(col < row, x, jnp.where(col > row, -yt, 0.0)).astype(BF16)
    scaled_re = (g_re.astype(F32) * gamma).astype(BF16).astype(F32)
    scaled_im = (g_im.astype(F32) * gamma).astype(BF16).astype(F32)
    m_re = (dot_nn(g_re, s_re) - dot_nn(g_im, s_im) + scaled_re).astype(BF16)
    m_im = (dot_nn(g_re, s_im) + dot_nn(g_im, s_re) + scaled_im).astype(BF16)
    return dot_nt(m_re, g_re) + dot_nt(m_im, g_im), dot_nt(m_im, g_re) - dot_nt(m_re, g_im)


def first_density_kernel(energy, first, g_ref, gamma_ref, x_ref, y_ref, *refs):
    for c, d in enumerate(density_terms(energy, g_ref, gamma_ref, x_ref, y_ref)):
        refs[-1][0, c] = d if first else d + refs[0][0, c]


def first_density(energy, green, broadening, x, y, held):
    lk, le, _, n, _ = green.shape
    alias = [] if held is None else [held]
    pair = pl.BlockSpec((1, 2, n, n), lambda k: (k, 0, 0, 0))
    one = pl.BlockSpec((1, n, n), lambda k: (k, 0, 0))
    return pl.pallas_call(
        functools.partial(first_density_kernel, energy, held is None),
        out_shape=jax.ShapeDtypeStruct((lk, 2, n, n), F32),
        grid=(lk,),
        in_specs=[
            pl.BlockSpec((1, 1, 2, n, n), lambda k: (k, energy, 0, 0, 0)),
            pl.BlockSpec((1, le, n), lambda k: (k, 0, 0)),
            one,
            one,
        ] + [pair] * len(alias),
        out_specs=pair,
        compiler_params=params(),
        cost_estimate=cost(16 * lk * n**3, lk * n * n * 20),
        name="density",
    )(green, broadening, x, y, *alias)


def last_density_kernel(scale, energy, odd, g_ref, gamma_ref, x_ref, y_ref, held_ref, keep_ref, send_ref, d_ref):
    groups, _, rows, _ = keep_ref.shape
    for c, d in enumerate(density_terms(energy, g_ref, gamma_ref, x_ref, y_ref)):
        d_ref[c] = (d + held_ref[0, c]) * scale
        for g in range(groups):
            mine = pl.multiple_of((2 * g + odd[0]) * rows, rows)
            other = pl.multiple_of((2 * g + 1 - odd[0]) * rows, rows)
            keep_ref[g, c] = d_ref[c, pl.ds(mine, rows), :].astype(BF16)
            send_ref[g, c] = d_ref[c, pl.ds(other, rows), :].astype(BF16)


def last_density(scale, energy, k, groups, odd, green, broadening, x, y, held):
    _, le, _, n, _ = green.shape
    rows = n // (2 * groups)
    one = pl.BlockSpec((1, n, n), lambda i, odd: (k, 0, 0))
    out = pl.BlockSpec((groups, 2, rows, n), lambda i, odd: (0, 0, 0, 0))
    return pl.pallas_call(
        functools.partial(last_density_kernel, scale, energy),
        out_shape=[jax.ShapeDtypeStruct((groups, 2, rows, n), BF16)] * 2,
        grid_spec=pltpu.PrefetchScalarGridSpec(
            num_scalar_prefetch=1,
            grid=(1,),
            in_specs=[
                pl.BlockSpec((1, 1, 2, n, n), lambda i, odd: (k, energy, 0, 0, 0)),
                pl.BlockSpec((1, le, n), lambda i, odd: (k, 0, 0)),
                one,
                one,
                pl.BlockSpec((1, 2, n, n), lambda i, odd: (k, 0, 0, 0)),
            ],
            out_specs=[out, out],
            scratch_shapes=[pltpu.VMEM((2, n, n), F32)],
        ),
        compiler_params=params(),
        cost_estimate=cost(16 * n**3, n * n * 20),
        name="density",
    )(odd[None], green, broadening, x, y, held)


def pair_sum_kernel(group, keep_ref, recv_ref, *outs):
    groups = len(outs)
    for d in range(groups):
        at = lax.rem(group[0] + d, groups)
        outs[d][...] = (keep_ref[at].astype(F32) + recv_ref[at].astype(F32)).astype(BF16)


def pair_sum(group, keep, recv):
    groups = keep.shape[0]
    vmem = pl.BlockSpec(memory_space=pltpu.VMEM)
    return pl.pallas_call(
        pair_sum_kernel,
        out_shape=[jax.ShapeDtypeStruct(keep.shape[1:], BF16)] * groups,
        in_specs=[pl.BlockSpec(memory_space=pltpu.SMEM), vmem, vmem],
        out_specs=[vmem] * groups,
        compiler_params=params(),
        cost_estimate=cost(keep.size, keep.size * 6),
        name="pairsum",
    )(group[None], keep, recv)


def staged(green_ret, broadening, coupling, shift_steps, mode_weight, occupation, momentum_map):
    lk, le, _, _, _ = green_ret.shape
    ne, nm = lax.axis_size("energy"), lax.axis_size("mom")
    if le != SHIFT_MAX or lk % 2 or ne % 2 or nm & (nm - 1):
        raise ValueError("unsupported sizes")
    hk, groups = lk // 2, ne // 2
    me, mine = lax.axis_index("energy").astype(jnp.int32), lax.axis_index("mom").astype(jnp.int32)
    odd, group = me & 1, me >> 1
    pairs = [(i, i ^ 1) for i in range(ne)]
    away = [(i, i + (2 if i % 2 else -2)) for i in range(ne) if 0 <= i + (2 if i % 2 else -2) < ne]
    across = [(i, i + (-2 if i % 2 else 2)) for i in range(ne) if 0 <= i + (-2 if i % 2 else 2) < ne]
    strides = []
    while (nm >> (len(strides) + 1)) > 0:
        strides.append(nm >> (len(strides) + 1))

    def over_energy(x, perm):
        return lax.ppermute(x, "energy", perm)

    def swap(x, stride):
        return lax.ppermute(x, "mom", [(i, i ^ stride) for i in range(nm)])

    def spread(x):
        held = [x]
        for s in strides:
            held = held + [swap(piece, s) for piece in held]
        return held

    order = [0]
    for s in strides:
        order = order + [o ^ s for o in order]

    weights = []
    for s in range(1, SHIFT_MAX + 1):
        held = shift_steps == s
        weights.append(jnp.sum(jnp.where(held, mode_weight * (occupation + 1.0), 0.0)))
        weights.append(jnp.sum(jnp.where(held, mode_weight * occupation, 0.0)))
    weights = jnp.stack(weights)

    owner, inner = momentum_map // lk, momentum_map % lk
    place = jnp.zeros_like(owner)
    for at, o in enumerate(order):
        place = jnp.where((owner ^ mine) == o, at, place)
    slots = (place * lk + ((inner // hk) ^ odd) * hk + inner % hk).astype(jnp.int32)
    own_slots = lax.dynamic_slice_in_dim(slots, mine * lk, lk, 0).reshape(-1)
    all_slots = slots.reshape(-1)

    coupling_pieces = spread(coupling)

    send = [lesser_packed((1 - odd) * hk + j, green_ret, broadening) for j in range(hk)]
    recv = [over_energy(send[j], pairs) for j in range(hk)]
    keep = [lesser_packed(odd * hk + j, green_ret, broadening) for j in range(hk)]
    kz = [over_energy(keep[j], away) for j in range(hk)]
    rz = [over_energy(recv[j], across) for j in range(hk)]
    got, last = [], None
    for j in range(hk):
        last = sources(odd, weights, j, hk, keep[j], recv[j], kz[j], rz[j], last)
        got.append(last)

    placed = None
    for at in sorted(range(nm), key=lambda a: (a & 1, a)):
        placed = place_coupling(mine ^ order[at], coupling_pieces[at], placed)
    full, turned = placed

    held_rows, held_density = None, None
    scale = 1.0 / (le * ne)
    late = []
    for e in range(le):
        use = [got[j] for j in range(hk)] if e == 0 else [last]
        fresh = [spread(part[e]) for part in use]
        back = [spread(over_energy(part[le + e], pairs)) for part in use]
        pieces = [part[at] for at in range(nm) for part in fresh + back]
        x, y = home_blocks(own_slots, pieces, full, turned, lk)
        if e < le - 1:
            held_density = first_density(e, green_ret, broadening, x, y, held_density)
        else:
            for k in range(lk):
                kept, sent = last_density(
                    scale, e, k, groups, odd, green_ret, broadening, x, y, held_density)
                other = over_energy(sent, pairs)
                parts = pair_sum(group, kept, other)
                total = parts[0].astype(F32)
                for d in range(1, groups):
                    perm = [(i, (i + 2 * d) % ne) for i in range(ne)]
                    total = total + over_energy(parts[d], perm).astype(F32)
                late.append(total)
        held_rows = own_rows(mine, all_slots, pieces, coupling, e, le, held_rows)
    density = jnp.transpose(jnp.stack(late), (2, 0, 1, 3))
    return held_rows, density


def solution(mesh):
    return jax.shard_map(
        staged,
        mesh=mesh,
        in_specs=(
            P("mom", "energy", None, None, None),
            P("mom", "energy", None),
            P(None, "mom", None),
            P(),
            P(),
            P(),
            P(),
        ),
        out_specs=(P(None, "energy", None, "mom", None), P("energy", "mom", None, None)),
        check_vma=False,
    )
```

profile of v0, /device:TPU:0, one launch (start us, length us, event | category | flops | bytes accessed | tf_op | source)
XLA Modules:
  0.0 360.1 jit_solution(16134007935540338587)
XLA Ops:
  0.6 4.1 %lesser.7 = bf16[2,512,512]{2,1,0:T(8,128)(2,1)} custom-call(s32[1]{0:T(128)} %bitcast.9.sel, bf16[4,2,2,512,512]{4,3,2,1,0:T(8,128)(2,1)} %g_ref.17, f32[4,2,512]{2,1,0:T(2,128)} %gamma_ref.17), custom_call_target="tpu_custom_call" | custom-call | flops 1610612736 | bytes 3145728 | tf_op jit(solution)/shard_map/lesser/pallas_call | solution.py:63
  4.8 3.0 collective-permute-start.3
  7.7 4.3 %lesser.6.keep = bf16[2,512,512]{2,1,0:T(8,128)(2,1)} custom-call(s32[1]{0:T(128)} %bitcast.8.sel, bf16[4,2,2,512,512]{4,3,2,1,0:T(8,128)(2,1)} %g_ref.17, f32[4,2,512]{2,1,0:T(2,128)} %gamma_ref.17), custom_call_target="tpu_custom_call" | custom-call | flops 1610612736 | bytes 3145728 | tf_op jit(solution)/shard_map/lesser/pallas_call | solution.py:63
  13.3 4.1 %lesser.5 = bf16[2,512,512]{2,1,0:T(8,128)(2,1)} custom-call(s32[1]{0:T(128)} %bitcast.7.sel, bf16[4,2,2,512,512]{4,3,2,1,0:T(8,128)(2,1)} %g_ref.17, f32[4,2,512]{2,1,0:T(2,128)} %gamma_ref.17), custom_call_target="tpu_custom_call" | custom-call | flops 1610612736 | bytes 3145728 | tf_op jit(solution)/shard_map/lesser/pallas_call | solution.py:63
  17.4 3.7 %collective-permute-start = (bf16[2,512,512]{2,1,0:T(8,128)(2,1)}, bf16[2,512,512]{2,1,0:T(8,128)(2,1)}, u32[]{:S(2)}, u32[]{:S(2)}) collective-permute-start(bf16[2,512,512]{2,1,0:T(8,128)(2,1)} %lesser.5), channel_id=1, source_target_pairs={{0,4},{4,0},{8,12},{12,8},{16,20},{20,16},{24,28},{28,24},{1,5},{5... | collective-permute-start | bytes 3145736 | tf_op jit(solution)/shard_map/ppermute | solution.py:409
  22.6 9.3 %collective-permute-done.3.recv = bf16[2,512,512]{2,1,0:T(8,128)(2,1)S(1)} collective-permute-done((bf16[2,512,512]{2,1,0:T(8,128)(2,1)}, bf16[2,512,512]{2,1,0:T(8,128)(2,1)S(1)}, u32[]{:S(2)}, u32[]{:S(2)}) %collective-permute-start.3) | collective-permute-done | bytes 1048608 | tf_op jit(solution)/shard_map/ppermute | solution.py:409
  32.0 4.0 %collective-permute-start.5 = (bf16[2,512,512]{2,1,0:T(8,128)(2,1)S(1)}, bf16[2,512,512]{2,1,0:T(8,128)(2,1)S(1)}, u32[]{:S(2)}, u32[]{:S(2)}) collective-permute-start(bf16[2,512,512]{2,1,0:T(8,128)(2,1)S(1)} %collective-permute-done.3.recv), channel_id=1, source_target_pairs={{0,8},{8,16},{12,4},{16,24},{20,12},{28,20},{1,9},{9,17},{13,5},{1... | collective-permute-start | bytes 3145736 | tf_op jit(solution)/shard_map/ppermute | solution.py:409
  36.0 4.1 %lesser.4.keep = bf16[2,512,512]{2,1,0:T(8,128)(2,1)} custom-call(s32[1]{0:T(128)} %bitcast.6.sel, bf16[4,2,2,512,512]{4,3,2,1,0:T(8,128)(2,1)} %g_ref.17, f32[4,2,512]{2,1,0:T(2,128)} %gamma_ref.17), custom_call_target="tpu_custom_call" | custom-call | flops 1610612736 | bytes 3145728 | tf_op jit(solution)/shard_map/lesser/pallas_call | solution.py:63
  41.4 12.3 %collective-permute-done.recv = bf16[2,512,512]{2,1,0:T(8,128)(2,1)} collective-permute-done((bf16[2,512,512]{2,1,0:T(8,128)(2,1)}, bf16[2,512,512]{2,1,0:T(8,128)(2,1)}, u32[]{:S(2)}, u32[]{:S(2)}) %collective-permute-start) | collective-permute-done | bytes 1048608 | tf_op jit(solution)/shard_map/ppermute | solution.py:409
  53.7 3.9 %collective-permute-start.2 = (bf16[2,512,512]{2,1,0:T(8,128)(2,1)}, bf16[2,512,512]{2,1,0:T(8,128)(2,1)S(1)}, u32[]{:S(2)}, u32[]{:S(2)}) collective-permute-start(bf16[2,512,512]{2,1,0:T(8,128)(2,1)} %collective-permute-done.recv), channel_id=1, source_target_pairs={{0,8},{8,16},{12,4},{16,24},{20,12},{28,20},{1,9},{9,17},{13,5},{1... | collective-permute-start | bytes 3145736 | tf_op jit(solution)/shard_map/ppermute | solution.py:409
  58.4 3.2 pad_maximum_fusion.w_ref
  62.5 5.6 %source.2 = (bf16[1,512,512]{2,1,0:T(8,128)(2,1)}, bf16[2,512,512]{2,1,0:T(8,128)(2,1)}, bf16[1,512,512]{2,1,0:T(8,128)(2,1)}, bf16[2,512,512]{2,1,0:T(8,128)(2,1)}) custom-call(s32[1]{0:T(128)} %bitcast.1.odd, f32[4]{0:T(128)} %pad_maximum_fusion.w_ref, bf16[2,512,512]{2,1,0:T(8,128)(2,1)} %lesser.6.keep, bf16[2,512,512]{2,1,0:T(8,128)(2,1)} %copy-done.12, ...), custom_call_target="tpu_custom_call" | custom-call | flops 8388608 | bytes 6291456 | tf_op jit(solution)/shard_map/source/pallas_call | solution.py:153
  68.1 11.2 %collective-permute-done.2.rz = bf16[2,512,512]{2,1,0:T(8,128)(2,1)S(1)} collective-permute-done((bf16[2,512,512]{2,1,0:T(8,128)(2,1)}, bf16[2,512,512]{2,1,0:T(8,128)(2,1)S(1)}, u32[]{:S(2)}, u32[]{:S(2)}) %collective-permute-start.2) | collective-permute-done | bytes 1048608 | tf_op jit(solution)/shard_map/ppermute | solution.py:409
  80.2 5.6 %source.3 = (bf16[1,512,512]{2,1,0:T(8,128)(2,1)}, bf16[2,512,512]{2,1,0:T(8,128)(2,1)}, bf16[1,512,512]{2,1,0:T(8,128)(2,1)}, bf16[2,512,512]{2,1,0:T(8,128)(2,1)}) custom-call(s32[1]{0:T(128)} %bitcast.1.odd, f32[4]{0:T(128)} %pad_maximum_fusion.w_ref, bf16[2,512,512]{2,1,0:T(8,128)(2,1)} %lesser.4.keep, ...), custom_call_target="tpu_custom_call", output_to_operand_aliasing={{1}: (6, {}), {3}: (7, {})} | custom-call | flops 8388608 | bytes 6291456 | tf_op jit(solution)/shard_map/source/pallas_call | solution.py:153
  85.8 2.3 collective-permute-start.14
  91.7 9.5 %collective-permute-done.14.refs_3_.refs_19_ = bf16[1,512,512]{2,1,0:T(8,128)(2,1)S(1)} collective-permute-done((bf16[1,512,512]{2,1,0:T(8,128)(2,1)}, bf16[1,512,512]{2,1,0:T(8,128)(2,1)S(1)}, u32[]{:S(2)}, u32[]{:S(2)}) %collective-permute-start.14) | collective-permute-done | bytes 524320 | tf_op jit(solution)/shard_map/ppermute | solution.py:409
  103.2 9.2 %collective-permute-done.13.refs_2_.refs_18_ = bf16[1,512,512]{2,1,0:T(8,128)(2,1)} collective-permute-done((bf16[1,512,512]{2,1,0:T(8,128)(2,1)}, bf16[1,512,512]{2,1,0:T(8,128)(2,1)}, u32[]{:S(2)}, u32[]{:S(2)}) %collective-permute-start.13) | collective-permute-done | bytes 524320 | tf_op jit(solution)/shard_map/ppermute | solution.py:409
  112.5 23.4 %collective-permute-done.15.refs_4_.refs_20_ = bf16[1,512,512]{2,1,0:T(8,128)(2,1)S(1)} collective-permute-done((bf16[1,512,512]{2,1,0:T(8,128)(2,1)}, bf16[1,512,512]{2,1,0:T(8,128)(2,1)S(1)}, u32[]{:S(2)}, u32[]{:S(2)}) %collective-permute-start.15) | collective-permute-done | bytes 524320 | tf_op jit(solution)/shard_map/ppermute | solution.py:412
  138.4 11.0 %collective-permute-done.18.refs_7_.refs_23_ = bf16[1,512,512]{2,1,0:T(8,128)(2,1)} collective-permute-done((bf16[1,512,512]{2,1,0:T(8,128)(2,1)S(1)}, bf16[1,512,512]{2,1,0:T(8,128)(2,1)}, u32[]{:S(2)}, u32[]{:S(2)}) %collective-permute-start.18) | collective-permute-done | bytes 524320 | tf_op jit(solution)/shard_map/ppermute | solution.py:412
  149.4 2.4 collective-permute-start.8
  152.5 8.2 %collective-permute-done.17.refs_6_.refs_22_ = bf16[1,512,512]{2,1,0:T(8,128)(2,1)} collective-permute-done((bf16[1,512,512]{2,1,0:T(8,128)(2,1)}, bf16[1,512,512]{2,1,0:T(8,128)(2,1)}, u32[]{:S(2)}, u32[]{:S(2)}) %collective-permute-start.17) | collective-permute-done | bytes 524320 | tf_op jit(solution)/shard_map/ppermute | solution.py:412
  163.5 15.3 %collective-permute-done.8.refs_3_.refs_11_ = bf16[2,512,512]{2,1,0:T(8,128)(2,1)S(1)} collective-permute-done((bf16[2,512,512]{2,1,0:T(8,128)(2,1)S(1)}, bf16[2,512,512]{2,1,0:T(8,128)(2,1)S(1)}, u32[]{:S(2)}, u32[]{:S(2)}) %collective-permute-start.8) | collective-permute-done | bytes 1048608 | tf_op jit(solution)/shard_map/ppermute | solution.py:412
  179.6 4.5 %place.4 = (bf16[16,512,512]{2,1,0:T(8,128)(2,1)}, bf16[16,512,512]{2,1,0:T(8,128)(2,1)}) custom-call(s32[1]{0:T(128)} %bitcast.mine.where, bf16[16,128,512]{2,1,0:T(8,128)(2,1)} %c_ref.1), custom_call_target="tpu_custom_call" | custom-call | flops 4194304 | bytes 6291456 | tf_op jit(solution)/shard_map/place/pallas_call | solution.py:92
  184.1 4.6 %place.5 = (bf16[16,512,512]{2,1,0:T(8,128)(2,1)}, bf16[16,512,512]{2,1,0:T(8,128)(2,1)}) custom-call(s32[1]{0:T(128)} %bitcast.13.where, bf16[16,128,512]{2,1,0:T(8,128)(2,1)} %collective-permute-done.29.c_ref, bf16[16,512,512]{2,1,0:T(8,128)(2,1)} %get-tuple-element.54.refs_0_, ...), custom_call_target="tpu_custom_call", output_to_operand_aliasing={{0}: (2, {}), {1}: (3, {})} | custom-call | flops 4194304 | bytes 6291456 | tf_op jit(solution)/shard_map/place/pallas_call | solution.py:92
  188.7 4.6 %place.6 = (bf16[16,512,512]{2,1,0:T(8,128)(2,1)}, bf16[16,512,512]{2,1,0:T(8,128)(2,1)}) custom-call(s32[1]{0:T(128)} %bitcast.12.where, bf16[16,128,512]{2,1,0:T(8,128)(2,1)} %collective-permute-done.27.c_ref, bf16[16,512,512]{2,1,0:T(8,128)(2,1)} %get-tuple-element.56.refs_0_, ...), custom_call_target="tpu_custom_call", output_to_operand_aliasing={{0}: (2, {}), {1}: (3, {})} | custom-call | flops 4194304 | bytes 6291456 | tf_op jit(solution)/shard_map/place/pallas_call | solution.py:92
  193.3 4.5 %place.7 = (bf16[16,512,512]{2,1,0:T(8,128)(2,1)}, bf16[16,512,512]{2,1,0:T(8,128)(2,1)}) custom-call(s32[1]{0:T(128)} %bitcast.11.where, bf16[16,128,512]{2,1,0:T(8,128)(2,1)} %collective-permute-done.28.c_ref, bf16[16,512,512]{2,1,0:T(8,128)(2,1)} %get-tuple-element.58.refs_0_, ...), custom_call_target="tpu_custom_call", output_to_operand_aliasing={{0}: (2, {}), {1}: (3, {})} | custom-call | flops 4194304 | bytes 6291456 | tf_op jit(solution)/shard_map/place/pallas_call | solution.py:92
  197.8 15.1 %home.3 = (bf16[4,512,512]{2,1,0:T(8,128)(2,1)}, bf16[4,512,512]{2,1,0:T(8,128)(2,1)}) custom-call(s32[64]{0:T(128)} %reshape.11.slots, bf16[1,512,512]{2,1,0:T(8,128)(2,1)} %get-tuple-element.50.refs_0_.refs_16_, bf16[1,512,512]{2,1,0:T(8,128)(2,1)} %get-tuple-element.51.refs_1_.refs_17_, bf16[1,512,512]{2,1,0:T(8,128)(2,1)} %collective-permute-done.13.refs_2_.refs_18_, ...), custom_call_target="tpu_custom_call" | custom-call | flops 67108864 | bytes 29360128 | tf_op jit(solution)/shard_map/home/pallas_call | solution.py:207
  212.9 13.0 %density.5.held_ref = f32[4,2,512,512]{3,2,1,0:T(8,128)} custom-call(bf16[4,2,2,512,512]{4,3,2,1,0:T(8,128)(2,1)} %g_ref.17, f32[4,2,512]{2,1,0:T(2,128)} %gamma_ref.17, bf16[4,512,512]{2,1,0:T(8,128)(2,1)} %get-tuple-element.64.x_ref, bf16[4,512,512]{2,1,0:T(8,128)(2,1)} %get-tuple-element.65.y_ref), custom_call_target="tpu_custom_call" | custom-call | flops 8589934592 | bytes 20971520 | tf_op jit(solution)/shard_map/density/pallas_call | solution.py:317
  225.9 15.1 %home.2 = (bf16[4,512,512]{2,1,0:T(8,128)(2,1)}, bf16[4,512,512]{2,1,0:T(8,128)(2,1)}) custom-call(s32[64]{0:T(128)} %reshape.11.slots, bf16[2,512,512]{2,1,0:T(8,128)(2,1)} %get-tuple-element.48.refs_0_.refs_8_, bf16[2,512,512]{2,1,0:T(8,128)(2,1)} %copy-done.1, bf16[2,512,512]{2,1,0:T(8,128)(2,1)} %copy-done.2, bf16[2,512,512]{2,1,0:T(8,128)(2,1)} %copy-done.3, ...), custom_call_target="tpu_custom_call" | custom-call | flops 67108864 | bytes 29360128 | tf_op jit(solution)/shard_map/home/pallas_call | solution.py:207
  241.0 5.8 %density.6 = (bf16[4,2,64,512]{3,2,1,0:T(8,128)(2,1)}, bf16[4,2,64,512]{3,2,1,0:T(8,128)(2,1)}) custom-call(s32[1]{0:T(128)} %bitcast.1.odd, bf16[4,2,2,512,512]{4,3,2,1,0:T(8,128)(2,1)} %g_ref.17, f32[4,2,512]{2,1,0:T(2,128)} %gamma_ref.17, bf16[4,512,512]{2,1,0:T(8,128)(2,1)} %get-tuple-element.62.x_ref, bf16[4,512,512]{2,1,0:T(8,128)(2,1)} %get-tuple-element.63.y_ref, ...), custom_call_target="tpu_custom_call" | custom-call | flops 2147483648 | bytes 5242880 | tf_op jit(solution)/shard_map/density/pallas_call | solution.py:350
  246.7 5.7 %density.7 = (bf16[4,2,64,512]{3,2,1,0:T(8,128)(2,1)}, bf16[4,2,64,512]{3,2,1,0:T(8,128)(2,1)}) custom-call(s32[1]{0:T(128)} %bitcast.1.odd, bf16[4,2,2,512,512]{4,3,2,1,0:T(8,128)(2,1)} %g_ref.17, f32[4,2,512]{2,1,0:T(2,128)} %gamma_ref.17, bf16[4,512,512]{2,1,0:T(8,128)(2,1)} %get-tuple-element.62.x_ref, bf16[4,512,512]{2,1,0:T(8,128)(2,1)} %get-tuple-element.63.y_ref, ...), custom_call_target="tpu_custom_call" | custom-call | flops 2147483648 | bytes 5242880 | tf_op jit(solution)/shard_map/density/pallas_call | solution.py:350
  252.5 5.8 %density.8 = (bf16[4,2,64,512]{3,2,1,0:T(8,128)(2,1)}, bf16[4,2,64,512]{3,2,1,0:T(8,128)(2,1)}) custom-call(s32[1]{0:T(128)} %bitcast.1.odd, bf16[4,2,2,512,512]{4,3,2,1,0:T(8,128)(2,1)} %g_ref.17, f32[4,2,512]{2,1,0:T(2,128)} %gamma_ref.17, bf16[4,512,512]{2,1,0:T(8,128)(2,1)} %get-tuple-element.62.x_ref, bf16[4,512,512]{2,1,0:T(8,128)(2,1)} %get-tuple-element.63.y_ref, ...), custom_call_target="tpu_custom_call" | custom-call | flops 2147483648 | bytes 5242880 | tf_op jit(solution)/shard_map/density/pallas_call | solution.py:350
  262.4 5.8 %density.9 = (bf16[4,2,64,512]{3,2,1,0:T(8,128)(2,1)}, bf16[4,2,64,512]{3,2,1,0:T(8,128)(2,1)}) custom-call(s32[1]{0:T(128)} %bitcast.1.odd, bf16[4,2,2,512,512]{4,3,2,1,0:T(8,128)(2,1)} %g_ref.17, f32[4,2,512]{2,1,0:T(2,128)} %gamma_ref.17, bf16[4,512,512]{2,1,0:T(8,128)(2,1)} %get-tuple-element.62.x_ref, bf16[4,512,512]{2,1,0:T(8,128)(2,1)} %get-tuple-element.63.y_ref, ...), custom_call_target="tpu_custom_call" | custom-call | flops 2147483648 | bytes 5242880 | tf_op jit(solution)/shard_map/density/pallas_call | solution.py:350
  268.2 4.9 %collective-permute-done.30.recv_ref = bf16[4,2,64,512]{3,2,1,0:T(8,128)(2,1)S(1)} collective-permute-done((bf16[4,2,64,512]{3,2,1,0:T(8,128)(2,1)S(1)}, bf16[4,2,64,512]{3,2,1,0:T(8,128)(2,1)S(1)}, u32[]{:S(2)}, u32[]{:S(2)}) %collective-permute-start.30) | collective-permute-done | bytes 524320 | tf_op jit(solution)/shard_map/ppermute | solution.py:409
  275.9 2.1 collective-permute-start.31
  278.0 2.6 collective-permute-start.32
  280.6 3.7 %collective-permute-done.34.recv_ref = bf16[4,2,64,512]{3,2,1,0:T(8,128)(2,1)S(1)} collective-permute-done((bf16[4,2,64,512]{3,2,1,0:T(8,128)(2,1)S(1)}, bf16[4,2,64,512]{3,2,1,0:T(8,128)(2,1)S(1)}, u32[]{:S(2)}, u32[]{:S(2)}) %collective-permute-start.34) | collective-permute-done | bytes 524320 | tf_op jit(solution)/shard_map/ppermute | solution.py:409
  284.3 4.1 %collective-permute-start.33 = (bf16[2,64,512]{2,1,0:T(8,128)(2,1)}, bf16[2,64,512]{2,1,0:T(8,128)(2,1)S(1)}, u32[]{:S(2)}, u32[]{:S(2)}) collective-permute-start(bf16[2,64,512]{2,1,0:T(8,128)(2,1)} %get-tuple-element.71), channel_id=1, source_target_pairs={{0,24},{4,28},{8,0},{12,4},{16,8},{20,12},{24,16},{28,20},{1,25},{... | collective-permute-start | bytes 393224 | tf_op jit(solution)/shard_map/ppermute | solution.py:409
  289.1 15.8 %rows.2.refs_17_ = bf16[16,2,2,128,512]{4,3,2,1,0:T(8,128)(2,1)} custom-call(s32[1]{0:T(128)} %bitcast.mine.where, s32[256]{0:T(256)} %reshape.10.slots, bf16[1,512,512]{2,1,0:T(8,128)(2,1)} %get-tuple-element.50.refs_0_.refs_16_, bf16[1,512,512]{2,1,0:T(8,128)(2,1)} %get-tuple-element.51.refs_1_.refs_17_, ...), custom_call_target="tpu_custom_call" | custom-call | flops 67108864 | bytes 10485760 | tf_op jit(solution)/shard_map/rows/pallas_call | solution.py:275
  304.9 15.3 %rows.3 = bf16[16,2,2,128,512]{4,3,2,1,0:T(8,128)(2,1)} custom-call(s32[1]{0:T(128)} %bitcast.mine.where, s32[256]{0:T(256)} %reshape.10.slots, bf16[2,512,512]{2,1,0:T(8,128)(2,1)} %get-tuple-element.48.refs_0_.refs_8_, bf16[2,512,512]{2,1,0:T(8,128)(2,1)} %copy-done.1, bf16[2,512,512]{2,1,0:T(8,128)(2,1)} %copy-done.2, ...), custom_call_target="tpu_custom_call", output_to_operand_aliasing={{}: (19, {})} | custom-call | flops 67108864 | bytes 10485760 | tf_op jit(solution)/shard_map/rows/pallas_call | solution.py:275
  323.0 2.1 pairsum.6
  328.0 3.1 collective-permute-start.37
  332.5 2.9 collective-permute-start.41
  335.8 4.0 %collective-permute-done.37 = bf16[2,64,512]{2,1,0:T(8,128)(2,1)S(1)} collective-permute-done((bf16[2,64,512]{2,1,0:T(8,128)(2,1)}, bf16[2,64,512]{2,1,0:T(8,128)(2,1)S(1)}, u32[]{:S(2)}, u32[]{:S(2)}) %collective-permute-start.37) | collective-permute-done | bytes 131104 | tf_op jit(solution)/shard_map/ppermute | solution.py:409
  339.8 4.3 %collective-permute-start.44 = (bf16[2,64,512]{2,1,0:T(8,128)(2,1)}, bf16[2,64,512]{2,1,0:T(8,128)(2,1)S(1)}, u32[]{:S(2)}, u32[]{:S(2)}) collective-permute-start(bf16[2,64,512]{2,1,0:T(8,128)(2,1)} %get-tuple-element.88), channel_id=1, source_target_pairs={{0,16},{4,20},{8,24},{12,28},{16,0},{20,4},{24,8},{28,12},{1,17},{... | collective-permute-start | bytes 393224 | tf_op jit(solution)/shard_map/ppermute | solution.py:409
  345.1 3.5 collective-permute-start.45
  348.5 2.6 collective-permute-done.40
  352.1 5.1 %collective-permute-done.44 = bf16[2,64,512]{2,1,0:T(8,128)(2,1)S(1)} collective-permute-done((bf16[2,64,512]{2,1,0:T(8,128)(2,1)}, bf16[2,64,512]{2,1,0:T(8,128)(2,1)S(1)}, u32[]{:S(2)}, u32[]{:S(2)}) %collective-permute-start.44) | collective-permute-done | bytes 131104 | tf_op jit(solution)/shard_map/ppermute | solution.py:409
  (133 shorter events, 38.9 us)
Async XLA Ops:
  4.8 27.2 %collective-permute-start.3 = (bf16[2,512,512]{2,1,0:T(8,128)(2,1)}, bf16[2,512,512]{2,1,0:T(8,128)(2,1)S(1)}, u32[]{:S(2)}, u32[]{:S(2)}) collective-permute-start(bf16[2,512,512]{2,1,0:T(8,128)(2,1)} %lesser.7), channel_id=1, source_target_pairs={{0,4},{4,0},{8,12},{12,8},{16,20},{20,16},{24,28},{28,24},{1,5},{5... | collective-permute-start | bytes 3145736 | tf_op jit(solution)/shard_map/ppermute | solution.py:409
  12.0 28.1 %collective-permute-start.4 = (bf16[2,512,512]{2,1,0:T(8,128)(2,1)}, bf16[2,512,512]{2,1,0:T(8,128)(2,1)}, u32[]{:S(2)}, u32[]{:S(2)}) collective-permute-start(bf16[2,512,512]{2,1,0:T(8,128)(2,1)} %lesser.6.keep), channel_id=1, source_target_pairs={{4,12},{8,0},{12,20},{16,8},{20,28},{24,16},{5,13},{9,1},{13,21},{... | collective-permute-start | bytes 3145736 | tf_op jit(solution)/shard_map/ppermute | solution.py:409
  17.4 36.2 %collective-permute-start = (bf16[2,512,512]{2,1,0:T(8,128)(2,1)}, bf16[2,512,512]{2,1,0:T(8,128)(2,1)}, u32[]{:S(2)}, u32[]{:S(2)}) collective-permute-start(bf16[2,512,512]{2,1,0:T(8,128)(2,1)} %lesser.5), channel_id=1, source_target_pairs={{0,4},{4,0},{8,12},{12,8},{16,20},{20,16},{24,28},{28,24},{1,5},{5... | collective-permute-start | bytes 3145736 | tf_op jit(solution)/shard_map/ppermute | solution.py:409
  21.1 68.5 %collective-permute-start.29 = (bf16[16,128,512]{2,1,0:T(8,128)(2,1)S(1)}, bf16[16,128,512]{2,1,0:T(8,128)(2,1)}, u32[]{:S(2)}, u32[]{:S(2)}) collective-permute-start(bf16[16,128,512]{2,1,0:T(8,128)(2,1)S(1)} %copy-done), channel_id=1, source_target_pairs={{0,1},{1,0},{2,3},{3,2},{4,5},{5,4},{6,7},{7,6},{8,9},{9,8},{10,11... | collective-permute-start | bytes 6291464 | tf_op jit(solution)/shard_map/ppermute | solution.py:412
  21.1 68.5 %collective-permute-start.27 = (bf16[16,128,512]{2,1,0:T(8,128)(2,1)S(1)}, bf16[16,128,512]{2,1,0:T(8,128)(2,1)}, u32[]{:S(2)}, u32[]{:S(2)}) collective-permute-start(bf16[16,128,512]{2,1,0:T(8,128)(2,1)S(1)} %copy-done), channel_id=1, source_target_pairs={{0,2},{1,3},{2,0},{3,1},{4,6},{5,7},{6,4},{7,5},{8,10},{9,11},{10,... | collective-permute-start | bytes 6291464 | tf_op jit(solution)/shard_map/ppermute | solution.py:412
  32.0 29.6 %collective-permute-start.5 = (bf16[2,512,512]{2,1,0:T(8,128)(2,1)S(1)}, bf16[2,512,512]{2,1,0:T(8,128)(2,1)S(1)}, u32[]{:S(2)}, u32[]{:S(2)}) collective-permute-start(bf16[2,512,512]{2,1,0:T(8,128)(2,1)S(1)} %collective-permute-done.3.recv), channel_id=1, source_target_pairs={{0,8},{8,16},{12,4},{16,24},{20,12},{28,20},{1,9},{9,17},{13,5},{1... | collective-permute-start | bytes 3145736 | tf_op jit(solution)/shard_map/ppermute | solution.py:409
  36.0 142.8 %copy-start.21 = (s32[16,16]{1,0:T(8,128)S(1)}, s32[16,16]{1,0:T(8,128)}, u32[]{:S(2)}) copy-start(s32[16,16]{1,0:T(8,128)} %param.13) | copy-start | bytes 3076
  40.1 27.9 %collective-permute-start.1 = (bf16[2,512,512]{2,1,0:T(8,128)(2,1)}, bf16[2,512,512]{2,1,0:T(8,128)(2,1)S(1)}, u32[]{:S(2)}, u32[]{:S(2)}) collective-permute-start(bf16[2,512,512]{2,1,0:T(8,128)(2,1)} %lesser.4.keep), channel_id=1, source_target_pairs={{4,12},{8,0},{12,20},{16,8},{20,28},{24,16},{5,13},{9,1},{13,21},{... | collective-permute-start | bytes 3145736 | tf_op jit(solution)/shard_map/ppermute | solution.py:409
  53.7 25.5 %collective-permute-start.2 = (bf16[2,512,512]{2,1,0:T(8,128)(2,1)}, bf16[2,512,512]{2,1,0:T(8,128)(2,1)S(1)}, u32[]{:S(2)}, u32[]{:S(2)}) collective-permute-start(bf16[2,512,512]{2,1,0:T(8,128)(2,1)} %collective-permute-done.recv), channel_id=1, source_target_pairs={{0,8},{8,16},{12,4},{16,24},{20,12},{28,20},{1,9},{9,17},{13,5},{1... | collective-permute-start | bytes 3145736 | tf_op jit(solution)/shard_map/ppermute | solution.py:409
  85.8 15.3 %collective-permute-start.14 = (bf16[1,512,512]{2,1,0:T(8,128)(2,1)}, bf16[1,512,512]{2,1,0:T(8,128)(2,1)S(1)}, u32[]{:S(2)}, u32[]{:S(2)}) collective-permute-start(bf16[1,512,512]{2,1,0:T(8,128)(2,1)} %get-tuple-element.53), channel_id=1, source_target_pairs={{0,4},{4,0},{8,12},{12,8},{16,20},{20,16},{24,28},{28,24},{1,5},{5... | collective-permute-start | bytes 1572872 | tf_op jit(solution)/shard_map/ppermute | solution.py:409
  88.1 14.5 %collective-permute-start.16 = (bf16[1,512,512]{2,1,0:T(8,128)(2,1)}, bf16[1,512,512]{2,1,0:T(8,128)(2,1)S(1)}, u32[]{:S(2)}, u32[]{:S(2)}) collective-permute-start(bf16[1,512,512]{2,1,0:T(8,128)(2,1)} %get-tuple-element.51.refs_1_.refs_17_), channel_id=1, source_target_pairs={{0,2},{1,3},{2,0},{3,1},{4,6},{5,7},{6,4},{7,5},{8,10},{9,11},{10,... | collective-permute-start | bytes 1572872 | tf_op jit(solution)/shard_map/ppermute | solution.py:412
  89.6 13.0 %collective-permute-start.20 = (bf16[1,512,512]{2,1,0:T(8,128)(2,1)}, bf16[1,512,512]{2,1,0:T(8,128)(2,1)S(1)}, u32[]{:S(2)}, u32[]{:S(2)}) collective-permute-start(bf16[1,512,512]{2,1,0:T(8,128)(2,1)} %get-tuple-element.51.refs_1_.refs_17_), channel_id=1, source_target_pairs={{0,1},{1,0},{2,3},{3,2},{4,5},{5,4},{6,7},{7,6},{8,9},{9,8},{10,11... | collective-permute-start | bytes 1572872 | tf_op jit(solution)/shard_map/ppermute | solution.py:412
  89.6 22.8 %collective-permute-start.13 = (bf16[1,512,512]{2,1,0:T(8,128)(2,1)}, bf16[1,512,512]{2,1,0:T(8,128)(2,1)}, u32[]{:S(2)}, u32[]{:S(2)}) collective-permute-start(bf16[1,512,512]{2,1,0:T(8,128)(2,1)} %get-tuple-element.52), channel_id=1, source_target_pairs={{0,4},{4,0},{8,12},{12,8},{16,20},{20,16},{24,28},{28,24},{1,5},{5... | collective-permute-start | bytes 1572872 | tf_op jit(solution)/shard_map/ppermute | solution.py:409
  89.7 47.7 %collective-permute-start.6 = (bf16[2,512,512]{2,1,0:T(8,128)(2,1)}, bf16[2,512,512]{2,1,0:T(8,128)(2,1)S(1)}, u32[]{:S(2)}, u32[]{:S(2)}) collective-permute-start(bf16[2,512,512]{2,1,0:T(8,128)(2,1)} %get-tuple-element.49), channel_id=1, source_target_pairs={{0,4},{4,0},{8,12},{12,8},{16,20},{20,16},{24,28},{28,24},{1,5},{5... | collective-permute-start | bytes 3145736 | tf_op jit(solution)/shard_map/ppermute | solution.py:409
  101.1 36.8 %collective-permute-start.7 = (bf16[2,512,512]{2,1,0:T(8,128)(2,1)}, bf16[2,512,512]{2,1,0:T(8,128)(2,1)S(1)}, u32[]{:S(2)}, u32[]{:S(2)}) collective-permute-start(bf16[2,512,512]{2,1,0:T(8,128)(2,1)} %get-tuple-element.48.refs_0_.refs_8_), channel_id=1, source_target_pairs={{0,2},{1,3},{2,0},{3,1},{4,6},{5,7},{6,4},{7,5},{8,10},{9,11},{10,... | collective-permute-start | bytes 3145736 | tf_op jit(solution)/shard_map/ppermute | solution.py:412
  102.6 60.5 %collective-permute-start.28 = (bf16[16,128,512]{2,1,0:T(8,128)(2,1)}, bf16[16,128,512]{2,1,0:T(8,128)(2,1)}, u32[]{:S(2)}, u32[]{:S(2)}) collective-permute-start(bf16[16,128,512]{2,1,0:T(8,128)(2,1)} %collective-permute-done.27.c_ref), channel_id=1, source_target_pairs={{0,1},{1,0},{2,3},{3,2},{4,5},{5,4},{6,7},{7,6},{8,9},{9,8},{10,11... | collective-permute-start | bytes 6291464 | tf_op jit(solution)/shard_map/ppermute | solution.py:412
  102.6 33.3 %collective-permute-start.15 = (bf16[1,512,512]{2,1,0:T(8,128)(2,1)}, bf16[1,512,512]{2,1,0:T(8,128)(2,1)S(1)}, u32[]{:S(2)}, u32[]{:S(2)}) collective-permute-start(bf16[1,512,512]{2,1,0:T(8,128)(2,1)} %get-tuple-element.50.refs_0_.refs_16_), channel_id=1, source_target_pairs={{0,2},{1,3},{2,0},{3,1},{4,6},{5,7},{6,4},{7,5},{8,10},{9,11},{10,... | collective-permute-start | bytes 1572872 | tf_op jit(solution)/shard_map/ppermute | solution.py:412
  112.5 24.9 %collective-permute-start.19 = (bf16[1,512,512]{2,1,0:T(8,128)(2,1)}, bf16[1,512,512]{2,1,0:T(8,128)(2,1)S(1)}, u32[]{:S(2)}, u32[]{:S(2)}) collective-permute-start(bf16[1,512,512]{2,1,0:T(8,128)(2,1)} %get-tuple-element.50.refs_0_.refs_16_), channel_id=1, source_target_pairs={{0,1},{1,0},{2,3},{3,2},{4,5},{5,4},{6,7},{7,6},{8,9},{9,8},{10,11... | collective-permute-start | bytes 1572872 | tf_op jit(solution)/shard_map/ppermute | solution.py:412
  135.9 13.6 %collective-permute-start.18 = (bf16[1,512,512]{2,1,0:T(8,128)(2,1)S(1)}, bf16[1,512,512]{2,1,0:T(8,128)(2,1)}, u32[]{:S(2)}, u32[]{:S(2)}) collective-permute-start(bf16[1,512,512]{2,1,0:T(8,128)(2,1)S(1)} %collective-permute-done.14.refs_3_.refs_19_), channel_id=1, source_target_pairs={{0,2},{1,3},{2,0},{3,1},{4,6},{5,7},{6,4},{7,5},{8,10},{9,11},{10,... | collective-permute-start | bytes 1572872 | tf_op jit(solution)/shard_map/ppermute | solution.py:412
  137.4 14.5 %collective-permute-start.24 = (bf16[1,512,512]{2,1,0:T(8,128)(2,1)S(1)}, bf16[1,512,512]{2,1,0:T(8,128)(2,1)S(1)}, u32[]{:S(2)}, u32[]{:S(2)}) collective-permute-start(bf16[1,512,512]{2,1,0:T(8,128)(2,1)S(1)} %collective-permute-done.16.refs_5_.refs_21_), channel_id=1, source_target_pairs={{0,1},{1,0},{2,3},{3,2},{4,5},{5,4},{6,7},{7,6},{8,9},{9,8},{10,11... | collective-permute-start | bytes 1572872 | tf_op jit(solution)/shard_map/ppermute | solution.py:412
  137.4 51.3 %copy-start.1 = (bf16[2,512,512]{2,1,0:T(8,128)(2,1)}, bf16[2,512,512]{2,1,0:T(8,128)(2,1)S(1)}, u32[]{:S(2)}) copy-start(bf16[2,512,512]{2,1,0:T(8,128)(2,1)S(1)} %collective-permute-done.6.refs_1_.refs_9_) | copy-start | bytes 3145732
  137.4 14.5 %collective-permute-start.22 = (bf16[1,512,512]{2,1,0:T(8,128)(2,1)S(1)}, bf16[1,512,512]{2,1,0:T(8,128)(2,1)S(1)}, u32[]{:S(2)}, u32[]{:S(2)}) collective-permute-start(bf16[1,512,512]{2,1,0:T(8,128)(2,1)S(1)} %collective-permute-done.14.refs_3_.refs_19_), channel_id=1, source_target_pairs={{0,1},{1,0},{2,3},{3,2},{4,5},{5,4},{6,7},{7,6},{8,9},{9,8},{10,11... | collective-permute-start | bytes 1572872 | tf_op jit(solution)/shard_map/ppermute | solution.py:412
  137.9 22.8 %collective-permute-start.17 = (bf16[1,512,512]{2,1,0:T(8,128)(2,1)}, bf16[1,512,512]{2,1,0:T(8,128)(2,1)}, u32[]{:S(2)}, u32[]{:S(2)}) collective-permute-start(bf16[1,512,512]{2,1,0:T(8,128)(2,1)} %collective-permute-done.13.refs_2_.refs_18_), channel_id=1, source_target_pairs={{0,2},{1,3},{2,0},{3,1},{4,6},{5,7},{6,4},{7,5},{8,10},{9,11},{10,... | collective-permute-start | bytes 1572872 | tf_op jit(solution)/shard_map/ppermute | solution.py:412
  149.4 29.3 %collective-permute-start.8 = (bf16[2,512,512]{2,1,0:T(8,128)(2,1)S(1)}, bf16[2,512,512]{2,1,0:T(8,128)(2,1)S(1)}, u32[]{:S(2)}, u32[]{:S(2)}) collective-permute-start(bf16[2,512,512]{2,1,0:T(8,128)(2,1)S(1)} %collective-permute-done.6.refs_1_.refs_9_), channel_id=1, source_target_pairs={{0,2},{1,3},{2,0},{3,1},{4,6},{5,7},{6,4},{7,5},{8,10},{9,11},{10,... | collective-permute-start | bytes 3145736 | tf_op jit(solution)/shard_map/ppermute | solution.py:412
  151.9 8.8 %collective-permute-start.23 = (bf16[1,512,512]{2,1,0:T(8,128)(2,1)S(1)}, bf16[1,512,512]{2,1,0:T(8,128)(2,1)S(1)}, u32[]{:S(2)}, u32[]{:S(2)}) collective-permute-start(bf16[1,512,512]{2,1,0:T(8,128)(2,1)S(1)} %collective-permute-done.15.refs_4_.refs_20_), channel_id=1, source_target_pairs={{0,1},{1,0},{2,3},{3,2},{4,5},{5,4},{6,7},{7,6},{8,9},{9,8},{10,11... | collective-permute-start | bytes 1572872 | tf_op jit(solution)/shard_map/ppermute | solution.py:412
  151.9 10.1 %collective-permute-start.21 = (bf16[1,512,512]{2,1,0:T(8,128)(2,1)}, bf16[1,512,512]{2,1,0:T(8,128)(2,1)}, u32[]{:S(2)}, u32[]{:S(2)}) collective-permute-start(bf16[1,512,512]{2,1,0:T(8,128)(2,1)} %collective-permute-done.13.refs_2_.refs_18_), channel_id=1, source_target_pairs={{0,1},{1,0},{2,3},{3,2},{4,5},{5,4},{6,7},{7,6},{8,9},{9,8},{10,11... | collective-permute-start | bytes 1572872 | tf_op jit(solution)/shard_map/ppermute | solution.py:412
  160.7 2.3 collective-permute-start.26
  161.5 36.3 %collective-permute-start.25 = (bf16[1,512,512]{2,1,0:T(8,128)(2,1)}, bf16[1,512,512]{2,1,0:T(8,128)(2,1)}, u32[]{:S(2)}, u32[]{:S(2)}) collective-permute-start(bf16[1,512,512]{2,1,0:T(8,128)(2,1)} %collective-permute-done.17.refs_6_.refs_22_), channel_id=1, source_target_pairs={{0,1},{1,0},{2,3},{3,2},{4,5},{5,4},{6,7},{7,6},{8,9},{9,8},{10,11... | collective-permute-start | bytes 1572872 | tf_op jit(solution)/shard_map/ppermute | solution.py:412
  162.0 63.8 %collective-permute-start.9 = (bf16[2,512,512]{2,1,0:T(8,128)(2,1)}, bf16[2,512,512]{2,1,0:T(8,128)(2,1)}, u32[]{:S(2)}, u32[]{:S(2)}) collective-permute-start(bf16[2,512,512]{2,1,0:T(8,128)(2,1)} %get-tuple-element.48.refs_0_.refs_8_), channel_id=1, source_target_pairs={{0,1},{1,0},{2,3},{3,2},{4,5},{5,4},{6,7},{7,6},{8,9},{9,8},{10,11... | collective-permute-start | bytes 3145736 | tf_op jit(solution)/shard_map/ppermute | solution.py:412
  162.9 62.9 %collective-permute-start.10 = (bf16[2,512,512]{2,1,0:T(8,128)(2,1)S(1)}, bf16[2,512,512]{2,1,0:T(8,128)(2,1)}, u32[]{:S(2)}, u32[]{:S(2)}) collective-permute-start(bf16[2,512,512]{2,1,0:T(8,128)(2,1)S(1)} %collective-permute-done.6.refs_1_.refs_9_), channel_id=1, source_target_pairs={{0,1},{1,0},{2,3},{3,2},{4,5},{5,4},{6,7},{7,6},{8,9},{9,8},{10,11... | collective-permute-start | bytes 3145736 | tf_op jit(solution)/shard_map/ppermute | solution.py:412
  163.1 62.8 %collective-permute-start.11 = (bf16[2,512,512]{2,1,0:T(8,128)(2,1)S(1)}, bf16[2,512,512]{2,1,0:T(8,128)(2,1)}, u32[]{:S(2)}, u32[]{:S(2)}) collective-permute-start(bf16[2,512,512]{2,1,0:T(8,128)(2,1)S(1)} %collective-permute-done.7.refs_2_.refs_10_), channel_id=1, source_target_pairs={{0,1},{1,0},{2,3},{3,2},{4,5},{5,4},{6,7},{7,6},{8,9},{9,8},{10,11... | collective-permute-start | bytes 3145736 | tf_op jit(solution)/shard_map/ppermute | solution.py:412
  178.8 47.1 %collective-permute-start.12 = (bf16[2,512,512]{2,1,0:T(8,128)(2,1)S(1)}, bf16[2,512,512]{2,1,0:T(8,128)(2,1)}, u32[]{:S(2)}, u32[]{:S(2)}) collective-permute-start(bf16[2,512,512]{2,1,0:T(8,128)(2,1)S(1)} %collective-permute-done.8.refs_3_.refs_11_), channel_id=1, source_target_pairs={{0,1},{1,0},{2,3},{3,2},{4,5},{5,4},{6,7},{7,6},{8,9},{9,8},{10,11... | collective-permute-start | bytes 3145736 | tf_op jit(solution)/shard_map/ppermute | solution.py:412
  258.3 14.8 %collective-permute-start.30 = (bf16[4,2,64,512]{3,2,1,0:T(8,128)(2,1)S(1)}, bf16[4,2,64,512]{3,2,1,0:T(8,128)(2,1)S(1)}, u32[]{:S(2)}, u32[]{:S(2)}) collective-permute-start(bf16[4,2,64,512]{3,2,1,0:T(8,128)(2,1)S(1)} %copy-done.26), channel_id=1, source_target_pairs={{0,4},{4,0},{8,12},{12,8},{16,20},{20,16},{24,28},{28,24},{1,5},{5... | collective-permute-start | bytes 1572872 | tf_op jit(solution)/shard_map/ppermute | solution.py:409
  260.3 24.0 %collective-permute-start.34 = (bf16[4,2,64,512]{3,2,1,0:T(8,128)(2,1)S(1)}, bf16[4,2,64,512]{3,2,1,0:T(8,128)(2,1)S(1)}, u32[]{:S(2)}, u32[]{:S(2)}) collective-permute-start(bf16[4,2,64,512]{3,2,1,0:T(8,128)(2,1)S(1)} %copy-done.25), channel_id=1, source_target_pairs={{0,4},{4,0},{8,12},{12,8},{16,20},{20,16},{24,28},{28,24},{1,5},{5... | collective-permute-start | bytes 1572872 | tf_op jit(solution)/shard_map/ppermute | solution.py:409
  260.4 61.8 %collective-permute-start.38 = (bf16[4,2,64,512]{3,2,1,0:T(8,128)(2,1)}, bf16[4,2,64,512]{3,2,1,0:T(8,128)(2,1)S(1)}, u32[]{:S(2)}, u32[]{:S(2)}) collective-permute-start(bf16[4,2,64,512]{3,2,1,0:T(8,128)(2,1)} %get-tuple-element.79), channel_id=1, source_target_pairs={{0,4},{4,0},{8,12},{12,8},{16,20},{20,16},{24,28},{28,24},{1,5},{5... | collective-permute-start | bytes 1572872 | tf_op jit(solution)/shard_map/ppermute | solution.py:409
  268.1 57.0 %collective-permute-start.42 = (bf16[4,2,64,512]{3,2,1,0:T(8,128)(2,1)}, bf16[4,2,64,512]{3,2,1,0:T(8,128)(2,1)S(1)}, u32[]{:S(2)}, u32[]{:S(2)}) collective-permute-start(bf16[4,2,64,512]{3,2,1,0:T(8,128)(2,1)} %get-tuple-element.85), channel_id=1, source_target_pairs={{0,4},{4,0},{8,12},{12,8},{16,20},{20,16},{24,28},{28,24},{1,5},{5... | collective-permute-start | bytes 1572872 | tf_op jit(solution)/shard_map/ppermute | solution.py:409
  275.9 52.0 %collective-permute-start.31 = (bf16[2,64,512]{2,1,0:T(8,128)(2,1)}, bf16[2,64,512]{2,1,0:T(8,128)(2,1)S(1)}, u32[]{:S(2)}, u32[]{:S(2)}) collective-permute-start(bf16[2,64,512]{2,1,0:T(8,128)(2,1)} %get-tuple-element.69), channel_id=1, source_target_pairs={{0,8},{4,12},{8,16},{12,20},{16,24},{20,28},{24,0},{28,4},{1,9},{5... | collective-permute-start | bytes 393224 | tf_op jit(solution)/shard_map/ppermute | solution.py:409
  278.0 53.0 %collective-permute-start.32 = (bf16[2,64,512]{2,1,0:T(8,128)(2,1)}, bf16[2,64,512]{2,1,0:T(8,128)(2,1)S(1)}, u32[]{:S(2)}, u32[]{:S(2)}) collective-permute-start(bf16[2,64,512]{2,1,0:T(8,128)(2,1)} %get-tuple-element.70), channel_id=1, source_target_pairs={{0,16},{4,20},{8,24},{12,28},{16,0},{20,4},{24,8},{28,12},{1,17},{... | collective-permute-start | bytes 393224 | tf_op jit(solution)/shard_map/ppermute | solution.py:409
  284.3 46.7 %collective-permute-start.33 = (bf16[2,64,512]{2,1,0:T(8,128)(2,1)}, bf16[2,64,512]{2,1,0:T(8,128)(2,1)S(1)}, u32[]{:S(2)}, u32[]{:S(2)}) collective-permute-start(bf16[2,64,512]{2,1,0:T(8,128)(2,1)} %get-tuple-element.71), channel_id=1, source_target_pairs={{0,24},{4,28},{8,0},{12,4},{16,8},{20,12},{24,16},{28,20},{1,25},{... | collective-permute-start | bytes 393224 | tf_op jit(solution)/shard_map/ppermute | solution.py:409
  322.2 10.2 %collective-permute-start.35 = (bf16[2,64,512]{2,1,0:T(8,128)(2,1)}, bf16[2,64,512]{2,1,0:T(8,128)(2,1)S(1)}, u32[]{:S(2)}, u32[]{:S(2)}) collective-permute-start(bf16[2,64,512]{2,1,0:T(8,128)(2,1)} %get-tuple-element.75), channel_id=1, source_target_pairs={{0,8},{4,12},{8,16},{12,20},{16,24},{20,28},{24,0},{28,4},{1,9},{5... | collective-permute-start | bytes 393224 | tf_op jit(solution)/shard_map/ppermute | solution.py:409
  325.1 10.7 %collective-permute-start.36 = (bf16[2,64,512]{2,1,0:T(8,128)(2,1)}, bf16[2,64,512]{2,1,0:T(8,128)(2,1)S(1)}, u32[]{:S(2)}, u32[]{:S(2)}) collective-permute-start(bf16[2,64,512]{2,1,0:T(8,128)(2,1)} %get-tuple-element.76), channel_id=1, source_target_pairs={{0,16},{4,20},{8,24},{12,28},{16,0},{20,4},{24,8},{28,12},{1,17},{... | collective-permute-start | bytes 393224 | tf_op jit(solution)/shard_map/ppermute | solution.py:409
  328.0 11.8 %collective-permute-start.37 = (bf16[2,64,512]{2,1,0:T(8,128)(2,1)}, bf16[2,64,512]{2,1,0:T(8,128)(2,1)S(1)}, u32[]{:S(2)}, u32[]{:S(2)}) collective-permute-start(bf16[2,64,512]{2,1,0:T(8,128)(2,1)} %get-tuple-element.77), channel_id=1, source_target_pairs={{0,24},{4,28},{8,0},{12,4},{16,8},{20,12},{24,16},{28,20},{1,25},{... | collective-permute-start | bytes 393224 | tf_op jit(solution)/shard_map/ppermute | solution.py:409
  331.0 14.0 %collective-permute-start.39 = (bf16[2,64,512]{2,1,0:T(8,128)(2,1)}, bf16[2,64,512]{2,1,0:T(8,128)(2,1)S(1)}, u32[]{:S(2)}, u32[]{:S(2)}) collective-permute-start(bf16[2,64,512]{2,1,0:T(8,128)(2,1)} %get-tuple-element.81), channel_id=1, source_target_pairs={{0,8},{4,12},{8,16},{12,20},{16,24},{20,28},{24,0},{28,4},{1,9},{5... | collective-permute-start | bytes 393224 | tf_op jit(solution)/shard_map/ppermute | solution.py:409
  331.0 20.1 %collective-permute-start.40 = (bf16[2,64,512]{2,1,0:T(8,128)(2,1)}, bf16[2,64,512]{2,1,0:T(8,128)(2,1)S(1)}, u32[]{:S(2)}, u32[]{:S(2)}) collective-permute-start(bf16[2,64,512]{2,1,0:T(8,128)(2,1)} %get-tuple-element.82), channel_id=1, source_target_pairs={{0,16},{4,20},{8,24},{12,28},{16,0},{20,4},{24,8},{28,12},{1,17},{... | collective-permute-start | bytes 393224 | tf_op jit(solution)/shard_map/ppermute | solution.py:409
  332.5 18.7 %collective-permute-start.41 = (bf16[2,64,512]{2,1,0:T(8,128)(2,1)}, bf16[2,64,512]{2,1,0:T(8,128)(2,1)S(1)}, u32[]{:S(2)}, u32[]{:S(2)}) collective-permute-start(bf16[2,64,512]{2,1,0:T(8,128)(2,1)} %get-tuple-element.83), channel_id=1, source_target_pairs={{0,24},{4,28},{8,0},{12,4},{16,8},{20,12},{24,16},{28,20},{1,25},{... | collective-permute-start | bytes 393224 | tf_op jit(solution)/shard_map/ppermute | solution.py:409
  335.8 16.3 %collective-permute-start.43 = (bf16[2,64,512]{2,1,0:T(8,128)(2,1)}, bf16[2,64,512]{2,1,0:T(8,128)(2,1)S(1)}, u32[]{:S(2)}, u32[]{:S(2)}) collective-permute-start(bf16[2,64,512]{2,1,0:T(8,128)(2,1)} %get-tuple-element.87), channel_id=1, source_target_pairs={{0,8},{4,12},{8,16},{12,20},{16,24},{20,28},{24,0},{28,4},{1,9},{5... | collective-permute-start | bytes 393224 | tf_op jit(solution)/shard_map/ppermute | solution.py:409
  339.8 17.5 %collective-permute-start.44 = (bf16[2,64,512]{2,1,0:T(8,128)(2,1)}, bf16[2,64,512]{2,1,0:T(8,128)(2,1)S(1)}, u32[]{:S(2)}, u32[]{:S(2)}) collective-permute-start(bf16[2,64,512]{2,1,0:T(8,128)(2,1)} %get-tuple-element.88), channel_id=1, source_target_pairs={{0,16},{4,20},{8,24},{12,28},{16,0},{20,4},{24,8},{28,12},{1,17},{... | collective-permute-start | bytes 393224 | tf_op jit(solution)/shard_map/ppermute | solution.py:409
  345.1 12.2 %collective-permute-start.45 = (bf16[2,64,512]{2,1,0:T(8,128)(2,1)}, bf16[2,64,512]{2,1,0:T(8,128)(2,1)S(1)}, u32[]{:S(2)}, u32[]{:S(2)}) collective-permute-start(bf16[2,64,512]{2,1,0:T(8,128)(2,1)} %get-tuple-element.89), channel_id=1, source_target_pairs={{0,24},{4,28},{8,0},{12,4},{16,8},{20,12},{24,16},{28,20},{1,25},{... | collective-permute-start | bytes 393224 | tf_op jit(solution)/shard_map/ppermute | solution.py:409
  (25 other events, 517.0 us)
where the time goes:
time: 361 us; the launch traced here: 360 us
  Pallas kernels  151 us (42%)
  waiting for transfers between devices  131 us (36%)
  starting transfers between devices  61.5 us (17%)
  local copies, waits for them, and re-layouts  8.07 us (2%)
  other arithmetic  6.96 us (2%)
    ppermute x25, waiting for transfers between devices, over_energy(): return lax.ppermute(x, 'energy', perm)  72.2 us
    ppermute x21, waiting for transfers between devices, swap(): return lax.ppermute(x, 'mom', [(i, i ^ stride) for i in range(nm)])  58.9 us
    ppermute x25, starting transfers between devices, over_energy(): return lax.ppermute(x, 'energy', perm)  49.9 us
    pallas_call x2, Pallas kernels, own_rows(): pl.pallas_call(functools.partial(rows_kernel, len(pieces)), out_shape=jax...  31.1 us
    pallas_call x2, Pallas kernels, home_blocks(): pl.pallas_call(functools.partial(home_kernel, lk, len(pieces)), out_shape...  30.2 us
    pallas_call x4, Pallas kernels, last_density(): pl.pallas_call(functools.partial(last_density_kernel, scale, energy), out...  23.1 us
    pallas_call x4, Pallas kernels, place_coupling(): pl.pallas_call(place_kernel, out_shape=[jax.ShapeDtypeStruct((nk, n, n),...  18.2 us
    pallas_call x4, Pallas kernels, lesser_packed(): pl.pallas_call(lesser_kernel, out_shape=jax.ShapeDtypeStruct((le, n, n),...  16.6 us
  transfers between devices with their start and end apart: 46, of which 16 were waited for; matrix products, arithmetic and copies ran while one was open for 2% of the time, Pallas kernels for 32%

commit v1 on v0

--- a/solution.py
+++ b/solution.py
@@ -13,8 +13,8 @@
 BF16 = jnp.bfloat16
 
 
-def params(**kw):
-    return pltpu.CompilerParams(vmem_limit_bytes=56 * 1024 * 1024, **kw)
+def params(mib):
+    return pltpu.CompilerParams(vmem_limit_bytes=mib * 1024 * 1024)
 
 
 def cost(flops, nbytes):
@@ -33,7 +33,7 @@
     return lax.broadcasted_iota(jnp.int32, (rows, cols), 0), lax.broadcasted_iota(jnp.int32, (rows, cols), 1)
 
 
-def lesser_kernel(sel, g_ref, gamma_ref, out_ref):
+def lesser_kernel(sel, g_ref, gamma_ref, *outs):
     n = g_ref.shape[-1]
     half = n // 2
     e = pl.program_id(0)
@@ -52,17 +52,16 @@
         return dot_nt(s_im[i], g_re[j]) - dot_nt(s_re[i], g_im[j])
 
     for d in range(2):
-        out_ref[0, d * half:(d + 1) * half, d * half:(d + 1) * half] = jnp.where(
-            col >= row, real(d, d), imag(d, d)).astype(BF16)
-    out_ref[0, :half, half:] = real(0, 1).astype(BF16)
-    out_ref[0, half:, :half] = imag(1, 0).astype(BF16)
+        outs[d][0, :, d * half:(d + 1) * half] = jnp.where(col >= row, real(d, d), imag(d, d)).astype(BF16)
+    outs[0][0, :, half:] = real(0, 1).astype(BF16)
+    outs[1][0, :, :half] = imag(1, 0).astype(BF16)
 
 
 def lesser_packed(which, green, broadening):
     _, le, _, n, _ = green.shape
     return pl.pallas_call(
         lesser_kernel,
-        out_shape=jax.ShapeDtypeStruct((le, n, n), BF16),
+        out_shape=[jax.ShapeDtypeStruct((le, n // 2, n), BF16)] * 2,
         grid_spec=pltpu.PrefetchScalarGridSpec(
             num_scalar_prefetch=1,
             grid=(le,),
@@ -70,9 +69,9 @@
                 pl.BlockSpec((1, 1, 2, n, n), lambda e, sel: (sel[0], e, 0, 0, 0)),
                 pl.BlockSpec((1, le, n), lambda e, sel: (sel[0], 0, 0)),
             ],
-            out_specs=pl.BlockSpec((1, n, n), lambda e, sel: (e, 0, 0)),
-        ),
-        compiler_params=params(),
+            out_specs=[pl.BlockSpec((1, n // 2, n), lambda e, sel: (e, 0, 0))] * 2,
+        ),
+        compiler_params=params(56),
         cost_estimate=cost(le * 6 * n**3, le * n * n * 6),
         name="lesser",
     )(which[None], green, broadening)
@@ -103,7 +102,7 @@
             ],
         ),
         input_output_aliases={2: 0, 3: 1} if alias else {},
-        compiler_params=params(),
+        compiler_params=params(56),
         cost_estimate=cost(nk * rows * n * 4, nk * rows * n * 6),
         name="place",
     )(where[None], piece, *alias)
@@ -135,33 +134,33 @@
         emit((kz, recv, keep, rz))
 
 
-def sources(odd, weights, j, hk, keep, recv, kz, rz, held):
-    le, n, _ = keep.shape
-    rows = n // 4
+def sources(odd, weights, j, h, hk, keep, recv, kz, rz, held):
+    le, half, n = keep.shape
+    rows = half // 2
+    at = h * (half // rows)
     big = pl.BlockSpec((le, rows, n), lambda r, *_: (0, r, 0))
-    first = pl.BlockSpec((1, rows, n), lambda r, *_: (0, r, 0))
-    later = pl.BlockSpec((1, rows, n), lambda r, *_: (j, r, 0))
+    first = pl.BlockSpec((1, rows, n), lambda r, *_: (0, at + r, 0))
+    later = pl.BlockSpec((1, rows, n), lambda r, *_: (j, at + r, 0))
     shapes = [(1 if e == 0 else hk, n, n) for e in range(le)] * 2
     specs = [first if e == 0 else later for e in range(le)] * 2
-    alias = {}
-    extra = []
+    alias, extra = {}, []
     if held is not None:
-        for at, value in enumerate(held):
-            if at % le:
-                alias[6 + len(extra)] = at
+        for i, value in enumerate(held):
+            if i % le or h:
+                alias[6 + len(extra)] = i
                 extra.append(value)
     return pl.pallas_call(
         source_kernel,
         out_shape=[jax.ShapeDtypeStruct(shape, BF16) for shape in shapes],
         grid_spec=pltpu.PrefetchScalarGridSpec(
             num_scalar_prefetch=2,
-            grid=(n // rows,),
+            grid=(half // rows,),
             in_specs=[big] * 4 + [pl.BlockSpec(memory_space=pl.ANY)] * len(extra),
             out_specs=specs,
         ),
         input_output_aliases=alias,
-        compiler_params=params(),
-        cost_estimate=cost(le * n * n * 16, le * n * n * 12),
+        compiler_params=params(56),
+        cost_estimate=cost(le * half * n * 16, le * half * n * 12),
         name="source",
     )(odd[None], weights, keep, recv, kz, rz, *extra)
 
@@ -214,7 +213,7 @@
             out_specs=[block(lk), block(lk)],
             scratch_shapes=[pltpu.VMEM((count, rows, n), BF16)],
         ),
-        compiler_params=params(),
+        compiler_params=params(56),
         cost_estimate=cost(4 * lk * count * n * n, n * n * (6 * count + 4 * lk)),
         name="home",
     )(slots, *pieces, full, turned)
@@ -283,7 +282,7 @@
             scratch_shapes=[pltpu.VMEM((count, rows, cols), BF16)] * 2,
         ),
         input_output_aliases={2 + len(in_specs) - 1: 0} if alias else {},
-        compiler_params=params(),
+        compiler_params=params(56),
         cost_estimate=cost(4 * count * count * rows * n, rows * n * count * 10),
         name="rows",
     )(mine[None], slots, *pieces, *pieces, coupling, *alias)
@@ -325,7 +324,7 @@
             one,
         ] + [pair] * len(alias),
         out_specs=pair,
-        compiler_params=params(),
+        compiler_params=params(56),
         cost_estimate=cost(16 * lk * n**3, lk * n * n * 20),
         name="density",
     )(green, broadening, x, y, *alias)
@@ -363,7 +362,7 @@
             out_specs=[out, out],
             scratch_shapes=[pltpu.VMEM((2, n, n), F32)],
         ),
-        compiler_params=params(),
+        compiler_params=params(56),
         cost_estimate=cost(16 * n**3, n * n * 20),
         name="density",
     )(odd[None], green, broadening, x, y, held)
@@ -384,7 +383,7 @@
         out_shape=[jax.ShapeDtypeStruct(keep.shape[1:], BF16)] * groups,
         in_specs=[pl.BlockSpec(memory_space=pltpu.SMEM), vmem, vmem],
         out_specs=[vmem] * groups,
-        compiler_params=params(),
+        compiler_params=params(56),
         cost_estimate=cost(keep.size, keep.size * 6),
         name="pairsum",
     )(group[None], keep, recv)
@@ -439,13 +438,15 @@
     coupling_pieces = spread(coupling)
 
     send = [lesser_packed((1 - odd) * hk + j, green_ret, broadening) for j in range(hk)]
-    recv = [over_energy(send[j], pairs) for j in range(hk)]
+    recv = [[over_energy(send[j][h], pairs) for h in range(2)] for j in range(hk)]
     keep = [lesser_packed(odd * hk + j, green_ret, broadening) for j in range(hk)]
-    kz = [over_energy(keep[j], away) for j in range(hk)]
-    rz = [over_energy(recv[j], across) for j in range(hk)]
+    kz = [[over_energy(keep[j][h], away) for h in range(2)] for j in range(hk)]
+    rz = [[over_energy(recv[j][h], across) for h in range(2)] for j in range(hk)]
     got, last = [], None
     for j in range(hk):
-        last = sources(odd, weights, j, hk, keep[j], recv[j], kz[j], rz[j], last)
+        for h in range(2):
+            last = sources(
+                odd, weights, j, h, hk, keep[j][h], recv[j][h], kz[j][h], rz[j][h], last)
         got.append(last)
 
     placed = None

time: 361 us -> 366 us (1.014)
  waiting for transfers between devices: 131 us -> 117 us
  starting transfers between devices: 61.5 us -> 74.8 us
    ppermute x25 -> x31, waiting for transfers between devices: 72.2 us -> 54.2 us  [over_energy(): return lax.ppermute(x, 'energy', perm)]
    ppermute x25 -> x31, starting transfers between devices: 49.9 us -> 63.5 us  [over_energy(): return lax.ppermute(x, 'energy', perm)]
    ppermute x21, waiting for transfers between devices: 58.9 us -> 62.9 us  [swap(): return lax.ppermute(x, 'mom', [(i, i ^ stride) for i in range(nm)])]
    pallas_call x2 -> x4, Pallas kernels: 11.1 us -> 14.1 us  [sources(): pl.pallas_call(source_kernel, out_shape=[jax.ShapeDtypeStruct(shape, BF16...]
    unnamed x55 -> x69, local copies, waits for them, and re-layouts: 6.7 us -> 8.73 us
  transfers between devices with their start and end apart: 46 -> 52, of which waited for: 16 -> 17; matrix products, arithmetic and copies ran while one was open for 2% -> 2% of each run, Pallas kernels for 32% -> 32%
where the time goes in v1:
time: 366 us; the launch traced here: 364 us
  Pallas kernels  154 us (42%)
  waiting for transfers between devices  117 us (32%)
  starting transfers between devices  74.8 us (20%)
  local copies, waits for them, and re-layouts  9.97 us (3%)
  other arithmetic  6.98 us (2%)
    ppermute x31, starting transfers between devices, over_energy(): return lax.ppermute(x, 'energy', perm)  63.5 us
    ppermute x21, waiting for transfers between devices, swap(): return lax.ppermute(x, 'mom', [(i, i ^ stride) for i in range(nm)])  62.9 us
    ppermute x31, waiting for transfers between devices, over_energy(): return lax.ppermute(x, 'energy', perm)  54.2 us
    pallas_call x2, Pallas kernels, own_rows(): pl.pallas_call(functools.partial(rows_kernel, len(pieces)), out_shape=jax...  31 us
    pallas_call x2, Pallas kernels, home_blocks(): pl.pallas_call(functools.partial(home_kernel, lk, len(pieces)), out_shape...  30.1 us
    pallas_call x4, Pallas kernels, last_density(): pl.pallas_call(functools.partial(last_density_kernel, scale, energy), out...  23.1 us
    pallas_call x4, Pallas kernels, place_coupling(): pl.pallas_call(place_kernel, out_shape=[jax.ShapeDtypeStruct((nk, n, n),...  18.2 us
    pallas_call x4, Pallas kernels, lesser_packed(): pl.pallas_call(lesser_kernel, out_shape=[jax.ShapeDtypeStruct((le, n // 2...  16.6 us
  transfers between devices with their start and end apart: 52, of which 17 were waited for; matrix products, arithmetic and copies ran while one was open for 2% of the time, Pallas kernels for 32%

profile of v1, /device:TPU:0, one launch (start us, length us, event | category | flops | bytes accessed | tf_op | source)
XLA Modules:
  0.0 364.4 jit_solution(7200216447652910812)
XLA Ops:
  0.6 4.1 %lesser.7 = (bf16[2,256,512]{2,1,0:T(8,128)(2,1)}, bf16[2,256,512]{2,1,0:T(8,128)(2,1)}) custom-call(s32[1]{0:T(128)} %bitcast.9.sel, bf16[4,2,2,512,512]{4,3,2,1,0:T(8,128)(2,1)} %g_ref.17, f32[4,2,512]{2,1,0:T(2,128)} %gamma_ref.17), custom_call_target="tpu_custom_call" | custom-call | flops 1610612736 | bytes 3145728 | tf_op jit(solution)/shard_map/lesser/pallas_call | solution.py:62
  4.8 3.0 collective-permute-start.9
  7.8 4.3 %lesser.6 = (bf16[2,256,512]{2,1,0:T(8,128)(2,1)}, bf16[2,256,512]{2,1,0:T(8,128)(2,1)}) custom-call(s32[1]{0:T(128)} %bitcast.8.sel, bf16[4,2,2,512,512]{4,3,2,1,0:T(8,128)(2,1)} %g_ref.17, f32[4,2,512]{2,1,0:T(2,128)} %gamma_ref.17), custom_call_target="tpu_custom_call" | custom-call | flops 1610612736 | bytes 3145728 | tf_op jit(solution)/shard_map/lesser/pallas_call | solution.py:62
  13.3 3.5 collective-permute-start.6
  18.1 4.1 %lesser.5 = (bf16[2,256,512]{2,1,0:T(8,128)(2,1)}, bf16[2,256,512]{2,1,0:T(8,128)(2,1)}) custom-call(s32[1]{0:T(128)} %bitcast.7.sel, bf16[4,2,2,512,512]{4,3,2,1,0:T(8,128)(2,1)} %g_ref.17, f32[4,2,512]{2,1,0:T(2,128)} %gamma_ref.17), custom_call_target="tpu_custom_call" | custom-call | flops 1610612736 | bytes 3145728 | tf_op jit(solution)/shard_map/lesser/pallas_call | solution.py:62
  22.2 2.7 collective-permute-start.3
  25.0 4.0 %collective-permute-done.10.kz = bf16[2,256,512]{2,1,0:T(8,128)(2,1)} collective-permute-done((bf16[2,256,512]{2,1,0:T(8,128)(2,1)}, bf16[2,256,512]{2,1,0:T(8,128)(2,1)}, u32[]{:S(2)}, u32[]{:S(2)}) %collective-permute-start.10) | collective-permute-done | bytes 524320 | tf_op jit(solution)/shard_map/ppermute | solution.py:408
  29.0 4.3 %collective-permute-start.11 = (bf16[2,256,512]{2,1,0:T(8,128)(2,1)S(1)}, bf16[2,256,512]{2,1,0:T(8,128)(2,1)}, u32[]{:S(2)}, u32[]{:S(2)}) collective-permute-start(bf16[2,256,512]{2,1,0:T(8,128)(2,1)S(1)} %collective-permute-done.9.recv), channel_id=1, source_target_pairs={{0,8},{8,16},{12,4},{16,24},{20,12},{28,20},{1,9},{9,17},{13,5},{1... | collective-permute-start | bytes 1572872 | tf_op jit(solution)/shard_map/ppermute | solution.py:408
  33.3 3.6 collective-permute-start.8
  40.3 4.1 %lesser.4 = (bf16[2,256,512]{2,1,0:T(8,128)(2,1)}, bf16[2,256,512]{2,1,0:T(8,128)(2,1)}) custom-call(s32[1]{0:T(128)} %bitcast.6.sel, bf16[4,2,2,512,512]{4,3,2,1,0:T(8,128)(2,1)} %g_ref.17, f32[4,2,512]{2,1,0:T(2,128)} %gamma_ref.17), custom_call_target="tpu_custom_call" | custom-call | flops 1610612736 | bytes 3145728 | tf_op jit(solution)/shard_map/lesser/pallas_call | solution.py:62
  45.7 8.0 %collective-permute-done.recv = bf16[2,256,512]{2,1,0:T(8,128)(2,1)} collective-permute-done((bf16[2,256,512]{2,1,0:T(8,128)(2,1)}, bf16[2,256,512]{2,1,0:T(8,128)(2,1)}, u32[]{:S(2)}, u32[]{:S(2)}) %collective-permute-start) | collective-permute-done | bytes 524320 | tf_op jit(solution)/shard_map/ppermute | solution.py:408
  53.7 3.7 %collective-permute-start.5 = (bf16[2,256,512]{2,1,0:T(8,128)(2,1)S(1)}, bf16[2,256,512]{2,1,0:T(8,128)(2,1)S(1)}, u32[]{:S(2)}, u32[]{:S(2)}) collective-permute-start(bf16[2,256,512]{2,1,0:T(8,128)(2,1)S(1)} %collective-permute-done.3.recv), channel_id=1, source_target_pairs={{0,8},{8,16},{12,4},{16,24},{20,12},{28,20},{1,9},{9,17},{13,5},{1... | collective-permute-start | bytes 1572872 | tf_op jit(solution)/shard_map/ppermute | solution.py:408
  58.8 4.8 %collective-permute-start.2 = (bf16[2,256,512]{2,1,0:T(8,128)(2,1)}, bf16[2,256,512]{2,1,0:T(8,128)(2,1)S(1)}, u32[]{:S(2)}, u32[]{:S(2)}) collective-permute-start(bf16[2,256,512]{2,1,0:T(8,128)(2,1)} %collective-permute-done.recv), channel_id=1, source_target_pairs={{0,8},{8,16},{12,4},{16,24},{20,12},{28,20},{1,9},{9,17},{13,5},{1... | collective-permute-start | bytes 1572872 | tf_op jit(solution)/shard_map/ppermute | solution.py:408
  64.2 3.2 pad_maximum_fusion.w_ref
  67.4 3.6 source.4
  71.1 3.5 source.5
  75.6 3.5 source.6
  80.1 3.5 source.7
  87.2 11.4 %collective-permute-done.20.refs_3_.refs_19_ = bf16[1,512,512]{2,1,0:T(8,128)(2,1)S(1)} collective-permute-done((bf16[1,512,512]{2,1,0:T(8,128)(2,1)}, bf16[1,512,512]{2,1,0:T(8,128)(2,1)S(1)}, u32[]{:S(2)}, u32[]{:S(2)}) %collective-permute-start.20) | collective-permute-done | bytes 524320 | tf_op jit(solution)/shard_map/ppermute | solution.py:408
  100.8 6.6 %collective-permute-done.19.refs_2_.refs_18_ = bf16[1,512,512]{2,1,0:T(8,128)(2,1)S(1)} collective-permute-done((bf16[1,512,512]{2,1,0:T(8,128)(2,1)S(1)}, bf16[1,512,512]{2,1,0:T(8,128)(2,1)S(1)}, u32[]{:S(2)}, u32[]{:S(2)}) %collective-permute-start.19) | collective-permute-done | bytes 524320 | tf_op jit(solution)/shard_map/ppermute | solution.py:408
  107.4 6.0 %collective-permute-done.21.refs_4_.refs_20_ = bf16[1,512,512]{2,1,0:T(8,128)(2,1)S(1)} collective-permute-done((bf16[1,512,512]{2,1,0:T(8,128)(2,1)S(1)}, bf16[1,512,512]{2,1,0:T(8,128)(2,1)S(1)}, u32[]{:S(2)}, u32[]{:S(2)}) %collective-permute-start.21) | collective-permute-done | bytes 524320 | tf_op jit(solution)/shard_map/ppermute | solution.py:411
  114.0 6.3 %collective-permute-done.24.refs_7_.refs_23_ = bf16[1,512,512]{2,1,0:T(8,128)(2,1)} collective-permute-done((bf16[1,512,512]{2,1,0:T(8,128)(2,1)S(1)}, bf16[1,512,512]{2,1,0:T(8,128)(2,1)}, u32[]{:S(2)}, u32[]{:S(2)}) %collective-permute-start.24) | collective-permute-done | bytes 524320 | tf_op jit(solution)/shard_map/ppermute | solution.py:411
  122.9 12.7 %collective-permute-done.23.refs_6_.refs_22_ = bf16[1,512,512]{2,1,0:T(8,128)(2,1)} collective-permute-done((bf16[1,512,512]{2,1,0:T(8,128)(2,1)S(1)}, bf16[1,512,512]{2,1,0:T(8,128)(2,1)}, u32[]{:S(2)}, u32[]{:S(2)}) %collective-permute-start.23) | collective-permute-done | bytes 524320 | tf_op jit(solution)/shard_map/ppermute | solution.py:411
  137.2 3.9 %collective-permute-done.12.refs_1_.refs_9_ = bf16[2,512,512]{2,1,0:T(8,128)(2,1)S(1)} collective-permute-done((bf16[2,512,512]{2,1,0:T(8,128)(2,1)}, bf16[2,512,512]{2,1,0:T(8,128)(2,1)S(1)}, u32[]{:S(2)}, u32[]{:S(2)}) %collective-permute-start.12) | collective-permute-done | bytes 1048608 | tf_op jit(solution)/shard_map/ppermute | solution.py:408
  144.7 17.3 %collective-permute-done.13.refs_2_.refs_10_ = bf16[2,512,512]{2,1,0:T(8,128)(2,1)} collective-permute-done((bf16[2,512,512]{2,1,0:T(8,128)(2,1)}, bf16[2,512,512]{2,1,0:T(8,128)(2,1)}, u32[]{:S(2)}, u32[]{:S(2)}) %collective-permute-start.13) | collective-permute-done | bytes 1048608 | tf_op jit(solution)/shard_map/ppermute | solution.py:411
  162.5 20.6 %collective-permute-done.14.refs_3_.refs_11_ = bf16[2,512,512]{2,1,0:T(8,128)(2,1)} collective-permute-done((bf16[2,512,512]{2,1,0:T(8,128)(2,1)S(1)}, bf16[2,512,512]{2,1,0:T(8,128)(2,1)}, u32[]{:S(2)}, u32[]{:S(2)}) %collective-permute-start.14) | collective-permute-done | bytes 1048608 | tf_op jit(solution)/shard_map/ppermute | solution.py:411
  184.2 4.5 %place.4 = (bf16[16,512,512]{2,1,0:T(8,128)(2,1)}, bf16[16,512,512]{2,1,0:T(8,128)(2,1)}) custom-call(s32[1]{0:T(128)} %bitcast.mine.where, bf16[16,128,512]{2,1,0:T(8,128)(2,1)} %c_ref.1), custom_call_target="tpu_custom_call" | custom-call | flops 4194304 | bytes 6291456 | tf_op jit(solution)/shard_map/place/pallas_call | solution.py:91
  188.8 4.6 %place.5 = (bf16[16,512,512]{2,1,0:T(8,128)(2,1)}, bf16[16,512,512]{2,1,0:T(8,128)(2,1)}) custom-call(s32[1]{0:T(128)} %bitcast.13.where, bf16[16,128,512]{2,1,0:T(8,128)(2,1)} %copy-done.15, bf16[16,512,512]{2,1,0:T(8,128)(2,1)} %get-tuple-element.86.refs_0_, ...), custom_call_target="tpu_custom_call", output_to_operand_aliasing={{0}: (2, {}), {1}: (3, {})} | custom-call | flops 4194304 | bytes 6291456 | tf_op jit(solution)/shard_map/place/pallas_call | solution.py:91
  193.3 4.6 %place.6 = (bf16[16,512,512]{2,1,0:T(8,128)(2,1)}, bf16[16,512,512]{2,1,0:T(8,128)(2,1)}) custom-call(s32[1]{0:T(128)} %bitcast.12.where, bf16[16,128,512]{2,1,0:T(8,128)(2,1)} %collective-permute-done.33.c_ref, bf16[16,512,512]{2,1,0:T(8,128)(2,1)} %get-tuple-element.88.refs_0_, ...), custom_call_target="tpu_custom_call", output_to_operand_aliasing={{0}: (2, {}), {1}: (3, {})} | custom-call | flops 4194304 | bytes 6291456 | tf_op jit(solution)/shard_map/place/pallas_call | solution.py:91
  197.9 4.5 %place.7 = (bf16[16,512,512]{2,1,0:T(8,128)(2,1)}, bf16[16,512,512]{2,1,0:T(8,128)(2,1)}) custom-call(s32[1]{0:T(128)} %bitcast.11.where, bf16[16,128,512]{2,1,0:T(8,128)(2,1)} %collective-permute-done.34.c_ref, bf16[16,512,512]{2,1,0:T(8,128)(2,1)} %get-tuple-element.90.refs_0_, ...), custom_call_target="tpu_custom_call", output_to_operand_aliasing={{0}: (2, {}), {1}: (3, {})} | custom-call | flops 4194304 | bytes 6291456 | tf_op jit(solution)/shard_map/place/pallas_call | solution.py:91
  202.5 15.1 %home.3 = (bf16[4,512,512]{2,1,0:T(8,128)(2,1)}, bf16[4,512,512]{2,1,0:T(8,128)(2,1)}) custom-call(s32[64]{0:T(128)} %reshape.11.slots, bf16[1,512,512]{2,1,0:T(8,128)(2,1)} %get-tuple-element.82.refs_0_.refs_16_, bf16[1,512,512]{2,1,0:T(8,128)(2,1)} %get-tuple-element.83.refs_1_.refs_17_, bf16[1,512,512]{2,1,0:T(8,128)(2,1)} %copy-done.8, ...), custom_call_target="tpu_custom_call" | custom-call | flops 67108864 | bytes 29360128 | tf_op jit(solution)/shard_map/home/pallas_call | solution.py:206
  217.5 13.0 %density.5.held_ref = f32[4,2,512,512]{3,2,1,0:T(8,128)} custom-call(bf16[4,2,2,512,512]{4,3,2,1,0:T(8,128)(2,1)} %g_ref.17, f32[4,2,512]{2,1,0:T(2,128)} %gamma_ref.17, bf16[4,512,512]{2,1,0:T(8,128)(2,1)} %get-tuple-element.96.x_ref, bf16[4,512,512]{2,1,0:T(8,128)(2,1)} %get-tuple-element.97.y_ref), custom_call_target="tpu_custom_call" | custom-call | flops 8589934592 | bytes 20971520 | tf_op jit(solution)/shard_map/density/pallas_call | solution.py:316
  231.8 15.1 %home.2 = (bf16[4,512,512]{2,1,0:T(8,128)(2,1)}, bf16[4,512,512]{2,1,0:T(8,128)(2,1)}) custom-call(s32[64]{0:T(128)} %reshape.11.slots, bf16[2,512,512]{2,1,0:T(8,128)(2,1)} %get-tuple-element.80.refs_0_.refs_8_, bf16[2,512,512]{2,1,0:T(8,128)(2,1)} %copy-done.1, bf16[2,512,512]{2,1,0:T(8,128)(2,1)} %collective-permute-done.13.refs_2_.refs_10_, ...), custom_call_target="tpu_custom_call" | custom-call | flops 67108864 | bytes 29360128 | tf_op jit(solution)/shard_map/home/pallas_call | solution.py:206
  246.9 5.7 %density.6 = (bf16[4,2,64,512]{3,2,1,0:T(8,128)(2,1)}, bf16[4,2,64,512]{3,2,1,0:T(8,128)(2,1)}) custom-call(s32[1]{0:T(128)} %bitcast.1.odd, bf16[4,2,2,512,512]{4,3,2,1,0:T(8,128)(2,1)} %g_ref.17, f32[4,2,512]{2,1,0:T(2,128)} %gamma_ref.17, bf16[4,512,512]{2,1,0:T(8,128)(2,1)} %get-tuple-element.94.x_ref, bf16[4,512,512]{2,1,0:T(8,128)(2,1)} %get-tuple-element.95.y_ref, ...), custom_call_target="tpu_custom_call" | custom-call | flops 2147483648 | bytes 5242880 | tf_op jit(solution)/shard_map/density/pallas_call | solution.py:349
  252.7 5.7 %density.7 = (bf16[4,2,64,512]{3,2,1,0:T(8,128)(2,1)}, bf16[4,2,64,512]{3,2,1,0:T(8,128)(2,1)}) custom-call(s32[1]{0:T(128)} %bitcast.1.odd, bf16[4,2,2,512,512]{4,3,2,1,0:T(8,128)(2,1)} %g_ref.17, f32[4,2,512]{2,1,0:T(2,128)} %gamma_ref.17, bf16[4,512,512]{2,1,0:T(8,128)(2,1)} %get-tuple-element.94.x_ref, bf16[4,512,512]{2,1,0:T(8,128)(2,1)} %get-tuple-element.95.y_ref, ...), custom_call_target="tpu_custom_call" | custom-call | flops 2147483648 | bytes 5242880 | tf_op jit(solution)/shard_map/density/pallas_call | solution.py:349
  258.4 5.8 %density.8 = (bf16[4,2,64,512]{3,2,1,0:T(8,128)(2,1)}, bf16[4,2,64,512]{3,2,1,0:T(8,128)(2,1)}) custom-call(s32[1]{0:T(128)} %bitcast.1.odd, bf16[4,2,2,512,512]{4,3,2,1,0:T(8,128)(2,1)} %g_ref.17, f32[4,2,512]{2,1,0:T(2,128)} %gamma_ref.17, bf16[4,512,512]{2,1,0:T(8,128)(2,1)} %get-tuple-element.94.x_ref, bf16[4,512,512]{2,1,0:T(8,128)(2,1)} %get-tuple-element.95.y_ref, ...), custom_call_target="tpu_custom_call" | custom-call | flops 2147483648 | bytes 5242880 | tf_op jit(solution)/shard_map/density/pallas_call | solution.py:349
  267.3 5.8 %density.9 = (bf16[4,2,64,512]{3,2,1,0:T(8,128)(2,1)}, bf16[4,2,64,512]{3,2,1,0:T(8,128)(2,1)}) custom-call(s32[1]{0:T(128)} %bitcast.1.odd, bf16[4,2,2,512,512]{4,3,2,1,0:T(8,128)(2,1)} %g_ref.17, f32[4,2,512]{2,1,0:T(2,128)} %gamma_ref.17, bf16[4,512,512]{2,1,0:T(8,128)(2,1)} %get-tuple-element.94.x_ref, bf16[4,512,512]{2,1,0:T(8,128)(2,1)} %get-tuple-element.95.y_ref, ...), custom_call_target="tpu_custom_call" | custom-call | flops 2147483648 | bytes 5242880 | tf_op jit(solution)/shard_map/density/pallas_call | solution.py:349
  274.1 5.0 %collective-permute-done.36.recv_ref = bf16[4,2,64,512]{3,2,1,0:T(8,128)(2,1)S(1)} collective-permute-done((bf16[4,2,64,512]{3,2,1,0:T(8,128)(2,1)S(1)}, bf16[4,2,64,512]{3,2,1,0:T(8,128)(2,1)S(1)}, u32[]{:S(2)}, u32[]{:S(2)}) %collective-permute-start.36) | collective-permute-done | bytes 524320 | tf_op jit(solution)/shard_map/ppermute | solution.py:408
  285.6 4.7 %collective-permute-done.40.recv_ref = bf16[4,2,64,512]{3,2,1,0:T(8,128)(2,1)S(1)} collective-permute-done((bf16[4,2,64,512]{3,2,1,0:T(8,128)(2,1)S(1)}, bf16[4,2,64,512]{3,2,1,0:T(8,128)(2,1)S(1)}, u32[]{:S(2)}, u32[]{:S(2)}) %collective-permute-start.40) | collective-permute-done | bytes 524320 | tf_op jit(solution)/shard_map/ppermute | solution.py:408
  290.3 3.1 collective-permute-start.39
  294.1 15.7 %rows.2.refs_17_ = bf16[16,2,2,128,512]{4,3,2,1,0:T(8,128)(2,1)} custom-call(s32[1]{0:T(128)} %bitcast.mine.where, s32[256]{0:T(256)} %reshape.10.slots, bf16[1,512,512]{2,1,0:T(8,128)(2,1)} %get-tuple-element.82.refs_0_.refs_16_, bf16[1,512,512]{2,1,0:T(8,128)(2,1)} %get-tuple-element.83.refs_1_.refs_17_, bf16[1,512,512]{2,1,0:T(8,128)(2,1)} %copy-done.8, ...), custom_call_target="tpu_custom_call" | custom-call | flops 67108864 | bytes 10485760 | tf_op jit(solution)/shard_map/rows/pallas_call | solution.py:274
  309.9 15.3 %rows.3 = bf16[16,2,2,128,512]{4,3,2,1,0:T(8,128)(2,1)} custom-call(s32[1]{0:T(128)} %bitcast.mine.where, s32[256]{0:T(256)} %reshape.10.slots, bf16[2,512,512]{2,1,0:T(8,128)(2,1)} %get-tuple-element.80.refs_0_.refs_8_, bf16[2,512,512]{2,1,0:T(8,128)(2,1)} %copy-done.1, ...), custom_call_target="tpu_custom_call", output_to_operand_aliasing={{}: (19, {})} | custom-call | flops 67108864 | bytes 10485760 | tf_op jit(solution)/shard_map/rows/pallas_call | solution.py:274
  332.9 3.1 collective-permute-start.43
  337.4 2.9 collective-permute-start.47
  340.5 3.0 collective-permute-start.49
  344.2 4.2 %collective-permute-start.50 = (bf16[2,64,512]{2,1,0:T(8,128)(2,1)}, bf16[2,64,512]{2,1,0:T(8,128)(2,1)S(1)}, u32[]{:S(2)}, u32[]{:S(2)}) collective-permute-start(bf16[2,64,512]{2,1,0:T(8,128)(2,1)} %get-tuple-element.120), channel_id=1, source_target_pairs={{0,16},{4,20},{8,24},{12,28},{16,0},{20,4},{24,8},{28,12},{1,17},{... | collective-permute-start | bytes 393224 | tf_op jit(solution)/shard_map/ppermute | solution.py:408
  349.3 3.5 collective-permute-start.51
  356.4 5.1 %collective-permute-done.50 = bf16[2,64,512]{2,1,0:T(8,128)(2,1)S(1)} collective-permute-done((bf16[2,64,512]{2,1,0:T(8,128)(2,1)}, bf16[2,64,512]{2,1,0:T(8,128)(2,1)S(1)}, u32[]{:S(2)}, u32[]{:S(2)}) %collective-permute-start.50) | collective-permute-done | bytes 131104 | tf_op jit(solution)/shard_map/ppermute | solution.py:408
  (161 shorter events, 57.0 us)
Async XLA Ops:
  4.8 20.1 %collective-permute-start.9 = (bf16[2,256,512]{2,1,0:T(8,128)(2,1)}, bf16[2,256,512]{2,1,0:T(8,128)(2,1)S(1)}, u32[]{:S(2)}, u32[]{:S(2)}) collective-permute-start(bf16[2,256,512]{2,1,0:T(8,128)(2,1)} %get-tuple-element.69), channel_id=1, source_target_pairs={{0,4},{4,0},{8,12},{12,8},{16,20},{20,16},{24,28},{28,24},{1,5},{5... | collective-permute-start | bytes 1572872 | tf_op jit(solution)/shard_map/ppermute | solution.py:408
  12.0 17.0 %collective-permute-start.10 = (bf16[2,256,512]{2,1,0:T(8,128)(2,1)}, bf16[2,256,512]{2,1,0:T(8,128)(2,1)}, u32[]{:S(2)}, u32[]{:S(2)}) collective-permute-start(bf16[2,256,512]{2,1,0:T(8,128)(2,1)} %get-tuple-element.68.keep), channel_id=1, source_target_pairs={{4,12},{8,0},{12,20},{16,8},{20,28},{24,16},{5,13},{9,1},{13,21},{... | collective-permute-start | bytes 1572872 | tf_op jit(solution)/shard_map/ppermute | solution.py:408
  13.3 20.0 %collective-permute-start.6 = (bf16[2,256,512]{2,1,0:T(8,128)(2,1)}, bf16[2,256,512]{2,1,0:T(8,128)(2,1)}, u32[]{:S(2)}, u32[]{:S(2)}) collective-permute-start(bf16[2,256,512]{2,1,0:T(8,128)(2,1)} %get-tuple-element.67), channel_id=1, source_target_pairs={{0,4},{4,0},{8,12},{12,8},{16,20},{20,16},{24,28},{28,24},{1,5},{5... | collective-permute-start | bytes 1572872 | tf_op jit(solution)/shard_map/ppermute | solution.py:408
  16.8 22.1 %collective-permute-start.7 = (bf16[2,256,512]{2,1,0:T(8,128)(2,1)}, bf16[2,256,512]{2,1,0:T(8,128)(2,1)}, u32[]{:S(2)}, u32[]{:S(2)}) collective-permute-start(bf16[2,256,512]{2,1,0:T(8,128)(2,1)} %get-tuple-element.66.keep), channel_id=1, source_target_pairs={{4,12},{8,0},{12,20},{16,8},{20,28},{24,16},{5,13},{9,1},{13,21},{... | collective-permute-start | bytes 1572872 | tf_op jit(solution)/shard_map/ppermute | solution.py:408
  22.2 22.2 %collective-permute-start.3 = (bf16[2,256,512]{2,1,0:T(8,128)(2,1)}, bf16[2,256,512]{2,1,0:T(8,128)(2,1)S(1)}, u32[]{:S(2)}, u32[]{:S(2)}) collective-permute-start(bf16[2,256,512]{2,1,0:T(8,128)(2,1)} %get-tuple-element.65), channel_id=1, source_target_pairs={{0,4},{4,0},{8,12},{12,8},{16,20},{20,16},{24,28},{28,24},{1,5},{5... | collective-permute-start | bytes 1572872 | tf_op jit(solution)/shard_map/ppermute | solution.py:408
  24.9 28.8 %collective-permute-start = (bf16[2,256,512]{2,1,0:T(8,128)(2,1)}, bf16[2,256,512]{2,1,0:T(8,128)(2,1)}, u32[]{:S(2)}, u32[]{:S(2)}) collective-permute-start(bf16[2,256,512]{2,1,0:T(8,128)(2,1)} %get-tuple-element.63), channel_id=1, source_target_pairs={{0,4},{4,0},{8,12},{12,8},{16,20},{20,16},{24,28},{28,24},{1,5},{5... | collective-permute-start | bytes 1572872 | tf_op jit(solution)/shard_map/ppermute | solution.py:408
  29.0 28.4 %collective-permute-start.11 = (bf16[2,256,512]{2,1,0:T(8,128)(2,1)S(1)}, bf16[2,256,512]{2,1,0:T(8,128)(2,1)}, u32[]{:S(2)}, u32[]{:S(2)}) collective-permute-start(bf16[2,256,512]{2,1,0:T(8,128)(2,1)S(1)} %collective-permute-done.9.recv), channel_id=1, source_target_pairs={{0,8},{8,16},{12,4},{16,24},{20,12},{28,20},{1,9},{9,17},{13,5},{1... | collective-permute-start | bytes 1572872 | tf_op jit(solution)/shard_map/ppermute | solution.py:408
  33.3 25.5 %collective-permute-start.8 = (bf16[2,256,512]{2,1,0:T(8,128)(2,1)}, bf16[2,256,512]{2,1,0:T(8,128)(2,1)}, u32[]{:S(2)}, u32[]{:S(2)}) collective-permute-start(bf16[2,256,512]{2,1,0:T(8,128)(2,1)} %collective-permute-done.6.recv), channel_id=1, source_target_pairs={{0,8},{8,16},{12,4},{16,24},{20,12},{28,20},{1,9},{9,17},{13,5},{1... | collective-permute-start | bytes 1572872 | tf_op jit(solution)/shard_map/ppermute | solution.py:408
  38.8 82.4 %collective-permute-start.33 = (bf16[16,128,512]{2,1,0:T(8,128)(2,1)S(1)}, bf16[16,128,512]{2,1,0:T(8,128)(2,1)}, u32[]{:S(2)}, u32[]{:S(2)}) collective-permute-start(bf16[16,128,512]{2,1,0:T(8,128)(2,1)S(1)} %copy-done), channel_id=1, source_target_pairs={{0,2},{1,3},{2,0},{3,1},{4,6},{5,7},{6,4},{7,5},{8,10},{9,11},{10,... | collective-permute-start | bytes 6291464 | tf_op jit(solution)/shard_map/ppermute | solution.py:411
  44.4 30.1 %collective-permute-start.4 = (bf16[2,256,512]{2,1,0:T(8,128)(2,1)}, bf16[2,256,512]{2,1,0:T(8,128)(2,1)S(1)}, u32[]{:S(2)}, u32[]{:S(2)}) collective-permute-start(bf16[2,256,512]{2,1,0:T(8,128)(2,1)} %get-tuple-element.64.keep), channel_id=1, source_target_pairs={{4,12},{8,0},{12,20},{16,8},{20,28},{24,16},{5,13},{9,1},{13,21},{... | collective-permute-start | bytes 1572872 | tf_op jit(solution)/shard_map/ppermute | solution.py:408
  53.7 20.9 %collective-permute-start.5 = (bf16[2,256,512]{2,1,0:T(8,128)(2,1)S(1)}, bf16[2,256,512]{2,1,0:T(8,128)(2,1)S(1)}, u32[]{:S(2)}, u32[]{:S(2)}) collective-permute-start(bf16[2,256,512]{2,1,0:T(8,128)(2,1)S(1)} %collective-permute-done.3.recv), channel_id=1, source_target_pairs={{0,8},{8,16},{12,4},{16,24},{20,12},{28,20},{1,9},{9,17},{13,5},{1... | collective-permute-start | bytes 1572872 | tf_op jit(solution)/shard_map/ppermute | solution.py:408
  57.4 21.6 %collective-permute-start.1 = (bf16[2,256,512]{2,1,0:T(8,128)(2,1)}, bf16[2,256,512]{2,1,0:T(8,128)(2,1)S(1)}, u32[]{:S(2)}, u32[]{:S(2)}) collective-permute-start(bf16[2,256,512]{2,1,0:T(8,128)(2,1)} %get-tuple-element.62.keep), channel_id=1, source_target_pairs={{4,12},{8,0},{12,20},{16,8},{20,28},{24,16},{5,13},{9,1},{13,21},{... | collective-permute-start | bytes 1572872 | tf_op jit(solution)/shard_map/ppermute | solution.py:408
  58.8 20.3 %collective-permute-start.2 = (bf16[2,256,512]{2,1,0:T(8,128)(2,1)}, bf16[2,256,512]{2,1,0:T(8,128)(2,1)S(1)}, u32[]{:S(2)}, u32[]{:S(2)}) collective-permute-start(bf16[2,256,512]{2,1,0:T(8,128)(2,1)} %collective-permute-done.recv), channel_id=1, source_target_pairs={{0,8},{8,16},{12,4},{16,24},{20,12},{28,20},{1,9},{9,17},{13,5},{1... | collective-permute-start | bytes 1572872 | tf_op jit(solution)/shard_map/ppermute | solution.py:408
  83.6 15.1 %collective-permute-start.20 = (bf16[1,512,512]{2,1,0:T(8,128)(2,1)}, bf16[1,512,512]{2,1,0:T(8,128)(2,1)S(1)}, u32[]{:S(2)}, u32[]{:S(2)}) collective-permute-start(bf16[1,512,512]{2,1,0:T(8,128)(2,1)} %get-tuple-element.85), channel_id=1, source_target_pairs={{0,4},{4,0},{8,12},{12,8},{16,20},{20,16},{24,28},{28,24},{1,5},{5... | collective-permute-start | bytes 1572872 | tf_op jit(solution)/shard_map/ppermute | solution.py:408
  85.7 14.5 %collective-permute-start.22 = (bf16[1,512,512]{2,1,0:T(8,128)(2,1)}, bf16[1,512,512]{2,1,0:T(8,128)(2,1)S(1)}, u32[]{:S(2)}, u32[]{:S(2)}) collective-permute-start(bf16[1,512,512]{2,1,0:T(8,128)(2,1)} %get-tuple-element.83.refs_1_.refs_17_), channel_id=1, source_target_pairs={{0,2},{1,3},{2,0},{3,1},{4,6},{5,7},{6,4},{7,5},{8,10},{9,11},{10,... | collective-permute-start | bytes 1572872 | tf_op jit(solution)/shard_map/ppermute | solution.py:411
  87.2 13.0 %collective-permute-start.26 = (bf16[1,512,512]{2,1,0:T(8,128)(2,1)}, bf16[1,512,512]{2,1,0:T(8,128)(2,1)S(1)}, u32[]{:S(2)}, u32[]{:S(2)}) collective-permute-start(bf16[1,512,512]{2,1,0:T(8,128)(2,1)} %get-tuple-element.83.refs_1_.refs_17_), channel_id=1, source_target_pairs={{0,1},{1,0},{2,3},{3,2},{4,5},{5,4},{6,7},{7,6},{8,9},{9,8},{10,11... | collective-permute-start | bytes 1572872 | tf_op jit(solution)/shard_map/ppermute | solution.py:411
  87.2 20.3 %collective-permute-start.19 = (bf16[1,512,512]{2,1,0:T(8,128)(2,1)S(1)}, bf16[1,512,512]{2,1,0:T(8,128)(2,1)S(1)}, u32[]{:S(2)}, u32[]{:S(2)}) collective-permute-start(bf16[1,512,512]{2,1,0:T(8,128)(2,1)S(1)} %copy-done.26), channel_id=1, source_target_pairs={{0,4},{4,0},{8,12},{12,8},{16,20},{20,16},{24,28},{28,24},{1,5},{5... | collective-permute-start | bytes 1572872 | tf_op jit(solution)/shard_map/ppermute | solution.py:408
  98.7 14.8 %collective-permute-start.21 = (bf16[1,512,512]{2,1,0:T(8,128)(2,1)S(1)}, bf16[1,512,512]{2,1,0:T(8,128)(2,1)S(1)}, u32[]{:S(2)}, u32[]{:S(2)}) collective-permute-start(bf16[1,512,512]{2,1,0:T(8,128)(2,1)S(1)} %copy-done.4), channel_id=1, source_target_pairs={{0,2},{1,3},{2,0},{3,1},{4,6},{5,7},{6,4},{7,5},{8,10},{9,11},{10,... | collective-permute-start | bytes 1572872 | tf_op jit(solution)/shard_map/ppermute | solution.py:411
  100.2 13.3 %collective-permute-start.25 = (bf16[1,512,512]{2,1,0:T(8,128)(2,1)S(1)}, bf16[1,512,512]{2,1,0:T(8,128)(2,1)S(1)}, u32[]{:S(2)}, u32[]{:S(2)}) collective-permute-start(bf16[1,512,512]{2,1,0:T(8,128)(2,1)S(1)} %copy-done.4), channel_id=1, source_target_pairs={{0,1},{1,0},{2,3},{3,2},{4,5},{5,4},{6,7},{7,6},{8,9},{9,8},{10,11... | collective-permute-start | bytes 1572872 | tf_op jit(solution)/shard_map/ppermute | solution.py:411
  100.2 20.1 %collective-permute-start.24 = (bf16[1,512,512]{2,1,0:T(8,128)(2,1)S(1)}, bf16[1,512,512]{2,1,0:T(8,128)(2,1)}, u32[]{:S(2)}, u32[]{:S(2)}) collective-permute-start(bf16[1,512,512]{2,1,0:T(8,128)(2,1)S(1)} %collective-permute-done.20.refs_3_.refs_19_), channel_id=1, source_target_pairs={{0,2},{1,3},{2,0},{3,1},{4,6},{5,7},{6,4},{7,5},{8,10},{9,11},{10,... | collective-permute-start | bytes 1572872 | tf_op jit(solution)/shard_map/ppermute | solution.py:411
  107.4 35.1 %collective-permute-start.35 = (bf16[16,128,512]{2,1,0:T(8,128)(2,1)S(1)}, bf16[16,128,512]{2,1,0:T(8,128)(2,1)S(1)}, u32[]{:S(2)}, u32[]{:S(2)}) collective-permute-start(bf16[16,128,512]{2,1,0:T(8,128)(2,1)S(1)} %copy-done), channel_id=1, source_target_pairs={{0,1},{1,0},{2,3},{3,2},{4,5},{5,4},{6,7},{7,6},{8,9},{9,8},{10,11... | collective-permute-start | bytes 6291464 | tf_op jit(solution)/shard_map/ppermute | solution.py:411
  120.2 20.8 %collective-permute-start.12 = (bf16[2,512,512]{2,1,0:T(8,128)(2,1)}, bf16[2,512,512]{2,1,0:T(8,128)(2,1)S(1)}, u32[]{:S(2)}, u32[]{:S(2)}) collective-permute-start(bf16[2,512,512]{2,1,0:T(8,128)(2,1)} %get-tuple-element.81), channel_id=1, source_target_pairs={{0,4},{4,0},{8,12},{12,8},{16,20},{20,16},{24,28},{28,24},{1,5},{5... | collective-permute-start | bytes 3145736 | tf_op jit(solution)/shard_map/ppermute | solution.py:408
  121.2 61.9 %collective-permute-start.34 = (bf16[16,128,512]{2,1,0:T(8,128)(2,1)}, bf16[16,128,512]{2,1,0:T(8,128)(2,1)}, u32[]{:S(2)}, u32[]{:S(2)}) collective-permute-start(bf16[16,128,512]{2,1,0:T(8,128)(2,1)} %collective-permute-done.33.c_ref), channel_id=1, source_target_pairs={{0,1},{1,0},{2,3},{3,2},{4,5},{5,4},{6,7},{7,6},{8,9},{9,8},{10,11... | collective-permute-start | bytes 6291464 | tf_op jit(solution)/shard_map/ppermute | solution.py:411
  121.2 14.4 %collective-permute-start.23 = (bf16[1,512,512]{2,1,0:T(8,128)(2,1)S(1)}, bf16[1,512,512]{2,1,0:T(8,128)(2,1)}, u32[]{:S(2)}, u32[]{:S(2)}) collective-permute-start(bf16[1,512,512]{2,1,0:T(8,128)(2,1)S(1)} %collective-permute-done.19.refs_2_.refs_18_), channel_id=1, source_target_pairs={{0,2},{1,3},{2,0},{3,1},{4,6},{5,7},{6,4},{7,5},{8,10},{9,11},{10,... | collective-permute-start | bytes 1572872 | tf_op jit(solution)/shard_map/ppermute | solution.py:411
  122.8 14.4 %collective-permute-start.27 = (bf16[1,512,512]{2,1,0:T(8,128)(2,1)S(1)}, bf16[1,512,512]{2,1,0:T(8,128)(2,1)S(1)}, u32[]{:S(2)}, u32[]{:S(2)}) collective-permute-start(bf16[1,512,512]{2,1,0:T(8,128)(2,1)S(1)} %collective-permute-done.19.refs_2_.refs_18_), channel_id=1, source_target_pairs={{0,1},{1,0},{2,3},{3,2},{4,5},{5,4},{6,7},{7,6},{8,9},{9,8},{10,11... | collective-permute-start | bytes 1572872 | tf_op jit(solution)/shard_map/ppermute | solution.py:411
  135.7 26.3 %collective-permute-start.13 = (bf16[2,512,512]{2,1,0:T(8,128)(2,1)}, bf16[2,512,512]{2,1,0:T(8,128)(2,1)}, u32[]{:S(2)}, u32[]{:S(2)}) collective-permute-start(bf16[2,512,512]{2,1,0:T(8,128)(2,1)} %get-tuple-element.80.refs_0_.refs_8_), channel_id=1, source_target_pairs={{0,2},{1,3},{2,0},{3,1},{4,6},{5,7},{6,4},{7,5},{8,10},{9,11},{10,... | collective-permute-start | bytes 3145736 | tf_op jit(solution)/shard_map/ppermute | solution.py:411
  141.1 42.0 %collective-permute-start.14 = (bf16[2,512,512]{2,1,0:T(8,128)(2,1)S(1)}, bf16[2,512,512]{2,1,0:T(8,128)(2,1)}, u32[]{:S(2)}, u32[]{:S(2)}) collective-permute-start(bf16[2,512,512]{2,1,0:T(8,128)(2,1)S(1)} %collective-permute-done.12.refs_1_.refs_9_), channel_id=1, source_target_pairs={{0,2},{1,3},{2,0},{3,1},{4,6},{5,7},{6,4},{7,5},{8,10},{9,11},{10,... | collective-permute-start | bytes 3145736 | tf_op jit(solution)/shard_map/ppermute | solution.py:411
  142.6 19.5 %collective-permute-start.32 = (bf16[1,512,512]{2,1,0:T(8,128)(2,1)}, bf16[1,512,512]{2,1,0:T(8,128)(2,1)}, u32[]{:S(2)}, u32[]{:S(2)}) collective-permute-start(bf16[1,512,512]{2,1,0:T(8,128)(2,1)} %collective-permute-done.24.refs_7_.refs_23_), channel_id=1, source_target_pairs={{0,1},{1,0},{2,3},{3,2},{4,5},{5,4},{6,7},{7,6},{8,9},{9,8},{10,11... | collective-permute-start | bytes 1572872 | tf_op jit(solution)/shard_map/ppermute | solution.py:411
  144.7 57.7 %collective-permute-start.31 = (bf16[1,512,512]{2,1,0:T(8,128)(2,1)}, bf16[1,512,512]{2,1,0:T(8,128)(2,1)}, u32[]{:S(2)}, u32[]{:S(2)}) collective-permute-start(bf16[1,512,512]{2,1,0:T(8,128)(2,1)} %collective-permute-done.23.refs_6_.refs_22_), channel_id=1, source_target_pairs={{0,1},{1,0},{2,3},{3,2},{4,5},{5,4},{6,7},{7,6},{8,9},{9,8},{10,11... | collective-permute-start | bytes 1572872 | tf_op jit(solution)/shard_map/ppermute | solution.py:411
  162.0 68.5 %collective-permute-start.15 = (bf16[2,512,512]{2,1,0:T(8,128)(2,1)}, bf16[2,512,512]{2,1,0:T(8,128)(2,1)S(1)}, u32[]{:S(2)}, u32[]{:S(2)}) collective-permute-start(bf16[2,512,512]{2,1,0:T(8,128)(2,1)} %get-tuple-element.80.refs_0_.refs_8_), channel_id=1, source_target_pairs={{0,1},{1,0},{2,3},{3,2},{4,5},{5,4},{6,7},{7,6},{8,9},{9,8},{10,11... | collective-permute-start | bytes 3145736 | tf_op jit(solution)/shard_map/ppermute | solution.py:411
  162.0 68.5 %collective-permute-start.16 = (bf16[2,512,512]{2,1,0:T(8,128)(2,1)S(1)}, bf16[2,512,512]{2,1,0:T(8,128)(2,1)S(1)}, u32[]{:S(2)}, u32[]{:S(2)}) collective-permute-start(bf16[2,512,512]{2,1,0:T(8,128)(2,1)S(1)} %collective-permute-done.12.refs_1_.refs_9_), channel_id=1, source_target_pairs={{0,1},{1,0},{2,3},{3,2},{4,5},{5,4},{6,7},{7,6},{8,9},{9,8},{10,11... | collective-permute-start | bytes 3145736 | tf_op jit(solution)/shard_map/ppermute | solution.py:411
  183.1 47.4 %collective-permute-start.17 = (bf16[2,512,512]{2,1,0:T(8,128)(2,1)}, bf16[2,512,512]{2,1,0:T(8,128)(2,1)}, u32[]{:S(2)}, u32[]{:S(2)}) collective-permute-start(bf16[2,512,512]{2,1,0:T(8,128)(2,1)} %collective-permute-done.13.refs_2_.refs_10_), channel_id=1, source_target_pairs={{0,1},{1,0},{2,3},{3,2},{4,5},{5,4},{6,7},{7,6},{8,9},{9,8},{10,11... | collective-permute-start | bytes 3145736 | tf_op jit(solution)/shard_map/ppermute | solution.py:411
  183.1 47.4 %collective-permute-start.18 = (bf16[2,512,512]{2,1,0:T(8,128)(2,1)}, bf16[2,512,512]{2,1,0:T(8,128)(2,1)}, u32[]{:S(2)}, u32[]{:S(2)}) collective-permute-start(bf16[2,512,512]{2,1,0:T(8,128)(2,1)} %collective-permute-done.14.refs_3_.refs_11_), channel_id=1, source_target_pairs={{0,1},{1,0},{2,3},{3,2},{4,5},{5,4},{6,7},{7,6},{8,9},{9,8},{10,11... | collective-permute-start | bytes 3145736 | tf_op jit(solution)/shard_map/ppermute | solution.py:411
  264.2 14.8 %collective-permute-start.36 = (bf16[4,2,64,512]{3,2,1,0:T(8,128)(2,1)S(1)}, bf16[4,2,64,512]{3,2,1,0:T(8,128)(2,1)S(1)}, u32[]{:S(2)}, u32[]{:S(2)}) collective-permute-start(bf16[4,2,64,512]{3,2,1,0:T(8,128)(2,1)S(1)} %copy-done.33), channel_id=1, source_target_pairs={{0,4},{4,0},{8,12},{12,8},{16,20},{20,16},{24,28},{28,24},{1,5},{5... | collective-permute-start | bytes 1572872 | tf_op jit(solution)/shard_map/ppermute | solution.py:408
  265.3 25.0 %collective-permute-start.40 = (bf16[4,2,64,512]{3,2,1,0:T(8,128)(2,1)S(1)}, bf16[4,2,64,512]{3,2,1,0:T(8,128)(2,1)S(1)}, u32[]{:S(2)}, u32[]{:S(2)}) collective-permute-start(bf16[4,2,64,512]{3,2,1,0:T(8,128)(2,1)S(1)} %copy-done.32), channel_id=1, source_target_pairs={{0,4},{4,0},{8,12},{12,8},{16,20},{20,16},{24,28},{28,24},{1,5},{5... | collective-permute-start | bytes 1572872 | tf_op jit(solution)/shard_map/ppermute | solution.py:408
  266.3 61.0 %collective-permute-start.44 = (bf16[4,2,64,512]{3,2,1,0:T(8,128)(2,1)}, bf16[4,2,64,512]{3,2,1,0:T(8,128)(2,1)S(1)}, u32[]{:S(2)}, u32[]{:S(2)}) collective-permute-start(bf16[4,2,64,512]{3,2,1,0:T(8,128)(2,1)} %get-tuple-element.111), channel_id=1, source_target_pairs={{0,4},{4,0},{8,12},{12,8},{16,20},{20,16},{24,28},{28,24},{1,5},{5... | collective-permute-start | bytes 1572872 | tf_op jit(solution)/shard_map/ppermute | solution.py:408
  273.1 57.0 %collective-permute-start.48 = (bf16[4,2,64,512]{3,2,1,0:T(8,128)(2,1)}, bf16[4,2,64,512]{3,2,1,0:T(8,128)(2,1)S(1)}, u32[]{:S(2)}, u32[]{:S(2)}) collective-permute-start(bf16[4,2,64,512]{3,2,1,0:T(8,128)(2,1)} %get-tuple-element.117), channel_id=1, source_target_pairs={{0,4},{4,0},{8,12},{12,8},{16,20},{20,16},{24,28},{28,24},{1,5},{5... | collective-permute-start | bytes 1572872 | tf_op jit(solution)/shard_map/ppermute | solution.py:408
  281.9 51.1 %collective-permute-start.37 = (bf16[2,64,512]{2,1,0:T(8,128)(2,1)}, bf16[2,64,512]{2,1,0:T(8,128)(2,1)S(1)}, u32[]{:S(2)}, u32[]{:S(2)}) collective-permute-start(bf16[2,64,512]{2,1,0:T(8,128)(2,1)} %get-tuple-element.101), channel_id=1, source_target_pairs={{0,8},{4,12},{8,16},{12,20},{16,24},{20,28},{24,0},{28,4},{1,9},{5... | collective-permute-start | bytes 393224 | tf_op jit(solution)/shard_map/ppermute | solution.py:408
  283.5 52.5 %collective-permute-start.38 = (bf16[2,64,512]{2,1,0:T(8,128)(2,1)}, bf16[2,64,512]{2,1,0:T(8,128)(2,1)S(1)}, u32[]{:S(2)}, u32[]{:S(2)}) collective-permute-start(bf16[2,64,512]{2,1,0:T(8,128)(2,1)} %get-tuple-element.102), channel_id=1, source_target_pairs={{0,16},{4,20},{8,24},{12,28},{16,0},{20,4},{24,8},{28,12},{1,17},{... | collective-permute-start | bytes 393224 | tf_op jit(solution)/shard_map/ppermute | solution.py:408
  290.3 45.7 %collective-permute-start.39 = (bf16[2,64,512]{2,1,0:T(8,128)(2,1)}, bf16[2,64,512]{2,1,0:T(8,128)(2,1)S(1)}, u32[]{:S(2)}, u32[]{:S(2)}) collective-permute-start(bf16[2,64,512]{2,1,0:T(8,128)(2,1)} %get-tuple-element.103), channel_id=1, source_target_pairs={{0,24},{4,28},{8,0},{12,4},{16,8},{20,12},{24,16},{28,20},{1,25},{... | collective-permute-start | bytes 393224 | tf_op jit(solution)/shard_map/ppermute | solution.py:408
  330.1 10.4 %collective-permute-start.42 = (bf16[2,64,512]{2,1,0:T(8,128)(2,1)}, bf16[2,64,512]{2,1,0:T(8,128)(2,1)S(1)}, u32[]{:S(2)}, u32[]{:S(2)}) collective-permute-start(bf16[2,64,512]{2,1,0:T(8,128)(2,1)} %get-tuple-element.108), channel_id=1, source_target_pairs={{0,16},{4,20},{8,24},{12,28},{16,0},{20,4},{24,8},{28,12},{1,17},{... | collective-permute-start | bytes 393224 | tf_op jit(solution)/shard_map/ppermute | solution.py:408
  332.9 11.3 %collective-permute-start.43 = (bf16[2,64,512]{2,1,0:T(8,128)(2,1)}, bf16[2,64,512]{2,1,0:T(8,128)(2,1)S(1)}, u32[]{:S(2)}, u32[]{:S(2)}) collective-permute-start(bf16[2,64,512]{2,1,0:T(8,128)(2,1)} %get-tuple-element.109), channel_id=1, source_target_pairs={{0,24},{4,28},{8,0},{12,4},{16,8},{20,12},{24,16},{28,20},{1,25},{... | collective-permute-start | bytes 393224 | tf_op jit(solution)/shard_map/ppermute | solution.py:408
  336.0 13.3 %collective-permute-start.45 = (bf16[2,64,512]{2,1,0:T(8,128)(2,1)}, bf16[2,64,512]{2,1,0:T(8,128)(2,1)S(1)}, u32[]{:S(2)}, u32[]{:S(2)}) collective-permute-start(bf16[2,64,512]{2,1,0:T(8,128)(2,1)} %get-tuple-element.113), channel_id=1, source_target_pairs={{0,8},{4,12},{8,16},{12,20},{16,24},{20,28},{24,0},{28,4},{1,9},{5... | collective-permute-start | bytes 393224 | tf_op jit(solution)/shard_map/ppermute | solution.py:408
  336.0 19.4 %collective-permute-start.46 = (bf16[2,64,512]{2,1,0:T(8,128)(2,1)}, bf16[2,64,512]{2,1,0:T(8,128)(2,1)S(1)}, u32[]{:S(2)}, u32[]{:S(2)}) collective-permute-start(bf16[2,64,512]{2,1,0:T(8,128)(2,1)} %get-tuple-element.114), channel_id=1, source_target_pairs={{0,16},{4,20},{8,24},{12,28},{16,0},{20,4},{24,8},{28,12},{1,17},{... | collective-permute-start | bytes 393224 | tf_op jit(solution)/shard_map/ppermute | solution.py:408
  337.4 18.0 %collective-permute-start.47 = (bf16[2,64,512]{2,1,0:T(8,128)(2,1)}, bf16[2,64,512]{2,1,0:T(8,128)(2,1)S(1)}, u32[]{:S(2)}, u32[]{:S(2)}) collective-permute-start(bf16[2,64,512]{2,1,0:T(8,128)(2,1)} %get-tuple-element.115), channel_id=1, source_target_pairs={{0,24},{4,28},{8,0},{12,4},{16,8},{20,12},{24,16},{28,20},{1,25},{... | collective-permute-start | bytes 393224 | tf_op jit(solution)/shard_map/ppermute | solution.py:408
  340.5 15.9 %collective-permute-start.49 = (bf16[2,64,512]{2,1,0:T(8,128)(2,1)}, bf16[2,64,512]{2,1,0:T(8,128)(2,1)S(1)}, u32[]{:S(2)}, u32[]{:S(2)}) collective-permute-start(bf16[2,64,512]{2,1,0:T(8,128)(2,1)} %get-tuple-element.119), channel_id=1, source_target_pairs={{0,8},{4,12},{8,16},{12,20},{16,24},{20,28},{24,0},{28,4},{1,9},{5... | collective-permute-start | bytes 393224 | tf_op jit(solution)/shard_map/ppermute | solution.py:408
  344.2 17.3 %collective-permute-start.50 = (bf16[2,64,512]{2,1,0:T(8,128)(2,1)}, bf16[2,64,512]{2,1,0:T(8,128)(2,1)S(1)}, u32[]{:S(2)}, u32[]{:S(2)}) collective-permute-start(bf16[2,64,512]{2,1,0:T(8,128)(2,1)} %get-tuple-element.120), channel_id=1, source_target_pairs={{0,16},{4,20},{8,24},{12,28},{16,0},{20,4},{24,8},{28,12},{1,17},{... | collective-permute-start | bytes 393224 | tf_op jit(solution)/shard_map/ppermute | solution.py:408
  349.3 12.2 %collective-permute-start.51 = (bf16[2,64,512]{2,1,0:T(8,128)(2,1)}, bf16[2,64,512]{2,1,0:T(8,128)(2,1)S(1)}, u32[]{:S(2)}, u32[]{:S(2)}) collective-permute-start(bf16[2,64,512]{2,1,0:T(8,128)(2,1)} %get-tuple-element.121), channel_id=1, source_target_pairs={{0,24},{4,28},{8,0},{12,4},{16,8},{20,12},{24,16},{28,20},{1,25},{... | collective-permute-start | bytes 393224 | tf_op jit(solution)/shard_map/ppermute | solution.py:408
  (38 other events, 817.1 us)

commit v2 on v1

--- a/solution.py
+++ b/solution.py
@@ -71,41 +71,38 @@
             ],
             out_specs=[pl.BlockSpec((1, n // 2, n), lambda e, sel: (e, 0, 0))] * 2,
         ),
-        compiler_params=params(56),
+        compiler_params=params(40),
         cost_estimate=cost(le * 6 * n**3, le * n * n * 6),
         name="lesser",
     )(which[None], green, broadening)
 
 
-def place_kernel(where, c_ref, *refs):
-    full_ref, turned_ref = refs[-2:]
-    full_ref[...] = c_ref[...]
-    for q in range(c_ref.shape[0]):
-        turned_ref[q] = c_ref[q].T
-
-
-def place_coupling(where, piece, held):
-    nk, rows, n = piece.shape
-    each = 4
-    alias = [] if held is None else list(held)
+def place_kernel(where, *refs):
+    pieces, (full_ref, turned_ref) = refs[:-2], refs[-2:]
+    rows = pieces[0].shape[1]
+    for at, c_ref in enumerate(pieces):
+        start = pl.ds(pl.multiple_of(where[at] * rows, rows), rows)
+        for q in range(c_ref.shape[0]):
+            full_ref[q, start, :] = c_ref[q]
+            turned_ref[q, :, start] = c_ref[q].T
+
+
+def place_coupling(where, pieces):
+    nk, rows, n = pieces[0].shape
+    each = 2
     return pl.pallas_call(
         place_kernel,
-        out_shape=[jax.ShapeDtypeStruct((nk, n, n), BF16)] * 2,
+        out_shape=[pltpu.VMEM((nk, n, n), BF16)] * 2,
         grid_spec=pltpu.PrefetchScalarGridSpec(
             num_scalar_prefetch=1,
             grid=(nk // each,),
-            in_specs=[pl.BlockSpec((each, rows, n), lambda q, w: (q, 0, 0))]
-            + [pl.BlockSpec(memory_space=pl.ANY)] * len(alias),
-            out_specs=[
-                pl.BlockSpec((each, rows, n), lambda q, w: (q, w[0], 0)),
-                pl.BlockSpec((each, n, rows), lambda q, w: (q, 0, w[0])),
-            ],
-        ),
-        input_output_aliases={2: 0, 3: 1} if alias else {},
-        compiler_params=params(56),
-        cost_estimate=cost(nk * rows * n * 4, nk * rows * n * 6),
+            in_specs=[pl.BlockSpec((each, rows, n), lambda q, w: (q, 0, 0))] * len(pieces),
+            out_specs=[pl.BlockSpec((each, n, n), lambda q, w: (q, 0, 0))] * 2,
+        ),
+        compiler_params=params(40),
+        cost_estimate=cost(nk * n * n * 4, nk * n * n * 6),
         name="place",
-    )(where[None], piece, *alias)
+    )(where, *pieces)
 
 
 def source_kernel(odd, w_ref, keep, recv, kz, rz, *refs):
@@ -159,7 +156,7 @@
             out_specs=specs,
         ),
         input_output_aliases=alias,
-        compiler_params=params(56),
+        compiler_params=params(40),
         cost_estimate=cost(le * half * n * 16, le * half * n * 12),
         name="source",
     )(odd[None], weights, keep, recv, kz, rz, *extra)
@@ -213,7 +210,7 @@
             out_specs=[block(lk), block(lk)],
             scratch_shapes=[pltpu.VMEM((count, rows, n), BF16)],
         ),
-        compiler_params=params(56),
+        compiler_params=params(40),
         cost_estimate=cost(4 * lk * count * n * n, n * n * (6 * count + 4 * lk)),
         name="home",
     )(slots, *pieces, full, turned)
@@ -282,7 +279,7 @@
             scratch_shapes=[pltpu.VMEM((count, rows, cols), BF16)] * 2,
         ),
         input_output_aliases={2 + len(in_specs) - 1: 0} if alias else {},
-        compiler_params=params(56),
+        compiler_params=params(40),
         cost_estimate=cost(4 * count * count * rows * n, rows * n * count * 10),
         name="rows",
     )(mine[None], slots, *pieces, *pieces, coupling, *alias)
@@ -324,46 +321,54 @@
             one,
         ] + [pair] * len(alias),
         out_specs=pair,
-        compiler_params=params(56),
+        compiler_params=params(40),
         cost_estimate=cost(16 * lk * n**3, lk * n * n * 20),
         name="density",
     )(green, broadening, x, y, *alias)
 
 
-def last_density_kernel(scale, energy, odd, g_ref, gamma_ref, x_ref, y_ref, held_ref, keep_ref, send_ref, d_ref):
-    groups, _, rows, _ = keep_ref.shape
+def last_density_kernel(scale, energy, odd, g_ref, gamma_ref, x_ref, y_ref, held_ref, *refs):
+    d_ref, outs = refs[-1], refs[:-1]
+    groups, _, rows, _ = outs[0].shape
     for c, d in enumerate(density_terms(energy, g_ref, gamma_ref, x_ref, y_ref)):
         d_ref[c] = (d + held_ref[0, c]) * scale
-        for g in range(groups):
-            mine = pl.multiple_of((2 * g + odd[0]) * rows, rows)
-            other = pl.multiple_of((2 * g + 1 - odd[0]) * rows, rows)
-            keep_ref[g, c] = d_ref[c, pl.ds(mine, rows), :].astype(BF16)
-            send_ref[g, c] = d_ref[c, pl.ds(other, rows), :].astype(BF16)
-
-
-def last_density(scale, energy, k, groups, odd, green, broadening, x, y, held):
+    for i in range(len(outs) // 2):
+        keep_ref, send_ref = outs[2 * i], outs[2 * i + 1]
+
+        @pl.when(pl.program_id(0) == i)
+        def _():
+            for c in range(2):
+                for g in range(groups):
+                    mine = pl.multiple_of((2 * g + odd[0]) * rows, rows)
+                    other = pl.multiple_of((2 * g + 1 - odd[0]) * rows, rows)
+                    keep_ref[g, c] = d_ref[c, pl.ds(mine, rows), :].astype(BF16)
+                    send_ref[g, c] = d_ref[c, pl.ds(other, rows), :].astype(BF16)
+
+
+def last_density(scale, energy, start, stop, groups, odd, green, broadening, x, y, held):
     _, le, _, n, _ = green.shape
     rows = n // (2 * groups)
-    one = pl.BlockSpec((1, n, n), lambda i, odd: (k, 0, 0))
+    count = stop - start
+    one = pl.BlockSpec((1, n, n), lambda i, odd: (start + i, 0, 0))
     out = pl.BlockSpec((groups, 2, rows, n), lambda i, odd: (0, 0, 0, 0))
     return pl.pallas_call(
         functools.partial(last_density_kernel, scale, energy),
-        out_shape=[jax.ShapeDtypeStruct((groups, 2, rows, n), BF16)] * 2,
+        out_shape=[jax.ShapeDtypeStruct((groups, 2, rows, n), BF16)] * (2 * count),
         grid_spec=pltpu.PrefetchScalarGridSpec(
             num_scalar_prefetch=1,
-            grid=(1,),
+            grid=(count,),
             in_specs=[
-                pl.BlockSpec((1, 1, 2, n, n), lambda i, odd: (k, energy, 0, 0, 0)),
-                pl.BlockSpec((1, le, n), lambda i, odd: (k, 0, 0)),
+                pl.BlockSpec((1, 1, 2, n, n), lambda i, odd: (start + i, energy, 0, 0, 0)),
+                pl.BlockSpec((1, le, n), lambda i, odd: (start + i, 0, 0)),
                 one,
                 one,
-                pl.BlockSpec((1, 2, n, n), lambda i, odd: (k, 0, 0, 0)),
+                pl.BlockSpec((1, 2, n, n), lambda i, odd: (start + i, 0, 0, 0)),
             ],
-            out_specs=[out, out],
+            out_specs=[out] * (2 * count),
             scratch_shapes=[pltpu.VMEM((2, n, n), F32)],
         ),
-        compiler_params=params(56),
-        cost_estimate=cost(16 * n**3, n * n * 20),
+        compiler_params=params(40),
+        cost_estimate=cost(count * 16 * n**3, count * n * n * 20),
         name="density",
     )(odd[None], green, broadening, x, y, held)
 
@@ -383,7 +388,7 @@
         out_shape=[jax.ShapeDtypeStruct(keep.shape[1:], BF16)] * groups,
         in_specs=[pl.BlockSpec(memory_space=pltpu.SMEM), vmem, vmem],
         out_specs=[vmem] * groups,
-        compiler_params=params(56),
+        compiler_params=params(40),
         cost_estimate=cost(keep.size, keep.size * 6),
         name="pairsum",
     )(group[None], keep, recv)
@@ -435,6 +440,7 @@
     own_slots = lax.dynamic_slice_in_dim(slots, mine * lk, lk, 0).reshape(-1)
     all_slots = slots.reshape(-1)
 
+    green_ret = pltpu.with_memory_space_constraint(green_ret, pltpu.HBM)
     coupling_pieces = spread(coupling)
 
     send = [lesser_packed((1 - odd) * hk + j, green_ret, broadening) for j in range(hk)]
@@ -449,10 +455,7 @@
                 odd, weights, j, h, hk, keep[j][h], recv[j][h], kz[j][h], rz[j][h], last)
         got.append(last)
 
-    placed = None
-    for at in sorted(range(nm), key=lambda a: (a & 1, a)):
-        placed = place_coupling(mine ^ order[at], coupling_pieces[at], placed)
-    full, turned = placed
+    full, turned = place_coupling(jnp.stack([mine ^ o for o in order]), coupling_pieces)
 
     held_rows, held_density = None, None
     scale = 1.0 / (le * ne)
@@ -466,9 +469,13 @@
         if e < le - 1:
             held_density = first_density(e, green_ret, broadening, x, y, held_density)
         else:
+            shares = []
+            for start, stop in ((0, 1), (1, lk)):
+                shares = shares + list(last_density(
+                    scale, e, start, stop, groups, odd,
+                    green_ret, broadening, x, y, held_density))
             for k in range(lk):
-                kept, sent = last_density(
-                    scale, e, k, groups, odd, green_ret, broadening, x, y, held_density)
+                kept, sent = shares[2 * k], shares[2 * k + 1]
                 other = over_energy(sent, pairs)
                 parts = pair_sum(group, kept, other)
                 total = parts[0].astype(F32)

time: 366 us -> 364 us (level)
  local copies, waits for them, and re-layouts: 9.97 us -> 48.3 us
  Pallas kernels: 154 us -> 120 us
  waiting for transfers between devices: 117 us -> 110 us
    unnamed x69 -> x135, local copies, waits for them, and re-layouts: 8.73 us -> 48.2 us
    pallas_call x4 -> x1, Pallas kernels: 18.2 us -> 8.24 us  [place_coupling(): pl.pallas_call(place_kernel, out_shape=[pltpu.VMEM((nk, n, n), BF16)] * 2...]
    pallas_call x4 -> x2, Pallas kernels: 23.1 us -> 15.8 us  [last_density(): pl.pallas_call(functools.partial(last_density_kernel, scale, energy), out...]
    pallas_call x2, Pallas kernels: 30.1 us -> 25.6 us  [home_blocks(): pl.pallas_call(functools.partial(home_kernel, lk, len(pieces)), out_shape...]
    ppermute x21, waiting for transfers between devices: 62.9 us -> 58.5 us  [swap(): return lax.ppermute(x, 'mom', [(i, i ^ stride) for i in range(nm)])]
    pallas_call x4, Pallas kernels: 14.1 us -> 9.72 us  [sources(): pl.pallas_call(source_kernel, out_shape=[jax.ShapeDtypeStruct(shape, BF16...]
  transfers between devices with their start and end apart: 52 -> 52, of which waited for: 17 -> 17; matrix products, arithmetic and copies ran while one was open for 2% -> 1% of each run, Pallas kernels for 32% -> 27%
where the time goes in v2:
time: 364 us; the launch traced here: 361 us
  Pallas kernels  120 us (33%)
  waiting for transfers between devices  110 us (30%)
  starting transfers between devices  76.5 us (21%)
  local copies, waits for them, and re-layouts  48.3 us (13%)
  other arithmetic  5.26 us (1%)
    ppermute x31, starting transfers between devices, over_energy(): return lax.ppermute(x, 'energy', perm)  64.6 us
    ppermute x21, waiting for transfers between devices, swap(): return lax.ppermute(x, 'mom', [(i, i ^ stride) for i in range(nm)])  58.5 us
    ppermute x31, waiting for transfers between devices, over_energy(): return lax.ppermute(x, 'energy', perm)  51.2 us
    unnamed x135, local copies, waits for them, and re-layouts  48.2 us
    pallas_call x2, Pallas kernels, own_rows(): pl.pallas_call(functools.partial(rows_kernel, len(pieces)), out_shape=jax...  28.7 us
    pallas_call x2, Pallas kernels, home_blocks(): pl.pallas_call(functools.partial(home_kernel, lk, len(pieces)), out_shape...  25.6 us
    pallas_call x2, Pallas kernels, last_density(): pl.pallas_call(functools.partial(last_density_kernel, scale, energy), out...  15.8 us
    pallas_call x4, Pallas kernels, lesser_packed(): pl.pallas_call(lesser_kernel, out_shape=[jax.ShapeDtypeStruct((le, n // 2...  15.7 us
  transfers between devices with their start and end apart: 52, of which 17 were waited for; matrix products, arithmetic and copies ran while one was open for 1% of the time, Pallas kernels for 27%

profile of v2, /device:TPU:0, one launch (start us, length us, event | category | flops | bytes accessed | tf_op | source)
XLA Modules:
  0.0 361.5 jit_solution(3149400669549997345)
XLA Ops:
  1.4 4.1 %lesser.7 = (bf16[2,256,512]{2,1,0:T(8,128)(2,1)}, bf16[2,256,512]{2,1,0:T(8,128)(2,1)}) custom-call(s32[1]{0:T(128)} %bitcast.9.sel, bf16[4,2,2,512,512]{4,3,2,1,0:T(8,128)(2,1)} %g_ref.13, f32[4,2,512]{2,1,0:T(2,128)S(1)} %copy-done.60), custom_call_target="tpu_custom_call" | custom-call | flops 1610612736 | bytes 3145728 | tf_op jit(solution)/shard_map/lesser/pallas_call | solution.py:62
  5.5 3.0 collective-permute-start.9
  8.5 4.0 %lesser.6 = (bf16[2,256,512]{2,1,0:T(8,128)(2,1)S(1)}, bf16[2,256,512]{2,1,0:T(8,128)(2,1)}) custom-call(s32[1]{0:T(128)} %bitcast.8.sel, bf16[4,2,2,512,512]{4,3,2,1,0:T(8,128)(2,1)} %g_ref.13, f32[4,2,512]{2,1,0:T(2,128)S(1)} %copy-done.61), custom_call_target="tpu_custom_call" | custom-call | flops 1610612736 | bytes 3145728 | tf_op jit(solution)/shard_map/lesser/pallas_call | solution.py:62
  13.7 3.5 collective-permute-start.6
  18.5 4.2 %lesser.5 = (bf16[2,256,512]{2,1,0:T(8,128)(2,1)}, bf16[2,256,512]{2,1,0:T(8,128)(2,1)}) custom-call(s32[1]{0:T(128)} %bitcast.7.sel, bf16[4,2,2,512,512]{4,3,2,1,0:T(8,128)(2,1)} %g_ref.13, f32[4,2,512]{2,1,0:T(2,128)S(1)} %copy-done.61), custom_call_target="tpu_custom_call" | custom-call | flops 1610612736 | bytes 3145728 | tf_op jit(solution)/shard_map/lesser/pallas_call | solution.py:62
  22.8 2.6 collective-permute-start.3
  25.5 3.7 %collective-permute-done.10.kz = bf16[2,256,512]{2,1,0:T(8,128)(2,1)} collective-permute-done((bf16[2,256,512]{2,1,0:T(8,128)(2,1)S(1)}, bf16[2,256,512]{2,1,0:T(8,128)(2,1)}, u32[]{:S(2)}, u32[]{:S(2)}) %collective-permute-start.10) | collective-permute-done | bytes 524320 | tf_op jit(solution)/shard_map/ppermute | solution.py:413
  29.2 3.5 collective-permute-start.11
  32.8 4.8 %collective-permute-start.8 = (bf16[2,256,512]{2,1,0:T(8,128)(2,1)}, bf16[2,256,512]{2,1,0:T(8,128)(2,1)}, u32[]{:S(2)}, u32[]{:S(2)}) collective-permute-start(bf16[2,256,512]{2,1,0:T(8,128)(2,1)} %collective-permute-done.6.recv), channel_id=1, source_target_pairs={{0,8},{8,16},{12,4},{16,24},{20,12},{28,20},{1,9},{9,17},{13,5},{1... | collective-permute-start | bytes 1572872 | tf_op jit(solution)/shard_map/ppermute | solution.py:413
  40.6 3.4 lesser.4
  45.3 9.1 %collective-permute-done.recv = bf16[2,256,512]{2,1,0:T(8,128)(2,1)} collective-permute-done((bf16[2,256,512]{2,1,0:T(8,128)(2,1)}, bf16[2,256,512]{2,1,0:T(8,128)(2,1)}, u32[]{:S(2)}, u32[]{:S(2)}) %collective-permute-start) | collective-permute-done | bytes 524320 | tf_op jit(solution)/shard_map/ppermute | solution.py:413
  54.4 3.7 %collective-permute-start.5 = (bf16[2,256,512]{2,1,0:T(8,128)(2,1)}, bf16[2,256,512]{2,1,0:T(8,128)(2,1)S(1)}, u32[]{:S(2)}, u32[]{:S(2)}) collective-permute-start(bf16[2,256,512]{2,1,0:T(8,128)(2,1)} %collective-permute-done.3.recv), channel_id=1, source_target_pairs={{0,8},{8,16},{12,4},{16,24},{20,12},{28,20},{1,9},{9,17},{13,5},{1... | collective-permute-start | bytes 1572872 | tf_op jit(solution)/shard_map/ppermute | solution.py:413
  60.2 4.8 %collective-permute-start.2 = (bf16[2,256,512]{2,1,0:T(8,128)(2,1)}, bf16[2,256,512]{2,1,0:T(8,128)(2,1)S(1)}, u32[]{:S(2)}, u32[]{:S(2)}) collective-permute-start(bf16[2,256,512]{2,1,0:T(8,128)(2,1)} %collective-permute-done.recv), channel_id=1, source_target_pairs={{0,8},{8,16},{12,4},{16,24},{20,12},{28,20},{1,9},{9,17},{13,5},{1... | collective-permute-start | bytes 1572872 | tf_op jit(solution)/shard_map/ppermute | solution.py:413
  65.7 2.6 pad_maximum_fusion.w_ref
  70.4 2.4 source.4
  72.8 2.6 source.5
  75.4 2.4 source.6
  77.8 2.1 collective-permute-done.2.rz
  80.0 2.4 source.7
  82.3 2.4 collective-permute-start.20
  87.1 10.4 %collective-permute-done.20.refs_3_.refs_19_ = bf16[1,512,512]{2,1,0:T(8,128)(2,1)S(1)} collective-permute-done((bf16[1,512,512]{2,1,0:T(8,128)(2,1)S(1)}, bf16[1,512,512]{2,1,0:T(8,128)(2,1)S(1)}, u32[]{:S(2)}, u32[]{:S(2)}) %collective-permute-start.20) | collective-permute-done | bytes 524320 | tf_op jit(solution)/shard_map/ppermute | solution.py:413
  100.4 5.9 %collective-permute-done.19.refs_2_.refs_18_ = bf16[1,512,512]{2,1,0:T(8,128)(2,1)S(1)} collective-permute-done((bf16[1,512,512]{2,1,0:T(8,128)(2,1)S(1)}, bf16[1,512,512]{2,1,0:T(8,128)(2,1)S(1)}, u32[]{:S(2)}, u32[]{:S(2)}) %collective-permute-start.19) | collective-permute-done | bytes 524320 | tf_op jit(solution)/shard_map/ppermute | solution.py:413
  106.2 6.0 %collective-permute-done.21.refs_4_.refs_20_ = bf16[1,512,512]{2,1,0:T(8,128)(2,1)S(1)} collective-permute-done((bf16[1,512,512]{2,1,0:T(8,128)(2,1)S(1)}, bf16[1,512,512]{2,1,0:T(8,128)(2,1)S(1)}, u32[]{:S(2)}, u32[]{:S(2)}) %collective-permute-start.21) | collective-permute-done | bytes 524320 | tf_op jit(solution)/shard_map/ppermute | solution.py:416
  115.2 3.9 %collective-permute-done.24.refs_7_.refs_23_ = bf16[1,512,512]{2,1,0:T(8,128)(2,1)} collective-permute-done((bf16[1,512,512]{2,1,0:T(8,128)(2,1)S(1)}, bf16[1,512,512]{2,1,0:T(8,128)(2,1)}, u32[]{:S(2)}, u32[]{:S(2)}) %collective-permute-start.24) | collective-permute-done | bytes 524320 | tf_op jit(solution)/shard_map/ppermute | solution.py:416
  124.2 11.1 %collective-permute-done.23.refs_6_.refs_22_ = bf16[1,512,512]{2,1,0:T(8,128)(2,1)} collective-permute-done((bf16[1,512,512]{2,1,0:T(8,128)(2,1)S(1)}, bf16[1,512,512]{2,1,0:T(8,128)(2,1)}, u32[]{:S(2)}, u32[]{:S(2)}) %collective-permute-start.23) | collective-permute-done | bytes 524320 | tf_op jit(solution)/shard_map/ppermute | solution.py:416
  144.6 16.8 %collective-permute-done.13.refs_2_.refs_10_ = bf16[2,512,512]{2,1,0:T(8,128)(2,1)} collective-permute-done((bf16[2,512,512]{2,1,0:T(8,128)(2,1)S(1)}, bf16[2,512,512]{2,1,0:T(8,128)(2,1)}, u32[]{:S(2)}, u32[]{:S(2)}) %collective-permute-start.13) | collective-permute-done | bytes 1048608 | tf_op jit(solution)/shard_map/ppermute | solution.py:416
  161.9 20.6 %collective-permute-done.14.refs_3_.refs_11_ = bf16[2,512,512]{2,1,0:T(8,128)(2,1)} collective-permute-done((bf16[2,512,512]{2,1,0:T(8,128)(2,1)}, bf16[2,512,512]{2,1,0:T(8,128)(2,1)}, u32[]{:S(2)}, u32[]{:S(2)}) %collective-permute-start.14) | collective-permute-done | bytes 1048608 | tf_op jit(solution)/shard_map/ppermute | solution.py:416
  183.8 8.2 %place.1 = (bf16[16,512,512]{2,1,0:T(8,128)(2,1)S(1)}, bf16[16,512,512]{2,1,0:T(8,128)(2,1)S(1)}) custom-call(s32[4]{0:T(128)} %pad_add_fusion.where, bf16[16,128,512]{2,1,0:T(8,128)(2,1)} %refs_0_.1, bf16[16,128,512]{2,1,0:T(8,128)(2,1)} %collective-permute-done.33.refs_1_, bf16[16,128,512]{2,1,0:T(8,128)(2,1)} %copy-done.62, ...), custom_call_target="tpu_custom_call" | custom-call | flops 16777216 | bytes 25165824 | tf_op jit(solution)/shard_map/place/pallas_call | solution.py:93
  192.1 3.4 copy-done
  195.5 3.3 copy-done.1
  202.0 12.4 %home.3 = (bf16[4,512,512]{2,1,0:T(8,128)(2,1)S(1)}, bf16[4,512,512]{2,1,0:T(8,128)(2,1)S(1)}) custom-call(s32[64]{0:T(128)S(1)} %reshape.11.slots, bf16[1,512,512]{2,1,0:T(8,128)(2,1)S(1)} %copy-done.12, bf16[1,512,512]{2,1,0:T(8,128)(2,1)S(1)} %copy-done.9, bf16[1,512,512]{2,1,0:T(8,128)(2,1)S(1)} %copy-done.26, bf16[1,512,512]{2,1,0:T(8,128)(2,1)S(1)} %copy-done.17, ...), custom_call_target="tpu_custom_call" | custom-call | flops 67108864 | bytes 29360128 | tf_op jit(solution)/shard_map/home/pallas_call | solution.py:203
  214.5 11.2 %density.3.held_ref = f32[4,2,512,512]{3,2,1,0:T(8,128)S(1)} custom-call(bf16[4,2,2,512,512]{4,3,2,1,0:T(8,128)(2,1)} %g_ref.13, f32[4,2,512]{2,1,0:T(2,128)S(1)} %copy-done.61, bf16[4,512,512]{2,1,0:T(8,128)(2,1)S(1)} %get-tuple-element.84.x_ref, bf16[4,512,512]{2,1,0:T(8,128)(2,1)S(1)} %get-tuple-element.85.y_ref), custom_call_target="tpu_custom_call" | custom-call | flops 8589934592 | bytes 20971520 | tf_op jit(solution)/shard_map/density/pallas_call | solution.py:313
  225.7 3.3 copy-done.14
  229.1 13.2 %home.2 = (bf16[4,512,512]{2,1,0:T(8,128)(2,1)S(1)}, bf16[4,512,512]{2,1,0:T(8,128)(2,1)S(1)}) custom-call(s32[64]{0:T(128)S(1)} %reshape.11.slots, bf16[2,512,512]{2,1,0:T(8,128)(2,1)S(1)} %get-tuple-element.74.refs_0_.refs_8_, bf16[2,512,512]{2,1,0:T(8,128)(2,1)} %collective-permute-done.12.refs_1_.refs_9_, ...), custom_call_target="tpu_custom_call" | custom-call | flops 67108864 | bytes 29360128 | tf_op jit(solution)/shard_map/home/pallas_call | solution.py:203
  242.3 3.4 copy-done.15
  245.7 4.7 %density.4 = (bf16[4,2,64,512]{3,2,1,0:T(8,128)(2,1)S(1)}, bf16[4,2,64,512]{3,2,1,0:T(8,128)(2,1)}) custom-call(s32[1]{0:T(128)} %bitcast.1.odd, bf16[4,2,2,512,512]{4,3,2,1,0:T(8,128)(2,1)} %g_ref.13, f32[4,2,512]{2,1,0:T(2,128)S(1)} %copy-done.61, bf16[4,512,512]{2,1,0:T(8,128)(2,1)S(1)} %get-tuple-element.82.x_ref, ...), custom_call_target="tpu_custom_call" | custom-call | flops 2147483648 | bytes 5242880 | tf_op jit(solution)/shard_map/density/pallas_call | solution.py:354
  251.5 11.1 %density.5 = (bf16[4,2,64,512]{3,2,1,0:T(8,128)(2,1)S(1)}, bf16[4,2,64,512]{3,2,1,0:T(8,128)(2,1)}, bf16[4,2,64,512]{3,2,1,0:T(8,128)(2,1)S(1)}, bf16[4,2,64,512...) custom-call(s32[1]{0:T(128)} %bitcast.1.odd, ...), custom_call_target="tpu_custom_call" | custom-call | flops 6442450944 | bytes 15728640 | tf_op jit(solution)/shard_map/density/pallas_call | solution.py:354
  272.3 2.2 collective-permute-start.38
  274.5 5.6 %collective-permute-done.40.recv_ref = bf16[4,2,64,512]{3,2,1,0:T(8,128)(2,1)} collective-permute-done((bf16[4,2,64,512]{3,2,1,0:T(8,128)(2,1)}, bf16[4,2,64,512]{3,2,1,0:T(8,128)(2,1)}, u32[]{:S(2)}, u32[]{:S(2)}) %collective-permute-start.40) | collective-permute-done | bytes 524320 | tf_op jit(solution)/shard_map/ppermute | solution.py:413
  280.1 3.0 collective-permute-start.39
  295.7 14.4 %rows.2.refs_17_ = bf16[16,2,2,128,512]{4,3,2,1,0:T(8,128)(2,1)} custom-call(s32[1]{0:T(128)} %bitcast.mine, s32[256]{0:T(256)S(1)} %reshape.10.slots, bf16[1,512,512]{2,1,0:T(8,128)(2,1)S(1)} %copy-done.13, bf16[1,512,512]{2,1,0:T(8,128)(2,1)S(1)} %copy-done.10, bf16[1,512,512]{2,1,0:T(8,128)(2,1)S(1)} %copy-done.27, bf16[1,512,512]{2,1,0:T(8,128)(2,1)S(1)} %copy-done.18, ...), custom_call_target="tpu_custom_call" | custom-call | flops 67108864 | bytes 10485760 | tf_op jit(solution)/shard_map/rows/pallas_call | solution.py:271
  310.1 14.4 %rows.3 = bf16[16,2,2,128,512]{4,3,2,1,0:T(8,128)(2,1)} custom-call(s32[1]{0:T(128)} %bitcast.mine, s32[256]{0:T(256)S(1)} %reshape.10.slots, bf16[2,512,512]{2,1,0:T(8,128)(2,1)S(1)} %get-tuple-element.74.refs_0_.refs_8_, bf16[2,512,512]{2,1,0:T(8,128)(2,1)} %collective-permute-done.12.refs_1_.refs_9_, ...), custom_call_target="tpu_custom_call", output_to_operand_aliasing={{}: (19, {})} | custom-call | flops 67108864 | bytes 10485760 | tf_op jit(solution)/shard_map/rows/pallas_call | solution.py:271
  329.8 2.3 collective-permute-start.43
  335.3 2.9 collective-permute-start.47
  338.2 2.7 collective-permute-done.42
  341.6 4.7 %collective-permute-start.50 = (bf16[2,64,512]{2,1,0:T(8,128)(2,1)S(1)}, bf16[2,64,512]{2,1,0:T(8,128)(2,1)S(1)}, u32[]{:S(2)}, u32[]{:S(2)}) collective-permute-start(bf16[2,64,512]{2,1,0:T(8,128)(2,1)S(1)} %get-tuple-element.108), channel_id=1, source_target_pairs={{0,16},{4,20},{8,24},{12,28},{16,0},{20,4},{24,8},{28,12},{1,17},{... | collective-permute-start | bytes 393224 | tf_op jit(solution)/shard_map/ppermute | solution.py:413
  346.4 5.0 %collective-permute-start.51 = (bf16[2,64,512]{2,1,0:T(8,128)(2,1)S(1)}, bf16[2,64,512]{2,1,0:T(8,128)(2,1)S(1)}, u32[]{:S(2)}, u32[]{:S(2)}) collective-permute-start(bf16[2,64,512]{2,1,0:T(8,128)(2,1)S(1)} %get-tuple-element.109), channel_id=1, source_target_pairs={{0,24},{4,28},{8,0},{12,4},{16,8},{20,12},{24,16},{28,20},{1,25},{... | collective-permute-start | bytes 393224 | tf_op jit(solution)/shard_map/ppermute | solution.py:413
  352.6 6.9 %collective-permute-done.50 = bf16[2,64,512]{2,1,0:T(8,128)(2,1)S(1)} collective-permute-done((bf16[2,64,512]{2,1,0:T(8,128)(2,1)S(1)}, bf16[2,64,512]{2,1,0:T(8,128)(2,1)S(1)}, u32[]{:S(2)}, u32[]{:S(2)}) %collective-permute-start.50) | collective-permute-done | bytes 131104 | tf_op jit(solution)/shard_map/ppermute | solution.py:413
  (223 shorter events, 75.8 us)
Async XLA Ops:
  5.5 20.0 %collective-permute-start.9 = (bf16[2,256,512]{2,1,0:T(8,128)(2,1)}, bf16[2,256,512]{2,1,0:T(8,128)(2,1)S(1)}, u32[]{:S(2)}, u32[]{:S(2)}) collective-permute-start(bf16[2,256,512]{2,1,0:T(8,128)(2,1)} %get-tuple-element.63), channel_id=1, source_target_pairs={{0,4},{4,0},{8,12},{12,8},{16,20},{20,16},{24,28},{28,24},{1,5},{5... | collective-permute-start | bytes 1572872 | tf_op jit(solution)/shard_map/ppermute | solution.py:413
  12.5 16.8 %collective-permute-start.10 = (bf16[2,256,512]{2,1,0:T(8,128)(2,1)S(1)}, bf16[2,256,512]{2,1,0:T(8,128)(2,1)}, u32[]{:S(2)}, u32[]{:S(2)}) collective-permute-start(bf16[2,256,512]{2,1,0:T(8,128)(2,1)S(1)} %get-tuple-element.62.keep), channel_id=1, source_target_pairs={{4,12},{8,0},{12,20},{16,8},{20,28},{24,16},{5,13},{9,1},{13,21},{... | collective-permute-start | bytes 1572872 | tf_op jit(solution)/shard_map/ppermute | solution.py:413
  13.7 19.0 %collective-permute-start.6 = (bf16[2,256,512]{2,1,0:T(8,128)(2,1)}, bf16[2,256,512]{2,1,0:T(8,128)(2,1)}, u32[]{:S(2)}, u32[]{:S(2)}) collective-permute-start(bf16[2,256,512]{2,1,0:T(8,128)(2,1)} %get-tuple-element.61), channel_id=1, source_target_pairs={{0,4},{4,0},{8,12},{12,8},{16,20},{20,16},{24,28},{28,24},{1,5},{5... | collective-permute-start | bytes 1572872 | tf_op jit(solution)/shard_map/ppermute | solution.py:413
  17.2 21.8 %collective-permute-start.7 = (bf16[2,256,512]{2,1,0:T(8,128)(2,1)}, bf16[2,256,512]{2,1,0:T(8,128)(2,1)}, u32[]{:S(2)}, u32[]{:S(2)}) collective-permute-start(bf16[2,256,512]{2,1,0:T(8,128)(2,1)} %get-tuple-element.60.keep), channel_id=1, source_target_pairs={{4,12},{8,0},{12,20},{16,8},{20,28},{24,16},{5,13},{9,1},{13,21},{... | collective-permute-start | bytes 1572872 | tf_op jit(solution)/shard_map/ppermute | solution.py:413
  22.8 21.2 %collective-permute-start.3 = (bf16[2,256,512]{2,1,0:T(8,128)(2,1)}, bf16[2,256,512]{2,1,0:T(8,128)(2,1)}, u32[]{:S(2)}, u32[]{:S(2)}) collective-permute-start(bf16[2,256,512]{2,1,0:T(8,128)(2,1)} %get-tuple-element.59), channel_id=1, source_target_pairs={{0,4},{4,0},{8,12},{12,8},{16,20},{20,16},{24,28},{28,24},{1,5},{5... | collective-permute-start | bytes 1572872 | tf_op jit(solution)/shard_map/ppermute | solution.py:413
  25.4 29.0 %collective-permute-start = (bf16[2,256,512]{2,1,0:T(8,128)(2,1)}, bf16[2,256,512]{2,1,0:T(8,128)(2,1)}, u32[]{:S(2)}, u32[]{:S(2)}) collective-permute-start(bf16[2,256,512]{2,1,0:T(8,128)(2,1)} %get-tuple-element.57), channel_id=1, source_target_pairs={{0,4},{4,0},{8,12},{12,8},{16,20},{20,16},{24,28},{28,24},{1,5},{5... | collective-permute-start | bytes 1572872 | tf_op jit(solution)/shard_map/ppermute | solution.py:413
  29.2 28.9 %collective-permute-start.11 = (bf16[2,256,512]{2,1,0:T(8,128)(2,1)S(1)}, bf16[2,256,512]{2,1,0:T(8,128)(2,1)S(1)}, u32[]{:S(2)}, u32[]{:S(2)}) collective-permute-start(bf16[2,256,512]{2,1,0:T(8,128)(2,1)S(1)} %collective-permute-done.9.recv), channel_id=1, source_target_pairs={{0,8},{8,16},{12,4},{16,24},{20,12},{28,20},{1,9},{9,17},{13,5},{1... | collective-permute-start | bytes 1572872 | tf_op jit(solution)/shard_map/ppermute | solution.py:413
  32.8 27.4 %collective-permute-start.8 = (bf16[2,256,512]{2,1,0:T(8,128)(2,1)}, bf16[2,256,512]{2,1,0:T(8,128)(2,1)}, u32[]{:S(2)}, u32[]{:S(2)}) collective-permute-start(bf16[2,256,512]{2,1,0:T(8,128)(2,1)} %collective-permute-done.6.recv), channel_id=1, source_target_pairs={{0,8},{8,16},{12,4},{16,24},{20,12},{28,20},{1,9},{9,17},{13,5},{1... | collective-permute-start | bytes 1572872 | tf_op jit(solution)/shard_map/ppermute | solution.py:413
  39.1 81.0 %collective-permute-start.33 = (bf16[16,128,512]{2,1,0:T(8,128)(2,1)S(1)}, bf16[16,128,512]{2,1,0:T(8,128)(2,1)}, u32[]{:S(2)}, u32[]{:S(2)}) collective-permute-start(bf16[16,128,512]{2,1,0:T(8,128)(2,1)S(1)} %copy-done.2), channel_id=1, source_target_pairs={{0,2},{1,3},{2,0},{3,1},{4,6},{5,7},{6,4},{7,5},{8,10},{9,11},{10,... | collective-permute-start | bytes 6291464 | tf_op jit(solution)/shard_map/ppermute | solution.py:416
  44.0 31.4 %collective-permute-start.4 = (bf16[2,256,512]{2,1,0:T(8,128)(2,1)S(1)}, bf16[2,256,512]{2,1,0:T(8,128)(2,1)S(1)}, u32[]{:S(2)}, u32[]{:S(2)}) collective-permute-start(bf16[2,256,512]{2,1,0:T(8,128)(2,1)S(1)} %get-tuple-element.58.keep), channel_id=1, source_target_pairs={{4,12},{8,0},{12,20},{16,8},{20,28},{24,16},{5,13},{9,1},{13,21},{... | collective-permute-start | bytes 1572872 | tf_op jit(solution)/shard_map/ppermute | solution.py:413
  54.4 21.0 %collective-permute-start.5 = (bf16[2,256,512]{2,1,0:T(8,128)(2,1)}, bf16[2,256,512]{2,1,0:T(8,128)(2,1)S(1)}, u32[]{:S(2)}, u32[]{:S(2)}) collective-permute-start(bf16[2,256,512]{2,1,0:T(8,128)(2,1)} %collective-permute-done.3.recv), channel_id=1, source_target_pairs={{0,8},{8,16},{12,4},{16,24},{20,12},{28,20},{1,9},{9,17},{13,5},{1... | collective-permute-start | bytes 1572872 | tf_op jit(solution)/shard_map/ppermute | solution.py:413
  58.9 18.9 %collective-permute-start.1 = (bf16[2,256,512]{2,1,0:T(8,128)(2,1)S(1)}, bf16[2,256,512]{2,1,0:T(8,128)(2,1)S(1)}, u32[]{:S(2)}, u32[]{:S(2)}) collective-permute-start(bf16[2,256,512]{2,1,0:T(8,128)(2,1)S(1)} %get-tuple-element.56.keep), channel_id=1, source_target_pairs={{4,12},{8,0},{12,20},{16,8},{20,28},{24,16},{5,13},{9,1},{13,21},{... | collective-permute-start | bytes 1572872 | tf_op jit(solution)/shard_map/ppermute | solution.py:413
  60.2 19.7 %collective-permute-start.2 = (bf16[2,256,512]{2,1,0:T(8,128)(2,1)}, bf16[2,256,512]{2,1,0:T(8,128)(2,1)S(1)}, u32[]{:S(2)}, u32[]{:S(2)}) collective-permute-start(bf16[2,256,512]{2,1,0:T(8,128)(2,1)} %collective-permute-done.recv), channel_id=1, source_target_pairs={{0,8},{8,16},{12,4},{16,24},{20,12},{28,20},{1,9},{9,17},{13,5},{1... | collective-permute-start | bytes 1572872 | tf_op jit(solution)/shard_map/ppermute | solution.py:413
  82.3 15.1 %collective-permute-start.20 = (bf16[1,512,512]{2,1,0:T(8,128)(2,1)S(1)}, bf16[1,512,512]{2,1,0:T(8,128)(2,1)S(1)}, u32[]{:S(2)}, u32[]{:S(2)}) collective-permute-start(bf16[1,512,512]{2,1,0:T(8,128)(2,1)S(1)} %get-tuple-element.79), channel_id=1, source_target_pairs={{0,4},{4,0},{8,12},{12,8},{16,20},{20,16},{24,28},{28,24},{1,5},{5... | collective-permute-start | bytes 1572872 | tf_op jit(solution)/shard_map/ppermute | solution.py:413
  84.7 14.3 %collective-permute-start.22 = (bf16[1,512,512]{2,1,0:T(8,128)(2,1)S(1)}, bf16[1,512,512]{2,1,0:T(8,128)(2,1)S(1)}, u32[]{:S(2)}, u32[]{:S(2)}) collective-permute-start(bf16[1,512,512]{2,1,0:T(8,128)(2,1)S(1)} %get-tuple-element.77.refs_1_.refs_17_), channel_id=1, source_target_pairs={{0,2},{1,3},{2,0},{3,1},{4,6},{5,7},{6,4},{7,5},{8,10},{9,11},{10,... | collective-permute-start | bytes 1572872 | tf_op jit(solution)/shard_map/ppermute | solution.py:416
  86.2 12.8 %collective-permute-start.26 = (bf16[1,512,512]{2,1,0:T(8,128)(2,1)S(1)}, bf16[1,512,512]{2,1,0:T(8,128)(2,1)S(1)}, u32[]{:S(2)}, u32[]{:S(2)}) collective-permute-start(bf16[1,512,512]{2,1,0:T(8,128)(2,1)S(1)} %get-tuple-element.77.refs_1_.refs_17_), channel_id=1, source_target_pairs={{0,1},{1,0},{2,3},{3,2},{4,5},{5,4},{6,7},{7,6},{8,9},{9,8},{10,11... | collective-permute-start | bytes 1572872 | tf_op jit(solution)/shard_map/ppermute | solution.py:416
  87.0 19.2 %collective-permute-start.19 = (bf16[1,512,512]{2,1,0:T(8,128)(2,1)S(1)}, bf16[1,512,512]{2,1,0:T(8,128)(2,1)S(1)}, u32[]{:S(2)}, u32[]{:S(2)}) collective-permute-start(bf16[1,512,512]{2,1,0:T(8,128)(2,1)S(1)} %get-tuple-element.78), channel_id=1, source_target_pairs={{0,4},{4,0},{8,12},{12,8},{16,20},{20,16},{24,28},{28,24},{1,5},{5... | collective-permute-start | bytes 1572872 | tf_op jit(solution)/shard_map/ppermute | solution.py:413
  97.5 14.8 %collective-permute-start.21 = (bf16[1,512,512]{2,1,0:T(8,128)(2,1)S(1)}, bf16[1,512,512]{2,1,0:T(8,128)(2,1)S(1)}, u32[]{:S(2)}, u32[]{:S(2)}) collective-permute-start(bf16[1,512,512]{2,1,0:T(8,128)(2,1)S(1)} %get-tuple-element.76.refs_0_.refs_16_), channel_id=1, source_target_pairs={{0,2},{1,3},{2,0},{3,1},{4,6},{5,7},{6,4},{7,5},{8,10},{9,11},{10,... | collective-permute-start | bytes 1572872 | tf_op jit(solution)/shard_map/ppermute | solution.py:416
  99.0 14.1 %collective-permute-start.25 = (bf16[1,512,512]{2,1,0:T(8,128)(2,1)S(1)}, bf16[1,512,512]{2,1,0:T(8,128)(2,1)S(1)}, u32[]{:S(2)}, u32[]{:S(2)}) collective-permute-start(bf16[1,512,512]{2,1,0:T(8,128)(2,1)S(1)} %get-tuple-element.76.refs_0_.refs_16_), channel_id=1, source_target_pairs={{0,1},{1,0},{2,3},{3,2},{4,5},{5,4},{6,7},{7,6},{8,9},{9,8},{10,11... | collective-permute-start | bytes 1572872 | tf_op jit(solution)/shard_map/ppermute | solution.py:416
  99.9 19.3 %collective-permute-start.24 = (bf16[1,512,512]{2,1,0:T(8,128)(2,1)S(1)}, bf16[1,512,512]{2,1,0:T(8,128)(2,1)}, u32[]{:S(2)}, u32[]{:S(2)}) collective-permute-start(bf16[1,512,512]{2,1,0:T(8,128)(2,1)S(1)} %collective-permute-done.20.refs_3_.refs_19_), channel_id=1, source_target_pairs={{0,2},{1,3},{2,0},{3,1},{4,6},{5,7},{6,4},{7,5},{8,10},{9,11},{10,... | collective-permute-start | bytes 1572872 | tf_op jit(solution)/shard_map/ppermute | solution.py:416
  106.2 36.5 %collective-permute-start.34 = (bf16[16,128,512]{2,1,0:T(8,128)(2,1)S(1)}, bf16[16,128,512]{2,1,0:T(8,128)(2,1)S(1)}, u32[]{:S(2)}, u32[]{:S(2)}) collective-permute-start(bf16[16,128,512]{2,1,0:T(8,128)(2,1)S(1)} %copy-done.2), channel_id=1, source_target_pairs={{0,1},{1,0},{2,3},{3,2},{4,5},{5,4},{6,7},{7,6},{8,9},{9,8},{10,11... | collective-permute-start | bytes 6291464 | tf_op jit(solution)/shard_map/ppermute | solution.py:416
  119.1 21.3 %collective-permute-start.12 = (bf16[2,512,512]{2,1,0:T(8,128)(2,1)S(1)}, bf16[2,512,512]{2,1,0:T(8,128)(2,1)}, u32[]{:S(2)}, u32[]{:S(2)}) collective-permute-start(bf16[2,512,512]{2,1,0:T(8,128)(2,1)S(1)} %get-tuple-element.75), channel_id=1, source_target_pairs={{0,4},{4,0},{8,12},{12,8},{16,20},{20,16},{24,28},{28,24},{1,5},{5... | collective-permute-start | bytes 3145736 | tf_op jit(solution)/shard_map/ppermute | solution.py:413
  120.0 62.5 %collective-permute-start.35 = (bf16[16,128,512]{2,1,0:T(8,128)(2,1)}, bf16[16,128,512]{2,1,0:T(8,128)(2,1)}, u32[]{:S(2)}, u32[]{:S(2)}) collective-permute-start(bf16[16,128,512]{2,1,0:T(8,128)(2,1)} %collective-permute-done.33.refs_1_), channel_id=1, source_target_pairs={{0,1},{1,0},{2,3},{3,2},{4,5},{5,4},{6,7},{7,6},{8,9},{9,8},{10,11... | collective-permute-start | bytes 6291464 | tf_op jit(solution)/shard_map/ppermute | solution.py:416
  120.8 14.4 %collective-permute-start.23 = (bf16[1,512,512]{2,1,0:T(8,128)(2,1)S(1)}, bf16[1,512,512]{2,1,0:T(8,128)(2,1)}, u32[]{:S(2)}, u32[]{:S(2)}) collective-permute-start(bf16[1,512,512]{2,1,0:T(8,128)(2,1)S(1)} %collective-permute-done.19.refs_2_.refs_18_), channel_id=1, source_target_pairs={{0,2},{1,3},{2,0},{3,1},{4,6},{5,7},{6,4},{7,5},{8,10},{9,11},{10,... | collective-permute-start | bytes 1572872 | tf_op jit(solution)/shard_map/ppermute | solution.py:416
  123.2 13.6 %collective-permute-start.27 = (bf16[1,512,512]{2,1,0:T(8,128)(2,1)S(1)}, bf16[1,512,512]{2,1,0:T(8,128)(2,1)S(1)}, u32[]{:S(2)}, u32[]{:S(2)}) collective-permute-start(bf16[1,512,512]{2,1,0:T(8,128)(2,1)S(1)} %collective-permute-done.19.refs_2_.refs_18_), channel_id=1, source_target_pairs={{0,1},{1,0},{2,3},{3,2},{4,5},{5,4},{6,7},{7,6},{8,9},{9,8},{10,11... | collective-permute-start | bytes 1572872 | tf_op jit(solution)/shard_map/ppermute | solution.py:416
  135.3 26.1 %collective-permute-start.13 = (bf16[2,512,512]{2,1,0:T(8,128)(2,1)S(1)}, bf16[2,512,512]{2,1,0:T(8,128)(2,1)}, u32[]{:S(2)}, u32[]{:S(2)}) collective-permute-start(bf16[2,512,512]{2,1,0:T(8,128)(2,1)S(1)} %get-tuple-element.74.refs_0_.refs_8_), channel_id=1, source_target_pairs={{0,2},{1,3},{2,0},{3,1},{4,6},{5,7},{6,4},{7,5},{8,10},{9,11},{10,... | collective-permute-start | bytes 3145736 | tf_op jit(solution)/shard_map/ppermute | solution.py:416
  140.4 42.1 %collective-permute-start.14 = (bf16[2,512,512]{2,1,0:T(8,128)(2,1)}, bf16[2,512,512]{2,1,0:T(8,128)(2,1)}, u32[]{:S(2)}, u32[]{:S(2)}) collective-permute-start(bf16[2,512,512]{2,1,0:T(8,128)(2,1)} %collective-permute-done.12.refs_1_.refs_9_), channel_id=1, source_target_pairs={{0,2},{1,3},{2,0},{3,1},{4,6},{5,7},{6,4},{7,5},{8,10},{9,11},{10,... | collective-permute-start | bytes 3145736 | tf_op jit(solution)/shard_map/ppermute | solution.py:416
  142.7 18.7 %collective-permute-start.32 = (bf16[1,512,512]{2,1,0:T(8,128)(2,1)}, bf16[1,512,512]{2,1,0:T(8,128)(2,1)}, u32[]{:S(2)}, u32[]{:S(2)}) collective-permute-start(bf16[1,512,512]{2,1,0:T(8,128)(2,1)} %collective-permute-done.24.refs_7_.refs_23_), channel_id=1, source_target_pairs={{0,1},{1,0},{2,3},{3,2},{4,5},{5,4},{6,7},{7,6},{8,9},{9,8},{10,11... | collective-permute-start | bytes 1572872 | tf_op jit(solution)/shard_map/ppermute | solution.py:416
  144.1 54.7 %collective-permute-start.31 = (bf16[1,512,512]{2,1,0:T(8,128)(2,1)}, bf16[1,512,512]{2,1,0:T(8,128)(2,1)}, u32[]{:S(2)}, u32[]{:S(2)}) collective-permute-start(bf16[1,512,512]{2,1,0:T(8,128)(2,1)} %collective-permute-done.23.refs_6_.refs_22_), channel_id=1, source_target_pairs={{0,1},{1,0},{2,3},{3,2},{4,5},{5,4},{6,7},{7,6},{8,9},{9,8},{10,11... | collective-permute-start | bytes 1572872 | tf_op jit(solution)/shard_map/ppermute | solution.py:416
  161.4 67.7 %collective-permute-start.15 = (bf16[2,512,512]{2,1,0:T(8,128)(2,1)S(1)}, bf16[2,512,512]{2,1,0:T(8,128)(2,1)S(1)}, u32[]{:S(2)}, u32[]{:S(2)}) collective-permute-start(bf16[2,512,512]{2,1,0:T(8,128)(2,1)S(1)} %get-tuple-element.74.refs_0_.refs_8_), channel_id=1, source_target_pairs={{0,1},{1,0},{2,3},{3,2},{4,5},{5,4},{6,7},{7,6},{8,9},{9,8},{10,11... | collective-permute-start | bytes 3145736 | tf_op jit(solution)/shard_map/ppermute | solution.py:416
  161.4 67.7 %collective-permute-start.16 = (bf16[2,512,512]{2,1,0:T(8,128)(2,1)}, bf16[2,512,512]{2,1,0:T(8,128)(2,1)S(1)}, u32[]{:S(2)}, u32[]{:S(2)}) collective-permute-start(bf16[2,512,512]{2,1,0:T(8,128)(2,1)} %collective-permute-done.12.refs_1_.refs_9_), channel_id=1, source_target_pairs={{0,1},{1,0},{2,3},{3,2},{4,5},{5,4},{6,7},{7,6},{8,9},{9,8},{10,11... | collective-permute-start | bytes 3145736 | tf_op jit(solution)/shard_map/ppermute | solution.py:416
  182.5 46.5 %collective-permute-start.17 = (bf16[2,512,512]{2,1,0:T(8,128)(2,1)}, bf16[2,512,512]{2,1,0:T(8,128)(2,1)}, u32[]{:S(2)}, u32[]{:S(2)}) collective-permute-start(bf16[2,512,512]{2,1,0:T(8,128)(2,1)} %collective-permute-done.13.refs_2_.refs_10_), channel_id=1, source_target_pairs={{0,1},{1,0},{2,3},{3,2},{4,5},{5,4},{6,7},{7,6},{8,9},{9,8},{10,11... | collective-permute-start | bytes 3145736 | tf_op jit(solution)/shard_map/ppermute | solution.py:416
  182.5 46.5 %collective-permute-start.18 = (bf16[2,512,512]{2,1,0:T(8,128)(2,1)}, bf16[2,512,512]{2,1,0:T(8,128)(2,1)}, u32[]{:S(2)}, u32[]{:S(2)}) collective-permute-start(bf16[2,512,512]{2,1,0:T(8,128)(2,1)} %collective-permute-done.14.refs_3_.refs_11_), channel_id=1, source_target_pairs={{0,1},{1,0},{2,3},{3,2},{4,5},{5,4},{6,7},{7,6},{8,9},{9,8},{10,11... | collective-permute-start | bytes 3145736 | tf_op jit(solution)/shard_map/ppermute | solution.py:416
  250.3 17.6 %collective-permute-start.36 = (bf16[4,2,64,512]{3,2,1,0:T(8,128)(2,1)}, bf16[4,2,64,512]{3,2,1,0:T(8,128)(2,1)}, u32[]{:S(2)}, u32[]{:S(2)}) collective-permute-start(bf16[4,2,64,512]{3,2,1,0:T(8,128)(2,1)} %get-tuple-element.87), channel_id=1, source_target_pairs={{0,4},{4,0},{8,12},{12,8},{16,20},{20,16},{24,28},{28,24},{1,5},{5... | collective-permute-start | bytes 1572872 | tf_op jit(solution)/shard_map/ppermute | solution.py:413
  265.0 15.1 %collective-permute-start.40 = (bf16[4,2,64,512]{3,2,1,0:T(8,128)(2,1)}, bf16[4,2,64,512]{3,2,1,0:T(8,128)(2,1)}, u32[]{:S(2)}, u32[]{:S(2)}) collective-permute-start(bf16[4,2,64,512]{3,2,1,0:T(8,128)(2,1)} %get-tuple-element.93), channel_id=1, source_target_pairs={{0,4},{4,0},{8,12},{12,8},{16,20},{20,16},{24,28},{28,24},{1,5},{5... | collective-permute-start | bytes 1572872 | tf_op jit(solution)/shard_map/ppermute | solution.py:413
  265.9 59.8 %collective-permute-start.44 = (bf16[4,2,64,512]{3,2,1,0:T(8,128)(2,1)}, bf16[4,2,64,512]{3,2,1,0:T(8,128)(2,1)}, u32[]{:S(2)}, u32[]{:S(2)}) collective-permute-start(bf16[4,2,64,512]{3,2,1,0:T(8,128)(2,1)} %get-tuple-element.99), channel_id=1, source_target_pairs={{0,4},{4,0},{8,12},{12,8},{16,20},{20,16},{24,28},{28,24},{1,5},{5... | collective-permute-start | bytes 1572872 | tf_op jit(solution)/shard_map/ppermute | solution.py:413
  267.0 60.0 %collective-permute-start.48 = (bf16[4,2,64,512]{3,2,1,0:T(8,128)(2,1)}, bf16[4,2,64,512]{3,2,1,0:T(8,128)(2,1)}, u32[]{:S(2)}, u32[]{:S(2)}) collective-permute-start(bf16[4,2,64,512]{3,2,1,0:T(8,128)(2,1)} %get-tuple-element.105), channel_id=1, source_target_pairs={{0,4},{4,0},{8,12},{12,8},{16,20},{20,16},{24,28},{28,24},{1,5},{5... | collective-permute-start | bytes 1572872 | tf_op jit(solution)/shard_map/ppermute | solution.py:413
  270.7 59.1 %collective-permute-start.37 = (bf16[2,64,512]{2,1,0:T(8,128)(2,1)}, bf16[2,64,512]{2,1,0:T(8,128)(2,1)}, u32[]{:S(2)}, u32[]{:S(2)}) collective-permute-start(bf16[2,64,512]{2,1,0:T(8,128)(2,1)} %get-tuple-element.89), channel_id=1, source_target_pairs={{0,8},{4,12},{8,16},{12,20},{16,24},{20,28},{24,0},{28,4},{1,9},{5... | collective-permute-start | bytes 393224 | tf_op jit(solution)/shard_map/ppermute | solution.py:413
  272.3 59.8 %collective-permute-start.38 = (bf16[2,64,512]{2,1,0:T(8,128)(2,1)S(1)}, bf16[2,64,512]{2,1,0:T(8,128)(2,1)}, u32[]{:S(2)}, u32[]{:S(2)}) collective-permute-start(bf16[2,64,512]{2,1,0:T(8,128)(2,1)S(1)} %get-tuple-element.90), channel_id=1, source_target_pairs={{0,16},{4,20},{8,24},{12,28},{16,0},{20,4},{24,8},{28,12},{1,17},{... | collective-permute-start | bytes 393224 | tf_op jit(solution)/shard_map/ppermute | solution.py:413
  280.1 52.6 %collective-permute-start.39 = (bf16[2,64,512]{2,1,0:T(8,128)(2,1)S(1)}, bf16[2,64,512]{2,1,0:T(8,128)(2,1)}, u32[]{:S(2)}, u32[]{:S(2)}) collective-permute-start(bf16[2,64,512]{2,1,0:T(8,128)(2,1)S(1)} %get-tuple-element.91), channel_id=1, source_target_pairs={{0,24},{4,28},{8,0},{12,4},{16,8},{20,12},{24,16},{28,20},{1,25},{... | collective-permute-start | bytes 393224 | tf_op jit(solution)/shard_map/ppermute | solution.py:413
  327.0 13.9 %collective-permute-start.42 = (bf16[2,64,512]{2,1,0:T(8,128)(2,1)S(1)}, bf16[2,64,512]{2,1,0:T(8,128)(2,1)S(1)}, u32[]{:S(2)}, u32[]{:S(2)}) collective-permute-start(bf16[2,64,512]{2,1,0:T(8,128)(2,1)S(1)} %get-tuple-element.96), channel_id=1, source_target_pairs={{0,16},{4,20},{8,24},{12,28},{16,0},{20,4},{24,8},{28,12},{1,17},{... | collective-permute-start | bytes 393224 | tf_op jit(solution)/shard_map/ppermute | solution.py:413
  329.8 11.8 %collective-permute-start.43 = (bf16[2,64,512]{2,1,0:T(8,128)(2,1)S(1)}, bf16[2,64,512]{2,1,0:T(8,128)(2,1)S(1)}, u32[]{:S(2)}, u32[]{:S(2)}) collective-permute-start(bf16[2,64,512]{2,1,0:T(8,128)(2,1)S(1)} %get-tuple-element.97), channel_id=1, source_target_pairs={{0,24},{4,28},{8,0},{12,4},{16,8},{20,12},{24,16},{28,20},{1,25},{... | collective-permute-start | bytes 393224 | tf_op jit(solution)/shard_map/ppermute | solution.py:413
  332.1 14.2 %collective-permute-start.45 = (bf16[2,64,512]{2,1,0:T(8,128)(2,1)S(1)}, bf16[2,64,512]{2,1,0:T(8,128)(2,1)S(1)}, u32[]{:S(2)}, u32[]{:S(2)}) collective-permute-start(bf16[2,64,512]{2,1,0:T(8,128)(2,1)S(1)} %get-tuple-element.101), channel_id=1, source_target_pairs={{0,8},{4,12},{8,16},{12,20},{16,24},{20,28},{24,0},{28,4},{1,9},{5... | collective-permute-start | bytes 393224 | tf_op jit(solution)/shard_map/ppermute | solution.py:413
  332.8 19.7 %collective-permute-start.46 = (bf16[2,64,512]{2,1,0:T(8,128)(2,1)S(1)}, bf16[2,64,512]{2,1,0:T(8,128)(2,1)S(1)}, u32[]{:S(2)}, u32[]{:S(2)}) collective-permute-start(bf16[2,64,512]{2,1,0:T(8,128)(2,1)S(1)} %get-tuple-element.102), channel_id=1, source_target_pairs={{0,16},{4,20},{8,24},{12,28},{16,0},{20,4},{24,8},{28,12},{1,17},{... | collective-permute-start | bytes 393224 | tf_op jit(solution)/shard_map/ppermute | solution.py:413
  335.3 17.2 %collective-permute-start.47 = (bf16[2,64,512]{2,1,0:T(8,128)(2,1)S(1)}, bf16[2,64,512]{2,1,0:T(8,128)(2,1)S(1)}, u32[]{:S(2)}, u32[]{:S(2)}) collective-permute-start(bf16[2,64,512]{2,1,0:T(8,128)(2,1)S(1)} %get-tuple-element.103), channel_id=1, source_target_pairs={{0,24},{4,28},{8,0},{12,4},{16,8},{20,12},{24,16},{28,20},{1,25},{... | collective-permute-start | bytes 393224 | tf_op jit(solution)/shard_map/ppermute | solution.py:413
  341.0 11.6 %collective-permute-start.49 = (bf16[2,64,512]{2,1,0:T(8,128)(2,1)S(1)}, bf16[2,64,512]{2,1,0:T(8,128)(2,1)S(1)}, u32[]{:S(2)}, u32[]{:S(2)}) collective-permute-start(bf16[2,64,512]{2,1,0:T(8,128)(2,1)S(1)} %get-tuple-element.107), channel_id=1, source_target_pairs={{0,8},{4,12},{8,16},{12,20},{16,24},{20,28},{24,0},{28,4},{1,9},{5... | collective-permute-start | bytes 393224 | tf_op jit(solution)/shard_map/ppermute | solution.py:413
  341.6 17.9 %collective-permute-start.50 = (bf16[2,64,512]{2,1,0:T(8,128)(2,1)S(1)}, bf16[2,64,512]{2,1,0:T(8,128)(2,1)S(1)}, u32[]{:S(2)}, u32[]{:S(2)}) collective-permute-start(bf16[2,64,512]{2,1,0:T(8,128)(2,1)S(1)} %get-tuple-element.108), channel_id=1, source_target_pairs={{0,16},{4,20},{8,24},{12,28},{16,0},{20,4},{24,8},{28,12},{1,17},{... | collective-permute-start | bytes 393224 | tf_op jit(solution)/shard_map/ppermute | solution.py:413
  346.4 13.2 %collective-permute-start.51 = (bf16[2,64,512]{2,1,0:T(8,128)(2,1)S(1)}, bf16[2,64,512]{2,1,0:T(8,128)(2,1)S(1)}, u32[]{:S(2)}, u32[]{:S(2)}) collective-permute-start(bf16[2,64,512]{2,1,0:T(8,128)(2,1)S(1)} %get-tuple-element.109), channel_id=1, source_target_pairs={{0,24},{4,28},{8,0},{12,4},{16,8},{20,12},{24,16},{28,20},{1,25},{... | collective-permute-start | bytes 393224 | tf_op jit(solution)/shard_map/ppermute | solution.py:413
  (71 other events, 629.8 us)

commit v3 on v2

--- a/solution.py
+++ b/solution.py
@@ -71,7 +71,7 @@
             ],
             out_specs=[pl.BlockSpec((1, n // 2, n), lambda e, sel: (e, 0, 0))] * 2,
         ),
-        compiler_params=params(40),
+        compiler_params=params(56),
         cost_estimate=cost(le * 6 * n**3, le * n * n * 6),
         name="lesser",
     )(which[None], green, broadening)
@@ -99,7 +99,7 @@
             in_specs=[pl.BlockSpec((each, rows, n), lambda q, w: (q, 0, 0))] * len(pieces),
             out_specs=[pl.BlockSpec((each, n, n), lambda q, w: (q, 0, 0))] * 2,
         ),
-        compiler_params=params(40),
+        compiler_params=params(42),
         cost_estimate=cost(nk * n * n * 4, nk * n * n * 6),
         name="place",
     )(where, *pieces)
@@ -156,61 +156,82 @@
             out_specs=specs,
         ),
         input_output_aliases=alias,
-        compiler_params=params(40),
+        compiler_params=params(56),
         cost_estimate=cost(le * half * n * 16, le * half * n * 12),
         name="source",
     )(odd[None], weights, keep, recv, kz, rz, *extra)
 
 
 def home_kernel(lk, pieces, slots, *refs):
-    ins, (c_ref, ct_ref, x_ref, y_ref, q_ref) = refs[:pieces], refs[pieces:]
-    each, rows, n = ins[0].shape
-    count = pieces * each
-    for s in range(pieces):
-        for j in range(each):
-            q_ref[s * each + j] = ins[s][j]
+    ins, (c_ref, ct_ref, x_ref, y_ref, q_ref, sems) = refs[:pieces], refs[pieces:]
+    each, n, _ = ins[0].shape
+    _, count, rows, _ = q_ref.shape
+    steps = n // rows
     tr, tc = 16, 256
 
-    def tile(index, _):
-        r = pl.ds(pl.multiple_of((index // (n // tc)) * tr, tr), tr)
-        m = pl.ds(pl.multiple_of((index % (n // tc)) * tc, tc), tc)
-        xs, ys = [None] * lk, [None] * lk
-        for q in range(0, count, 4):
-            px, py = [None] * lk, [None] * lk
-            for p in (q, q + 2):
-                c, ct = [c_ref[p + i, r, m] for i in range(2)], [ct_ref[p + i, r, m] for i in range(2)]
+    def fetch(g, slot):
+        at = pl.ds(pl.multiple_of(g * rows, rows), rows)
+        return [
+            pltpu.make_async_copy(
+                ins[s].at[j, at, :], q_ref.at[slot, s * each + j], sems.at[slot, s * each + j])
+            for s in range(pieces) for j in range(each)
+        ]
+
+    for copy in fetch(0, 0):
+        copy.start()
+
+    def step(g, _):
+        slot = lax.rem(g, 2)
+
+        @pl.when(g + 1 < steps)
+        def _():
+            for copy in fetch(g + 1, 1 - slot):
+                copy.start()
+
+        for copy in fetch(g, slot):
+            copy.wait()
+
+        def tile(index, _):
+            within = pl.multiple_of((index // (n // tc)) * tr, tr)
+            r = pl.ds(within, tr)
+            w = pl.ds(pl.multiple_of(g * rows + within, tr), tr)
+            m = pl.ds(pl.multiple_of((index % (n // tc)) * tc, tc), tc)
+            xs, ys = [None] * lk, [None] * lk
+            for q in range(0, count, 4):
+                px, py = [None] * lk, [None] * lk
+                for p in (q, q + 2):
+                    c, ct = [c_ref[p + i, w, m] for i in range(2)], [ct_ref[p + i, w, m] for i in range(2)]
+                    for k in range(lk):
+                        v = [q_ref[slot, slots[k * count + p + i], r, m] for i in range(2)]
+                        x, y = c[0] * v[0] + c[1] * v[1], ct[0] * v[0] + ct[1] * v[1]
+                        px[k] = x if p == q else px[k] + x
+                        py[k] = y if p == q else py[k] + y
                 for k in range(lk):
-                    v = [q_ref[slots[k * count + p + i], r, m] for i in range(2)]
-                    x, y = c[0] * v[0] + c[1] * v[1], ct[0] * v[0] + ct[1] * v[1]
-                    px[k] = x if p == q else px[k] + x
-                    py[k] = y if p == q else py[k] + y
+                    xs[k] = px[k] if q == 0 else xs[k] + px[k]
+                    ys[k] = py[k] if q == 0 else ys[k] + py[k]
             for k in range(lk):
-                xs[k] = px[k] if q == 0 else xs[k] + px[k]
-                ys[k] = py[k] if q == 0 else ys[k] + py[k]
-        for k in range(lk):
-            x_ref[k, r, m] = xs[k]
-            y_ref[k, r, m] = ys[k]
-        return 0
-
-    lax.fori_loop(0, (rows // tr) * (n // tc), tile, 0)
+                x_ref[k, w, m] = xs[k]
+                y_ref[k, w, m] = ys[k]
+            return 0
+
+        return lax.fori_loop(0, (rows // tr) * (n // tc), tile, 0)
+
+    lax.fori_loop(0, steps, step, 0)
 
 
 def home_blocks(slots, pieces, full, turned, lk):
     each, n, _ = pieces[0].shape
     count = each * len(pieces)
     rows = n // 8
-    block = lambda lead: pl.BlockSpec((lead, rows, n), lambda g, s: (0, g, 0))
+    vmem = pl.BlockSpec(memory_space=pltpu.VMEM)
     return pl.pallas_call(
         functools.partial(home_kernel, lk, len(pieces)),
         out_shape=[jax.ShapeDtypeStruct((lk, n, n), BF16)] * 2,
-        grid_spec=pltpu.PrefetchScalarGridSpec(
-            num_scalar_prefetch=1,
-            grid=(n // rows,),
-            in_specs=[block(each)] * len(pieces) + [block(count), block(count)],
-            out_specs=[block(lk), block(lk)],
-            scratch_shapes=[pltpu.VMEM((count, rows, n), BF16)],
-        ),
-        compiler_params=params(40),
+        in_specs=[pl.BlockSpec(memory_space=pltpu.SMEM)]
+        + [pl.BlockSpec(memory_space=pl.ANY)] * len(pieces) + [vmem, vmem],
+        out_specs=[vmem, vmem],
+        scratch_shapes=[pltpu.VMEM((2, count, rows, n), BF16), pltpu.SemaphoreType.DMA((2, count))],
+        compiler_params=params(38),
         cost_estimate=cost(4 * lk * count * n * n, n * n * (6 * count + 4 * lk)),
         name="home",
     )(slots, *pieces, full, turned)
@@ -279,7 +300,7 @@
             scratch_shapes=[pltpu.VMEM((count, rows, cols), BF16)] * 2,
         ),
         input_output_aliases={2 + len(in_specs) - 1: 0} if alias else {},
-        compiler_params=params(40),
+        compiler_params=params(42),
         cost_estimate=cost(4 * count * count * rows * n, rows * n * count * 10),
         name="rows",
     )(mine[None], slots, *pieces, *pieces, coupling, *alias)
@@ -312,7 +333,7 @@
     one = pl.BlockSpec((1, n, n), lambda k: (k, 0, 0))
     return pl.pallas_call(
         functools.partial(first_density_kernel, energy, held is None),
-        out_shape=jax.ShapeDtypeStruct((lk, 2, n, n), F32),
+        out_shape=pltpu.HBM((lk, 2, n, n), F32),
         grid=(lk,),
         in_specs=[
             pl.BlockSpec((1, 1, 2, n, n), lambda k: (k, energy, 0, 0, 0)),
@@ -321,7 +342,7 @@
             one,
         ] + [pair] * len(alias),
         out_specs=pair,
-        compiler_params=params(40),
+        compiler_params=params(38),
         cost_estimate=cost(16 * lk * n**3, lk * n * n * 20),
         name="density",
     )(green, broadening, x, y, *alias)
@@ -345,11 +366,10 @@
                     send_ref[g, c] = d_ref[c, pl.ds(other, rows), :].astype(BF16)
 
 
-def last_density(scale, energy, start, stop, groups, odd, green, broadening, x, y, held):
+def last_density(scale, energy, start, count, groups, odd, green, broadening, x, y, held):
     _, le, _, n, _ = green.shape
     rows = n // (2 * groups)
-    count = stop - start
-    one = pl.BlockSpec((1, n, n), lambda i, odd: (start + i, 0, 0))
+    one = pl.BlockSpec((1, n, n), lambda i, odd: (i, 0, 0))
     out = pl.BlockSpec((groups, 2, rows, n), lambda i, odd: (0, 0, 0, 0))
     return pl.pallas_call(
         functools.partial(last_density_kernel, scale, energy),
@@ -367,7 +387,7 @@
             out_specs=[out] * (2 * count),
             scratch_shapes=[pltpu.VMEM((2, n, n), F32)],
         ),
-        compiler_params=params(40),
+        compiler_params=params(38),
         cost_estimate=cost(count * 16 * n**3, count * n * n * 20),
         name="density",
     )(odd[None], green, broadening, x, y, held)
@@ -388,7 +408,7 @@
         out_shape=[jax.ShapeDtypeStruct(keep.shape[1:], BF16)] * groups,
         in_specs=[pl.BlockSpec(memory_space=pltpu.SMEM), vmem, vmem],
         out_specs=[vmem] * groups,
-        compiler_params=params(40),
+        compiler_params=params(56),
         cost_estimate=cost(keep.size, keep.size * 6),
         name="pairsum",
     )(group[None], keep, recv)
@@ -441,6 +461,7 @@
     all_slots = slots.reshape(-1)
 
     green_ret = pltpu.with_memory_space_constraint(green_ret, pltpu.HBM)
+    coupling = pltpu.with_memory_space_constraint(coupling, pltpu.HBM)
     coupling_pieces = spread(coupling)
 
     send = [lesser_packed((1 - odd) * hk + j, green_ret, broadening) for j in range(hk)]
@@ -465,14 +486,18 @@
         fresh = [spread(part[e]) for part in use]
         back = [spread(over_energy(part[le + e], pairs)) for part in use]
         pieces = [part[at] for at in range(nm) for part in fresh + back]
-        x, y = home_blocks(own_slots, pieces, full, turned, lk)
         if e < le - 1:
+            x, y = home_blocks(own_slots, pieces, full, turned, lk)
             held_density = first_density(e, green_ret, broadening, x, y, held_density)
         else:
             shares = []
-            for start, stop in ((0, 1), (1, lk)):
+            nk = lk * nm
+            for half in range(2):
+                first = half * hk
+                some = lax.slice_in_dim(own_slots, first * nk, (first + hk) * nk)
+                x, y = home_blocks(some, pieces, full, turned, hk)
                 shares = shares + list(last_density(
-                    scale, e, start, stop, groups, odd,
+                    scale, e, first, hk, groups, odd,
                     green_ret, broadening, x, y, held_density))
             for k in range(lk):
                 kept, sent = shares[2 * k], shares[2 * k + 1]

time: 364 us -> 387 us (1.063)
  Pallas kernels: 120 us -> 159 us
  local copies, waits for them, and re-layouts: 48.3 us -> 38.3 us
  waiting for transfers between devices: 110 us -> 105 us
    pallas_call x2 -> x3, Pallas kernels: 25.6 us -> 55.1 us  [home_blocks(): pl.pallas_call(functools.partial(home_kernel, lk, len(pieces)), out_shape...]
    unnamed x135 -> x119, local copies, waits for them, and re-layouts: 48.2 us -> 38 us
    ppermute x31, waiting for transfers between devices: 51.2 us -> 42.6 us  [over_energy(): return lax.ppermute(x, 'energy', perm)]
    pallas_call x4, Pallas kernels: 9.72 us -> 14.2 us  [sources(): pl.pallas_call(source_kernel, out_shape=[jax.ShapeDtypeStruct(shape, BF16...]
  transfers between devices with their start and end apart: 52 -> 52, of which waited for: 17 -> 13; matrix products, arithmetic and copies ran while one was open for 1% -> 2% of each run, Pallas kernels for 27% -> 34%
where the time goes in v3:
time: 387 us; the launch traced here: 385 us
  Pallas kernels  159 us (41%)
  waiting for transfers between devices  105 us (27%)
  starting transfers between devices  73.8 us (19%)
  local copies, waits for them, and re-layouts  38.3 us (10%)
  other arithmetic  7.48 us (2%)
    ppermute x31, starting transfers between devices, over_energy(): return lax.ppermute(x, 'energy', perm)  62.5 us
    ppermute x21, waiting for transfers between devices, swap(): return lax.ppermute(x, 'mom', [(i, i ^ stride) for i in range(nm)])  62.3 us
    pallas_call x3, Pallas kernels, home_blocks(): pl.pallas_call(functools.partial(home_kernel, lk, len(pieces)), out_shape...  55.1 us
    ppermute x31, waiting for transfers between devices, over_energy(): return lax.ppermute(x, 'energy', perm)  42.6 us
    unnamed x119, local copies, waits for them, and re-layouts  38 us
    pallas_call x2, Pallas kernels, own_rows(): pl.pallas_call(functools.partial(rows_kernel, len(pieces)), out_shape=jax...  29.6 us
    pallas_call x4, Pallas kernels, lesser_packed(): pl.pallas_call(lesser_kernel, out_shape=[jax.ShapeDtypeStruct((le, n // 2...  16.5 us
    pallas_call x2, Pallas kernels, last_density(): pl.pallas_call(functools.partial(last_density_kernel, scale, energy), out...  15.1 us
  transfers between devices with their start and end apart: 52, of which 13 were waited for; matrix products, arithmetic and copies ran while one was open for 2% of the time, Pallas kernels for 34%

profile of v3, /device:TPU:0, one launch (start us, length us, event | category | flops | bytes accessed | tf_op | source)
XLA Modules:
  0.0 384.8 jit_solution(5378813032263050594)
XLA Ops:
  0.6 4.1 %lesser.7 = (bf16[2,256,512]{2,1,0:T(8,128)(2,1)}, bf16[2,256,512]{2,1,0:T(8,128)(2,1)}) custom-call(s32[1]{0:T(128)} %bitcast.9.sel, bf16[4,2,2,512,512]{4,3,2,1,0:T(8,128)(2,1)} %g_ref.13, f32[4,2,512]{2,1,0:T(2,128)} %gamma_ref.13), custom_call_target="tpu_custom_call" | custom-call | flops 1610612736 | bytes 3145728 | tf_op jit(solution)/shard_map/lesser/pallas_call | solution.py:62
  4.8 3.0 collective-permute-start.6
  7.8 4.1 %lesser.6 = (bf16[2,256,512]{2,1,0:T(8,128)(2,1)}, bf16[2,256,512]{2,1,0:T(8,128)(2,1)}) custom-call(s32[1]{0:T(128)} %bitcast.8.sel, bf16[4,2,2,512,512]{4,3,2,1,0:T(8,128)(2,1)} %g_ref.13, f32[4,2,512]{2,1,0:T(2,128)} %gamma_ref.13), custom_call_target="tpu_custom_call" | custom-call | flops 1610612736 | bytes 3145728 | tf_op jit(solution)/shard_map/lesser/pallas_call | solution.py:62
  14.5 4.1 %lesser.5 = (bf16[2,256,512]{2,1,0:T(8,128)(2,1)}, bf16[2,256,512]{2,1,0:T(8,128)(2,1)}) custom-call(s32[1]{0:T(128)} %bitcast.7.sel, bf16[4,2,2,512,512]{4,3,2,1,0:T(8,128)(2,1)} %g_ref.13, f32[4,2,512]{2,1,0:T(2,128)} %gamma_ref.13), custom_call_target="tpu_custom_call" | custom-call | flops 1610612736 | bytes 3145728 | tf_op jit(solution)/shard_map/lesser/pallas_call | solution.py:62
  18.6 6.4 %collective-permute-start = (bf16[2,256,512]{2,1,0:T(8,128)(2,1)}, bf16[2,256,512]{2,1,0:T(8,128)(2,1)S(1)}, u32[]{:S(2)}, u32[]{:S(2)}) collective-permute-start(bf16[2,256,512]{2,1,0:T(8,128)(2,1)} %get-tuple-element.59), channel_id=1, source_target_pairs={{0,4},{4,0},{8,12},{12,8},{16,20},{20,16},{24,28},{28,24},{1,5},{5... | collective-permute-start | bytes 1572872 | tf_op jit(solution)/shard_map/ppermute | solution.py:433
  25.1 6.9 %collective-permute-done.9.recv = bf16[2,256,512]{2,1,0:T(8,128)(2,1)S(1)} collective-permute-done((bf16[2,256,512]{2,1,0:T(8,128)(2,1)}, bf16[2,256,512]{2,1,0:T(8,128)(2,1)S(1)}, u32[]{:S(2)}, u32[]{:S(2)}) %collective-permute-start.9) | collective-permute-done | bytes 524320 | tf_op jit(solution)/shard_map/ppermute | solution.py:433
  32.0 4.8 %collective-permute-start.8 = (bf16[2,256,512]{2,1,0:T(8,128)(2,1)S(1)}, bf16[2,256,512]{2,1,0:T(8,128)(2,1)}, u32[]{:S(2)}, u32[]{:S(2)}) collective-permute-start(bf16[2,256,512]{2,1,0:T(8,128)(2,1)S(1)} %collective-permute-done.6.recv), channel_id=1, source_target_pairs={{0,8},{8,16},{12,4},{16,24},{20,12},{28,20},{1,9},{9,17},{13,5},{1... | collective-permute-start | bytes 1572872 | tf_op jit(solution)/shard_map/ppermute | solution.py:433
  36.8 2.7 collective-permute-start.11
  41.1 4.1 %lesser.4 = (bf16[2,256,512]{2,1,0:T(8,128)(2,1)}, bf16[2,256,512]{2,1,0:T(8,128)(2,1)}) custom-call(s32[1]{0:T(128)} %bitcast.6.sel, bf16[4,2,2,512,512]{4,3,2,1,0:T(8,128)(2,1)} %g_ref.13, f32[4,2,512]{2,1,0:T(2,128)} %gamma_ref.13), custom_call_target="tpu_custom_call" | custom-call | flops 1610612736 | bytes 3145728 | tf_op jit(solution)/shard_map/lesser/pallas_call | solution.py:62
  46.5 7.1 %collective-permute-done.3.recv = bf16[2,256,512]{2,1,0:T(8,128)(2,1)S(1)} collective-permute-done((bf16[2,256,512]{2,1,0:T(8,128)(2,1)}, bf16[2,256,512]{2,1,0:T(8,128)(2,1)S(1)}, u32[]{:S(2)}, u32[]{:S(2)}) %collective-permute-start.3) | collective-permute-done | bytes 524320 | tf_op jit(solution)/shard_map/ppermute | solution.py:433
  53.6 3.7 collective-permute-start.5
  58.7 4.8 %collective-permute-start.2 = (bf16[2,256,512]{2,1,0:T(8,128)(2,1)S(1)}, bf16[2,256,512]{2,1,0:T(8,128)(2,1)S(1)}, u32[]{:S(2)}, u32[]{:S(2)}) collective-permute-start(bf16[2,256,512]{2,1,0:T(8,128)(2,1)S(1)} %collective-permute-done.recv), channel_id=1, source_target_pairs={{0,8},{8,16},{12,4},{16,24},{20,12},{28,20},{1,9},{9,17},{13,5},{1... | collective-permute-start | bytes 1572872 | tf_op jit(solution)/shard_map/ppermute | solution.py:433
  64.1 3.1 pad_maximum_fusion.w_ref
  67.2 3.6 source.4
  70.9 3.5 source.5
  75.4 3.5 source.6
  79.9 3.5 source.7
  83.4 2.3 collective-permute-start.20
  87.4 11.3 %collective-permute-done.20.refs_3_.refs_19_ = bf16[1,512,512]{2,1,0:T(8,128)(2,1)S(1)} collective-permute-done((bf16[1,512,512]{2,1,0:T(8,128)(2,1)}, bf16[1,512,512]{2,1,0:T(8,128)(2,1)S(1)}, u32[]{:S(2)}, u32[]{:S(2)}) %collective-permute-start.20) | collective-permute-done | bytes 524320 | tf_op jit(solution)/shard_map/ppermute | solution.py:433
  101.3 6.3 %collective-permute-done.19.refs_2_.refs_18_ = bf16[1,512,512]{2,1,0:T(8,128)(2,1)S(1)} collective-permute-done((bf16[1,512,512]{2,1,0:T(8,128)(2,1)S(1)}, bf16[1,512,512]{2,1,0:T(8,128)(2,1)S(1)}, u32[]{:S(2)}, u32[]{:S(2)}) %collective-permute-start.19) | collective-permute-done | bytes 524320 | tf_op jit(solution)/shard_map/ppermute | solution.py:433
  111.6 2.8 collective-permute-done.21.refs_4_.refs_20_
  117.5 7.8 %collective-permute-done.24.refs_7_.refs_23_ = bf16[1,512,512]{2,1,0:T(8,128)(2,1)} collective-permute-done((bf16[1,512,512]{2,1,0:T(8,128)(2,1)S(1)}, bf16[1,512,512]{2,1,0:T(8,128)(2,1)}, u32[]{:S(2)}, u32[]{:S(2)}) %collective-permute-start.24) | collective-permute-done | bytes 524320 | tf_op jit(solution)/shard_map/ppermute | solution.py:436
  129.7 11.3 %collective-permute-done.23.refs_6_.refs_22_ = bf16[1,512,512]{2,1,0:T(8,128)(2,1)} collective-permute-done((bf16[1,512,512]{2,1,0:T(8,128)(2,1)S(1)}, bf16[1,512,512]{2,1,0:T(8,128)(2,1)}, u32[]{:S(2)}, u32[]{:S(2)}) %collective-permute-start.23) | collective-permute-done | bytes 524320 | tf_op jit(solution)/shard_map/ppermute | solution.py:436
  144.4 19.0 %collective-permute-done.13.refs_2_.refs_10_ = bf16[2,512,512]{2,1,0:T(8,128)(2,1)S(1)} collective-permute-done((bf16[2,512,512]{2,1,0:T(8,128)(2,1)}, bf16[2,512,512]{2,1,0:T(8,128)(2,1)S(1)}, u32[]{:S(2)}, u32[]{:S(2)}) %collective-permute-start.13) | collective-permute-done | bytes 1048608 | tf_op jit(solution)/shard_map/ppermute | solution.py:436
  164.1 21.4 %collective-permute-done.14.refs_3_.refs_11_ = bf16[2,512,512]{2,1,0:T(8,128)(2,1)} collective-permute-done((bf16[2,512,512]{2,1,0:T(8,128)(2,1)S(1)}, bf16[2,512,512]{2,1,0:T(8,128)(2,1)}, u32[]{:S(2)}, u32[]{:S(2)}) %collective-permute-start.14) | collective-permute-done | bytes 1048608 | tf_op jit(solution)/shard_map/ppermute | solution.py:436
  186.8 7.8 %place.1 = (bf16[16,512,512]{2,1,0:T(8,128)(2,1)S(1)}, bf16[16,512,512]{2,1,0:T(8,128)(2,1)S(1)}) custom-call(s32[4]{0:T(128)} %pad_add_fusion.where, bf16[16,128,512]{2,1,0:T(8,128)(2,1)} %refs_0_.1, bf16[16,128,512]{2,1,0:T(8,128)(2,1)} %collective-permute-done.33.refs_1_, bf16[16,128,512]{2,1,0:T(8,128)(2,1)} %collective-permute-done.34.refs_2_, ...), custom_call_target="tpu_custom_call" | custom-call | flops 16777216 | bytes 25165824 | tf_op jit(solution)/shard_map/place/pallas_call | solution.py:93
  194.7 3.4 copy-done
  198.0 3.3 copy-done.1
  206.7 22.5 %home.4 = (bf16[4,512,512]{2,1,0:T(8,128)(2,1)S(1)}, bf16[4,512,512]{2,1,0:T(8,128)(2,1)S(1)}) custom-call(s32[64]{0:T(128)S(1)} %reshape.13.slots, bf16[1,512,512]{2,1,0:T(8,128)(2,1)S(1)} %copy-done.6, bf16[1,512,512]{2,1,0:T(8,128)(2,1)S(1)} %copy-done.4, bf16[1,512,512]{2,1,0:T(8,128)(2,1)S(1)} %copy-done.18, bf16[1,512,512]{2,1,0:T(8,128)(2,1)S(1)} %copy-done.9, ...), custom_call_target="tpu_custom_call" | custom-call | flops 67108864 | bytes 29360128 | tf_op jit(solution)/shard_map/home/pallas_call | solution.py:227
  229.2 12.6 %density.3.held_ref = f32[4,2,512,512]{3,2,1,0:T(8,128)} custom-call(bf16[4,2,2,512,512]{4,3,2,1,0:T(8,128)(2,1)} %g_ref.13, f32[4,2,512]{2,1,0:T(2,128)S(1)} %copy-done.38, bf16[4,512,512]{2,1,0:T(8,128)(2,1)S(1)} %get-tuple-element.86.x_ref, bf16[4,512,512]{2,1,0:T(8,128)(2,1)S(1)} %get-tuple-element.87.y_ref), custom_call_target="tpu_custom_call" | custom-call | flops 8589934592 | bytes 20971520 | tf_op jit(solution)/shard_map/density/pallas_call | solution.py:334
  241.9 16.6 %home.5 = (bf16[2,512,512]{2,1,0:T(8,128)(2,1)S(1)}, bf16[2,512,512]{2,1,0:T(8,128)(2,1)S(1)}) custom-call(s32[32]{0:T(128)S(1)} %slice.15.slots, bf16[2,512,512]{2,1,0:T(8,128)(2,1)S(1)} %copy-done.2, bf16[2,512,512]{2,1,0:T(8,128)(2,1)S(1)} %collective-permute-done.12.refs_1_.refs_9_, bf16[2,512,512]{2,1,0:T(8,128)(2,1)S(1)} %collective-permute-done.13.refs_2_.refs_10_, ...), custom_call_target="tpu_custom_call" | custom-call | flops 33554432 | bytes 27262976 | tf_op jit(solution)/shard_map/home/pallas_call | solution.py:227
  258.5 7.6 %density.5 = (bf16[4,2,64,512]{3,2,1,0:T(8,128)(2,1)S(1)}, bf16[4,2,64,512]{3,2,1,0:T(8,128)(2,1)}, bf16[4,2,64,512]{3,2,1,0:T(8,128)(2,1)S(1)}, bf16[4,2,64,512]{3,2,1,0:T(8,128)(2,1)}) custom-call(s32[1]{0:T(128)} %bitcast.1.odd, bf16[4,2,2,512,512]{4,3,2,1,0:T(8,128)(2,1)} %g_ref.13, f32[4,2,512]{2,1,0:T(2,128)S(1)} %copy-done.38, ...), custom_call_target="tpu_custom_call" | custom-call | flops 4294967296 | bytes 10485760 | tf_op jit(solution)/shard_map/density/pallas_call | solution.py:374
  268.2 16.0 %home.3 = (bf16[2,512,512]{2,1,0:T(8,128)(2,1)S(1)}, bf16[2,512,512]{2,1,0:T(8,128)(2,1)S(1)}) custom-call(s32[32]{0:T(128)S(1)} %slice.13.slots, bf16[2,512,512]{2,1,0:T(8,128)(2,1)S(1)} %copy-done.2, bf16[2,512,512]{2,1,0:T(8,128)(2,1)S(1)} %collective-permute-done.12.refs_1_.refs_9_, bf16[2,512,512]{2,1,0:T(8,128)(2,1)S(1)} %collective-permute-done.13.refs_2_.refs_10_, ...), custom_call_target="tpu_custom_call" | custom-call | flops 33554432 | bytes 27262976 | tf_op jit(solution)/shard_map/home/pallas_call | solution.py:227
  284.2 7.6 %density.4 = (bf16[4,2,64,512]{3,2,1,0:T(8,128)(2,1)S(1)}, bf16[4,2,64,512]{3,2,1,0:T(8,128)(2,1)}, bf16[4,2,64,512]{3,2,1,0:T(8,128)(2,1)S(1)}, bf16[4,2,64,512]{3,2,1,0:T(8,128)(2,1)}) custom-call(s32[1]{0:T(128)} %bitcast.1.odd, bf16[4,2,2,512,512]{4,3,2,1,0:T(8,128)(2,1)} %g_ref.13, f32[4,2,512]{2,1,0:T(2,128)S(1)} %copy-done.38, ...), custom_call_target="tpu_custom_call" | custom-call | flops 4294967296 | bytes 10485760 | tf_op jit(solution)/shard_map/density/pallas_call | solution.py:374
  295.4 2.1 pairsum.6
  297.4 2.0 collective-permute-start.45
  299.5 2.6 collective-permute-start.46
  316.0 14.8 %rows.2.refs_17_ = bf16[16,2,2,128,512]{4,3,2,1,0:T(8,128)(2,1)} custom-call(s32[1]{0:T(128)} %bitcast.mine, s32[256]{0:T(256)S(1)} %reshape.12.slots, bf16[1,512,512]{2,1,0:T(8,128)(2,1)S(1)} %copy-done.7, bf16[1,512,512]{2,1,0:T(8,128)(2,1)S(1)} %copy-done.5, bf16[1,512,512]{2,1,0:T(8,128)(2,1)S(1)} %copy-done.19, bf16[1,512,512]{2,1,0:T(8,128)(2,1)S(1)} %copy-done.10, ...), custom_call_target="tpu_custom_call" | custom-call | flops 67108864 | bytes 10485760 | tf_op jit(solution)/shard_map/rows/pallas_call | solution.py:292
  330.9 14.8 %rows.3 = bf16[16,2,2,128,512]{4,3,2,1,0:T(8,128)(2,1)} custom-call(s32[1]{0:T(128)} %bitcast.mine, s32[256]{0:T(256)S(1)} %reshape.12.slots, bf16[2,512,512]{2,1,0:T(8,128)(2,1)S(1)} %copy-done.2, bf16[2,512,512]{2,1,0:T(8,128)(2,1)S(1)} %collective-permute-done.12.refs_1_.refs_9_, ...), custom_call_target="tpu_custom_call", output_to_operand_aliasing={{}: (19, {})} | custom-call | flops 67108864 | bytes 10485760 | tf_op jit(solution)/shard_map/rows/pallas_call | solution.py:292
  348.3 2.1 pairsum.4
  350.7 2.1 pairsum.5
  352.8 2.8 collective-permute-start.51
  357.8 2.9 collective-permute-start.39
  360.7 2.5 collective-permute-done.50
  364.3 4.5 %collective-permute-start.42 = (bf16[2,64,512]{2,1,0:T(8,128)(2,1)}, bf16[2,64,512]{2,1,0:T(8,128)(2,1)S(1)}, u32[]{:S(2)}, u32[]{:S(2)}) collective-permute-start(bf16[2,64,512]{2,1,0:T(8,128)(2,1)} %get-tuple-element.98), channel_id=1, source_target_pairs={{0,16},{4,20},{8,24},{12,28},{16,0},{20,4},{24,8},{28,12},{1,17},{... | collective-permute-start | bytes 393224 | tf_op jit(solution)/shard_map/ppermute | solution.py:433
  369.8 3.5 collective-permute-start.43
  373.3 3.1 collective-permute-done.38
  377.3 4.6 %collective-permute-done.42 = bf16[2,64,512]{2,1,0:T(8,128)(2,1)S(1)} collective-permute-done((bf16[2,64,512]{2,1,0:T(8,128)(2,1)}, bf16[2,64,512]{2,1,0:T(8,128)(2,1)S(1)}, u32[]{:S(2)}, u32[]{:S(2)}) %collective-permute-start.42) | collective-permute-done | bytes 131104 | tf_op jit(solution)/shard_map/ppermute | solution.py:433
  (211 shorter events, 66.6 us)
Async XLA Ops:
  4.8 20.3 %collective-permute-start.6 = (bf16[2,256,512]{2,1,0:T(8,128)(2,1)}, bf16[2,256,512]{2,1,0:T(8,128)(2,1)S(1)}, u32[]{:S(2)}, u32[]{:S(2)}) collective-permute-start(bf16[2,256,512]{2,1,0:T(8,128)(2,1)} %get-tuple-element.63), channel_id=1, source_target_pairs={{0,4},{4,0},{8,12},{12,8},{16,20},{20,16},{24,28},{28,24},{1,5},{5... | collective-permute-start | bytes 1572872 | tf_op jit(solution)/shard_map/ppermute | solution.py:433
  7.8 24.2 %collective-permute-start.9 = (bf16[2,256,512]{2,1,0:T(8,128)(2,1)}, bf16[2,256,512]{2,1,0:T(8,128)(2,1)S(1)}, u32[]{:S(2)}, u32[]{:S(2)}) collective-permute-start(bf16[2,256,512]{2,1,0:T(8,128)(2,1)} %get-tuple-element.65), channel_id=1, source_target_pairs={{0,4},{4,0},{8,12},{12,8},{16,20},{20,16},{24,28},{28,24},{1,5},{5... | collective-permute-start | bytes 1572872 | tf_op jit(solution)/shard_map/ppermute | solution.py:433
  11.9 24.9 %collective-permute-start.7 = (bf16[2,256,512]{2,1,0:T(8,128)(2,1)}, bf16[2,256,512]{2,1,0:T(8,128)(2,1)}, u32[]{:S(2)}, u32[]{:S(2)}) collective-permute-start(bf16[2,256,512]{2,1,0:T(8,128)(2,1)} %get-tuple-element.62.keep), channel_id=1, source_target_pairs={{4,12},{8,0},{12,20},{16,8},{20,28},{24,16},{5,13},{9,1},{13,21},{... | collective-permute-start | bytes 1572872 | tf_op jit(solution)/shard_map/ppermute | solution.py:433
  13.2 26.3 %collective-permute-start.10 = (bf16[2,256,512]{2,1,0:T(8,128)(2,1)}, bf16[2,256,512]{2,1,0:T(8,128)(2,1)S(1)}, u32[]{:S(2)}, u32[]{:S(2)}) collective-permute-start(bf16[2,256,512]{2,1,0:T(8,128)(2,1)} %get-tuple-element.64.keep), channel_id=1, source_target_pairs={{4,12},{8,0},{12,20},{16,8},{20,28},{24,16},{5,13},{9,1},{13,21},{... | collective-permute-start | bytes 1572872 | tf_op jit(solution)/shard_map/ppermute | solution.py:433
  18.6 26.6 %collective-permute-start = (bf16[2,256,512]{2,1,0:T(8,128)(2,1)}, bf16[2,256,512]{2,1,0:T(8,128)(2,1)S(1)}, u32[]{:S(2)}, u32[]{:S(2)}) collective-permute-start(bf16[2,256,512]{2,1,0:T(8,128)(2,1)} %get-tuple-element.59), channel_id=1, source_target_pairs={{0,4},{4,0},{8,12},{12,8},{16,20},{20,16},{24,28},{28,24},{1,5},{5... | collective-permute-start | bytes 1572872 | tf_op jit(solution)/shard_map/ppermute | solution.py:433
  25.0 28.6 %collective-permute-start.3 = (bf16[2,256,512]{2,1,0:T(8,128)(2,1)}, bf16[2,256,512]{2,1,0:T(8,128)(2,1)S(1)}, u32[]{:S(2)}, u32[]{:S(2)}) collective-permute-start(bf16[2,256,512]{2,1,0:T(8,128)(2,1)} %get-tuple-element.61), channel_id=1, source_target_pairs={{0,4},{4,0},{8,12},{12,8},{16,20},{20,16},{24,28},{28,24},{1,5},{5... | collective-permute-start | bytes 1572872 | tf_op jit(solution)/shard_map/ppermute | solution.py:433
  32.0 25.4 %collective-permute-start.8 = (bf16[2,256,512]{2,1,0:T(8,128)(2,1)S(1)}, bf16[2,256,512]{2,1,0:T(8,128)(2,1)}, u32[]{:S(2)}, u32[]{:S(2)}) collective-permute-start(bf16[2,256,512]{2,1,0:T(8,128)(2,1)S(1)} %collective-permute-done.6.recv), channel_id=1, source_target_pairs={{0,8},{8,16},{12,4},{16,24},{20,12},{28,20},{1,9},{9,17},{13,5},{1... | collective-permute-start | bytes 1572872 | tf_op jit(solution)/shard_map/ppermute | solution.py:433
  36.8 21.9 %collective-permute-start.11 = (bf16[2,256,512]{2,1,0:T(8,128)(2,1)S(1)}, bf16[2,256,512]{2,1,0:T(8,128)(2,1)S(1)}, u32[]{:S(2)}, u32[]{:S(2)}) collective-permute-start(bf16[2,256,512]{2,1,0:T(8,128)(2,1)S(1)} %collective-permute-done.9.recv), channel_id=1, source_target_pairs={{0,8},{8,16},{12,4},{16,24},{20,12},{28,20},{1,9},{9,17},{13,5},{1... | collective-permute-start | bytes 1572872 | tf_op jit(solution)/shard_map/ppermute | solution.py:433
  39.5 77.7 %collective-permute-start.33 = (bf16[16,128,512]{2,1,0:T(8,128)(2,1)}, bf16[16,128,512]{2,1,0:T(8,128)(2,1)}, u32[]{:S(2)}, u32[]{:S(2)}) collective-permute-start(bf16[16,128,512]{2,1,0:T(8,128)(2,1)} %refs_0_.1), channel_id=1, source_target_pairs={{0,2},{1,3},{2,0},{3,1},{4,6},{5,7},{6,4},{7,5},{8,10},{9,11},{10,... | collective-permute-start | bytes 6291464 | tf_op jit(solution)/shard_map/ppermute | solution.py:436
  45.2 29.2 %collective-permute-start.4 = (bf16[2,256,512]{2,1,0:T(8,128)(2,1)}, bf16[2,256,512]{2,1,0:T(8,128)(2,1)S(1)}, u32[]{:S(2)}, u32[]{:S(2)}) collective-permute-start(bf16[2,256,512]{2,1,0:T(8,128)(2,1)} %get-tuple-element.60.keep), channel_id=1, source_target_pairs={{4,12},{8,0},{12,20},{16,8},{20,28},{24,16},{5,13},{9,1},{13,21},{... | collective-permute-start | bytes 1572872 | tf_op jit(solution)/shard_map/ppermute | solution.py:433
  53.6 20.8 %collective-permute-start.5 = (bf16[2,256,512]{2,1,0:T(8,128)(2,1)S(1)}, bf16[2,256,512]{2,1,0:T(8,128)(2,1)S(1)}, u32[]{:S(2)}, u32[]{:S(2)}) collective-permute-start(bf16[2,256,512]{2,1,0:T(8,128)(2,1)S(1)} %collective-permute-done.3.recv), channel_id=1, source_target_pairs={{0,8},{8,16},{12,4},{16,24},{20,12},{28,20},{1,9},{9,17},{13,5},{1... | collective-permute-start | bytes 1572872 | tf_op jit(solution)/shard_map/ppermute | solution.py:433
  57.4 21.6 %collective-permute-start.1 = (bf16[2,256,512]{2,1,0:T(8,128)(2,1)}, bf16[2,256,512]{2,1,0:T(8,128)(2,1)S(1)}, u32[]{:S(2)}, u32[]{:S(2)}) collective-permute-start(bf16[2,256,512]{2,1,0:T(8,128)(2,1)} %get-tuple-element.58.keep), channel_id=1, source_target_pairs={{4,12},{8,0},{12,20},{16,8},{20,28},{24,16},{5,13},{9,1},{13,21},{... | collective-permute-start | bytes 1572872 | tf_op jit(solution)/shard_map/ppermute | solution.py:433
  58.7 20.3 %collective-permute-start.2 = (bf16[2,256,512]{2,1,0:T(8,128)(2,1)S(1)}, bf16[2,256,512]{2,1,0:T(8,128)(2,1)S(1)}, u32[]{:S(2)}, u32[]{:S(2)}) collective-permute-start(bf16[2,256,512]{2,1,0:T(8,128)(2,1)S(1)} %collective-permute-done.recv), channel_id=1, source_target_pairs={{0,8},{8,16},{12,4},{16,24},{20,12},{28,20},{1,9},{9,17},{13,5},{1... | collective-permute-start | bytes 1572872 | tf_op jit(solution)/shard_map/ppermute | solution.py:433
  83.4 15.3 %collective-permute-start.20 = (bf16[1,512,512]{2,1,0:T(8,128)(2,1)}, bf16[1,512,512]{2,1,0:T(8,128)(2,1)S(1)}, u32[]{:S(2)}, u32[]{:S(2)}) collective-permute-start(bf16[1,512,512]{2,1,0:T(8,128)(2,1)} %get-tuple-element.81), channel_id=1, source_target_pairs={{0,4},{4,0},{8,12},{12,8},{16,20},{20,16},{24,28},{28,24},{1,5},{5... | collective-permute-start | bytes 1572872 | tf_op jit(solution)/shard_map/ppermute | solution.py:433
  85.8 13.0 %collective-permute-start.26 = (bf16[1,512,512]{2,1,0:T(8,128)(2,1)}, bf16[1,512,512]{2,1,0:T(8,128)(2,1)S(1)}, u32[]{:S(2)}, u32[]{:S(2)}) collective-permute-start(bf16[1,512,512]{2,1,0:T(8,128)(2,1)} %get-tuple-element.79.refs_1_.refs_17_), channel_id=1, source_target_pairs={{0,1},{1,0},{2,3},{3,2},{4,5},{5,4},{6,7},{7,6},{8,9},{9,8},{10,11... | collective-permute-start | bytes 1572872 | tf_op jit(solution)/shard_map/ppermute | solution.py:436
  85.8 15.3 %collective-permute-start.22 = (bf16[1,512,512]{2,1,0:T(8,128)(2,1)}, bf16[1,512,512]{2,1,0:T(8,128)(2,1)S(1)}, u32[]{:S(2)}, u32[]{:S(2)}) collective-permute-start(bf16[1,512,512]{2,1,0:T(8,128)(2,1)} %get-tuple-element.79.refs_1_.refs_17_), channel_id=1, source_target_pairs={{0,2},{1,3},{2,0},{3,1},{4,6},{5,7},{6,4},{7,5},{8,10},{9,11},{10,... | collective-permute-start | bytes 1572872 | tf_op jit(solution)/shard_map/ppermute | solution.py:436
  87.2 20.4 %collective-permute-start.19 = (bf16[1,512,512]{2,1,0:T(8,128)(2,1)S(1)}, bf16[1,512,512]{2,1,0:T(8,128)(2,1)S(1)}, u32[]{:S(2)}, u32[]{:S(2)}) collective-permute-start(bf16[1,512,512]{2,1,0:T(8,128)(2,1)S(1)} %copy-done.53), channel_id=1, source_target_pairs={{0,4},{4,0},{8,12},{12,8},{16,20},{20,16},{24,28},{28,24},{1,5},{5... | collective-permute-start | bytes 1572872 | tf_op jit(solution)/shard_map/ppermute | solution.py:433
  99.6 14.8 %collective-permute-start.21 = (bf16[1,512,512]{2,1,0:T(8,128)(2,1)S(1)}, bf16[1,512,512]{2,1,0:T(8,128)(2,1)S(1)}, u32[]{:S(2)}, u32[]{:S(2)}) collective-permute-start(bf16[1,512,512]{2,1,0:T(8,128)(2,1)S(1)} %copy-done.6), channel_id=1, source_target_pairs={{0,2},{1,3},{2,0},{3,1},{4,6},{5,7},{6,4},{7,5},{8,10},{9,11},{10,... | collective-permute-start | bytes 1572872 | tf_op jit(solution)/shard_map/ppermute | solution.py:436
  101.1 13.3 %collective-permute-start.28 = (bf16[1,512,512]{2,1,0:T(8,128)(2,1)S(1)}, bf16[1,512,512]{2,1,0:T(8,128)(2,1)S(1)}, u32[]{:S(2)}, u32[]{:S(2)}) collective-permute-start(bf16[1,512,512]{2,1,0:T(8,128)(2,1)S(1)} %collective-permute-done.20.refs_3_.refs_19_), channel_id=1, source_target_pairs={{0,1},{1,0},{2,3},{3,2},{4,5},{5,4},{6,7},{7,6},{8,9},{9,8},{10,11... | collective-permute-start | bytes 1572872 | tf_op jit(solution)/shard_map/ppermute | solution.py:436
  107.6 17.7 %collective-permute-start.24 = (bf16[1,512,512]{2,1,0:T(8,128)(2,1)S(1)}, bf16[1,512,512]{2,1,0:T(8,128)(2,1)}, u32[]{:S(2)}, u32[]{:S(2)}) collective-permute-start(bf16[1,512,512]{2,1,0:T(8,128)(2,1)S(1)} %collective-permute-done.20.refs_3_.refs_19_), channel_id=1, source_target_pairs={{0,2},{1,3},{2,0},{3,1},{4,6},{5,7},{6,4},{7,5},{8,10},{9,11},{10,... | collective-permute-start | bytes 1572872 | tf_op jit(solution)/shard_map/ppermute | solution.py:436
  110.8 14.5 %collective-permute-start.30 = (bf16[1,512,512]{2,1,0:T(8,128)(2,1)S(1)}, bf16[1,512,512]{2,1,0:T(8,128)(2,1)S(1)}, u32[]{:S(2)}, u32[]{:S(2)}) collective-permute-start(bf16[1,512,512]{2,1,0:T(8,128)(2,1)S(1)} %collective-permute-done.22.refs_5_.refs_21_), channel_id=1, source_target_pairs={{0,1},{1,0},{2,3},{3,2},{4,5},{5,4},{6,7},{7,6},{8,9},{9,8},{10,11... | collective-permute-start | bytes 1572872 | tf_op jit(solution)/shard_map/ppermute | solution.py:436
  114.4 49.1 %collective-permute-start.34 = (bf16[16,128,512]{2,1,0:T(8,128)(2,1)}, bf16[16,128,512]{2,1,0:T(8,128)(2,1)}, u32[]{:S(2)}, u32[]{:S(2)}) collective-permute-start(bf16[16,128,512]{2,1,0:T(8,128)(2,1)} %refs_0_.1), channel_id=1, source_target_pairs={{0,1},{1,0},{2,3},{3,2},{4,5},{5,4},{6,7},{7,6},{8,9},{9,8},{10,11... | collective-permute-start | bytes 6291464 | tf_op jit(solution)/shard_map/ppermute | solution.py:436
  115.2 26.6 %collective-permute-start.12 = (bf16[2,512,512]{2,1,0:T(8,128)(2,1)}, bf16[2,512,512]{2,1,0:T(8,128)(2,1)S(1)}, u32[]{:S(2)}, u32[]{:S(2)}) collective-permute-start(bf16[2,512,512]{2,1,0:T(8,128)(2,1)} %get-tuple-element.77), channel_id=1, source_target_pairs={{0,4},{4,0},{8,12},{12,8},{16,20},{20,16},{24,28},{28,24},{1,5},{5... | collective-permute-start | bytes 3145736 | tf_op jit(solution)/shard_map/ppermute | solution.py:433
  117.2 68.2 %collective-permute-start.35 = (bf16[16,128,512]{2,1,0:T(8,128)(2,1)}, bf16[16,128,512]{2,1,0:T(8,128)(2,1)}, u32[]{:S(2)}, u32[]{:S(2)}) collective-permute-start(bf16[16,128,512]{2,1,0:T(8,128)(2,1)} %collective-permute-done.33.refs_1_), channel_id=1, source_target_pairs={{0,1},{1,0},{2,3},{3,2},{4,5},{5,4},{6,7},{7,6},{8,9},{9,8},{10,11... | collective-permute-start | bytes 6291464 | tf_op jit(solution)/shard_map/ppermute | solution.py:436
  126.1 14.9 %collective-permute-start.23 = (bf16[1,512,512]{2,1,0:T(8,128)(2,1)S(1)}, bf16[1,512,512]{2,1,0:T(8,128)(2,1)}, u32[]{:S(2)}, u32[]{:S(2)}) collective-permute-start(bf16[1,512,512]{2,1,0:T(8,128)(2,1)S(1)} %collective-permute-done.19.refs_2_.refs_18_), channel_id=1, source_target_pairs={{0,2},{1,3},{2,0},{3,1},{4,6},{5,7},{6,4},{7,5},{8,10},{9,11},{10,... | collective-permute-start | bytes 1572872 | tf_op jit(solution)/shard_map/ppermute | solution.py:436
  129.2 34.2 %collective-permute-start.13 = (bf16[2,512,512]{2,1,0:T(8,128)(2,1)}, bf16[2,512,512]{2,1,0:T(8,128)(2,1)S(1)}, u32[]{:S(2)}, u32[]{:S(2)}) collective-permute-start(bf16[2,512,512]{2,1,0:T(8,128)(2,1)} %get-tuple-element.76.refs_0_.refs_8_), channel_id=1, source_target_pairs={{0,2},{1,3},{2,0},{3,1},{4,6},{5,7},{6,4},{7,5},{8,10},{9,11},{10,... | collective-permute-start | bytes 3145736 | tf_op jit(solution)/shard_map/ppermute | solution.py:436
  141.8 43.7 %collective-permute-start.14 = (bf16[2,512,512]{2,1,0:T(8,128)(2,1)S(1)}, bf16[2,512,512]{2,1,0:T(8,128)(2,1)}, u32[]{:S(2)}, u32[]{:S(2)}) collective-permute-start(bf16[2,512,512]{2,1,0:T(8,128)(2,1)S(1)} %collective-permute-done.12.refs_1_.refs_9_), channel_id=1, source_target_pairs={{0,2},{1,3},{2,0},{3,1},{4,6},{5,7},{6,4},{7,5},{8,10},{9,11},{10,... | collective-permute-start | bytes 3145736 | tf_op jit(solution)/shard_map/ppermute | solution.py:436
  144.1 19.9 %collective-permute-start.32 = (bf16[1,512,512]{2,1,0:T(8,128)(2,1)}, bf16[1,512,512]{2,1,0:T(8,128)(2,1)}, u32[]{:S(2)}, u32[]{:S(2)}) collective-permute-start(bf16[1,512,512]{2,1,0:T(8,128)(2,1)} %collective-permute-done.24.refs_7_.refs_23_), channel_id=1, source_target_pairs={{0,1},{1,0},{2,3},{3,2},{4,5},{5,4},{6,7},{7,6},{8,9},{9,8},{10,11... | collective-permute-start | bytes 1572872 | tf_op jit(solution)/shard_map/ppermute | solution.py:436
  163.4 38.0 %collective-permute-start.31 = (bf16[1,512,512]{2,1,0:T(8,128)(2,1)}, bf16[1,512,512]{2,1,0:T(8,128)(2,1)}, u32[]{:S(2)}, u32[]{:S(2)}) collective-permute-start(bf16[1,512,512]{2,1,0:T(8,128)(2,1)} %collective-permute-done.23.refs_6_.refs_22_), channel_id=1, source_target_pairs={{0,1},{1,0},{2,3},{3,2},{4,5},{5,4},{6,7},{7,6},{8,9},{9,8},{10,11... | collective-permute-start | bytes 1572872 | tf_op jit(solution)/shard_map/ppermute | solution.py:436
  163.5 78.4 %collective-permute-start.15 = (bf16[2,512,512]{2,1,0:T(8,128)(2,1)}, bf16[2,512,512]{2,1,0:T(8,128)(2,1)}, u32[]{:S(2)}, u32[]{:S(2)}) collective-permute-start(bf16[2,512,512]{2,1,0:T(8,128)(2,1)} %get-tuple-element.76.refs_0_.refs_8_), channel_id=1, source_target_pairs={{0,1},{1,0},{2,3},{3,2},{4,5},{5,4},{6,7},{7,6},{8,9},{9,8},{10,11... | collective-permute-start | bytes 3145736 | tf_op jit(solution)/shard_map/ppermute | solution.py:436
  164.0 77.8 %collective-permute-start.16 = (bf16[2,512,512]{2,1,0:T(8,128)(2,1)S(1)}, bf16[2,512,512]{2,1,0:T(8,128)(2,1)}, u32[]{:S(2)}, u32[]{:S(2)}) collective-permute-start(bf16[2,512,512]{2,1,0:T(8,128)(2,1)S(1)} %collective-permute-done.12.refs_1_.refs_9_), channel_id=1, source_target_pairs={{0,1},{1,0},{2,3},{3,2},{4,5},{5,4},{6,7},{7,6},{8,9},{9,8},{10,11... | collective-permute-start | bytes 3145736 | tf_op jit(solution)/shard_map/ppermute | solution.py:436
  185.5 56.4 %collective-permute-start.17 = (bf16[2,512,512]{2,1,0:T(8,128)(2,1)S(1)}, bf16[2,512,512]{2,1,0:T(8,128)(2,1)}, u32[]{:S(2)}, u32[]{:S(2)}) collective-permute-start(bf16[2,512,512]{2,1,0:T(8,128)(2,1)S(1)} %collective-permute-done.13.refs_2_.refs_10_), channel_id=1, source_target_pairs={{0,1},{1,0},{2,3},{3,2},{4,5},{5,4},{6,7},{7,6},{8,9},{9,8},{10,11... | collective-permute-start | bytes 3145736 | tf_op jit(solution)/shard_map/ppermute | solution.py:436
  185.5 56.4 %collective-permute-start.18 = (bf16[2,512,512]{2,1,0:T(8,128)(2,1)}, bf16[2,512,512]{2,1,0:T(8,128)(2,1)}, u32[]{:S(2)}, u32[]{:S(2)}) collective-permute-start(bf16[2,512,512]{2,1,0:T(8,128)(2,1)} %collective-permute-done.14.refs_3_.refs_11_), channel_id=1, source_target_pairs={{0,1},{1,0},{2,3},{3,2},{4,5},{5,4},{6,7},{7,6},{8,9},{9,8},{10,11... | collective-permute-start | bytes 3145736 | tf_op jit(solution)/shard_map/ppermute | solution.py:436
  266.1 29.3 %collective-permute-start.44 = (bf16[4,2,64,512]{3,2,1,0:T(8,128)(2,1)}, bf16[4,2,64,512]{3,2,1,0:T(8,128)(2,1)}, u32[]{:S(2)}, u32[]{:S(2)}) collective-permute-start(bf16[4,2,64,512]{3,2,1,0:T(8,128)(2,1)} %get-tuple-element.103), channel_id=1, source_target_pairs={{0,4},{4,0},{8,12},{12,8},{16,20},{20,16},{24,28},{28,24},{1,5},{5... | collective-permute-start | bytes 1572872 | tf_op jit(solution)/shard_map/ppermute | solution.py:433
  268.1 34.0 %collective-permute-start.48 = (bf16[4,2,64,512]{3,2,1,0:T(8,128)(2,1)}, bf16[4,2,64,512]{3,2,1,0:T(8,128)(2,1)}, u32[]{:S(2)}, u32[]{:S(2)}) collective-permute-start(bf16[4,2,64,512]{3,2,1,0:T(8,128)(2,1)} %get-tuple-element.109), channel_id=1, source_target_pairs={{0,4},{4,0},{8,12},{12,8},{16,20},{20,16},{24,28},{28,24},{1,5},{5... | collective-permute-start | bytes 1572872 | tf_op jit(solution)/shard_map/ppermute | solution.py:433
  293.4 54.3 %collective-permute-start.36 = (bf16[4,2,64,512]{3,2,1,0:T(8,128)(2,1)}, bf16[4,2,64,512]{3,2,1,0:T(8,128)(2,1)}, u32[]{:S(2)}, u32[]{:S(2)}) collective-permute-start(bf16[4,2,64,512]{3,2,1,0:T(8,128)(2,1)} %get-tuple-element.89), channel_id=1, source_target_pairs={{0,4},{4,0},{8,12},{12,8},{16,20},{20,16},{24,28},{28,24},{1,5},{5... | collective-permute-start | bytes 1572872 | tf_op jit(solution)/shard_map/ppermute | solution.py:433
  295.3 55.0 %collective-permute-start.40 = (bf16[4,2,64,512]{3,2,1,0:T(8,128)(2,1)}, bf16[4,2,64,512]{3,2,1,0:T(8,128)(2,1)}, u32[]{:S(2)}, u32[]{:S(2)}) collective-permute-start(bf16[4,2,64,512]{3,2,1,0:T(8,128)(2,1)} %get-tuple-element.95), channel_id=1, source_target_pairs={{0,4},{4,0},{8,12},{12,8},{16,20},{20,16},{24,28},{28,24},{1,5},{5... | collective-permute-start | bytes 1572872 | tf_op jit(solution)/shard_map/ppermute | solution.py:433
  297.4 55.3 %collective-permute-start.45 = (bf16[2,64,512]{2,1,0:T(8,128)(2,1)}, bf16[2,64,512]{2,1,0:T(8,128)(2,1)S(1)}, u32[]{:S(2)}, u32[]{:S(2)}) collective-permute-start(bf16[2,64,512]{2,1,0:T(8,128)(2,1)} %get-tuple-element.105), channel_id=1, source_target_pairs={{0,8},{4,12},{8,16},{12,20},{16,24},{20,28},{24,0},{28,4},{1,9},{5... | collective-permute-start | bytes 393224 | tf_op jit(solution)/shard_map/ppermute | solution.py:433
  299.5 56.1 %collective-permute-start.46 = (bf16[2,64,512]{2,1,0:T(8,128)(2,1)}, bf16[2,64,512]{2,1,0:T(8,128)(2,1)S(1)}, u32[]{:S(2)}, u32[]{:S(2)}) collective-permute-start(bf16[2,64,512]{2,1,0:T(8,128)(2,1)} %get-tuple-element.106), channel_id=1, source_target_pairs={{0,16},{4,20},{8,24},{12,28},{16,0},{20,4},{24,8},{28,12},{1,17},{... | collective-permute-start | bytes 393224 | tf_op jit(solution)/shard_map/ppermute | solution.py:433
  302.1 54.2 %collective-permute-start.47 = (bf16[2,64,512]{2,1,0:T(8,128)(2,1)}, bf16[2,64,512]{2,1,0:T(8,128)(2,1)S(1)}, u32[]{:S(2)}, u32[]{:S(2)}) collective-permute-start(bf16[2,64,512]{2,1,0:T(8,128)(2,1)} %get-tuple-element.107), channel_id=1, source_target_pairs={{0,24},{4,28},{8,0},{12,4},{16,8},{20,12},{24,16},{28,20},{1,25},{... | collective-permute-start | bytes 393224 | tf_op jit(solution)/shard_map/ppermute | solution.py:433
  350.3 12.9 %collective-permute-start.50 = (bf16[2,64,512]{2,1,0:T(8,128)(2,1)}, bf16[2,64,512]{2,1,0:T(8,128)(2,1)S(1)}, u32[]{:S(2)}, u32[]{:S(2)}) collective-permute-start(bf16[2,64,512]{2,1,0:T(8,128)(2,1)} %get-tuple-element.112), channel_id=1, source_target_pairs={{0,16},{4,20},{8,24},{12,28},{16,0},{20,4},{24,8},{28,12},{1,17},{... | collective-permute-start | bytes 393224 | tf_op jit(solution)/shard_map/ppermute | solution.py:433
  352.8 11.6 %collective-permute-start.51 = (bf16[2,64,512]{2,1,0:T(8,128)(2,1)}, bf16[2,64,512]{2,1,0:T(8,128)(2,1)S(1)}, u32[]{:S(2)}, u32[]{:S(2)}) collective-permute-start(bf16[2,64,512]{2,1,0:T(8,128)(2,1)} %get-tuple-element.113), channel_id=1, source_target_pairs={{0,24},{4,28},{8,0},{12,4},{16,8},{20,12},{24,16},{28,20},{1,25},{... | collective-permute-start | bytes 393224 | tf_op jit(solution)/shard_map/ppermute | solution.py:433
  355.6 14.2 %collective-permute-start.37 = (bf16[2,64,512]{2,1,0:T(8,128)(2,1)}, bf16[2,64,512]{2,1,0:T(8,128)(2,1)S(1)}, u32[]{:S(2)}, u32[]{:S(2)}) collective-permute-start(bf16[2,64,512]{2,1,0:T(8,128)(2,1)} %get-tuple-element.91), channel_id=1, source_target_pairs={{0,8},{4,12},{8,16},{12,20},{16,24},{20,28},{24,0},{28,4},{1,9},{5... | collective-permute-start | bytes 393224 | tf_op jit(solution)/shard_map/ppermute | solution.py:433
  356.2 20.1 %collective-permute-start.38 = (bf16[2,64,512]{2,1,0:T(8,128)(2,1)}, bf16[2,64,512]{2,1,0:T(8,128)(2,1)S(1)}, u32[]{:S(2)}, u32[]{:S(2)}) collective-permute-start(bf16[2,64,512]{2,1,0:T(8,128)(2,1)} %get-tuple-element.92), channel_id=1, source_target_pairs={{0,16},{4,20},{8,24},{12,28},{16,0},{20,4},{24,8},{28,12},{1,17},{... | collective-permute-start | bytes 393224 | tf_op jit(solution)/shard_map/ppermute | solution.py:433
  357.8 18.5 %collective-permute-start.39 = (bf16[2,64,512]{2,1,0:T(8,128)(2,1)}, bf16[2,64,512]{2,1,0:T(8,128)(2,1)S(1)}, u32[]{:S(2)}, u32[]{:S(2)}) collective-permute-start(bf16[2,64,512]{2,1,0:T(8,128)(2,1)} %get-tuple-element.93), channel_id=1, source_target_pairs={{0,24},{4,28},{8,0},{12,4},{16,8},{20,12},{24,16},{28,20},{1,25},{... | collective-permute-start | bytes 393224 | tf_op jit(solution)/shard_map/ppermute | solution.py:433
  363.2 14.1 %collective-permute-start.41 = (bf16[2,64,512]{2,1,0:T(8,128)(2,1)}, bf16[2,64,512]{2,1,0:T(8,128)(2,1)S(1)}, u32[]{:S(2)}, u32[]{:S(2)}) collective-permute-start(bf16[2,64,512]{2,1,0:T(8,128)(2,1)} %get-tuple-element.97), channel_id=1, source_target_pairs={{0,8},{4,12},{8,16},{12,20},{16,24},{20,28},{24,0},{28,4},{1,9},{5... | collective-permute-start | bytes 393224 | tf_op jit(solution)/shard_map/ppermute | solution.py:433
  364.3 17.6 %collective-permute-start.42 = (bf16[2,64,512]{2,1,0:T(8,128)(2,1)}, bf16[2,64,512]{2,1,0:T(8,128)(2,1)S(1)}, u32[]{:S(2)}, u32[]{:S(2)}) collective-permute-start(bf16[2,64,512]{2,1,0:T(8,128)(2,1)} %get-tuple-element.98), channel_id=1, source_target_pairs={{0,16},{4,20},{8,24},{12,28},{16,0},{20,4},{24,8},{28,12},{1,17},{... | collective-permute-start | bytes 393224 | tf_op jit(solution)/shard_map/ppermute | solution.py:433
  369.8 12.2 %collective-permute-start.43 = (bf16[2,64,512]{2,1,0:T(8,128)(2,1)}, bf16[2,64,512]{2,1,0:T(8,128)(2,1)S(1)}, u32[]{:S(2)}, u32[]{:S(2)}) collective-permute-start(bf16[2,64,512]{2,1,0:T(8,128)(2,1)} %get-tuple-element.99), channel_id=1, source_target_pairs={{0,24},{4,28},{8,0},{12,4},{16,8},{20,12},{24,16},{28,20},{1,25},{... | collective-permute-start | bytes 393224 | tf_op jit(solution)/shard_map/ppermute | solution.py:433
  (63 other events, 825.8 us)

commit v4 on v2

--- a/solution.py
+++ b/solution.py
@@ -15,6 +15,10 @@
 
 def params(mib):
     return pltpu.CompilerParams(vmem_limit_bytes=mib * 1024 * 1024)
+
+
+def hbm(x):
+    return pltpu.with_memory_space_constraint(x, pltpu.HBM)
 
 
 def cost(flops, nbytes):
@@ -61,7 +65,7 @@
     _, le, _, n, _ = green.shape
     return pl.pallas_call(
         lesser_kernel,
-        out_shape=[jax.ShapeDtypeStruct((le, n // 2, n), BF16)] * 2,
+        out_shape=[pltpu.HBM((le, n // 2, n), BF16)] * 2,
         grid_spec=pltpu.PrefetchScalarGridSpec(
             num_scalar_prefetch=1,
             grid=(le,),
@@ -71,7 +75,7 @@
             ],
             out_specs=[pl.BlockSpec((1, n // 2, n), lambda e, sel: (e, 0, 0))] * 2,
         ),
-        compiler_params=params(40),
+        compiler_params=params(56),
         cost_estimate=cost(le * 6 * n**3, le * n * n * 6),
         name="lesser",
     )(which[None], green, broadening)
@@ -92,14 +96,14 @@
     each = 2
     return pl.pallas_call(
         place_kernel,
-        out_shape=[pltpu.VMEM((nk, n, n), BF16)] * 2,
+        out_shape=[pltpu.HBM((nk, n, n), BF16)] * 2,
         grid_spec=pltpu.PrefetchScalarGridSpec(
             num_scalar_prefetch=1,
             grid=(nk // each,),
             in_specs=[pl.BlockSpec((each, rows, n), lambda q, w: (q, 0, 0))] * len(pieces),
             out_specs=[pl.BlockSpec((each, n, n), lambda q, w: (q, 0, 0))] * 2,
         ),
-        compiler_params=params(40),
+        compiler_params=params(56),
         cost_estimate=cost(nk * n * n * 4, nk * n * n * 6),
         name="place",
     )(where, *pieces)
@@ -148,7 +152,7 @@
                 extra.append(value)
     return pl.pallas_call(
         source_kernel,
-        out_shape=[jax.ShapeDtypeStruct(shape, BF16) for shape in shapes],
+        out_shape=[pltpu.HBM(shape, BF16) for shape in shapes],
         grid_spec=pltpu.PrefetchScalarGridSpec(
             num_scalar_prefetch=2,
             grid=(half // rows,),
@@ -156,7 +160,7 @@
             out_specs=specs,
         ),
         input_output_aliases=alias,
-        compiler_params=params(40),
+        compiler_params=params(56),
         cost_estimate=cost(le * half * n * 16, le * half * n * 12),
         name="source",
     )(odd[None], weights, keep, recv, kz, rz, *extra)
@@ -202,7 +206,7 @@
     block = lambda lead: pl.BlockSpec((lead, rows, n), lambda g, s: (0, g, 0))
     return pl.pallas_call(
         functools.partial(home_kernel, lk, len(pieces)),
-        out_shape=[jax.ShapeDtypeStruct((lk, n, n), BF16)] * 2,
+        out_shape=[pltpu.HBM((lk, n, n), BF16)] * 2,
         grid_spec=pltpu.PrefetchScalarGridSpec(
             num_scalar_prefetch=1,
             grid=(n // rows,),
@@ -210,7 +214,7 @@
             out_specs=[block(lk), block(lk)],
             scratch_shapes=[pltpu.VMEM((count, rows, n), BF16)],
         ),
-        compiler_params=params(40),
+        compiler_params=params(56),
         cost_estimate=cost(4 * lk * count * n * n, n * n * (6 * count + 4 * lk)),
         name="home",
     )(slots, *pieces, full, turned)
@@ -279,7 +283,7 @@
             scratch_shapes=[pltpu.VMEM((count, rows, cols), BF16)] * 2,
         ),
         input_output_aliases={2 + len(in_specs) - 1: 0} if alias else {},
-        compiler_params=params(40),
+        compiler_params=params(56),
         cost_estimate=cost(4 * count * count * rows * n, rows * n * count * 10),
         name="rows",
     )(mine[None], slots, *pieces, *pieces, coupling, *alias)
@@ -312,7 +316,7 @@
     one = pl.BlockSpec((1, n, n), lambda k: (k, 0, 0))
     return pl.pallas_call(
         functools.partial(first_density_kernel, energy, held is None),
-        out_shape=jax.ShapeDtypeStruct((lk, 2, n, n), F32),
+        out_shape=pltpu.HBM((lk, 2, n, n), F32),
         grid=(lk,),
         in_specs=[
             pl.BlockSpec((1, 1, 2, n, n), lambda k: (k, energy, 0, 0, 0)),
@@ -321,7 +325,7 @@
             one,
         ] + [pair] * len(alias),
         out_specs=pair,
-        compiler_params=params(40),
+        compiler_params=params(56),
         cost_estimate=cost(16 * lk * n**3, lk * n * n * 20),
         name="density",
     )(green, broadening, x, y, *alias)
@@ -345,10 +349,9 @@
                     send_ref[g, c] = d_ref[c, pl.ds(other, rows), :].astype(BF16)
 
 
-def last_density(scale, energy, start, stop, groups, odd, green, broadening, x, y, held):
+def last_density(scale, energy, start, count, groups, odd, green, broadening, x, y, held):
     _, le, _, n, _ = green.shape
     rows = n // (2 * groups)
-    count = stop - start
     one = pl.BlockSpec((1, n, n), lambda i, odd: (start + i, 0, 0))
     out = pl.BlockSpec((groups, 2, rows, n), lambda i, odd: (0, 0, 0, 0))
     return pl.pallas_call(
@@ -367,7 +370,7 @@
             out_specs=[out] * (2 * count),
             scratch_shapes=[pltpu.VMEM((2, n, n), F32)],
         ),
-        compiler_params=params(40),
+        compiler_params=params(56),
         cost_estimate=cost(count * 16 * n**3, count * n * n * 20),
         name="density",
     )(odd[None], green, broadening, x, y, held)
@@ -388,7 +391,7 @@
         out_shape=[jax.ShapeDtypeStruct(keep.shape[1:], BF16)] * groups,
         in_specs=[pl.BlockSpec(memory_space=pltpu.SMEM), vmem, vmem],
         out_specs=[vmem] * groups,
-        compiler_params=params(40),
+        compiler_params=params(56),
         cost_estimate=cost(keep.size, keep.size * 6),
         name="pairsum",
     )(group[None], keep, recv)
@@ -409,11 +412,15 @@
     while (nm >> (len(strides) + 1)) > 0:
         strides.append(nm >> (len(strides) + 1))
 
+    def permuted(x, perm):
+        return lax.ppermute(x, "energy", perm)
+
     def over_energy(x, perm):
-        return lax.ppermute(x, "energy", perm)
+        return hbm(permuted(x, perm))
 
     def swap(x, stride):
-        return lax.ppermute(x, "mom", [(i, i ^ stride) for i in range(nm)])
+        moved = lax.ppermute(x, "mom", [(i, i ^ stride) for i in range(nm)])
+        return hbm(moved)
 
     def spread(x):
         held = [x]
@@ -440,7 +447,8 @@
     own_slots = lax.dynamic_slice_in_dim(slots, mine * lk, lk, 0).reshape(-1)
     all_slots = slots.reshape(-1)
 
-    green_ret = pltpu.with_memory_space_constraint(green_ret, pltpu.HBM)
+    green_ret = hbm(green_ret)
+    coupling = hbm(coupling)
     coupling_pieces = spread(coupling)
 
     send = [lesser_packed((1 - odd) * hk + j, green_ret, broadening) for j in range(hk)]
@@ -465,23 +473,24 @@
         fresh = [spread(part[e]) for part in use]
         back = [spread(over_energy(part[le + e], pairs)) for part in use]
         pieces = [part[at] for at in range(nm) for part in fresh + back]
-        x, y = home_blocks(own_slots, pieces, full, turned, lk)
         if e < le - 1:
+            x, y = home_blocks(own_slots, pieces, full, turned, lk)
             held_density = first_density(e, green_ret, broadening, x, y, held_density)
         else:
             shares = []
-            for start, stop in ((0, 1), (1, lk)):
+            x, y = home_blocks(own_slots, pieces, full, turned, lk)
+            for first, count in ((0, 1), (1, lk - 1)):
                 shares = shares + list(last_density(
-                    scale, e, start, stop, groups, odd,
+                    scale, e, first, count, groups, odd,
                     green_ret, broadening, x, y, held_density))
             for k in range(lk):
                 kept, sent = shares[2 * k], shares[2 * k + 1]
-                other = over_energy(sent, pairs)
+                other = permuted(sent, pairs)
                 parts = pair_sum(group, kept, other)
                 total = parts[0].astype(F32)
                 for d in range(1, groups):
                     perm = [(i, (i + 2 * d) % ne) for i in range(ne)]
-                    total = total + over_energy(parts[d], perm).astype(F32)
+                    total = total + permuted(parts[d], perm).astype(F32)
                 late.append(total)
         held_rows = own_rows(mine, all_slots, pieces, coupling, e, le, held_rows)
     density = jnp.transpose(jnp.stack(late), (2, 0, 1, 3))

time: 364 us -> 349 us (0.959)
  local copies, waits for them, and re-layouts: 48.3 us -> 9.85 us
  Pallas kernels: 120 us -> 142 us
    unnamed x135 -> x73, local copies, waits for them, and re-layouts: 48.2 us -> 8.57 us
    pallas_call x9, Pallas kernels: 33.7 us -> 42.4 us  [the longest x4 16.7 us: lesser_packed(): pl.pallas_call(lesser_kernel, out_shape=[pltpu.HBM((le, n // 2, n), BF16)...]
    pallas_call x2, Pallas kernels: 25.6 us -> 30.2 us  [home_blocks(): pl.pallas_call(functools.partial(home_kernel, lk, len(pieces)), out_shape...]
  transfers between devices with their start and end apart: 52 -> 52, of which waited for: 17 -> 16; matrix products, arithmetic and copies ran while one was open for 1% -> 2% of each run, Pallas kernels for 27% -> 34%
where the time goes in v4:
time: 349 us; the launch traced here: 348 us
  Pallas kernels  142 us (41%)
  waiting for transfers between devices  113 us (32%)
  starting transfers between devices  76.8 us (22%)
  local copies, waits for them, and re-layouts  9.85 us (3%)
  other arithmetic  4.77 us (1%)
    ppermute x31, starting transfers between devices, permuted(): return lax.ppermute(x, 'energy', perm)  65.5 us
    ppermute x21, waiting for transfers between devices, swap(): moved = lax.ppermute(x, 'mom', [(i, i ^ stride) for i in range(nm)])  62.9 us
    ppermute x31, waiting for transfers between devices, permuted(): return lax.ppermute(x, 'energy', perm)  50 us
    pallas_call x2, Pallas kernels, own_rows(): pl.pallas_call(functools.partial(rows_kernel, len(pieces)), out_shape=jax...  30.7 us
    pallas_call x2, Pallas kernels, home_blocks(): pl.pallas_call(functools.partial(home_kernel, lk, len(pieces)), out_shape...  30.2 us
    pallas_call x2, Pallas kernels, last_density(): pl.pallas_call(functools.partial(last_density_kernel, scale, energy), out...  17.7 us
    pallas_call x4, Pallas kernels, lesser_packed(): pl.pallas_call(lesser_kernel, out_shape=[pltpu.HBM((le, n // 2, n), BF16)...  16.7 us
    pallas_call x4, Pallas kernels, sources(): pl.pallas_call(source_kernel, out_shape=[pltpu.HBM(shape, BF16) for shape...  14.1 us
  transfers between devices with their start and end apart: 52, of which 16 were waited for; matrix products, arithmetic and copies ran while one was open for 2% of the time, Pallas kernels for 34%

profile of v4, /device:TPU:0, one launch (start us, length us, event | category | flops | bytes accessed | tf_op | source)
XLA Modules:
  0.0 347.7 jit_solution(34479605012562632)
XLA Ops:
  0.6 4.1 %lesser.7 = (bf16[2,256,512]{2,1,0:T(8,128)(2,1)}, bf16[2,256,512]{2,1,0:T(8,128)(2,1)}) custom-call(s32[1]{0:T(128)} %bitcast.9.sel, bf16[4,2,2,512,512]{4,3,2,1,0:T(8,128)(2,1)} %g_ref.13, f32[4,2,512]{2,1,0:T(2,128)} %gamma_ref.13), custom_call_target="tpu_custom_call" | custom-call | flops 1610612736 | bytes 3145728 | tf_op jit(solution)/shard_map/lesser/pallas_call | solution.py:66
  4.8 3.0 collective-permute-start.9
  7.8 4.1 %lesser.6 = (bf16[2,256,512]{2,1,0:T(8,128)(2,1)}, bf16[2,256,512]{2,1,0:T(8,128)(2,1)}) custom-call(s32[1]{0:T(128)} %bitcast.8.sel, bf16[4,2,2,512,512]{4,3,2,1,0:T(8,128)(2,1)} %g_ref.13, f32[4,2,512]{2,1,0:T(2,128)} %gamma_ref.13), custom_call_target="tpu_custom_call" | custom-call | flops 1610612736 | bytes 3145728 | tf_op jit(solution)/shard_map/lesser/pallas_call | solution.py:66
  13.2 3.5 %collective-permute-start.6 = (bf16[2,256,512]{2,1,0:T(8,128)(2,1)}, bf16[2,256,512]{2,1,0:T(8,128)(2,1)}, u32[]{:S(2)}, u32[]{:S(2)}) collective-permute-start(bf16[2,256,512]{2,1,0:T(8,128)(2,1)} %get-tuple-element.61), channel_id=1, source_target_pairs={{0,4},{4,0},{8,12},{12,8},{16,20},{20,16},{24,28},{28,24},{1,5},{5... | collective-permute-start | bytes 1572872 | tf_op jit(solution)/shard_map/ppermute | solution.py:416
  18.0 4.3 %lesser.5 = (bf16[2,256,512]{2,1,0:T(8,128)(2,1)}, bf16[2,256,512]{2,1,0:T(8,128)(2,1)}) custom-call(s32[1]{0:T(128)} %bitcast.7.sel, bf16[4,2,2,512,512]{4,3,2,1,0:T(8,128)(2,1)} %g_ref.13, f32[4,2,512]{2,1,0:T(2,128)} %gamma_ref.13), custom_call_target="tpu_custom_call" | custom-call | flops 1610612736 | bytes 3145728 | tf_op jit(solution)/shard_map/lesser/pallas_call | solution.py:66
  22.2 2.6 collective-permute-start.3
  24.9 3.9 %collective-permute-done.10.kz = bf16[2,256,512]{2,1,0:T(8,128)(2,1)} collective-permute-done((bf16[2,256,512]{2,1,0:T(8,128)(2,1)}, bf16[2,256,512]{2,1,0:T(8,128)(2,1)}, u32[]{:S(2)}, u32[]{:S(2)}) %collective-permute-start.10) | collective-permute-done | bytes 524320 | tf_op jit(solution)/shard_map/ppermute | solution.py:416
  28.9 4.3 %collective-permute-start.11 = (bf16[2,256,512]{2,1,0:T(8,128)(2,1)S(1)}, bf16[2,256,512]{2,1,0:T(8,128)(2,1)}, u32[]{:S(2)}, u32[]{:S(2)}) collective-permute-start(bf16[2,256,512]{2,1,0:T(8,128)(2,1)S(1)} %collective-permute-done.9.recv), channel_id=1, source_target_pairs={{0,8},{8,16},{12,4},{16,24},{20,12},{28,20},{1,9},{9,17},{13,5},{1... | collective-permute-start | bytes 1572872 | tf_op jit(solution)/shard_map/ppermute | solution.py:416
  33.2 3.8 %collective-permute-start.8 = (bf16[2,256,512]{2,1,0:T(8,128)(2,1)}, bf16[2,256,512]{2,1,0:T(8,128)(2,1)}, u32[]{:S(2)}, u32[]{:S(2)}) collective-permute-start(bf16[2,256,512]{2,1,0:T(8,128)(2,1)} %collective-permute-done.6.recv), channel_id=1, source_target_pairs={{0,8},{8,16},{12,4},{16,24},{20,12},{28,20},{1,9},{9,17},{13,5},{1... | collective-permute-start | bytes 1572872 | tf_op jit(solution)/shard_map/ppermute | solution.py:416
  40.2 4.2 %lesser.4 = (bf16[2,256,512]{2,1,0:T(8,128)(2,1)}, bf16[2,256,512]{2,1,0:T(8,128)(2,1)}) custom-call(s32[1]{0:T(128)} %bitcast.6.sel, bf16[4,2,2,512,512]{4,3,2,1,0:T(8,128)(2,1)} %g_ref.13, f32[4,2,512]{2,1,0:T(2,128)} %gamma_ref.13), custom_call_target="tpu_custom_call" | custom-call | flops 1610612736 | bytes 3145728 | tf_op jit(solution)/shard_map/lesser/pallas_call | solution.py:66
  45.7 8.0 %collective-permute-done.recv = bf16[2,256,512]{2,1,0:T(8,128)(2,1)} collective-permute-done((bf16[2,256,512]{2,1,0:T(8,128)(2,1)}, bf16[2,256,512]{2,1,0:T(8,128)(2,1)}, u32[]{:S(2)}, u32[]{:S(2)}) %collective-permute-start) | collective-permute-done | bytes 524320 | tf_op jit(solution)/shard_map/ppermute | solution.py:416
  53.7 3.7 %collective-permute-start.5 = (bf16[2,256,512]{2,1,0:T(8,128)(2,1)S(1)}, bf16[2,256,512]{2,1,0:T(8,128)(2,1)S(1)}, u32[]{:S(2)}, u32[]{:S(2)}) collective-permute-start(bf16[2,256,512]{2,1,0:T(8,128)(2,1)S(1)} %collective-permute-done.3.recv), channel_id=1, source_target_pairs={{0,8},{8,16},{12,4},{16,24},{20,12},{28,20},{1,9},{9,17},{13,5},{1... | collective-permute-start | bytes 1572872 | tf_op jit(solution)/shard_map/ppermute | solution.py:416
  58.8 4.8 %collective-permute-start.2 = (bf16[2,256,512]{2,1,0:T(8,128)(2,1)}, bf16[2,256,512]{2,1,0:T(8,128)(2,1)S(1)}, u32[]{:S(2)}, u32[]{:S(2)}) collective-permute-start(bf16[2,256,512]{2,1,0:T(8,128)(2,1)} %collective-permute-done.recv), channel_id=1, source_target_pairs={{0,8},{8,16},{12,4},{16,24},{20,12},{28,20},{1,9},{9,17},{13,5},{1... | collective-permute-start | bytes 1572872 | tf_op jit(solution)/shard_map/ppermute | solution.py:416
  64.2 3.1 pad_maximum_fusion.w_ref
  67.3 3.5 %source.4 = (bf16[1,512,512]{2,1,0:T(8,128)(2,1)}, bf16[2,512,512]{2,1,0:T(8,128)(2,1)}, bf16[1,512,512]{2,1,0:T(8,128)(2,1)}, bf16[2,512,512]{2,1,0:T(8,128)(2,1)}) custom-call(s32[1]{0:T(128)} %bitcast.1.odd, f32[4]{0:T(128)} %pad_maximum_fusion.w_ref, bf16[2,256,512]{2,1,0:T(8,128)(2,1)} %get-tuple-element.62.keep, bf16[2,256,512]{2,1,0:T(8,128)(2,1)} %copy-done.23, ...), custom_call_target="tpu_custom_call" | custom-call | flops 4194304 | bytes 3145728 | tf_op jit(solution)/shard_map/source/pallas_call | solution.py:153
  70.8 3.5 %source.5 = (bf16[1,512,512]{2,1,0:T(8,128)(2,1)}, bf16[2,512,512]{2,1,0:T(8,128)(2,1)}, bf16[1,512,512]{2,1,0:T(8,128)(2,1)}, bf16[2,512,512]{2,1,0:T(8,128)(2,1)}) custom-call(s32[1]{0:T(128)} %bitcast.1.odd, f32[4]{0:T(128)} %pad_maximum_fusion.w_ref, ...), custom_call_target="tpu_custom_call", output_to_operand_aliasing={{0}: (6, {}), {1}: (7, {}), {2}: (8, {}), {3}: (9, {})} | custom-call | flops 4194304 | bytes 3145728 | tf_op jit(solution)/shard_map/source/pallas_call | solution.py:153
  75.4 3.5 %source.6 = (bf16[1,512,512]{2,1,0:T(8,128)(2,1)}, bf16[2,512,512]{2,1,0:T(8,128)(2,1)}, bf16[1,512,512]{2,1,0:T(8,128)(2,1)}, bf16[2,512,512]{2,1,0:T(8,128)(2,1)}) custom-call(s32[1]{0:T(128)} %bitcast.1.odd, f32[4]{0:T(128)} %pad_maximum_fusion.w_ref, bf16[2,256,512]{2,1,0:T(8,128)(2,1)} %get-tuple-element.58.keep, ...), custom_call_target="tpu_custom_call", output_to_operand_aliasing={{1}: (6, {}), {3}: (7, {})} | custom-call | flops 4194304 | bytes 3145728 | tf_op jit(solution)/shard_map/source/pallas_call | solution.py:153
  79.9 3.6 %source.7 = (bf16[1,512,512]{2,1,0:T(8,128)(2,1)}, bf16[2,512,512]{2,1,0:T(8,128)(2,1)}, bf16[1,512,512]{2,1,0:T(8,128)(2,1)}, bf16[2,512,512]{2,1,0:T(8,128)(2,1)}) custom-call(s32[1]{0:T(128)} %bitcast.1.odd, f32[4]{0:T(128)} %pad_maximum_fusion.w_ref, ...), custom_call_target="tpu_custom_call", output_to_operand_aliasing={{0}: (6, {}), {1}: (7, {}), {2}: (8, {}), {3}: (9, {})} | custom-call | flops 4194304 | bytes 3145728 | tf_op jit(solution)/shard_map/source/pallas_call | solution.py:153
  83.5 2.3 collective-permute-start.20
  87.4 11.4 %collective-permute-done.20.refs_3_.refs_19_ = bf16[1,512,512]{2,1,0:T(8,128)(2,1)S(1)} collective-permute-done((bf16[1,512,512]{2,1,0:T(8,128)(2,1)}, bf16[1,512,512]{2,1,0:T(8,128)(2,1)S(1)}, u32[]{:S(2)}, u32[]{:S(2)}) %collective-permute-start.20) | collective-permute-done | bytes 524320 | tf_op jit(solution)/shard_map/ppermute | solution.py:416
  101.0 6.6 %collective-permute-done.19.refs_2_.refs_18_ = bf16[1,512,512]{2,1,0:T(8,128)(2,1)S(1)} collective-permute-done((bf16[1,512,512]{2,1,0:T(8,128)(2,1)S(1)}, bf16[1,512,512]{2,1,0:T(8,128)(2,1)S(1)}, u32[]{:S(2)}, u32[]{:S(2)}) %collective-permute-start.19) | collective-permute-done | bytes 524320 | tf_op jit(solution)/shard_map/ppermute | solution.py:416
  107.6 6.0 %collective-permute-done.21.refs_4_.refs_20_ = bf16[1,512,512]{2,1,0:T(8,128)(2,1)S(1)} collective-permute-done((bf16[1,512,512]{2,1,0:T(8,128)(2,1)S(1)}, bf16[1,512,512]{2,1,0:T(8,128)(2,1)S(1)}, u32[]{:S(2)}, u32[]{:S(2)}) %collective-permute-start.21) | collective-permute-done | bytes 524320 | tf_op jit(solution)/shard_map/ppermute | solution.py:422
  114.2 6.3 %collective-permute-done.24.refs_7_.refs_23_ = bf16[1,512,512]{2,1,0:T(8,128)(2,1)} collective-permute-done((bf16[1,512,512]{2,1,0:T(8,128)(2,1)S(1)}, bf16[1,512,512]{2,1,0:T(8,128)(2,1)}, u32[]{:S(2)}, u32[]{:S(2)}) %collective-permute-start.24) | collective-permute-done | bytes 524320 | tf_op jit(solution)/shard_map/ppermute | solution.py:422
  123.1 12.7 %collective-permute-done.23.refs_6_.refs_22_ = bf16[1,512,512]{2,1,0:T(8,128)(2,1)} collective-permute-done((bf16[1,512,512]{2,1,0:T(8,128)(2,1)S(1)}, bf16[1,512,512]{2,1,0:T(8,128)(2,1)}, u32[]{:S(2)}, u32[]{:S(2)}) %collective-permute-start.23) | collective-permute-done | bytes 524320 | tf_op jit(solution)/shard_map/ppermute | solution.py:422
  137.3 3.9 %collective-permute-done.12.refs_1_.refs_9_ = bf16[2,512,512]{2,1,0:T(8,128)(2,1)S(1)} collective-permute-done((bf16[2,512,512]{2,1,0:T(8,128)(2,1)}, bf16[2,512,512]{2,1,0:T(8,128)(2,1)S(1)}, u32[]{:S(2)}, u32[]{:S(2)}) %collective-permute-start.12) | collective-permute-done | bytes 1048608 | tf_op jit(solution)/shard_map/ppermute | solution.py:416
  144.9 17.3 %collective-permute-done.13.refs_2_.refs_10_ = bf16[2,512,512]{2,1,0:T(8,128)(2,1)} collective-permute-done((bf16[2,512,512]{2,1,0:T(8,128)(2,1)}, bf16[2,512,512]{2,1,0:T(8,128)(2,1)}, u32[]{:S(2)}, u32[]{:S(2)}) %collective-permute-start.13) | collective-permute-done | bytes 1048608 | tf_op jit(solution)/shard_map/ppermute | solution.py:422
  162.7 20.6 %collective-permute-done.14.refs_3_.refs_11_ = bf16[2,512,512]{2,1,0:T(8,128)(2,1)} collective-permute-done((bf16[2,512,512]{2,1,0:T(8,128)(2,1)S(1)}, bf16[2,512,512]{2,1,0:T(8,128)(2,1)}, u32[]{:S(2)}, u32[]{:S(2)}) %collective-permute-start.14) | collective-permute-done | bytes 1048608 | tf_op jit(solution)/shard_map/ppermute | solution.py:422
  185.1 11.6 %place.1 = (bf16[16,512,512]{2,1,0:T(8,128)(2,1)}, bf16[16,512,512]{2,1,0:T(8,128)(2,1)}) custom-call(s32[4]{0:T(128)} %pad_add_fusion.where, bf16[16,128,512]{2,1,0:T(8,128)(2,1)} %refs_0_.1, bf16[16,128,512]{2,1,0:T(8,128)(2,1)} %collective-permute-done.33.refs_1_, bf16[16,128,512]{2,1,0:T(8,128)(2,1)} %copy-done.15, ...), custom_call_target="tpu_custom_call" | custom-call | flops 16777216 | bytes 25165824 | tf_op jit(solution)/shard_map/place/pallas_call | solution.py:97
  196.6 15.1 %home.3 = (bf16[4,512,512]{2,1,0:T(8,128)(2,1)}, bf16[4,512,512]{2,1,0:T(8,128)(2,1)}) custom-call(s32[64]{0:T(128)} %reshape.11.slots, bf16[1,512,512]{2,1,0:T(8,128)(2,1)} %get-tuple-element.76.refs_0_.refs_16_, bf16[1,512,512]{2,1,0:T(8,128)(2,1)} %get-tuple-element.77.refs_1_.refs_17_, bf16[1,512,512]{2,1,0:T(8,128)(2,1)} %copy-done.8, ...), custom_call_target="tpu_custom_call" | custom-call | flops 67108864 | bytes 29360128 | tf_op jit(solution)/shard_map/home/pallas_call | solution.py:207
  211.8 13.0 %density.3.held_ref = f32[4,2,512,512]{3,2,1,0:T(8,128)} custom-call(bf16[4,2,2,512,512]{4,3,2,1,0:T(8,128)(2,1)} %g_ref.13, f32[4,2,512]{2,1,0:T(2,128)} %gamma_ref.13, bf16[4,512,512]{2,1,0:T(8,128)(2,1)} %get-tuple-element.84.x_ref, bf16[4,512,512]{2,1,0:T(8,128)(2,1)} %get-tuple-element.85.y_ref), custom_call_target="tpu_custom_call" | custom-call | flops 8589934592 | bytes 20971520 | tf_op jit(solution)/shard_map/density/pallas_call | solution.py:317
  226.1 15.1 %home.2 = (bf16[4,512,512]{2,1,0:T(8,128)(2,1)}, bf16[4,512,512]{2,1,0:T(8,128)(2,1)}) custom-call(s32[64]{0:T(128)} %reshape.11.slots, bf16[2,512,512]{2,1,0:T(8,128)(2,1)} %get-tuple-element.74.refs_0_.refs_8_, bf16[2,512,512]{2,1,0:T(8,128)(2,1)} %copy-done.1, bf16[2,512,512]{2,1,0:T(8,128)(2,1)} %collective-permute-done.13.refs_2_.refs_10_, ...), custom_call_target="tpu_custom_call" | custom-call | flops 67108864 | bytes 29360128 | tf_op jit(solution)/shard_map/home/pallas_call | solution.py:207
  241.2 5.9 %density.4 = (bf16[4,2,64,512]{3,2,1,0:T(8,128)(2,1)}, bf16[4,2,64,512]{3,2,1,0:T(8,128)(2,1)}) custom-call(s32[1]{0:T(128)} %bitcast.1.odd, bf16[4,2,2,512,512]{4,3,2,1,0:T(8,128)(2,1)} %g_ref.13, f32[4,2,512]{2,1,0:T(2,128)} %gamma_ref.13, bf16[4,512,512]{2,1,0:T(8,128)(2,1)} %get-tuple-element.82.x_ref, bf16[4,512,512]{2,1,0:T(8,128)(2,1)} %get-tuple-element.83.y_ref, ...), custom_call_target="tpu_custom_call" | custom-call | flops 2147483648 | bytes 5242880 | tf_op jit(solution)/shard_map/density/pallas_call | solution.py:357
  248.1 11.8 %density.5 = (bf16[4,2,64,512]{3,2,1,0:T(8,128)(2,1)}, bf16[4,2,64,512]{3,2,1,0:T(8,128)(2,1)}, bf16[4,2,64,512]{3,2,1,0:T(8,128)(2,1)}, bf16[4,2,64,512]{3,2,1,...) custom-call(s32[1]{0:T(128)} %bitcast.1.odd, bf16[4,2,2,512,512]{4,3,2,1,0:T(8,128)(2,1)} %g_ref.13, ...), custom_call_target="tpu_custom_call" | custom-call | flops 6442450944 | bytes 15728640 | tf_op jit(solution)/shard_map/density/pallas_call | solution.py:357
  263.8 2.1 pairsum.4
  267.4 2.1 collective-permute-start.38
  269.5 5.4 %collective-permute-done.40.recv_ref = bf16[4,2,64,512]{3,2,1,0:T(8,128)(2,1)S(1)} collective-permute-done((bf16[4,2,64,512]{3,2,1,0:T(8,128)(2,1)}, bf16[4,2,64,512]{3,2,1,0:T(8,128)(2,1)S(1)}, u32[]{:S(2)}, u32[]{:S(2)}) %collective-permute-start.40) | collective-permute-done | bytes 524320 | tf_op jit(solution)/shard_map/ppermute | solution.py:416
  275.0 3.1 collective-permute-start.39
  278.7 15.5 %rows.2.refs_17_ = bf16[16,2,2,128,512]{4,3,2,1,0:T(8,128)(2,1)} custom-call(s32[1]{0:T(128)} %bitcast.mine, s32[256]{0:T(256)} %reshape.10.slots, bf16[1,512,512]{2,1,0:T(8,128)(2,1)} %get-tuple-element.76.refs_0_.refs_16_, bf16[1,512,512]{2,1,0:T(8,128)(2,1)} %get-tuple-element.77.refs_1_.refs_17_, bf16[1,512,512]{2,1,0:T(8,128)(2,1)} %copy-done.8, ...), custom_call_target="tpu_custom_call" | custom-call | flops 67108864 | bytes 10485760 | tf_op jit(solution)/shard_map/rows/pallas_call | solution.py:275
  294.2 15.2 %rows.3 = bf16[16,2,2,128,512]{4,3,2,1,0:T(8,128)(2,1)} custom-call(s32[1]{0:T(128)} %bitcast.mine, s32[256]{0:T(256)} %reshape.10.slots, bf16[2,512,512]{2,1,0:T(8,128)(2,1)} %get-tuple-element.74.refs_0_.refs_8_, bf16[2,512,512]{2,1,0:T(8,128)(2,1)} %copy-done.1, ...), custom_call_target="tpu_custom_call", output_to_operand_aliasing={{}: (19, {})} | custom-call | flops 67108864 | bytes 10485760 | tf_op jit(solution)/shard_map/rows/pallas_call | solution.py:275
  309.4 2.1 pairsum.5
  312.3 2.1 pairsum.6
  315.3 2.0 pairsum.7
  317.3 3.0 collective-permute-start.43
  321.8 2.9 collective-permute-start.47
  328.0 4.8 %collective-permute-start.50 = (bf16[2,64,512]{2,1,0:T(8,128)(2,1)}, bf16[2,64,512]{2,1,0:T(8,128)(2,1)S(1)}, u32[]{:S(2)}, u32[]{:S(2)}) collective-permute-start(bf16[2,64,512]{2,1,0:T(8,128)(2,1)} %get-tuple-element.108), channel_id=1, source_target_pairs={{0,16},{4,20},{8,24},{12,28},{16,0},{20,4},{24,8},{28,12},{1,17},{... | collective-permute-start | bytes 393224 | tf_op jit(solution)/shard_map/ppermute | solution.py:416
  332.9 5.8 %collective-permute-start.51 = (bf16[2,64,512]{2,1,0:T(8,128)(2,1)}, bf16[2,64,512]{2,1,0:T(8,128)(2,1)S(1)}, u32[]{:S(2)}, u32[]{:S(2)}) collective-permute-start(bf16[2,64,512]{2,1,0:T(8,128)(2,1)} %get-tuple-element.109), channel_id=1, source_target_pairs={{0,24},{4,28},{8,0},{12,4},{16,8},{20,12},{24,16},{28,20},{1,25},{... | collective-permute-start | bytes 393224 | tf_op jit(solution)/shard_map/ppermute | solution.py:416
  338.8 6.9 %collective-permute-done.50 = bf16[2,64,512]{2,1,0:T(8,128)(2,1)S(1)} collective-permute-done((bf16[2,64,512]{2,1,0:T(8,128)(2,1)}, bf16[2,64,512]{2,1,0:T(8,128)(2,1)S(1)}, u32[]{:S(2)}, u32[]{:S(2)}) %collective-permute-start.50) | collective-permute-done | bytes 131104 | tf_op jit(solution)/shard_map/ppermute | solution.py:416
  346.0 1.8 copy.20
  (161 shorter events, 40.7 us)
Async XLA Ops:
  4.8 20.1 %collective-permute-start.9 = (bf16[2,256,512]{2,1,0:T(8,128)(2,1)}, bf16[2,256,512]{2,1,0:T(8,128)(2,1)S(1)}, u32[]{:S(2)}, u32[]{:S(2)}) collective-permute-start(bf16[2,256,512]{2,1,0:T(8,128)(2,1)} %get-tuple-element.63), channel_id=1, source_target_pairs={{0,4},{4,0},{8,12},{12,8},{16,20},{20,16},{24,28},{28,24},{1,5},{5... | collective-permute-start | bytes 1572872 | tf_op jit(solution)/shard_map/ppermute | solution.py:416
  11.9 17.0 %collective-permute-start.10 = (bf16[2,256,512]{2,1,0:T(8,128)(2,1)}, bf16[2,256,512]{2,1,0:T(8,128)(2,1)}, u32[]{:S(2)}, u32[]{:S(2)}) collective-permute-start(bf16[2,256,512]{2,1,0:T(8,128)(2,1)} %get-tuple-element.62.keep), channel_id=1, source_target_pairs={{4,12},{8,0},{12,20},{16,8},{20,28},{24,16},{5,13},{9,1},{13,21},{... | collective-permute-start | bytes 1572872 | tf_op jit(solution)/shard_map/ppermute | solution.py:416
  13.2 20.0 %collective-permute-start.6 = (bf16[2,256,512]{2,1,0:T(8,128)(2,1)}, bf16[2,256,512]{2,1,0:T(8,128)(2,1)}, u32[]{:S(2)}, u32[]{:S(2)}) collective-permute-start(bf16[2,256,512]{2,1,0:T(8,128)(2,1)} %get-tuple-element.61), channel_id=1, source_target_pairs={{0,4},{4,0},{8,12},{12,8},{16,20},{20,16},{24,28},{28,24},{1,5},{5... | collective-permute-start | bytes 1572872 | tf_op jit(solution)/shard_map/ppermute | solution.py:416
  16.7 22.0 %collective-permute-start.7 = (bf16[2,256,512]{2,1,0:T(8,128)(2,1)}, bf16[2,256,512]{2,1,0:T(8,128)(2,1)}, u32[]{:S(2)}, u32[]{:S(2)}) collective-permute-start(bf16[2,256,512]{2,1,0:T(8,128)(2,1)} %get-tuple-element.60.keep), channel_id=1, source_target_pairs={{4,12},{8,0},{12,20},{16,8},{20,28},{24,16},{5,13},{9,1},{13,21},{... | collective-permute-start | bytes 1572872 | tf_op jit(solution)/shard_map/ppermute | solution.py:416
  22.2 22.2 %collective-permute-start.3 = (bf16[2,256,512]{2,1,0:T(8,128)(2,1)}, bf16[2,256,512]{2,1,0:T(8,128)(2,1)S(1)}, u32[]{:S(2)}, u32[]{:S(2)}) collective-permute-start(bf16[2,256,512]{2,1,0:T(8,128)(2,1)} %get-tuple-element.59), channel_id=1, source_target_pairs={{0,4},{4,0},{8,12},{12,8},{16,20},{20,16},{24,28},{28,24},{1,5},{5... | collective-permute-start | bytes 1572872 | tf_op jit(solution)/shard_map/ppermute | solution.py:416
  24.9 28.9 %collective-permute-start = (bf16[2,256,512]{2,1,0:T(8,128)(2,1)}, bf16[2,256,512]{2,1,0:T(8,128)(2,1)}, u32[]{:S(2)}, u32[]{:S(2)}) collective-permute-start(bf16[2,256,512]{2,1,0:T(8,128)(2,1)} %get-tuple-element.57), channel_id=1, source_target_pairs={{0,4},{4,0},{8,12},{12,8},{16,20},{20,16},{24,28},{28,24},{1,5},{5... | collective-permute-start | bytes 1572872 | tf_op jit(solution)/shard_map/ppermute | solution.py:416
  28.9 28.6 %collective-permute-start.11 = (bf16[2,256,512]{2,1,0:T(8,128)(2,1)S(1)}, bf16[2,256,512]{2,1,0:T(8,128)(2,1)}, u32[]{:S(2)}, u32[]{:S(2)}) collective-permute-start(bf16[2,256,512]{2,1,0:T(8,128)(2,1)S(1)} %collective-permute-done.9.recv), channel_id=1, source_target_pairs={{0,8},{8,16},{12,4},{16,24},{20,12},{28,20},{1,9},{9,17},{13,5},{1... | collective-permute-start | bytes 1572872 | tf_op jit(solution)/shard_map/ppermute | solution.py:416
  33.2 25.6 %collective-permute-start.8 = (bf16[2,256,512]{2,1,0:T(8,128)(2,1)}, bf16[2,256,512]{2,1,0:T(8,128)(2,1)}, u32[]{:S(2)}, u32[]{:S(2)}) collective-permute-start(bf16[2,256,512]{2,1,0:T(8,128)(2,1)} %collective-permute-done.6.recv), channel_id=1, source_target_pairs={{0,8},{8,16},{12,4},{16,24},{20,12},{28,20},{1,9},{9,17},{13,5},{1... | collective-permute-start | bytes 1572872 | tf_op jit(solution)/shard_map/ppermute | solution.py:416
  38.7 82.7 %collective-permute-start.33 = (bf16[16,128,512]{2,1,0:T(8,128)(2,1)S(1)}, bf16[16,128,512]{2,1,0:T(8,128)(2,1)}, u32[]{:S(2)}, u32[]{:S(2)}) collective-permute-start(bf16[16,128,512]{2,1,0:T(8,128)(2,1)S(1)} %copy-done), channel_id=1, source_target_pairs={{0,2},{1,3},{2,0},{3,1},{4,6},{5,7},{6,4},{7,5},{8,10},{9,11},{10,... | collective-permute-start | bytes 6291464 | tf_op jit(solution)/shard_map/ppermute | solution.py:422
  44.4 30.0 %collective-permute-start.4 = (bf16[2,256,512]{2,1,0:T(8,128)(2,1)}, bf16[2,256,512]{2,1,0:T(8,128)(2,1)S(1)}, u32[]{:S(2)}, u32[]{:S(2)}) collective-permute-start(bf16[2,256,512]{2,1,0:T(8,128)(2,1)} %get-tuple-element.58.keep), channel_id=1, source_target_pairs={{4,12},{8,0},{12,20},{16,8},{20,28},{24,16},{5,13},{9,1},{13,21},{... | collective-permute-start | bytes 1572872 | tf_op jit(solution)/shard_map/ppermute | solution.py:416
  53.7 20.7 %collective-permute-start.5 = (bf16[2,256,512]{2,1,0:T(8,128)(2,1)S(1)}, bf16[2,256,512]{2,1,0:T(8,128)(2,1)S(1)}, u32[]{:S(2)}, u32[]{:S(2)}) collective-permute-start(bf16[2,256,512]{2,1,0:T(8,128)(2,1)S(1)} %collective-permute-done.3.recv), channel_id=1, source_target_pairs={{0,8},{8,16},{12,4},{16,24},{20,12},{28,20},{1,9},{9,17},{13,5},{1... | collective-permute-start | bytes 1572872 | tf_op jit(solution)/shard_map/ppermute | solution.py:416
  57.5 21.4 %collective-permute-start.1 = (bf16[2,256,512]{2,1,0:T(8,128)(2,1)}, bf16[2,256,512]{2,1,0:T(8,128)(2,1)S(1)}, u32[]{:S(2)}, u32[]{:S(2)}) collective-permute-start(bf16[2,256,512]{2,1,0:T(8,128)(2,1)} %get-tuple-element.56.keep), channel_id=1, source_target_pairs={{4,12},{8,0},{12,20},{16,8},{20,28},{24,16},{5,13},{9,1},{13,21},{... | collective-permute-start | bytes 1572872 | tf_op jit(solution)/shard_map/ppermute | solution.py:416
  58.8 20.3 %collective-permute-start.2 = (bf16[2,256,512]{2,1,0:T(8,128)(2,1)}, bf16[2,256,512]{2,1,0:T(8,128)(2,1)S(1)}, u32[]{:S(2)}, u32[]{:S(2)}) collective-permute-start(bf16[2,256,512]{2,1,0:T(8,128)(2,1)} %collective-permute-done.recv), channel_id=1, source_target_pairs={{0,8},{8,16},{12,4},{16,24},{20,12},{28,20},{1,9},{9,17},{13,5},{1... | collective-permute-start | bytes 1572872 | tf_op jit(solution)/shard_map/ppermute | solution.py:416
  83.5 15.3 %collective-permute-start.20 = (bf16[1,512,512]{2,1,0:T(8,128)(2,1)}, bf16[1,512,512]{2,1,0:T(8,128)(2,1)S(1)}, u32[]{:S(2)}, u32[]{:S(2)}) collective-permute-start(bf16[1,512,512]{2,1,0:T(8,128)(2,1)} %get-tuple-element.79), channel_id=1, source_target_pairs={{0,4},{4,0},{8,12},{12,8},{16,20},{20,16},{24,28},{28,24},{1,5},{5... | collective-permute-start | bytes 1572872 | tf_op jit(solution)/shard_map/ppermute | solution.py:416
  85.9 14.5 %collective-permute-start.22 = (bf16[1,512,512]{2,1,0:T(8,128)(2,1)}, bf16[1,512,512]{2,1,0:T(8,128)(2,1)S(1)}, u32[]{:S(2)}, u32[]{:S(2)}) collective-permute-start(bf16[1,512,512]{2,1,0:T(8,128)(2,1)} %get-tuple-element.77.refs_1_.refs_17_), channel_id=1, source_target_pairs={{0,2},{1,3},{2,0},{3,1},{4,6},{5,7},{6,4},{7,5},{8,10},{9,11},{10,... | collective-permute-start | bytes 1572872 | tf_op jit(solution)/shard_map/ppermute | solution.py:422
  87.3 13.0 %collective-permute-start.26 = (bf16[1,512,512]{2,1,0:T(8,128)(2,1)}, bf16[1,512,512]{2,1,0:T(8,128)(2,1)S(1)}, u32[]{:S(2)}, u32[]{:S(2)}) collective-permute-start(bf16[1,512,512]{2,1,0:T(8,128)(2,1)} %get-tuple-element.77.refs_1_.refs_17_), channel_id=1, source_target_pairs={{0,1},{1,0},{2,3},{3,2},{4,5},{5,4},{6,7},{7,6},{8,9},{9,8},{10,11... | collective-permute-start | bytes 1572872 | tf_op jit(solution)/shard_map/ppermute | solution.py:422
  87.3 20.3 %collective-permute-start.19 = (bf16[1,512,512]{2,1,0:T(8,128)(2,1)S(1)}, bf16[1,512,512]{2,1,0:T(8,128)(2,1)S(1)}, u32[]{:S(2)}, u32[]{:S(2)}) collective-permute-start(bf16[1,512,512]{2,1,0:T(8,128)(2,1)S(1)} %copy-done.26), channel_id=1, source_target_pairs={{0,4},{4,0},{8,12},{12,8},{16,20},{20,16},{24,28},{28,24},{1,5},{5... | collective-permute-start | bytes 1572872 | tf_op jit(solution)/shard_map/ppermute | solution.py:416
  98.8 14.8 %collective-permute-start.21 = (bf16[1,512,512]{2,1,0:T(8,128)(2,1)S(1)}, bf16[1,512,512]{2,1,0:T(8,128)(2,1)S(1)}, u32[]{:S(2)}, u32[]{:S(2)}) collective-permute-start(bf16[1,512,512]{2,1,0:T(8,128)(2,1)S(1)} %copy-done.4), channel_id=1, source_target_pairs={{0,2},{1,3},{2,0},{3,1},{4,6},{5,7},{6,4},{7,5},{8,10},{9,11},{10,... | collective-permute-start | bytes 1572872 | tf_op jit(solution)/shard_map/ppermute | solution.py:422
  100.3 13.3 %collective-permute-start.25 = (bf16[1,512,512]{2,1,0:T(8,128)(2,1)S(1)}, bf16[1,512,512]{2,1,0:T(8,128)(2,1)S(1)}, u32[]{:S(2)}, u32[]{:S(2)}) collective-permute-start(bf16[1,512,512]{2,1,0:T(8,128)(2,1)S(1)} %copy-done.4), channel_id=1, source_target_pairs={{0,1},{1,0},{2,3},{3,2},{4,5},{5,4},{6,7},{7,6},{8,9},{9,8},{10,11... | collective-permute-start | bytes 1572872 | tf_op jit(solution)/shard_map/ppermute | solution.py:422
  100.4 20.1 %collective-permute-start.24 = (bf16[1,512,512]{2,1,0:T(8,128)(2,1)S(1)}, bf16[1,512,512]{2,1,0:T(8,128)(2,1)}, u32[]{:S(2)}, u32[]{:S(2)}) collective-permute-start(bf16[1,512,512]{2,1,0:T(8,128)(2,1)S(1)} %collective-permute-done.20.refs_3_.refs_19_), channel_id=1, source_target_pairs={{0,2},{1,3},{2,0},{3,1},{4,6},{5,7},{6,4},{7,5},{8,10},{9,11},{10,... | collective-permute-start | bytes 1572872 | tf_op jit(solution)/shard_map/ppermute | solution.py:422
  107.6 35.1 %collective-permute-start.34 = (bf16[16,128,512]{2,1,0:T(8,128)(2,1)S(1)}, bf16[16,128,512]{2,1,0:T(8,128)(2,1)S(1)}, u32[]{:S(2)}, u32[]{:S(2)}) collective-permute-start(bf16[16,128,512]{2,1,0:T(8,128)(2,1)S(1)} %copy-done), channel_id=1, source_target_pairs={{0,1},{1,0},{2,3},{3,2},{4,5},{5,4},{6,7},{7,6},{8,9},{9,8},{10,11... | collective-permute-start | bytes 6291464 | tf_op jit(solution)/shard_map/ppermute | solution.py:422
  120.4 20.8 %collective-permute-start.12 = (bf16[2,512,512]{2,1,0:T(8,128)(2,1)}, bf16[2,512,512]{2,1,0:T(8,128)(2,1)S(1)}, u32[]{:S(2)}, u32[]{:S(2)}) collective-permute-start(bf16[2,512,512]{2,1,0:T(8,128)(2,1)} %get-tuple-element.75), channel_id=1, source_target_pairs={{0,4},{4,0},{8,12},{12,8},{16,20},{20,16},{24,28},{28,24},{1,5},{5... | collective-permute-start | bytes 3145736 | tf_op jit(solution)/shard_map/ppermute | solution.py:416
  121.4 61.9 %collective-permute-start.35 = (bf16[16,128,512]{2,1,0:T(8,128)(2,1)}, bf16[16,128,512]{2,1,0:T(8,128)(2,1)}, u32[]{:S(2)}, u32[]{:S(2)}) collective-permute-start(bf16[16,128,512]{2,1,0:T(8,128)(2,1)} %collective-permute-done.33.refs_1_), channel_id=1, source_target_pairs={{0,1},{1,0},{2,3},{3,2},{4,5},{5,4},{6,7},{7,6},{8,9},{9,8},{10,11... | collective-permute-start | bytes 6291464 | tf_op jit(solution)/shard_map/ppermute | solution.py:422
  121.4 14.4 %collective-permute-start.23 = (bf16[1,512,512]{2,1,0:T(8,128)(2,1)S(1)}, bf16[1,512,512]{2,1,0:T(8,128)(2,1)}, u32[]{:S(2)}, u32[]{:S(2)}) collective-permute-start(bf16[1,512,512]{2,1,0:T(8,128)(2,1)S(1)} %collective-permute-done.19.refs_2_.refs_18_), channel_id=1, source_target_pairs={{0,2},{1,3},{2,0},{3,1},{4,6},{5,7},{6,4},{7,5},{8,10},{9,11},{10,... | collective-permute-start | bytes 1572872 | tf_op jit(solution)/shard_map/ppermute | solution.py:422
  123.0 14.4 %collective-permute-start.27 = (bf16[1,512,512]{2,1,0:T(8,128)(2,1)S(1)}, bf16[1,512,512]{2,1,0:T(8,128)(2,1)S(1)}, u32[]{:S(2)}, u32[]{:S(2)}) collective-permute-start(bf16[1,512,512]{2,1,0:T(8,128)(2,1)S(1)} %collective-permute-done.19.refs_2_.refs_18_), channel_id=1, source_target_pairs={{0,1},{1,0},{2,3},{3,2},{4,5},{5,4},{6,7},{7,6},{8,9},{9,8},{10,11... | collective-permute-start | bytes 1572872 | tf_op jit(solution)/shard_map/ppermute | solution.py:422
  135.8 26.3 %collective-permute-start.13 = (bf16[2,512,512]{2,1,0:T(8,128)(2,1)}, bf16[2,512,512]{2,1,0:T(8,128)(2,1)}, u32[]{:S(2)}, u32[]{:S(2)}) collective-permute-start(bf16[2,512,512]{2,1,0:T(8,128)(2,1)} %get-tuple-element.74.refs_0_.refs_8_), channel_id=1, source_target_pairs={{0,2},{1,3},{2,0},{3,1},{4,6},{5,7},{6,4},{7,5},{8,10},{9,11},{10,... | collective-permute-start | bytes 3145736 | tf_op jit(solution)/shard_map/ppermute | solution.py:422
  141.2 42.0 %collective-permute-start.14 = (bf16[2,512,512]{2,1,0:T(8,128)(2,1)S(1)}, bf16[2,512,512]{2,1,0:T(8,128)(2,1)}, u32[]{:S(2)}, u32[]{:S(2)}) collective-permute-start(bf16[2,512,512]{2,1,0:T(8,128)(2,1)S(1)} %collective-permute-done.12.refs_1_.refs_9_), channel_id=1, source_target_pairs={{0,2},{1,3},{2,0},{3,1},{4,6},{5,7},{6,4},{7,5},{8,10},{9,11},{10,... | collective-permute-start | bytes 3145736 | tf_op jit(solution)/shard_map/ppermute | solution.py:422
  142.7 19.5 %collective-permute-start.32 = (bf16[1,512,512]{2,1,0:T(8,128)(2,1)}, bf16[1,512,512]{2,1,0:T(8,128)(2,1)}, u32[]{:S(2)}, u32[]{:S(2)}) collective-permute-start(bf16[1,512,512]{2,1,0:T(8,128)(2,1)} %collective-permute-done.24.refs_7_.refs_23_), channel_id=1, source_target_pairs={{0,1},{1,0},{2,3},{3,2},{4,5},{5,4},{6,7},{7,6},{8,9},{9,8},{10,11... | collective-permute-start | bytes 1572872 | tf_op jit(solution)/shard_map/ppermute | solution.py:422
  144.9 51.8 %collective-permute-start.31 = (bf16[1,512,512]{2,1,0:T(8,128)(2,1)}, bf16[1,512,512]{2,1,0:T(8,128)(2,1)}, u32[]{:S(2)}, u32[]{:S(2)}) collective-permute-start(bf16[1,512,512]{2,1,0:T(8,128)(2,1)} %collective-permute-done.23.refs_6_.refs_22_), channel_id=1, source_target_pairs={{0,1},{1,0},{2,3},{3,2},{4,5},{5,4},{6,7},{7,6},{8,9},{9,8},{10,11... | collective-permute-start | bytes 1572872 | tf_op jit(solution)/shard_map/ppermute | solution.py:422
  162.2 62.5 %collective-permute-start.15 = (bf16[2,512,512]{2,1,0:T(8,128)(2,1)}, bf16[2,512,512]{2,1,0:T(8,128)(2,1)S(1)}, u32[]{:S(2)}, u32[]{:S(2)}) collective-permute-start(bf16[2,512,512]{2,1,0:T(8,128)(2,1)} %get-tuple-element.74.refs_0_.refs_8_), channel_id=1, source_target_pairs={{0,1},{1,0},{2,3},{3,2},{4,5},{5,4},{6,7},{7,6},{8,9},{9,8},{10,11... | collective-permute-start | bytes 3145736 | tf_op jit(solution)/shard_map/ppermute | solution.py:422
  162.2 62.5 %collective-permute-start.16 = (bf16[2,512,512]{2,1,0:T(8,128)(2,1)S(1)}, bf16[2,512,512]{2,1,0:T(8,128)(2,1)S(1)}, u32[]{:S(2)}, u32[]{:S(2)}) collective-permute-start(bf16[2,512,512]{2,1,0:T(8,128)(2,1)S(1)} %collective-permute-done.12.refs_1_.refs_9_), channel_id=1, source_target_pairs={{0,1},{1,0},{2,3},{3,2},{4,5},{5,4},{6,7},{7,6},{8,9},{9,8},{10,11... | collective-permute-start | bytes 3145736 | tf_op jit(solution)/shard_map/ppermute | solution.py:422
  183.3 41.5 %collective-permute-start.17 = (bf16[2,512,512]{2,1,0:T(8,128)(2,1)}, bf16[2,512,512]{2,1,0:T(8,128)(2,1)}, u32[]{:S(2)}, u32[]{:S(2)}) collective-permute-start(bf16[2,512,512]{2,1,0:T(8,128)(2,1)} %collective-permute-done.13.refs_2_.refs_10_), channel_id=1, source_target_pairs={{0,1},{1,0},{2,3},{3,2},{4,5},{5,4},{6,7},{7,6},{8,9},{9,8},{10,11... | collective-permute-start | bytes 3145736 | tf_op jit(solution)/shard_map/ppermute | solution.py:422
  183.3 41.5 %collective-permute-start.18 = (bf16[2,512,512]{2,1,0:T(8,128)(2,1)}, bf16[2,512,512]{2,1,0:T(8,128)(2,1)}, u32[]{:S(2)}, u32[]{:S(2)}) collective-permute-start(bf16[2,512,512]{2,1,0:T(8,128)(2,1)} %collective-permute-done.14.refs_3_.refs_11_), channel_id=1, source_target_pairs={{0,1},{1,0},{2,3},{3,2},{4,5},{5,4},{6,7},{7,6},{8,9},{9,8},{10,11... | collective-permute-start | bytes 3145736 | tf_op jit(solution)/shard_map/ppermute | solution.py:422
  247.1 15.9 %collective-permute-start.36 = (bf16[4,2,64,512]{3,2,1,0:T(8,128)(2,1)}, bf16[4,2,64,512]{3,2,1,0:T(8,128)(2,1)S(1)}, u32[]{:S(2)}, u32[]{:S(2)}) collective-permute-start(bf16[4,2,64,512]{3,2,1,0:T(8,128)(2,1)} %get-tuple-element.87), channel_id=1, source_target_pairs={{0,4},{4,0},{8,12},{12,8},{16,20},{20,16},{24,28},{28,24},{1,5},{5... | collective-permute-start | bytes 1572872 | tf_op jit(solution)/shard_map/ppermute | solution.py:416
  259.9 15.0 %collective-permute-start.40 = (bf16[4,2,64,512]{3,2,1,0:T(8,128)(2,1)}, bf16[4,2,64,512]{3,2,1,0:T(8,128)(2,1)S(1)}, u32[]{:S(2)}, u32[]{:S(2)}) collective-permute-start(bf16[4,2,64,512]{3,2,1,0:T(8,128)(2,1)} %get-tuple-element.93), channel_id=1, source_target_pairs={{0,4},{4,0},{8,12},{12,8},{16,20},{20,16},{24,28},{28,24},{1,5},{5... | collective-permute-start | bytes 1572872 | tf_op jit(solution)/shard_map/ppermute | solution.py:416
  260.9 50.6 %collective-permute-start.44 = (bf16[4,2,64,512]{3,2,1,0:T(8,128)(2,1)}, bf16[4,2,64,512]{3,2,1,0:T(8,128)(2,1)S(1)}, u32[]{:S(2)}, u32[]{:S(2)}) collective-permute-start(bf16[4,2,64,512]{3,2,1,0:T(8,128)(2,1)} %get-tuple-element.99), channel_id=1, source_target_pairs={{0,4},{4,0},{8,12},{12,8},{16,20},{20,16},{24,28},{28,24},{1,5},{5... | collective-permute-start | bytes 1572872 | tf_op jit(solution)/shard_map/ppermute | solution.py:416
  262.0 52.4 %collective-permute-start.48 = (bf16[4,2,64,512]{3,2,1,0:T(8,128)(2,1)}, bf16[4,2,64,512]{3,2,1,0:T(8,128)(2,1)S(1)}, u32[]{:S(2)}, u32[]{:S(2)}) collective-permute-start(bf16[4,2,64,512]{3,2,1,0:T(8,128)(2,1)} %get-tuple-element.105), channel_id=1, source_target_pairs={{0,4},{4,0},{8,12},{12,8},{16,20},{20,16},{24,28},{28,24},{1,5},{5... | collective-permute-start | bytes 1572872 | tf_op jit(solution)/shard_map/ppermute | solution.py:416
  265.8 51.5 %collective-permute-start.37 = (bf16[2,64,512]{2,1,0:T(8,128)(2,1)}, bf16[2,64,512]{2,1,0:T(8,128)(2,1)S(1)}, u32[]{:S(2)}, u32[]{:S(2)}) collective-permute-start(bf16[2,64,512]{2,1,0:T(8,128)(2,1)} %get-tuple-element.89), channel_id=1, source_target_pairs={{0,8},{4,12},{8,16},{12,20},{16,24},{20,28},{24,0},{28,4},{1,9},{5... | collective-permute-start | bytes 393224 | tf_op jit(solution)/shard_map/ppermute | solution.py:416
  267.4 52.9 %collective-permute-start.38 = (bf16[2,64,512]{2,1,0:T(8,128)(2,1)}, bf16[2,64,512]{2,1,0:T(8,128)(2,1)S(1)}, u32[]{:S(2)}, u32[]{:S(2)}) collective-permute-start(bf16[2,64,512]{2,1,0:T(8,128)(2,1)} %get-tuple-element.90), channel_id=1, source_target_pairs={{0,16},{4,20},{8,24},{12,28},{16,0},{20,4},{24,8},{28,12},{1,17},{... | collective-permute-start | bytes 393224 | tf_op jit(solution)/shard_map/ppermute | solution.py:416
  275.0 45.4 %collective-permute-start.39 = (bf16[2,64,512]{2,1,0:T(8,128)(2,1)}, bf16[2,64,512]{2,1,0:T(8,128)(2,1)S(1)}, u32[]{:S(2)}, u32[]{:S(2)}) collective-permute-start(bf16[2,64,512]{2,1,0:T(8,128)(2,1)} %get-tuple-element.91), channel_id=1, source_target_pairs={{0,24},{4,28},{8,0},{12,4},{16,8},{20,12},{24,16},{28,20},{1,25},{... | collective-permute-start | bytes 393224 | tf_op jit(solution)/shard_map/ppermute | solution.py:416
  314.3 12.0 %collective-permute-start.42 = (bf16[2,64,512]{2,1,0:T(8,128)(2,1)}, bf16[2,64,512]{2,1,0:T(8,128)(2,1)S(1)}, u32[]{:S(2)}, u32[]{:S(2)}) collective-permute-start(bf16[2,64,512]{2,1,0:T(8,128)(2,1)} %get-tuple-element.96), channel_id=1, source_target_pairs={{0,16},{4,20},{8,24},{12,28},{16,0},{20,4},{24,8},{28,12},{1,17},{... | collective-permute-start | bytes 393224 | tf_op jit(solution)/shard_map/ppermute | solution.py:416
  317.3 10.7 %collective-permute-start.43 = (bf16[2,64,512]{2,1,0:T(8,128)(2,1)S(1)}, bf16[2,64,512]{2,1,0:T(8,128)(2,1)S(1)}, u32[]{:S(2)}, u32[]{:S(2)}) collective-permute-start(bf16[2,64,512]{2,1,0:T(8,128)(2,1)S(1)} %copy-done.35), channel_id=1, source_target_pairs={{0,24},{4,28},{8,0},{12,4},{16,8},{20,12},{24,16},{28,20},{1,25},{... | collective-permute-start | bytes 393224 | tf_op jit(solution)/shard_map/ppermute | solution.py:416
  320.3 12.5 %collective-permute-start.45 = (bf16[2,64,512]{2,1,0:T(8,128)(2,1)}, bf16[2,64,512]{2,1,0:T(8,128)(2,1)S(1)}, u32[]{:S(2)}, u32[]{:S(2)}) collective-permute-start(bf16[2,64,512]{2,1,0:T(8,128)(2,1)} %get-tuple-element.101), channel_id=1, source_target_pairs={{0,8},{4,12},{8,16},{12,20},{16,24},{20,28},{24,0},{28,4},{1,9},{5... | collective-permute-start | bytes 393224 | tf_op jit(solution)/shard_map/ppermute | solution.py:416
  320.3 18.4 %collective-permute-start.46 = (bf16[2,64,512]{2,1,0:T(8,128)(2,1)}, bf16[2,64,512]{2,1,0:T(8,128)(2,1)S(1)}, u32[]{:S(2)}, u32[]{:S(2)}) collective-permute-start(bf16[2,64,512]{2,1,0:T(8,128)(2,1)} %get-tuple-element.102), channel_id=1, source_target_pairs={{0,16},{4,20},{8,24},{12,28},{16,0},{20,4},{24,8},{28,12},{1,17},{... | collective-permute-start | bytes 393224 | tf_op jit(solution)/shard_map/ppermute | solution.py:416
  321.8 16.9 %collective-permute-start.47 = (bf16[2,64,512]{2,1,0:T(8,128)(2,1)}, bf16[2,64,512]{2,1,0:T(8,128)(2,1)S(1)}, u32[]{:S(2)}, u32[]{:S(2)}) collective-permute-start(bf16[2,64,512]{2,1,0:T(8,128)(2,1)} %get-tuple-element.103), channel_id=1, source_target_pairs={{0,24},{4,28},{8,0},{12,4},{16,8},{20,12},{24,16},{28,20},{1,25},{... | collective-permute-start | bytes 393224 | tf_op jit(solution)/shard_map/ppermute | solution.py:416
  326.3 12.5 %collective-permute-start.49 = (bf16[2,64,512]{2,1,0:T(8,128)(2,1)}, bf16[2,64,512]{2,1,0:T(8,128)(2,1)S(1)}, u32[]{:S(2)}, u32[]{:S(2)}) collective-permute-start(bf16[2,64,512]{2,1,0:T(8,128)(2,1)} %get-tuple-element.107), channel_id=1, source_target_pairs={{0,8},{4,12},{8,16},{12,20},{16,24},{20,28},{24,0},{28,4},{1,9},{5... | collective-permute-start | bytes 393224 | tf_op jit(solution)/shard_map/ppermute | solution.py:416
  328.0 17.7 %collective-permute-start.50 = (bf16[2,64,512]{2,1,0:T(8,128)(2,1)}, bf16[2,64,512]{2,1,0:T(8,128)(2,1)S(1)}, u32[]{:S(2)}, u32[]{:S(2)}) collective-permute-start(bf16[2,64,512]{2,1,0:T(8,128)(2,1)} %get-tuple-element.108), channel_id=1, source_target_pairs={{0,16},{4,20},{8,24},{12,28},{16,0},{20,4},{24,8},{28,12},{1,17},{... | collective-permute-start | bytes 393224 | tf_op jit(solution)/shard_map/ppermute | solution.py:416
  332.9 12.9 %collective-permute-start.51 = (bf16[2,64,512]{2,1,0:T(8,128)(2,1)}, bf16[2,64,512]{2,1,0:T(8,128)(2,1)S(1)}, u32[]{:S(2)}, u32[]{:S(2)}) collective-permute-start(bf16[2,64,512]{2,1,0:T(8,128)(2,1)} %get-tuple-element.109), channel_id=1, source_target_pairs={{0,24},{4,28},{8,0},{12,4},{16,8},{20,12},{24,16},{28,20},{1,25},{... | collective-permute-start | bytes 393224 | tf_op jit(solution)/shard_map/ppermute | solution.py:416
  (40 other events, 749.7 us)

commit v5 on v4

--- a/solution.py
+++ b/solution.py
@@ -202,11 +202,11 @@
 def home_blocks(slots, pieces, full, turned, lk):
     each, n, _ = pieces[0].shape
     count = each * len(pieces)
-    rows = n // 8
+    rows = n // 4
     block = lambda lead: pl.BlockSpec((lead, rows, n), lambda g, s: (0, g, 0))
     return pl.pallas_call(
         functools.partial(home_kernel, lk, len(pieces)),
-        out_shape=[pltpu.HBM((lk, n, n), BF16)] * 2,
+        out_shape=[pltpu.VMEM((lk, n, n), BF16)] * 2,
         grid_spec=pltpu.PrefetchScalarGridSpec(
             num_scalar_prefetch=1,
             grid=(n // rows,),
@@ -214,7 +214,7 @@
             out_specs=[block(lk), block(lk)],
             scratch_shapes=[pltpu.VMEM((count, rows, n), BF16)],
         ),
-        compiler_params=params(56),
+        compiler_params=params(44),
         cost_estimate=cost(4 * lk * count * n * n, n * n * (6 * count + 4 * lk)),
         name="home",
     )(slots, *pieces, full, turned)
@@ -222,7 +222,7 @@
 
 def rows_kernel(pieces, mine, slots, *refs):
     a_refs, b_refs, refs = refs[:pieces], refs[pieces:2 * pieces], refs[2 * pieces:]
-    c_ref, out_ref, re_ref, im_ref = (refs[0],) + refs[-3:]
+    c_ref, out_ref, d_ref = (refs[0],) + refs[-2:]
     each, rows, cols = a_refs[0].shape
     count = pieces * each
     row, col = row_col(rows, cols)
@@ -230,9 +230,9 @@
     for s in range(pieces):
         for j in range(each):
             a, b = a_refs[s][j].astype(F32), b_refs[s][j].astype(F32).T
-            re_ref[s * each + j] = jnp.where(above >= 0, a, b).astype(BF16)
-            im_ref[s * each + j] = jnp.where(above < 0, a, jnp.where(above > 0, -b, 0.0)).astype(BF16)
-    tr, kg, tc = 16, 4, 256
+            d_ref[s * each + j, 0] = jnp.where(above >= 0, a, b).astype(BF16)
+            d_ref[s * each + j, 1] = jnp.where(above < 0, a, jnp.where(above > 0, -b, 0.0)).astype(BF16)
+    tr, kg, tc = 32, 2, 256
     wide = cols // tc
 
     def tile(index, _):
@@ -246,8 +246,8 @@
                 c = [c_ref[p + i, r, m] for i in range(2)]
                 for k in range(kg):
                     slot = [slots[(k0 + k) * count + p + i] for i in range(2)]
-                    u = c[0] * re_ref[slot[0], r, m] + c[1] * re_ref[slot[1], r, m]
-                    v = c[0] * im_ref[slot[0], r, m] + c[1] * im_ref[slot[1], r, m]
+                    u = c[0] * d_ref[slot[0], 0, r, m] + c[1] * d_ref[slot[1], 0, r, m]
+                    v = c[0] * d_ref[slot[0], 1, r, m] + c[1] * d_ref[slot[1], 1, r, m]
                     pu[k] = u if p == q else pu[k] + u
                     pv[k] = v if p == q else pv[k] + v
             for k in range(kg):
@@ -280,7 +280,7 @@
             grid=(n // cols,),
             in_specs=in_specs,
             out_specs=pl.BlockSpec((count, 1, 2, rows, cols), lambda t, mine, slots: (0, energy, 0, 0, t)),
-            scratch_shapes=[pltpu.VMEM((count, rows, cols), BF16)] * 2,
+            scratch_shapes=[pltpu.VMEM((count, 2, rows, cols), BF16)],
         ),
         input_output_aliases={2 + len(in_specs) - 1: 0} if alias else {},
         compiler_params=params(56),
@@ -325,7 +325,7 @@
             one,
         ] + [pair] * len(alias),
         out_specs=pair,
-        compiler_params=params(56),
+        compiler_params=params(44),
         cost_estimate=cost(16 * lk * n**3, lk * n * n * 20),
         name="density",
     )(green, broadening, x, y, *alias)
@@ -370,7 +370,7 @@
             out_specs=[out] * (2 * count),
             scratch_shapes=[pltpu.VMEM((2, n, n), F32)],
         ),
-        compiler_params=params(56),
+        compiler_params=params(44),
         cost_estimate=cost(count * 16 * n**3, count * n * n * 20),
         name="density",
     )(odd[None], green, broadening, x, y, held)
@@ -391,7 +391,7 @@
         out_shape=[jax.ShapeDtypeStruct(keep.shape[1:], BF16)] * groups,
         in_specs=[pl.BlockSpec(memory_space=pltpu.SMEM), vmem, vmem],
         out_specs=[vmem] * groups,
-        compiler_params=params(56),
+        compiler_params=params(16),
         cost_estimate=cost(keep.size, keep.size * 6),
         name="pairsum",
     )(group[None], keep, recv)

time: 349 us -> 331 us (0.948)
  Pallas kernels: 142 us -> 124 us
    pallas_call x4, Pallas kernels: 8.28 us -> 2.12 us  [pair_sum(): pl.pallas_call(pair_sum_kernel, out_shape=[jax.ShapeDtypeStruct(keep.shap...]
    pallas_call x2, Pallas kernels: 30.2 us -> 24.5 us  [home_blocks(): pl.pallas_call(functools.partial(home_kernel, lk, len(pieces)), out_shape...]
    pallas_call x2, Pallas kernels: 30.7 us -> 25.7 us  [own_rows(): pl.pallas_call(functools.partial(rows_kernel, len(pieces)), out_shape=jax...]
    ppermute x31, waiting for transfers between devices: 50 us -> 53.5 us  [permuted(): return lax.ppermute(x, 'energy', perm)]
    unnamed x73 -> x67, local copies, waits for them, and re-layouts: 8.57 us -> 6.75 us
  transfers between devices with their start and end apart: 52 -> 52, of which waited for: 16 -> 17; matrix products, arithmetic and copies ran while one was open for 2% -> 2% of each run, Pallas kernels for 34% -> 31%
where the time goes in v5:
time: 331 us; the launch traced here: 330 us
  Pallas kernels  124 us (37%)
  waiting for transfers between devices  116 us (35%)
  starting transfers between devices  75.8 us (23%)
  local copies, waits for them, and re-layouts  7.51 us (2%)
  other arithmetic  5.92 us (2%)
    ppermute x31, starting transfers between devices, permuted(): return lax.ppermute(x, 'energy', perm)  64.4 us
    ppermute x21, waiting for transfers between devices, swap(): moved = lax.ppermute(x, 'mom', [(i, i ^ stride) for i in range(nm)])  62.7 us
    ppermute x31, waiting for transfers between devices, permuted(): return lax.ppermute(x, 'energy', perm)  53.5 us
    pallas_call x2, Pallas kernels, own_rows(): pl.pallas_call(functools.partial(rows_kernel, len(pieces)), out_shape=jax...  25.7 us
    pallas_call x2, Pallas kernels, home_blocks(): pl.pallas_call(functools.partial(home_kernel, lk, len(pieces)), out_shape...  24.5 us
    pallas_call x4, Pallas kernels, lesser_packed(): pl.pallas_call(lesser_kernel, out_shape=[pltpu.HBM((le, n // 2, n), BF16)...  16.5 us
    pallas_call x2, Pallas kernels, last_density(): pl.pallas_call(functools.partial(last_density_kernel, scale, energy), out...  16.3 us
    pallas_call x4, Pallas kernels, sources(): pl.pallas_call(source_kernel, out_shape=[pltpu.HBM(shape, BF16) for shape...  14.1 us
  transfers between devices with their start and end apart: 52, of which 17 were waited for; matrix products, arithmetic and copies ran while one was open for 2% of the time, Pallas kernels for 31%

profile of v5, /device:TPU:0, one launch (start us, length us, event | category | flops | bytes accessed | tf_op | source)
XLA Modules:
  0.0 330.4 jit_solution(9747274883144610836)
XLA Ops:
  0.6 4.1 %lesser.7 = (bf16[2,256,512]{2,1,0:T(8,128)(2,1)}, bf16[2,256,512]{2,1,0:T(8,128)(2,1)}) custom-call(s32[1]{0:T(128)} %bitcast.9.sel, bf16[4,2,2,512,512]{4,3,2,1,0:T(8,128)(2,1)} %g_ref.13, f32[4,2,512]{2,1,0:T(2,128)} %gamma_ref.13), custom_call_target="tpu_custom_call" | custom-call | flops 1610612736 | bytes 3145728 | tf_op jit(solution)/shard_map/lesser/pallas_call | solution.py:66
  4.8 3.0 collective-permute-start.9
  7.8 4.1 %lesser.6 = (bf16[2,256,512]{2,1,0:T(8,128)(2,1)}, bf16[2,256,512]{2,1,0:T(8,128)(2,1)}) custom-call(s32[1]{0:T(128)} %bitcast.8.sel, bf16[4,2,2,512,512]{4,3,2,1,0:T(8,128)(2,1)} %g_ref.13, f32[4,2,512]{2,1,0:T(2,128)} %gamma_ref.13), custom_call_target="tpu_custom_call" | custom-call | flops 1610612736 | bytes 3145728 | tf_op jit(solution)/shard_map/lesser/pallas_call | solution.py:66
  13.1 2.8 collective-permute-start.6
  17.2 4.1 %lesser.5 = (bf16[2,256,512]{2,1,0:T(8,128)(2,1)}, bf16[2,256,512]{2,1,0:T(8,128)(2,1)}) custom-call(s32[1]{0:T(128)} %bitcast.7.sel, bf16[4,2,2,512,512]{4,3,2,1,0:T(8,128)(2,1)} %g_ref.13, f32[4,2,512]{2,1,0:T(2,128)} %gamma_ref.13), custom_call_target="tpu_custom_call" | custom-call | flops 1610612736 | bytes 3145728 | tf_op jit(solution)/shard_map/lesser/pallas_call | solution.py:66
  21.3 3.3 %collective-permute-start.3 = (bf16[2,256,512]{2,1,0:T(8,128)(2,1)}, bf16[2,256,512]{2,1,0:T(8,128)(2,1)S(1)}, u32[]{:S(2)}, u32[]{:S(2)}) collective-permute-start(bf16[2,256,512]{2,1,0:T(8,128)(2,1)} %get-tuple-element.59), channel_id=1, source_target_pairs={{0,4},{4,0},{8,12},{12,8},{16,20},{20,16},{24,28},{28,24},{1,5},{5... | collective-permute-start | bytes 1572872 | tf_op jit(solution)/shard_map/ppermute | solution.py:416
  24.8 4.0 %collective-permute-done.10.kz = bf16[2,256,512]{2,1,0:T(8,128)(2,1)S(1)} collective-permute-done((bf16[2,256,512]{2,1,0:T(8,128)(2,1)}, bf16[2,256,512]{2,1,0:T(8,128)(2,1)S(1)}, u32[]{:S(2)}, u32[]{:S(2)}) %collective-permute-start.10) | collective-permute-done | bytes 524320 | tf_op jit(solution)/shard_map/ppermute | solution.py:416
  28.7 3.5 %collective-permute-start.11 = (bf16[2,256,512]{2,1,0:T(8,128)(2,1)S(1)}, bf16[2,256,512]{2,1,0:T(8,128)(2,1)S(1)}, u32[]{:S(2)}, u32[]{:S(2)}) collective-permute-start(bf16[2,256,512]{2,1,0:T(8,128)(2,1)S(1)} %collective-permute-done.9.recv), channel_id=1, source_target_pairs={{0,8},{8,16},{12,4},{16,24},{20,12},{28,20},{1,9},{9,17},{13,5},{1... | collective-permute-start | bytes 1572872 | tf_op jit(solution)/shard_map/ppermute | solution.py:416
  32.3 4.5 %collective-permute-start.8 = (bf16[2,256,512]{2,1,0:T(8,128)(2,1)S(1)}, bf16[2,256,512]{2,1,0:T(8,128)(2,1)}, u32[]{:S(2)}, u32[]{:S(2)}) collective-permute-start(bf16[2,256,512]{2,1,0:T(8,128)(2,1)S(1)} %collective-permute-done.6.recv), channel_id=1, source_target_pairs={{0,8},{8,16},{12,4},{16,24},{20,12},{28,20},{1,9},{9,17},{13,5},{1... | collective-permute-start | bytes 1572872 | tf_op jit(solution)/shard_map/ppermute | solution.py:416
  36.8 1.9 collective-permute-done.7.kz
  40.2 4.2 %lesser.4 = (bf16[2,256,512]{2,1,0:T(8,128)(2,1)}, bf16[2,256,512]{2,1,0:T(8,128)(2,1)}) custom-call(s32[1]{0:T(128)} %bitcast.6.sel, bf16[4,2,2,512,512]{4,3,2,1,0:T(8,128)(2,1)} %g_ref.13, f32[4,2,512]{2,1,0:T(2,128)} %gamma_ref.13), custom_call_target="tpu_custom_call" | custom-call | flops 1610612736 | bytes 3145728 | tf_op jit(solution)/shard_map/lesser/pallas_call | solution.py:66
  45.7 7.9 %collective-permute-done.recv = bf16[2,256,512]{2,1,0:T(8,128)(2,1)S(1)} collective-permute-done((bf16[2,256,512]{2,1,0:T(8,128)(2,1)}, bf16[2,256,512]{2,1,0:T(8,128)(2,1)S(1)}, u32[]{:S(2)}, u32[]{:S(2)}) %collective-permute-start) | collective-permute-done | bytes 524320 | tf_op jit(solution)/shard_map/ppermute | solution.py:416
  53.6 3.7 %collective-permute-start.5 = (bf16[2,256,512]{2,1,0:T(8,128)(2,1)S(1)}, bf16[2,256,512]{2,1,0:T(8,128)(2,1)S(1)}, u32[]{:S(2)}, u32[]{:S(2)}) collective-permute-start(bf16[2,256,512]{2,1,0:T(8,128)(2,1)S(1)} %collective-permute-done.3.recv), channel_id=1, source_target_pairs={{0,8},{8,16},{12,4},{16,24},{20,12},{28,20},{1,9},{9,17},{13,5},{1... | collective-permute-start | bytes 1572872 | tf_op jit(solution)/shard_map/ppermute | solution.py:416
  58.7 4.8 %collective-permute-start.2 = (bf16[2,256,512]{2,1,0:T(8,128)(2,1)S(1)}, bf16[2,256,512]{2,1,0:T(8,128)(2,1)S(1)}, u32[]{:S(2)}, u32[]{:S(2)}) collective-permute-start(bf16[2,256,512]{2,1,0:T(8,128)(2,1)S(1)} %collective-permute-done.recv), channel_id=1, source_target_pairs={{0,8},{8,16},{12,4},{16,24},{20,12},{28,20},{1,9},{9,17},{13,5},{1... | collective-permute-start | bytes 1572872 | tf_op jit(solution)/shard_map/ppermute | solution.py:416
  64.1 3.2 pad_maximum_fusion.w_ref
  67.3 3.5 %source.4 = (bf16[1,512,512]{2,1,0:T(8,128)(2,1)}, bf16[2,512,512]{2,1,0:T(8,128)(2,1)}, bf16[1,512,512]{2,1,0:T(8,128)(2,1)}, bf16[2,512,512]{2,1,0:T(8,128)(2,1)}) custom-call(s32[1]{0:T(128)} %bitcast.1.odd, f32[4]{0:T(128)} %pad_maximum_fusion.w_ref, bf16[2,256,512]{2,1,0:T(8,128)(2,1)} %get-tuple-element.62.keep, bf16[2,256,512]{2,1,0:T(8,128)(2,1)} %copy-done.21, ...), custom_call_target="tpu_custom_call" | custom-call | flops 4194304 | bytes 3145728 | tf_op jit(solution)/shard_map/source/pallas_call | solution.py:153
  70.8 3.5 %source.5 = (bf16[1,512,512]{2,1,0:T(8,128)(2,1)}, bf16[2,512,512]{2,1,0:T(8,128)(2,1)}, bf16[1,512,512]{2,1,0:T(8,128)(2,1)}, bf16[2,512,512]{2,1,0:T(8,128)(2,1)}) custom-call(s32[1]{0:T(128)} %bitcast.1.odd, f32[4]{0:T(128)} %pad_maximum_fusion.w_ref, ...), custom_call_target="tpu_custom_call", output_to_operand_aliasing={{0}: (6, {}), {1}: (7, {}), {2}: (8, {}), {3}: (9, {})} | custom-call | flops 4194304 | bytes 3145728 | tf_op jit(solution)/shard_map/source/pallas_call | solution.py:153
  75.3 3.5 %source.6 = (bf16[1,512,512]{2,1,0:T(8,128)(2,1)}, bf16[2,512,512]{2,1,0:T(8,128)(2,1)}, bf16[1,512,512]{2,1,0:T(8,128)(2,1)}, bf16[2,512,512]{2,1,0:T(8,128)(2,1)}) custom-call(s32[1]{0:T(128)} %bitcast.1.odd, f32[4]{0:T(128)} %pad_maximum_fusion.w_ref, bf16[2,256,512]{2,1,0:T(8,128)(2,1)} %get-tuple-element.58.keep, ...), custom_call_target="tpu_custom_call", output_to_operand_aliasing={{1}: (6, {}), {3}: (7, {})} | custom-call | flops 4194304 | bytes 3145728 | tf_op jit(solution)/shard_map/source/pallas_call | solution.py:153
  79.8 3.6 %source.7 = (bf16[1,512,512]{2,1,0:T(8,128)(2,1)}, bf16[2,512,512]{2,1,0:T(8,128)(2,1)}, bf16[1,512,512]{2,1,0:T(8,128)(2,1)}, bf16[2,512,512]{2,1,0:T(8,128)(2,1)}) custom-call(s32[1]{0:T(128)} %bitcast.1.odd, f32[4]{0:T(128)} %pad_maximum_fusion.w_ref, ...), custom_call_target="tpu_custom_call", output_to_operand_aliasing={{0}: (6, {}), {1}: (7, {}), {2}: (8, {}), {3}: (9, {})} | custom-call | flops 4194304 | bytes 3145728 | tf_op jit(solution)/shard_map/source/pallas_call | solution.py:153
  83.5 2.3 collective-permute-start.20
  87.4 11.4 %collective-permute-done.20.refs_3_.refs_19_ = bf16[1,512,512]{2,1,0:T(8,128)(2,1)S(1)} collective-permute-done((bf16[1,512,512]{2,1,0:T(8,128)(2,1)}, bf16[1,512,512]{2,1,0:T(8,128)(2,1)S(1)}, u32[]{:S(2)}, u32[]{:S(2)}) %collective-permute-start.20) | collective-permute-done | bytes 524320 | tf_op jit(solution)/shard_map/ppermute | solution.py:416
  100.9 6.8 %collective-permute-done.19.refs_2_.refs_18_ = bf16[1,512,512]{2,1,0:T(8,128)(2,1)S(1)} collective-permute-done((bf16[1,512,512]{2,1,0:T(8,128)(2,1)S(1)}, bf16[1,512,512]{2,1,0:T(8,128)(2,1)S(1)}, u32[]{:S(2)}, u32[]{:S(2)}) %collective-permute-start.19) | collective-permute-done | bytes 524320 | tf_op jit(solution)/shard_map/ppermute | solution.py:416
  107.7 5.9 %collective-permute-done.21.refs_4_.refs_20_ = bf16[1,512,512]{2,1,0:T(8,128)(2,1)S(1)} collective-permute-done((bf16[1,512,512]{2,1,0:T(8,128)(2,1)S(1)}, bf16[1,512,512]{2,1,0:T(8,128)(2,1)S(1)}, u32[]{:S(2)}, u32[]{:S(2)}) %collective-permute-start.21) | collective-permute-done | bytes 524320 | tf_op jit(solution)/shard_map/ppermute | solution.py:422
  114.1 6.4 %collective-permute-done.24.refs_7_.refs_23_ = bf16[1,512,512]{2,1,0:T(8,128)(2,1)} collective-permute-done((bf16[1,512,512]{2,1,0:T(8,128)(2,1)S(1)}, bf16[1,512,512]{2,1,0:T(8,128)(2,1)}, u32[]{:S(2)}, u32[]{:S(2)}) %collective-permute-start.24) | collective-permute-done | bytes 524320 | tf_op jit(solution)/shard_map/ppermute | solution.py:422
  123.1 12.7 %collective-permute-done.23.refs_6_.refs_22_ = bf16[1,512,512]{2,1,0:T(8,128)(2,1)} collective-permute-done((bf16[1,512,512]{2,1,0:T(8,128)(2,1)S(1)}, bf16[1,512,512]{2,1,0:T(8,128)(2,1)}, u32[]{:S(2)}, u32[]{:S(2)}) %collective-permute-start.23) | collective-permute-done | bytes 524320 | tf_op jit(solution)/shard_map/ppermute | solution.py:422
  137.3 4.1 %collective-permute-done.12.refs_1_.refs_9_ = bf16[2,512,512]{2,1,0:T(8,128)(2,1)S(1)} collective-permute-done((bf16[2,512,512]{2,1,0:T(8,128)(2,1)}, bf16[2,512,512]{2,1,0:T(8,128)(2,1)S(1)}, u32[]{:S(2)}, u32[]{:S(2)}) %collective-permute-start.12) | collective-permute-done | bytes 1048608 | tf_op jit(solution)/shard_map/ppermute | solution.py:416
  145.0 17.1 %collective-permute-done.13.refs_2_.refs_10_ = bf16[2,512,512]{2,1,0:T(8,128)(2,1)} collective-permute-done((bf16[2,512,512]{2,1,0:T(8,128)(2,1)}, bf16[2,512,512]{2,1,0:T(8,128)(2,1)}, u32[]{:S(2)}, u32[]{:S(2)}) %collective-permute-start.13) | collective-permute-done | bytes 1048608 | tf_op jit(solution)/shard_map/ppermute | solution.py:422
  162.7 20.6 %collective-permute-done.14.refs_3_.refs_11_ = bf16[2,512,512]{2,1,0:T(8,128)(2,1)} collective-permute-done((bf16[2,512,512]{2,1,0:T(8,128)(2,1)S(1)}, bf16[2,512,512]{2,1,0:T(8,128)(2,1)}, u32[]{:S(2)}, u32[]{:S(2)}) %collective-permute-start.14) | collective-permute-done | bytes 1048608 | tf_op jit(solution)/shard_map/ppermute | solution.py:422
  184.5 11.7 %place.1 = (bf16[16,512,512]{2,1,0:T(8,128)(2,1)}, bf16[16,512,512]{2,1,0:T(8,128)(2,1)}) custom-call(s32[4]{0:T(128)} %pad_add_fusion.where, bf16[16,128,512]{2,1,0:T(8,128)(2,1)} %refs_0_.1, bf16[16,128,512]{2,1,0:T(8,128)(2,1)} %collective-permute-done.33.refs_1_, bf16[16,128,512]{2,1,0:T(8,128)(2,1)} %copy-done.17, ...), custom_call_target="tpu_custom_call" | custom-call | flops 16777216 | bytes 25165824 | tf_op jit(solution)/shard_map/place/pallas_call | solution.py:97
  196.3 12.3 %home.3 = (bf16[4,512,512]{2,1,0:T(8,128)(2,1)S(1)}, bf16[4,512,512]{2,1,0:T(8,128)(2,1)S(1)}) custom-call(s32[64]{0:T(128)S(1)} %reshape.11.slots, bf16[1,512,512]{2,1,0:T(8,128)(2,1)S(1)} %copy-done.2, bf16[1,512,512]{2,1,0:T(8,128)(2,1)S(1)} %copy-done.1, bf16[1,512,512]{2,1,0:T(8,128)(2,1)} %copy-done.10, bf16[1,512,512]{2,1,0:T(8,128)(2,1)} %copy-done.7, ...), custom_call_target="tpu_custom_call" | custom-call | flops 67108864 | bytes 29360128 | tf_op jit(solution)/shard_map/home/pallas_call | solution.py:207
  208.7 12.7 %density.3.held_ref = f32[4,2,512,512]{3,2,1,0:T(8,128)} custom-call(bf16[4,2,2,512,512]{4,3,2,1,0:T(8,128)(2,1)} %g_ref.13, f32[4,2,512]{2,1,0:T(2,128)S(1)} %copy-done.5, bf16[4,512,512]{2,1,0:T(8,128)(2,1)S(1)} %get-tuple-element.84.x_ref, bf16[4,512,512]{2,1,0:T(8,128)(2,1)S(1)} %get-tuple-element.85.y_ref), custom_call_target="tpu_custom_call" | custom-call | flops 8589934592 | bytes 20971520 | tf_op jit(solution)/shard_map/density/pallas_call | solution.py:317
  221.4 12.2 %home.2 = (bf16[4,512,512]{2,1,0:T(8,128)(2,1)S(1)}, bf16[4,512,512]{2,1,0:T(8,128)(2,1)S(1)}) custom-call(s32[64]{0:T(128)S(1)} %reshape.11.slots, bf16[2,512,512]{2,1,0:T(8,128)(2,1)S(1)} %copy-done, bf16[2,512,512]{2,1,0:T(8,128)(2,1)} %copy-done.6, bf16[2,512,512]{2,1,0:T(8,128)(2,1)} %collective-permute-done.13.refs_2_.refs_10_, ...), custom_call_target="tpu_custom_call" | custom-call | flops 67108864 | bytes 29360128 | tf_op jit(solution)/shard_map/home/pallas_call | solution.py:207
  233.6 5.3 %density.4 = (bf16[4,2,64,512]{3,2,1,0:T(8,128)(2,1)S(1)}, bf16[4,2,64,512]{3,2,1,0:T(8,128)(2,1)}) custom-call(s32[1]{0:T(128)} %bitcast.1.odd, bf16[4,2,2,512,512]{4,3,2,1,0:T(8,128)(2,1)} %g_ref.13, f32[4,2,512]{2,1,0:T(2,128)S(1)} %copy-done.5, bf16[4,512,512]{2,1,0:T(8,128)(2,1)S(1)} %get-tuple-element.82.x_ref, ...), custom_call_target="tpu_custom_call" | custom-call | flops 2147483648 | bytes 5242880 | tf_op jit(solution)/shard_map/density/pallas_call | solution.py:357
  240.1 11.0 %density.5 = (bf16[4,2,64,512]{3,2,1,0:T(8,128)(2,1)S(1)}, bf16[4,2,64,512]{3,2,1,0:T(8,128)(2,1)}, bf16[4,2,64,512]{3,2,1,0:T(8,128)(2,1)S(1)}, bf16[4,2,64,512...) custom-call(s32[1]{0:T(128)} %bitcast.1.odd, ...), custom_call_target="tpu_custom_call" | custom-call | flops 6442450944 | bytes 15728640 | tf_op jit(solution)/shard_map/density/pallas_call | solution.py:357
  255.0 1.7 pairsum.4
  258.3 2.2 collective-permute-start.38
  260.6 5.5 %collective-permute-done.40.recv_ref = bf16[4,2,64,512]{3,2,1,0:T(8,128)(2,1)S(1)} collective-permute-done((bf16[4,2,64,512]{3,2,1,0:T(8,128)(2,1)}, bf16[4,2,64,512]{3,2,1,0:T(8,128)(2,1)S(1)}, u32[]{:S(2)}, u32[]{:S(2)}) %collective-permute-start.40) | collective-permute-done | bytes 524320 | tf_op jit(solution)/shard_map/ppermute | solution.py:416
  266.1 2.9 collective-permute-start.39
  269.7 13.0 %rows.2.refs_17_ = bf16[16,2,2,128,512]{4,3,2,1,0:T(8,128)(2,1)} custom-call(s32[1]{0:T(128)} %bitcast.mine, s32[256]{0:T(256)} %reshape.10.slots, bf16[1,512,512]{2,1,0:T(8,128)(2,1)} %get-tuple-element.76.refs_0_.refs_16_, bf16[1,512,512]{2,1,0:T(8,128)(2,1)} %get-tuple-element.77.refs_1_.refs_17_, bf16[1,512,512]{2,1,0:T(8,128)(2,1)} %copy-done.10, ...), custom_call_target="tpu_custom_call" | custom-call | flops 67108864 | bytes 10485760 | tf_op jit(solution)/shard_map/rows/pallas_call | solution.py:275
  282.7 12.7 %rows.3 = bf16[16,2,2,128,512]{4,3,2,1,0:T(8,128)(2,1)} custom-call(s32[1]{0:T(128)} %bitcast.mine, s32[256]{0:T(256)} %reshape.10.slots, bf16[2,512,512]{2,1,0:T(8,128)(2,1)} %get-tuple-element.74.refs_0_.refs_8_, bf16[2,512,512]{2,1,0:T(8,128)(2,1)} %copy-done.6, ...), custom_call_target="tpu_custom_call", output_to_operand_aliasing={{}: (19, {})} | custom-call | flops 67108864 | bytes 10485760 | tf_op jit(solution)/shard_map/rows/pallas_call | solution.py:275
  297.7 2.2 collective-permute-start.43
  303.9 2.1 collective-permute-start.47
  306.0 2.8 collective-permute-done.42
  308.8 2.3 collective-permute-start.49
  311.1 5.5 %collective-permute-start.50 = (bf16[2,64,512]{2,1,0:T(8,128)(2,1)S(1)}, bf16[2,64,512]{2,1,0:T(8,128)(2,1)S(1)}, u32[]{:S(2)}, u32[]{:S(2)}) collective-permute-start(bf16[2,64,512]{2,1,0:T(8,128)(2,1)S(1)} %get-tuple-element.108), channel_id=1, source_target_pairs={{0,16},{4,20},{8,24},{12,28},{16,0},{20,4},{24,8},{28,12},{1,17},{... | collective-permute-start | bytes 393224 | tf_op jit(solution)/shard_map/ppermute | solution.py:416
  316.6 3.6 %collective-permute-start.51 = (bf16[2,64,512]{2,1,0:T(8,128)(2,1)S(1)}, bf16[2,64,512]{2,1,0:T(8,128)(2,1)S(1)}, u32[]{:S(2)}, u32[]{:S(2)}) collective-permute-start(bf16[2,64,512]{2,1,0:T(8,128)(2,1)S(1)} %get-tuple-element.109), channel_id=1, source_target_pairs={{0,24},{4,28},{8,0},{12,4},{16,8},{20,12},{24,16},{28,20},{1,25},{... | collective-permute-start | bytes 393224 | tf_op jit(solution)/shard_map/ppermute | solution.py:416
  321.5 6.9 %collective-permute-done.50 = bf16[2,64,512]{2,1,0:T(8,128)(2,1)S(1)} collective-permute-done((bf16[2,64,512]{2,1,0:T(8,128)(2,1)S(1)}, bf16[2,64,512]{2,1,0:T(8,128)(2,1)S(1)}, u32[]{:S(2)}, u32[]{:S(2)}) %collective-permute-start.50) | collective-permute-done | bytes 131104 | tf_op jit(solution)/shard_map/ppermute | solution.py:416
  328.6 1.8 copy.20
  (155 shorter events, 38.1 us)
Async XLA Ops:
  4.8 19.9 %collective-permute-start.9 = (bf16[2,256,512]{2,1,0:T(8,128)(2,1)}, bf16[2,256,512]{2,1,0:T(8,128)(2,1)S(1)}, u32[]{:S(2)}, u32[]{:S(2)}) collective-permute-start(bf16[2,256,512]{2,1,0:T(8,128)(2,1)} %get-tuple-element.63), channel_id=1, source_target_pairs={{0,4},{4,0},{8,12},{12,8},{16,20},{20,16},{24,28},{28,24},{1,5},{5... | collective-permute-start | bytes 1572872 | tf_op jit(solution)/shard_map/ppermute | solution.py:416
  11.9 16.9 %collective-permute-start.10 = (bf16[2,256,512]{2,1,0:T(8,128)(2,1)}, bf16[2,256,512]{2,1,0:T(8,128)(2,1)S(1)}, u32[]{:S(2)}, u32[]{:S(2)}) collective-permute-start(bf16[2,256,512]{2,1,0:T(8,128)(2,1)} %get-tuple-element.62.keep), channel_id=1, source_target_pairs={{4,12},{8,0},{12,20},{16,8},{20,28},{24,16},{5,13},{9,1},{13,21},{... | collective-permute-start | bytes 1572872 | tf_op jit(solution)/shard_map/ppermute | solution.py:416
  13.1 19.1 %collective-permute-start.6 = (bf16[2,256,512]{2,1,0:T(8,128)(2,1)}, bf16[2,256,512]{2,1,0:T(8,128)(2,1)S(1)}, u32[]{:S(2)}, u32[]{:S(2)}) collective-permute-start(bf16[2,256,512]{2,1,0:T(8,128)(2,1)} %get-tuple-element.61), channel_id=1, source_target_pairs={{0,4},{4,0},{8,12},{12,8},{16,20},{20,16},{24,28},{28,24},{1,5},{5... | collective-permute-start | bytes 1572872 | tf_op jit(solution)/shard_map/ppermute | solution.py:416
  15.9 22.7 %collective-permute-start.7 = (bf16[2,256,512]{2,1,0:T(8,128)(2,1)}, bf16[2,256,512]{2,1,0:T(8,128)(2,1)}, u32[]{:S(2)}, u32[]{:S(2)}) collective-permute-start(bf16[2,256,512]{2,1,0:T(8,128)(2,1)} %get-tuple-element.60.keep), channel_id=1, source_target_pairs={{4,12},{8,0},{12,20},{16,8},{20,28},{24,16},{5,13},{9,1},{13,21},{... | collective-permute-start | bytes 1572872 | tf_op jit(solution)/shard_map/ppermute | solution.py:416
  21.3 23.0 %collective-permute-start.3 = (bf16[2,256,512]{2,1,0:T(8,128)(2,1)}, bf16[2,256,512]{2,1,0:T(8,128)(2,1)S(1)}, u32[]{:S(2)}, u32[]{:S(2)}) collective-permute-start(bf16[2,256,512]{2,1,0:T(8,128)(2,1)} %get-tuple-element.59), channel_id=1, source_target_pairs={{0,4},{4,0},{8,12},{12,8},{16,20},{20,16},{24,28},{28,24},{1,5},{5... | collective-permute-start | bytes 1572872 | tf_op jit(solution)/shard_map/ppermute | solution.py:416
  24.7 28.9 %collective-permute-start = (bf16[2,256,512]{2,1,0:T(8,128)(2,1)}, bf16[2,256,512]{2,1,0:T(8,128)(2,1)S(1)}, u32[]{:S(2)}, u32[]{:S(2)}) collective-permute-start(bf16[2,256,512]{2,1,0:T(8,128)(2,1)} %get-tuple-element.57), channel_id=1, source_target_pairs={{0,4},{4,0},{8,12},{12,8},{16,20},{20,16},{24,28},{28,24},{1,5},{5... | collective-permute-start | bytes 1572872 | tf_op jit(solution)/shard_map/ppermute | solution.py:416
  28.7 28.6 %collective-permute-start.11 = (bf16[2,256,512]{2,1,0:T(8,128)(2,1)S(1)}, bf16[2,256,512]{2,1,0:T(8,128)(2,1)S(1)}, u32[]{:S(2)}, u32[]{:S(2)}) collective-permute-start(bf16[2,256,512]{2,1,0:T(8,128)(2,1)S(1)} %collective-permute-done.9.recv), channel_id=1, source_target_pairs={{0,8},{8,16},{12,4},{16,24},{20,12},{28,20},{1,9},{9,17},{13,5},{1... | collective-permute-start | bytes 1572872 | tf_op jit(solution)/shard_map/ppermute | solution.py:416
  32.3 26.4 %collective-permute-start.8 = (bf16[2,256,512]{2,1,0:T(8,128)(2,1)S(1)}, bf16[2,256,512]{2,1,0:T(8,128)(2,1)}, u32[]{:S(2)}, u32[]{:S(2)}) collective-permute-start(bf16[2,256,512]{2,1,0:T(8,128)(2,1)S(1)} %collective-permute-done.6.recv), channel_id=1, source_target_pairs={{0,8},{8,16},{12,4},{16,24},{20,12},{28,20},{1,9},{9,17},{13,5},{1... | collective-permute-start | bytes 1572872 | tf_op jit(solution)/shard_map/ppermute | solution.py:416
  38.7 82.7 %collective-permute-start.33 = (bf16[16,128,512]{2,1,0:T(8,128)(2,1)}, bf16[16,128,512]{2,1,0:T(8,128)(2,1)}, u32[]{:S(2)}, u32[]{:S(2)}) collective-permute-start(bf16[16,128,512]{2,1,0:T(8,128)(2,1)} %refs_0_.1), channel_id=1, source_target_pairs={{0,2},{1,3},{2,0},{3,1},{4,6},{5,7},{6,4},{7,5},{8,10},{9,11},{10,... | collective-permute-start | bytes 6291464 | tf_op jit(solution)/shard_map/ppermute | solution.py:422
  44.4 29.9 %collective-permute-start.4 = (bf16[2,256,512]{2,1,0:T(8,128)(2,1)}, bf16[2,256,512]{2,1,0:T(8,128)(2,1)S(1)}, u32[]{:S(2)}, u32[]{:S(2)}) collective-permute-start(bf16[2,256,512]{2,1,0:T(8,128)(2,1)} %get-tuple-element.58.keep), channel_id=1, source_target_pairs={{4,12},{8,0},{12,20},{16,8},{20,28},{24,16},{5,13},{9,1},{13,21},{... | collective-permute-start | bytes 1572872 | tf_op jit(solution)/shard_map/ppermute | solution.py:416
  53.6 20.8 %collective-permute-start.5 = (bf16[2,256,512]{2,1,0:T(8,128)(2,1)S(1)}, bf16[2,256,512]{2,1,0:T(8,128)(2,1)S(1)}, u32[]{:S(2)}, u32[]{:S(2)}) collective-permute-start(bf16[2,256,512]{2,1,0:T(8,128)(2,1)S(1)} %collective-permute-done.3.recv), channel_id=1, source_target_pairs={{0,8},{8,16},{12,4},{16,24},{20,12},{28,20},{1,9},{9,17},{13,5},{1... | collective-permute-start | bytes 1572872 | tf_op jit(solution)/shard_map/ppermute | solution.py:416
  57.4 21.5 %collective-permute-start.1 = (bf16[2,256,512]{2,1,0:T(8,128)(2,1)}, bf16[2,256,512]{2,1,0:T(8,128)(2,1)S(1)}, u32[]{:S(2)}, u32[]{:S(2)}) collective-permute-start(bf16[2,256,512]{2,1,0:T(8,128)(2,1)} %get-tuple-element.56.keep), channel_id=1, source_target_pairs={{4,12},{8,0},{12,20},{16,8},{20,28},{24,16},{5,13},{9,1},{13,21},{... | collective-permute-start | bytes 1572872 | tf_op jit(solution)/shard_map/ppermute | solution.py:416
  58.7 20.3 %collective-permute-start.2 = (bf16[2,256,512]{2,1,0:T(8,128)(2,1)S(1)}, bf16[2,256,512]{2,1,0:T(8,128)(2,1)S(1)}, u32[]{:S(2)}, u32[]{:S(2)}) collective-permute-start(bf16[2,256,512]{2,1,0:T(8,128)(2,1)S(1)} %collective-permute-done.recv), channel_id=1, source_target_pairs={{0,8},{8,16},{12,4},{16,24},{20,12},{28,20},{1,9},{9,17},{13,5},{1... | collective-permute-start | bytes 1572872 | tf_op jit(solution)/shard_map/ppermute | solution.py:416
  83.5 15.3 %collective-permute-start.20 = (bf16[1,512,512]{2,1,0:T(8,128)(2,1)}, bf16[1,512,512]{2,1,0:T(8,128)(2,1)S(1)}, u32[]{:S(2)}, u32[]{:S(2)}) collective-permute-start(bf16[1,512,512]{2,1,0:T(8,128)(2,1)} %get-tuple-element.79), channel_id=1, source_target_pairs={{0,4},{4,0},{8,12},{12,8},{16,20},{20,16},{24,28},{28,24},{1,5},{5... | collective-permute-start | bytes 1572872 | tf_op jit(solution)/shard_map/ppermute | solution.py:416
  85.8 14.5 %collective-permute-start.22 = (bf16[1,512,512]{2,1,0:T(8,128)(2,1)}, bf16[1,512,512]{2,1,0:T(8,128)(2,1)S(1)}, u32[]{:S(2)}, u32[]{:S(2)}) collective-permute-start(bf16[1,512,512]{2,1,0:T(8,128)(2,1)} %get-tuple-element.77.refs_1_.refs_17_), channel_id=1, source_target_pairs={{0,2},{1,3},{2,0},{3,1},{4,6},{5,7},{6,4},{7,5},{8,10},{9,11},{10,... | collective-permute-start | bytes 1572872 | tf_op jit(solution)/shard_map/ppermute | solution.py:422
  87.3 13.0 %collective-permute-start.26 = (bf16[1,512,512]{2,1,0:T(8,128)(2,1)}, bf16[1,512,512]{2,1,0:T(8,128)(2,1)S(1)}, u32[]{:S(2)}, u32[]{:S(2)}) collective-permute-start(bf16[1,512,512]{2,1,0:T(8,128)(2,1)} %get-tuple-element.77.refs_1_.refs_17_), channel_id=1, source_target_pairs={{0,1},{1,0},{2,3},{3,2},{4,5},{5,4},{6,7},{7,6},{8,9},{9,8},{10,11... | collective-permute-start | bytes 1572872 | tf_op jit(solution)/shard_map/ppermute | solution.py:422
  87.3 20.4 %collective-permute-start.19 = (bf16[1,512,512]{2,1,0:T(8,128)(2,1)S(1)}, bf16[1,512,512]{2,1,0:T(8,128)(2,1)S(1)}, u32[]{:S(2)}, u32[]{:S(2)}) collective-permute-start(bf16[1,512,512]{2,1,0:T(8,128)(2,1)S(1)} %copy-done.28), channel_id=1, source_target_pairs={{0,4},{4,0},{8,12},{12,8},{16,20},{20,16},{24,28},{28,24},{1,5},{5... | collective-permute-start | bytes 1572872 | tf_op jit(solution)/shard_map/ppermute | solution.py:416
  98.8 14.8 %collective-permute-start.21 = (bf16[1,512,512]{2,1,0:T(8,128)(2,1)S(1)}, bf16[1,512,512]{2,1,0:T(8,128)(2,1)S(1)}, u32[]{:S(2)}, u32[]{:S(2)}) collective-permute-start(bf16[1,512,512]{2,1,0:T(8,128)(2,1)S(1)} %copy-done.2), channel_id=1, source_target_pairs={{0,2},{1,3},{2,0},{3,1},{4,6},{5,7},{6,4},{7,5},{8,10},{9,11},{10,... | collective-permute-start | bytes 1572872 | tf_op jit(solution)/shard_map/ppermute | solution.py:422
  100.3 13.3 %collective-permute-start.25 = (bf16[1,512,512]{2,1,0:T(8,128)(2,1)S(1)}, bf16[1,512,512]{2,1,0:T(8,128)(2,1)S(1)}, u32[]{:S(2)}, u32[]{:S(2)}) collective-permute-start(bf16[1,512,512]{2,1,0:T(8,128)(2,1)S(1)} %copy-done.2), channel_id=1, source_target_pairs={{0,1},{1,0},{2,3},{3,2},{4,5},{5,4},{6,7},{7,6},{8,9},{9,8},{10,11... | collective-permute-start | bytes 1572872 | tf_op jit(solution)/shard_map/ppermute | solution.py:422
  100.3 20.2 %collective-permute-start.24 = (bf16[1,512,512]{2,1,0:T(8,128)(2,1)S(1)}, bf16[1,512,512]{2,1,0:T(8,128)(2,1)}, u32[]{:S(2)}, u32[]{:S(2)}) collective-permute-start(bf16[1,512,512]{2,1,0:T(8,128)(2,1)S(1)} %collective-permute-done.20.refs_3_.refs_19_), channel_id=1, source_target_pairs={{0,2},{1,3},{2,0},{3,1},{4,6},{5,7},{6,4},{7,5},{8,10},{9,11},{10,... | collective-permute-start | bytes 1572872 | tf_op jit(solution)/shard_map/ppermute | solution.py:422
  107.7 35.3 %collective-permute-start.34 = (bf16[16,128,512]{2,1,0:T(8,128)(2,1)}, bf16[16,128,512]{2,1,0:T(8,128)(2,1)S(1)}, u32[]{:S(2)}, u32[]{:S(2)}) collective-permute-start(bf16[16,128,512]{2,1,0:T(8,128)(2,1)} %refs_0_.1), channel_id=1, source_target_pairs={{0,1},{1,0},{2,3},{3,2},{4,5},{5,4},{6,7},{7,6},{8,9},{9,8},{10,11... | collective-permute-start | bytes 6291464 | tf_op jit(solution)/shard_map/ppermute | solution.py:422
  120.5 20.9 %collective-permute-start.12 = (bf16[2,512,512]{2,1,0:T(8,128)(2,1)}, bf16[2,512,512]{2,1,0:T(8,128)(2,1)S(1)}, u32[]{:S(2)}, u32[]{:S(2)}) collective-permute-start(bf16[2,512,512]{2,1,0:T(8,128)(2,1)} %get-tuple-element.75), channel_id=1, source_target_pairs={{0,4},{4,0},{8,12},{12,8},{16,20},{20,16},{24,28},{28,24},{1,5},{5... | collective-permute-start | bytes 3145736 | tf_op jit(solution)/shard_map/ppermute | solution.py:416
  121.4 61.9 %collective-permute-start.35 = (bf16[16,128,512]{2,1,0:T(8,128)(2,1)}, bf16[16,128,512]{2,1,0:T(8,128)(2,1)}, u32[]{:S(2)}, u32[]{:S(2)}) collective-permute-start(bf16[16,128,512]{2,1,0:T(8,128)(2,1)} %collective-permute-done.33.refs_1_), channel_id=1, source_target_pairs={{0,1},{1,0},{2,3},{3,2},{4,5},{5,4},{6,7},{7,6},{8,9},{9,8},{10,11... | collective-permute-start | bytes 6291464 | tf_op jit(solution)/shard_map/ppermute | solution.py:422
  121.4 14.4 %collective-permute-start.23 = (bf16[1,512,512]{2,1,0:T(8,128)(2,1)S(1)}, bf16[1,512,512]{2,1,0:T(8,128)(2,1)}, u32[]{:S(2)}, u32[]{:S(2)}) collective-permute-start(bf16[1,512,512]{2,1,0:T(8,128)(2,1)S(1)} %collective-permute-done.19.refs_2_.refs_18_), channel_id=1, source_target_pairs={{0,2},{1,3},{2,0},{3,1},{4,6},{5,7},{6,4},{7,5},{8,10},{9,11},{10,... | collective-permute-start | bytes 1572872 | tf_op jit(solution)/shard_map/ppermute | solution.py:422
  122.9 14.4 %collective-permute-start.27 = (bf16[1,512,512]{2,1,0:T(8,128)(2,1)S(1)}, bf16[1,512,512]{2,1,0:T(8,128)(2,1)S(1)}, u32[]{:S(2)}, u32[]{:S(2)}) collective-permute-start(bf16[1,512,512]{2,1,0:T(8,128)(2,1)S(1)} %collective-permute-done.19.refs_2_.refs_18_), channel_id=1, source_target_pairs={{0,1},{1,0},{2,3},{3,2},{4,5},{5,4},{6,7},{7,6},{8,9},{9,8},{10,11... | collective-permute-start | bytes 1572872 | tf_op jit(solution)/shard_map/ppermute | solution.py:422
  135.8 26.3 %collective-permute-start.13 = (bf16[2,512,512]{2,1,0:T(8,128)(2,1)}, bf16[2,512,512]{2,1,0:T(8,128)(2,1)}, u32[]{:S(2)}, u32[]{:S(2)}) collective-permute-start(bf16[2,512,512]{2,1,0:T(8,128)(2,1)} %get-tuple-element.74.refs_0_.refs_8_), channel_id=1, source_target_pairs={{0,2},{1,3},{2,0},{3,1},{4,6},{5,7},{6,4},{7,5},{8,10},{9,11},{10,... | collective-permute-start | bytes 3145736 | tf_op jit(solution)/shard_map/ppermute | solution.py:422
  141.4 41.8 %collective-permute-start.14 = (bf16[2,512,512]{2,1,0:T(8,128)(2,1)S(1)}, bf16[2,512,512]{2,1,0:T(8,128)(2,1)}, u32[]{:S(2)}, u32[]{:S(2)}) collective-permute-start(bf16[2,512,512]{2,1,0:T(8,128)(2,1)S(1)} %collective-permute-done.12.refs_1_.refs_9_), channel_id=1, source_target_pairs={{0,2},{1,3},{2,0},{3,1},{4,6},{5,7},{6,4},{7,5},{8,10},{9,11},{10,... | collective-permute-start | bytes 3145736 | tf_op jit(solution)/shard_map/ppermute | solution.py:422
  142.9 19.2 %collective-permute-start.32 = (bf16[1,512,512]{2,1,0:T(8,128)(2,1)}, bf16[1,512,512]{2,1,0:T(8,128)(2,1)}, u32[]{:S(2)}, u32[]{:S(2)}) collective-permute-start(bf16[1,512,512]{2,1,0:T(8,128)(2,1)} %collective-permute-done.24.refs_7_.refs_23_), channel_id=1, source_target_pairs={{0,1},{1,0},{2,3},{3,2},{4,5},{5,4},{6,7},{7,6},{8,9},{9,8},{10,11... | collective-permute-start | bytes 1572872 | tf_op jit(solution)/shard_map/ppermute | solution.py:422
  145.0 51.3 %collective-permute-start.31 = (bf16[1,512,512]{2,1,0:T(8,128)(2,1)}, bf16[1,512,512]{2,1,0:T(8,128)(2,1)}, u32[]{:S(2)}, u32[]{:S(2)}) collective-permute-start(bf16[1,512,512]{2,1,0:T(8,128)(2,1)} %collective-permute-done.23.refs_6_.refs_22_), channel_id=1, source_target_pairs={{0,1},{1,0},{2,3},{3,2},{4,5},{5,4},{6,7},{7,6},{8,9},{9,8},{10,11... | collective-permute-start | bytes 1572872 | tf_op jit(solution)/shard_map/ppermute | solution.py:422
  162.1 59.2 %collective-permute-start.15 = (bf16[2,512,512]{2,1,0:T(8,128)(2,1)}, bf16[2,512,512]{2,1,0:T(8,128)(2,1)}, u32[]{:S(2)}, u32[]{:S(2)}) collective-permute-start(bf16[2,512,512]{2,1,0:T(8,128)(2,1)} %get-tuple-element.74.refs_0_.refs_8_), channel_id=1, source_target_pairs={{0,1},{1,0},{2,3},{3,2},{4,5},{5,4},{6,7},{7,6},{8,9},{9,8},{10,11... | collective-permute-start | bytes 3145736 | tf_op jit(solution)/shard_map/ppermute | solution.py:422
  162.2 59.2 %collective-permute-start.16 = (bf16[2,512,512]{2,1,0:T(8,128)(2,1)S(1)}, bf16[2,512,512]{2,1,0:T(8,128)(2,1)}, u32[]{:S(2)}, u32[]{:S(2)}) collective-permute-start(bf16[2,512,512]{2,1,0:T(8,128)(2,1)S(1)} %collective-permute-done.12.refs_1_.refs_9_), channel_id=1, source_target_pairs={{0,1},{1,0},{2,3},{3,2},{4,5},{5,4},{6,7},{7,6},{8,9},{9,8},{10,11... | collective-permute-start | bytes 3145736 | tf_op jit(solution)/shard_map/ppermute | solution.py:422
  183.2 38.2 %collective-permute-start.17 = (bf16[2,512,512]{2,1,0:T(8,128)(2,1)}, bf16[2,512,512]{2,1,0:T(8,128)(2,1)}, u32[]{:S(2)}, u32[]{:S(2)}) collective-permute-start(bf16[2,512,512]{2,1,0:T(8,128)(2,1)} %collective-permute-done.13.refs_2_.refs_10_), channel_id=1, source_target_pairs={{0,1},{1,0},{2,3},{3,2},{4,5},{5,4},{6,7},{7,6},{8,9},{9,8},{10,11... | collective-permute-start | bytes 3145736 | tf_op jit(solution)/shard_map/ppermute | solution.py:422
  183.2 38.2 %collective-permute-start.18 = (bf16[2,512,512]{2,1,0:T(8,128)(2,1)}, bf16[2,512,512]{2,1,0:T(8,128)(2,1)}, u32[]{:S(2)}, u32[]{:S(2)}) collective-permute-start(bf16[2,512,512]{2,1,0:T(8,128)(2,1)} %collective-permute-done.14.refs_3_.refs_11_), channel_id=1, source_target_pairs={{0,1},{1,0},{2,3},{3,2},{4,5},{5,4},{6,7},{7,6},{8,9},{9,8},{10,11... | collective-permute-start | bytes 3145736 | tf_op jit(solution)/shard_map/ppermute | solution.py:422
  238.9 15.0 %collective-permute-start.36 = (bf16[4,2,64,512]{3,2,1,0:T(8,128)(2,1)}, bf16[4,2,64,512]{3,2,1,0:T(8,128)(2,1)}, u32[]{:S(2)}, u32[]{:S(2)}) collective-permute-start(bf16[4,2,64,512]{3,2,1,0:T(8,128)(2,1)} %get-tuple-element.87), channel_id=1, source_target_pairs={{0,4},{4,0},{8,12},{12,8},{16,20},{20,16},{24,28},{28,24},{1,5},{5... | collective-permute-start | bytes 1572872 | tf_op jit(solution)/shard_map/ppermute | solution.py:416
  251.1 15.0 %collective-permute-start.40 = (bf16[4,2,64,512]{3,2,1,0:T(8,128)(2,1)}, bf16[4,2,64,512]{3,2,1,0:T(8,128)(2,1)S(1)}, u32[]{:S(2)}, u32[]{:S(2)}) collective-permute-start(bf16[4,2,64,512]{3,2,1,0:T(8,128)(2,1)} %get-tuple-element.93), channel_id=1, source_target_pairs={{0,4},{4,0},{8,12},{12,8},{16,20},{20,16},{24,28},{28,24},{1,5},{5... | collective-permute-start | bytes 1572872 | tf_op jit(solution)/shard_map/ppermute | solution.py:416
  251.9 43.6 %collective-permute-start.44 = (bf16[4,2,64,512]{3,2,1,0:T(8,128)(2,1)}, bf16[4,2,64,512]{3,2,1,0:T(8,128)(2,1)S(1)}, u32[]{:S(2)}, u32[]{:S(2)}) collective-permute-start(bf16[4,2,64,512]{3,2,1,0:T(8,128)(2,1)} %get-tuple-element.99), channel_id=1, source_target_pairs={{0,4},{4,0},{8,12},{12,8},{16,20},{20,16},{24,28},{28,24},{1,5},{5... | collective-permute-start | bytes 1572872 | tf_op jit(solution)/shard_map/ppermute | solution.py:416
  253.1 42.7 %collective-permute-start.48 = (bf16[4,2,64,512]{3,2,1,0:T(8,128)(2,1)}, bf16[4,2,64,512]{3,2,1,0:T(8,128)(2,1)S(1)}, u32[]{:S(2)}, u32[]{:S(2)}) collective-permute-start(bf16[4,2,64,512]{3,2,1,0:T(8,128)(2,1)} %get-tuple-element.105), channel_id=1, source_target_pairs={{0,4},{4,0},{8,12},{12,8},{16,20},{20,16},{24,28},{28,24},{1,5},{5... | collective-permute-start | bytes 1572872 | tf_op jit(solution)/shard_map/ppermute | solution.py:416
  256.8 40.9 %collective-permute-start.37 = (bf16[2,64,512]{2,1,0:T(8,128)(2,1)}, bf16[2,64,512]{2,1,0:T(8,128)(2,1)}, u32[]{:S(2)}, u32[]{:S(2)}) collective-permute-start(bf16[2,64,512]{2,1,0:T(8,128)(2,1)} %get-tuple-element.89), channel_id=1, source_target_pairs={{0,8},{4,12},{8,16},{12,20},{16,24},{20,28},{24,0},{28,4},{1,9},{5... | collective-permute-start | bytes 393224 | tf_op jit(solution)/shard_map/ppermute | solution.py:416
  258.3 41.6 %collective-permute-start.38 = (bf16[2,64,512]{2,1,0:T(8,128)(2,1)S(1)}, bf16[2,64,512]{2,1,0:T(8,128)(2,1)}, u32[]{:S(2)}, u32[]{:S(2)}) collective-permute-start(bf16[2,64,512]{2,1,0:T(8,128)(2,1)S(1)} %get-tuple-element.90), channel_id=1, source_target_pairs={{0,16},{4,20},{8,24},{12,28},{16,0},{20,4},{24,8},{28,12},{1,17},{... | collective-permute-start | bytes 393224 | tf_op jit(solution)/shard_map/ppermute | solution.py:416
  266.1 34.4 %collective-permute-start.39 = (bf16[2,64,512]{2,1,0:T(8,128)(2,1)S(1)}, bf16[2,64,512]{2,1,0:T(8,128)(2,1)}, u32[]{:S(2)}, u32[]{:S(2)}) collective-permute-start(bf16[2,64,512]{2,1,0:T(8,128)(2,1)S(1)} %get-tuple-element.91), channel_id=1, source_target_pairs={{0,24},{4,28},{8,0},{12,4},{16,8},{20,12},{24,16},{28,20},{1,25},{... | collective-permute-start | bytes 393224 | tf_op jit(solution)/shard_map/ppermute | solution.py:416
  295.8 12.9 %collective-permute-start.42 = (bf16[2,64,512]{2,1,0:T(8,128)(2,1)S(1)}, bf16[2,64,512]{2,1,0:T(8,128)(2,1)S(1)}, u32[]{:S(2)}, u32[]{:S(2)}) collective-permute-start(bf16[2,64,512]{2,1,0:T(8,128)(2,1)S(1)} %get-tuple-element.96), channel_id=1, source_target_pairs={{0,16},{4,20},{8,24},{12,28},{16,0},{20,4},{24,8},{28,12},{1,17},{... | collective-permute-start | bytes 393224 | tf_op jit(solution)/shard_map/ppermute | solution.py:416
  297.7 13.4 %collective-permute-start.43 = (bf16[2,64,512]{2,1,0:T(8,128)(2,1)S(1)}, bf16[2,64,512]{2,1,0:T(8,128)(2,1)S(1)}, u32[]{:S(2)}, u32[]{:S(2)}) collective-permute-start(bf16[2,64,512]{2,1,0:T(8,128)(2,1)S(1)} %get-tuple-element.97), channel_id=1, source_target_pairs={{0,24},{4,28},{8,0},{12,4},{16,8},{20,12},{24,16},{28,20},{1,25},{... | collective-permute-start | bytes 393224 | tf_op jit(solution)/shard_map/ppermute | solution.py:416
  299.9 16.7 %collective-permute-start.45 = (bf16[2,64,512]{2,1,0:T(8,128)(2,1)S(1)}, bf16[2,64,512]{2,1,0:T(8,128)(2,1)S(1)}, u32[]{:S(2)}, u32[]{:S(2)}) collective-permute-start(bf16[2,64,512]{2,1,0:T(8,128)(2,1)S(1)} %get-tuple-element.101), channel_id=1, source_target_pairs={{0,8},{4,12},{8,16},{12,20},{16,24},{20,28},{24,0},{28,4},{1,9},{5... | collective-permute-start | bytes 393224 | tf_op jit(solution)/shard_map/ppermute | solution.py:416
  300.5 20.9 %collective-permute-start.46 = (bf16[2,64,512]{2,1,0:T(8,128)(2,1)S(1)}, bf16[2,64,512]{2,1,0:T(8,128)(2,1)S(1)}, u32[]{:S(2)}, u32[]{:S(2)}) collective-permute-start(bf16[2,64,512]{2,1,0:T(8,128)(2,1)S(1)} %get-tuple-element.102), channel_id=1, source_target_pairs={{0,16},{4,20},{8,24},{12,28},{16,0},{20,4},{24,8},{28,12},{1,17},{... | collective-permute-start | bytes 393224 | tf_op jit(solution)/shard_map/ppermute | solution.py:416
  303.9 17.5 %collective-permute-start.47 = (bf16[2,64,512]{2,1,0:T(8,128)(2,1)S(1)}, bf16[2,64,512]{2,1,0:T(8,128)(2,1)S(1)}, u32[]{:S(2)}, u32[]{:S(2)}) collective-permute-start(bf16[2,64,512]{2,1,0:T(8,128)(2,1)S(1)} %get-tuple-element.103), channel_id=1, source_target_pairs={{0,24},{4,28},{8,0},{12,4},{16,8},{20,12},{24,16},{28,20},{1,25},{... | collective-permute-start | bytes 393224 | tf_op jit(solution)/shard_map/ppermute | solution.py:416
  308.8 12.7 %collective-permute-start.49 = (bf16[2,64,512]{2,1,0:T(8,128)(2,1)S(1)}, bf16[2,64,512]{2,1,0:T(8,128)(2,1)S(1)}, u32[]{:S(2)}, u32[]{:S(2)}) collective-permute-start(bf16[2,64,512]{2,1,0:T(8,128)(2,1)S(1)} %get-tuple-element.107), channel_id=1, source_target_pairs={{0,8},{4,12},{8,16},{12,20},{16,24},{20,28},{24,0},{28,4},{1,9},{5... | collective-permute-start | bytes 393224 | tf_op jit(solution)/shard_map/ppermute | solution.py:416
  311.1 17.4 %collective-permute-start.50 = (bf16[2,64,512]{2,1,0:T(8,128)(2,1)S(1)}, bf16[2,64,512]{2,1,0:T(8,128)(2,1)S(1)}, u32[]{:S(2)}, u32[]{:S(2)}) collective-permute-start(bf16[2,64,512]{2,1,0:T(8,128)(2,1)S(1)} %get-tuple-element.108), channel_id=1, source_target_pairs={{0,16},{4,20},{8,24},{12,28},{16,0},{20,4},{24,8},{28,12},{1,17},{... | collective-permute-start | bytes 393224 | tf_op jit(solution)/shard_map/ppermute | solution.py:416
  316.6 11.8 %collective-permute-start.51 = (bf16[2,64,512]{2,1,0:T(8,128)(2,1)S(1)}, bf16[2,64,512]{2,1,0:T(8,128)(2,1)S(1)}, u32[]{:S(2)}, u32[]{:S(2)}) collective-permute-start(bf16[2,64,512]{2,1,0:T(8,128)(2,1)S(1)} %get-tuple-element.109), channel_id=1, source_target_pairs={{0,24},{4,28},{8,0},{12,4},{16,8},{20,12},{24,16},{28,20},{1,25},{... | collective-permute-start | bytes 393224 | tf_op jit(solution)/shard_map/ppermute | solution.py:416
  (37 other events, 871.1 us)

commit v6 on v5

--- a/solution.py
+++ b/solution.py
@@ -109,8 +109,15 @@
     )(where, *pieces)
 
 
-def source_kernel(odd, w_ref, keep, recv, kz, rz, *refs):
+def source_kernel(odd, steps, strength, boson, keep, recv, kz, rz, *refs):
     le = keep.shape[0]
+    weights = []
+    for s in range(1, SHIFT_MAX + 1):
+        up, down = jnp.float32(0), jnp.float32(0)
+        for m in range(steps.shape[0]):
+            held = jnp.where(steps[m] == s, strength[m], 0.0)
+            up, down = up + held * (boson[m] + 1.0), down + held * boson[m]
+        weights = weights + [up, down]
     outs = refs[-2 * le:]
 
     def emit(order):
@@ -122,7 +129,7 @@
                 for s in range(1, SHIFT_MAX + 1):
                     for j, sign in ((0, s), (1, -s)):
                         source, index = line[at + sign]
-                        term = w_ref[2 * (s - 1) + j] * source[index].astype(F32)
+                        term = weights[2 * (s - 1) + j] * source[index].astype(F32)
                         total = term if total is None else total + term
                 target[0] = total.astype(BF16)
 
@@ -135,7 +142,7 @@
         emit((kz, recv, keep, rz))
 
 
-def sources(odd, weights, j, h, hk, keep, recv, kz, rz, held):
+def sources(odd, modes, j, h, hk, keep, recv, kz, rz, held):
     le, half, n = keep.shape
     rows = half // 2
     at = h * (half // rows)
@@ -148,25 +155,26 @@
     if held is not None:
         for i, value in enumerate(held):
             if i % le or h:
-                alias[6 + len(extra)] = i
+                alias[5 + len(modes) + len(extra)] = i
                 extra.append(value)
     return pl.pallas_call(
         source_kernel,
         out_shape=[pltpu.HBM(shape, BF16) for shape in shapes],
         grid_spec=pltpu.PrefetchScalarGridSpec(
-            num_scalar_prefetch=2,
+            num_scalar_prefetch=1 + len(modes),
             grid=(half // rows,),
             in_specs=[big] * 4 + [pl.BlockSpec(memory_space=pl.ANY)] * len(extra),
             out_specs=specs,
         ),
         input_output_aliases=alias,
-        compiler_params=params(56),
+        compiler_params=params(16),
         cost_estimate=cost(le * half * n * 16, le * half * n * 12),
         name="source",
-    )(odd[None], weights, keep, recv, kz, rz, *extra)
-
-
-def home_kernel(lk, pieces, slots, *refs):
+    )(odd[None], *modes, keep, recv, kz, rz, *extra)
+
+
+def home_kernel(lk, pieces, mine, slots, *refs):
+    first = mine[0] * lk
     ins, (c_ref, ct_ref, x_ref, y_ref, q_ref) = refs[:pieces], refs[pieces:]
     each, rows, n = ins[0].shape
     count = pieces * each
@@ -184,7 +192,7 @@
             for p in (q, q + 2):
                 c, ct = [c_ref[p + i, r, m] for i in range(2)], [ct_ref[p + i, r, m] for i in range(2)]
                 for k in range(lk):
-                    v = [q_ref[slots[k * count + p + i], r, m] for i in range(2)]
+                    v = [q_ref[slots[first + k, p + i], r, m] for i in range(2)]
                     x, y = c[0] * v[0] + c[1] * v[1], ct[0] * v[0] + ct[1] * v[1]
                     px[k] = x if p == q else px[k] + x
                     py[k] = y if p == q else py[k] + y
@@ -199,16 +207,16 @@
     lax.fori_loop(0, (rows // tr) * (n // tc), tile, 0)
 
 
-def home_blocks(slots, pieces, full, turned, lk):
+def home_blocks(mine, slots, pieces, full, turned, lk):
     each, n, _ = pieces[0].shape
     count = each * len(pieces)
     rows = n // 4
-    block = lambda lead: pl.BlockSpec((lead, rows, n), lambda g, s: (0, g, 0))
+    block = lambda lead: pl.BlockSpec((lead, rows, n), lambda g, *_: (0, g, 0))
     return pl.pallas_call(
         functools.partial(home_kernel, lk, len(pieces)),
         out_shape=[pltpu.VMEM((lk, n, n), BF16)] * 2,
         grid_spec=pltpu.PrefetchScalarGridSpec(
-            num_scalar_prefetch=1,
+            num_scalar_prefetch=2,
             grid=(n // rows,),
             in_specs=[block(each)] * len(pieces) + [block(count), block(count)],
             out_specs=[block(lk), block(lk)],
@@ -217,7 +225,7 @@
         compiler_params=params(44),
         cost_estimate=cost(4 * lk * count * n * n, n * n * (6 * count + 4 * lk)),
         name="home",
-    )(slots, *pieces, full, turned)
+    )(mine[None], slots, *pieces, full, turned)
 
 
 def rows_kernel(pieces, mine, slots, *refs):
@@ -245,7 +253,7 @@
             for p in (q, q + 2):
                 c = [c_ref[p + i, r, m] for i in range(2)]
                 for k in range(kg):
-                    slot = [slots[(k0 + k) * count + p + i] for i in range(2)]
+                    slot = [slots[k0 + k, p + i] for i in range(2)]
                     u = c[0] * d_ref[slot[0], 0, r, m] + c[1] * d_ref[slot[1], 0, r, m]
                     v = c[0] * d_ref[slot[0], 1, r, m] + c[1] * d_ref[slot[1], 1, r, m]
                     pu[k] = u if p == q else pu[k] + u
@@ -432,20 +440,13 @@
     for s in strides:
         order = order + [o ^ s for o in order]
 
-    weights = []
-    for s in range(1, SHIFT_MAX + 1):
-        held = shift_steps == s
-        weights.append(jnp.sum(jnp.where(held, mode_weight * (occupation + 1.0), 0.0)))
-        weights.append(jnp.sum(jnp.where(held, mode_weight * occupation, 0.0)))
-    weights = jnp.stack(weights)
+    modes = (shift_steps, mode_weight, occupation)
 
     owner, inner = momentum_map // lk, momentum_map % lk
     place = jnp.zeros_like(owner)
     for at, o in enumerate(order):
         place = jnp.where((owner ^ mine) == o, at, place)
     slots = (place * lk + ((inner // hk) ^ odd) * hk + inner % hk).astype(jnp.int32)
-    own_slots = lax.dynamic_slice_in_dim(slots, mine * lk, lk, 0).reshape(-1)
-    all_slots = slots.reshape(-1)
 
     green_ret = hbm(green_ret)
     coupling = hbm(coupling)
@@ -454,13 +455,13 @@
     send = [lesser_packed((1 - odd) * hk + j, green_ret, broadening) for j in range(hk)]
     recv = [[over_energy(send[j][h], pairs) for h in range(2)] for j in range(hk)]
     keep = [lesser_packed(odd * hk + j, green_ret, broadening) for j in range(hk)]
-    kz = [[over_energy(keep[j][h], away) for h in range(2)] for j in range(hk)]
-    rz = [[over_energy(recv[j][h], across) for h in range(2)] for j in range(hk)]
+    kz = [[permuted(keep[j][h], away) for h in range(2)] for j in range(hk)]
+    rz = [[permuted(recv[j][h], across) for h in range(2)] for j in range(hk)]
     got, last = [], None
     for j in range(hk):
         for h in range(2):
             last = sources(
-                odd, weights, j, h, hk, keep[j][h], recv[j][h], kz[j][h], rz[j][h], last)
+                odd, modes, j, h, hk, keep[j][h], recv[j][h], kz[j][h], rz[j][h], last)
         got.append(last)
 
     full, turned = place_coupling(jnp.stack([mine ^ o for o in order]), coupling_pieces)
@@ -474,11 +475,11 @@
         back = [spread(over_energy(part[le + e], pairs)) for part in use]
         pieces = [part[at] for at in range(nm) for part in fresh + back]
         if e < le - 1:
-            x, y = home_blocks(own_slots, pieces, full, turned, lk)
+            x, y = home_blocks(mine, slots, pieces, full, turned, lk)
             held_density = first_density(e, green_ret, broadening, x, y, held_density)
         else:
             shares = []
-            x, y = home_blocks(own_slots, pieces, full, turned, lk)
+            x, y = home_blocks(mine, slots, pieces, full, turned, lk)
             for first, count in ((0, 1), (1, lk - 1)):
                 shares = shares + list(last_density(
                     scale, e, first, count, groups, odd,
@@ -492,7 +493,7 @@
                     perm = [(i, (i + 2 * d) % ne) for i in range(ne)]
                     total = total + permuted(parts[d], perm).astype(F32)
                 late.append(total)
-        held_rows = own_rows(mine, all_slots, pieces, coupling, e, le, held_rows)
+        held_rows = own_rows(mine, slots, pieces, coupling, e, le, held_rows)
     density = jnp.transpose(jnp.stack(late), (2, 0, 1, 3))
     return held_rows, density
 

time: 331 us -> 335 us (1.012)
  waiting for transfers between devices: 116 us -> 123 us
  other arithmetic: 5.92 us -> 1.03 us
    ppermute x31, waiting for transfers between devices: 53.5 us -> 60.1 us  [permuted(): return lax.ppermute(x, 'energy', perm)]
    unnamed x67 -> x77, local copies, waits for them, and re-layouts: 6.75 us -> 10 us
  transfers between devices with their start and end apart: 52 -> 52, of which waited for: 17 -> 17; matrix products, arithmetic and copies ran while one was open for 2% -> 0% of each run, Pallas kernels for 31% -> 30%
where the time goes in v6:
time: 335 us; the launch traced here: 334 us
  Pallas kernels  124 us (37%)
  waiting for transfers between devices  123 us (37%)
  starting transfers between devices  74.9 us (22%)
  local copies, waits for them, and re-layouts  10 us (3%)
    ppermute x31, starting transfers between devices, permuted(): return lax.ppermute(x, 'energy', perm)  63.5 us
    ppermute x21, waiting for transfers between devices, swap(): moved = lax.ppermute(x, 'mom', [(i, i ^ stride) for i in range(nm)])  62.7 us
    ppermute x31, waiting for transfers between devices, permuted(): return lax.ppermute(x, 'energy', perm)  60.1 us
    pallas_call x2, Pallas kernels, own_rows(): pl.pallas_call(functools.partial(rows_kernel, len(pieces)), out_shape=jax...  25.9 us
    pallas_call x2, Pallas kernels, home_blocks(): pl.pallas_call(functools.partial(home_kernel, lk, len(pieces)), out_shape...  25.9 us
    pallas_call x4, Pallas kernels, lesser_packed(): pl.pallas_call(lesser_kernel, out_shape=[pltpu.HBM((le, n // 2, n), BF16)...  16.5 us
    pallas_call x2, Pallas kernels, last_density(): pl.pallas_call(functools.partial(last_density_kernel, scale, energy), out...  16.3 us
    pallas_call x4, Pallas kernels, sources(): pl.pallas_call(source_kernel, out_shape=[pltpu.HBM(shape, BF16) for shape...  13.2 us
  transfers between devices with their start and end apart: 52, of which 17 were waited for; matrix products, arithmetic and copies ran while one was open for 0% of the time, Pallas kernels for 30%

profile of v6, /device:TPU:0, one launch (start us, length us, event | category | flops | bytes accessed | tf_op | source)
XLA Modules:
  0.0 333.9 jit_solution(12784213799960418699)
XLA Ops:
  0.6 4.1 %lesser.7 = (bf16[2,256,512]{2,1,0:T(8,128)(2,1)}, bf16[2,256,512]{2,1,0:T(8,128)(2,1)}) custom-call(s32[1]{0:T(128)} %bitcast.5.sel, bf16[4,2,2,512,512]{4,3,2,1,0:T(8,128)(2,1)} %g_ref.13, f32[4,2,512]{2,1,0:T(2,128)} %gamma_ref.13), custom_call_target="tpu_custom_call" | custom-call | flops 1610612736 | bytes 3145728 | tf_op jit(solution)/shard_map/lesser/pallas_call | solution.py:66
  4.8 3.0 collective-permute-start.9
  7.8 4.1 %lesser.6 = (bf16[2,256,512]{2,1,0:T(8,128)(2,1)}, bf16[2,256,512]{2,1,0:T(8,128)(2,1)}) custom-call(s32[1]{0:T(128)} %bitcast.4.sel, bf16[4,2,2,512,512]{4,3,2,1,0:T(8,128)(2,1)} %g_ref.13, f32[4,2,512]{2,1,0:T(2,128)} %gamma_ref.13), custom_call_target="tpu_custom_call" | custom-call | flops 1610612736 | bytes 3145728 | tf_op jit(solution)/shard_map/lesser/pallas_call | solution.py:66
  13.2 2.8 collective-permute-start.6
  17.2 4.1 %lesser.5 = (bf16[2,256,512]{2,1,0:T(8,128)(2,1)}, bf16[2,256,512]{2,1,0:T(8,128)(2,1)}) custom-call(s32[1]{0:T(128)} %bitcast.3.sel, bf16[4,2,2,512,512]{4,3,2,1,0:T(8,128)(2,1)} %g_ref.13, f32[4,2,512]{2,1,0:T(2,128)} %gamma_ref.13), custom_call_target="tpu_custom_call" | custom-call | flops 1610612736 | bytes 3145728 | tf_op jit(solution)/shard_map/lesser/pallas_call | solution.py:66
  21.4 2.6 collective-permute-start.3
  24.0 4.7 %collective-permute-done.10.kz = bf16[2,256,512]{2,1,0:T(8,128)(2,1)S(1)} collective-permute-done((bf16[2,256,512]{2,1,0:T(8,128)(2,1)}, bf16[2,256,512]{2,1,0:T(8,128)(2,1)S(1)}, u32[]{:S(2)}, u32[]{:S(2)}) %collective-permute-start.10) | collective-permute-done | bytes 524320 | tf_op jit(solution)/shard_map/ppermute | solution.py:424
  28.7 3.5 %collective-permute-start.11 = (bf16[2,256,512]{2,1,0:T(8,128)(2,1)S(1)}, bf16[2,256,512]{2,1,0:T(8,128)(2,1)S(1)}, u32[]{:S(2)}, u32[]{:S(2)}) collective-permute-start(bf16[2,256,512]{2,1,0:T(8,128)(2,1)S(1)} %collective-permute-done.9.recv), channel_id=1, source_target_pairs={{0,8},{8,16},{12,4},{16,24},{20,12},{28,20},{1,9},{9,17},{13,5},{1... | collective-permute-start | bytes 1572872 | tf_op jit(solution)/shard_map/ppermute | solution.py:424
  32.3 4.5 %collective-permute-start.8 = (bf16[2,256,512]{2,1,0:T(8,128)(2,1)S(1)}, bf16[2,256,512]{2,1,0:T(8,128)(2,1)}, u32[]{:S(2)}, u32[]{:S(2)}) collective-permute-start(bf16[2,256,512]{2,1,0:T(8,128)(2,1)S(1)} %collective-permute-done.6.recv), channel_id=1, source_target_pairs={{0,8},{8,16},{12,4},{16,24},{20,12},{28,20},{1,9},{9,17},{13,5},{1... | collective-permute-start | bytes 1572872 | tf_op jit(solution)/shard_map/ppermute | solution.py:424
  36.8 1.8 collective-permute-done.7.kz
  40.1 4.2 %lesser.4 = (bf16[2,256,512]{2,1,0:T(8,128)(2,1)}, bf16[2,256,512]{2,1,0:T(8,128)(2,1)}) custom-call(s32[1]{0:T(128)} %bitcast.2.sel, bf16[4,2,2,512,512]{4,3,2,1,0:T(8,128)(2,1)} %g_ref.13, f32[4,2,512]{2,1,0:T(2,128)} %gamma_ref.13), custom_call_target="tpu_custom_call" | custom-call | flops 1610612736 | bytes 3145728 | tf_op jit(solution)/shard_map/lesser/pallas_call | solution.py:66
  45.7 7.9 %collective-permute-done.recv = bf16[2,256,512]{2,1,0:T(8,128)(2,1)S(1)} collective-permute-done((bf16[2,256,512]{2,1,0:T(8,128)(2,1)}, bf16[2,256,512]{2,1,0:T(8,128)(2,1)S(1)}, u32[]{:S(2)}, u32[]{:S(2)}) %collective-permute-start) | collective-permute-done | bytes 524320 | tf_op jit(solution)/shard_map/ppermute | solution.py:424
  53.6 3.7 %collective-permute-start.5 = (bf16[2,256,512]{2,1,0:T(8,128)(2,1)}, bf16[2,256,512]{2,1,0:T(8,128)(2,1)S(1)}, u32[]{:S(2)}, u32[]{:S(2)}) collective-permute-start(bf16[2,256,512]{2,1,0:T(8,128)(2,1)} %collective-permute-done.3.recv), channel_id=1, source_target_pairs={{0,8},{8,16},{12,4},{16,24},{20,12},{28,20},{1,9},{9,17},{13,5},{1... | collective-permute-start | bytes 1572872 | tf_op jit(solution)/shard_map/ppermute | solution.py:424
  59.5 4.8 %collective-permute-start.2 = (bf16[2,256,512]{2,1,0:T(8,128)(2,1)S(1)}, bf16[2,256,512]{2,1,0:T(8,128)(2,1)S(1)}, u32[]{:S(2)}, u32[]{:S(2)}) collective-permute-start(bf16[2,256,512]{2,1,0:T(8,128)(2,1)S(1)} %collective-permute-done.recv), channel_id=1, source_target_pairs={{0,8},{8,16},{12,4},{16,24},{20,12},{28,20},{1,9},{9,17},{13,5},{1... | collective-permute-start | bytes 1572872 | tf_op jit(solution)/shard_map/ppermute | solution.py:424
  64.3 3.3 source.4
  67.6 3.3 source.5
  71.7 3.3 source.6
  75.0 4.2 %collective-permute-done.2.rz = bf16[2,256,512]{2,1,0:T(8,128)(2,1)S(1)} collective-permute-done((bf16[2,256,512]{2,1,0:T(8,128)(2,1)S(1)}, bf16[2,256,512]{2,1,0:T(8,128)(2,1)S(1)}, u32[]{:S(2)}, u32[]{:S(2)}) %collective-permute-start.2) | collective-permute-done | bytes 524320 | tf_op jit(solution)/shard_map/ppermute | solution.py:424
  80.0 3.3 source.7
  83.3 2.4 collective-permute-start.20
  87.2 11.4 %collective-permute-done.20.refs_3_.refs_19_ = bf16[1,512,512]{2,1,0:T(8,128)(2,1)S(1)} collective-permute-done((bf16[1,512,512]{2,1,0:T(8,128)(2,1)}, bf16[1,512,512]{2,1,0:T(8,128)(2,1)S(1)}, u32[]{:S(2)}, u32[]{:S(2)}) %collective-permute-start.20) | collective-permute-done | bytes 524320 | tf_op jit(solution)/shard_map/ppermute | solution.py:424
  100.8 6.8 %collective-permute-done.19.refs_2_.refs_18_ = bf16[1,512,512]{2,1,0:T(8,128)(2,1)S(1)} collective-permute-done((bf16[1,512,512]{2,1,0:T(8,128)(2,1)S(1)}, bf16[1,512,512]{2,1,0:T(8,128)(2,1)S(1)}, u32[]{:S(2)}, u32[]{:S(2)}) %collective-permute-start.19) | collective-permute-done | bytes 524320 | tf_op jit(solution)/shard_map/ppermute | solution.py:424
  107.5 5.9 %collective-permute-done.21.refs_4_.refs_20_ = bf16[1,512,512]{2,1,0:T(8,128)(2,1)S(1)} collective-permute-done((bf16[1,512,512]{2,1,0:T(8,128)(2,1)S(1)}, bf16[1,512,512]{2,1,0:T(8,128)(2,1)S(1)}, u32[]{:S(2)}, u32[]{:S(2)}) %collective-permute-start.21) | collective-permute-done | bytes 524320 | tf_op jit(solution)/shard_map/ppermute | solution.py:430
  114.0 6.4 %collective-permute-done.24.refs_7_.refs_23_ = bf16[1,512,512]{2,1,0:T(8,128)(2,1)} collective-permute-done((bf16[1,512,512]{2,1,0:T(8,128)(2,1)S(1)}, bf16[1,512,512]{2,1,0:T(8,128)(2,1)}, u32[]{:S(2)}, u32[]{:S(2)}) %collective-permute-start.24) | collective-permute-done | bytes 524320 | tf_op jit(solution)/shard_map/ppermute | solution.py:430
  122.9 12.7 %collective-permute-done.23.refs_6_.refs_22_ = bf16[1,512,512]{2,1,0:T(8,128)(2,1)} collective-permute-done((bf16[1,512,512]{2,1,0:T(8,128)(2,1)S(1)}, bf16[1,512,512]{2,1,0:T(8,128)(2,1)}, u32[]{:S(2)}, u32[]{:S(2)}) %collective-permute-start.23) | collective-permute-done | bytes 524320 | tf_op jit(solution)/shard_map/ppermute | solution.py:430
  137.2 4.1 %collective-permute-done.12.refs_1_.refs_9_ = bf16[2,512,512]{2,1,0:T(8,128)(2,1)S(1)} collective-permute-done((bf16[2,512,512]{2,1,0:T(8,128)(2,1)}, bf16[2,512,512]{2,1,0:T(8,128)(2,1)S(1)}, u32[]{:S(2)}, u32[]{:S(2)}) %collective-permute-start.12) | collective-permute-done | bytes 1048608 | tf_op jit(solution)/shard_map/ppermute | solution.py:424
  144.9 17.1 %collective-permute-done.13.refs_2_.refs_10_ = bf16[2,512,512]{2,1,0:T(8,128)(2,1)} collective-permute-done((bf16[2,512,512]{2,1,0:T(8,128)(2,1)}, bf16[2,512,512]{2,1,0:T(8,128)(2,1)}, u32[]{:S(2)}, u32[]{:S(2)}) %collective-permute-start.13) | collective-permute-done | bytes 1048608 | tf_op jit(solution)/shard_map/ppermute | solution.py:430
  162.5 20.6 %collective-permute-done.14.refs_3_.refs_11_ = bf16[2,512,512]{2,1,0:T(8,128)(2,1)} collective-permute-done((bf16[2,512,512]{2,1,0:T(8,128)(2,1)S(1)}, bf16[2,512,512]{2,1,0:T(8,128)(2,1)}, u32[]{:S(2)}, u32[]{:S(2)}) %collective-permute-start.14) | collective-permute-done | bytes 1048608 | tf_op jit(solution)/shard_map/ppermute | solution.py:430
  184.3 11.8 %place.1 = (bf16[16,512,512]{2,1,0:T(8,128)(2,1)}, bf16[16,512,512]{2,1,0:T(8,128)(2,1)}) custom-call(s32[4]{0:T(128)} %pad_add_fusion.where, bf16[16,128,512]{2,1,0:T(8,128)(2,1)} %refs_0_.1, bf16[16,128,512]{2,1,0:T(8,128)(2,1)} %collective-permute-done.33.refs_1_, bf16[16,128,512]{2,1,0:T(8,128)(2,1)} %copy-done.29, ...), custom_call_target="tpu_custom_call" | custom-call | flops 16777216 | bytes 25165824 | tf_op jit(solution)/shard_map/place/pallas_call | solution.py:97
  196.2 12.9 %home.3 = (bf16[4,512,512]{2,1,0:T(8,128)(2,1)S(1)}, bf16[4,512,512]{2,1,0:T(8,128)(2,1)S(1)}) custom-call(s32[1]{0:T(128)} %bitcast.mine, s32[16,16]{1,0:T(8,128)S(1)} %fusion.4.slots, bf16[1,512,512]{2,1,0:T(8,128)(2,1)S(1)} %copy-done.2, bf16[1,512,512]{2,1,0:T(8,128)(2,1)S(1)} %copy-done.1, bf16[1,512,512]{2,1,0:T(8,128)(2,1)} %copy-done.22, ...), custom_call_target="tpu_custom_call" | custom-call | flops 67108864 | bytes 29360128 | tf_op jit(solution)/shard_map/home/pallas_call | solution.py:215
  209.2 12.7 %density.3.held_ref = f32[4,2,512,512]{3,2,1,0:T(8,128)} custom-call(bf16[4,2,2,512,512]{4,3,2,1,0:T(8,128)(2,1)} %g_ref.13, f32[4,2,512]{2,1,0:T(2,128)S(1)} %copy-done.9, bf16[4,512,512]{2,1,0:T(8,128)(2,1)S(1)} %get-tuple-element.84.x_ref, bf16[4,512,512]{2,1,0:T(8,128)(2,1)S(1)} %get-tuple-element.85.y_ref), custom_call_target="tpu_custom_call" | custom-call | flops 8589934592 | bytes 20971520 | tf_op jit(solution)/shard_map/density/pallas_call | solution.py:325
  224.6 12.9 %home.2 = (bf16[4,512,512]{2,1,0:T(8,128)(2,1)S(1)}, bf16[4,512,512]{2,1,0:T(8,128)(2,1)S(1)}) custom-call(s32[1]{0:T(128)} %bitcast.mine, s32[16,16]{1,0:T(8,128)S(1)} %fusion.4.slots, bf16[2,512,512]{2,1,0:T(8,128)(2,1)S(1)} %copy-done, bf16[2,512,512]{2,1,0:T(8,128)(2,1)} %copy-done.14, bf16[2,512,512]{2,1,0:T(8,128)(2,1)} %collective-permute-done.13.refs_2_.refs_10_, ...), custom_call_target="tpu_custom_call" | custom-call | flops 67108864 | bytes 29360128 | tf_op jit(solution)/shard_map/home/pallas_call | solution.py:215
  237.6 5.3 %density.4 = (bf16[4,2,64,512]{3,2,1,0:T(8,128)(2,1)S(1)}, bf16[4,2,64,512]{3,2,1,0:T(8,128)(2,1)}) custom-call(s32[1]{0:T(128)} %bitcast.1.odd, bf16[4,2,2,512,512]{4,3,2,1,0:T(8,128)(2,1)} %g_ref.13, f32[4,2,512]{2,1,0:T(2,128)S(1)} %copy-done.9, bf16[4,512,512]{2,1,0:T(8,128)(2,1)S(1)} %get-tuple-element.82.x_ref, ...), custom_call_target="tpu_custom_call" | custom-call | flops 2147483648 | bytes 5242880 | tf_op jit(solution)/shard_map/density/pallas_call | solution.py:365
  244.1 11.0 %density.5 = (bf16[4,2,64,512]{3,2,1,0:T(8,128)(2,1)S(1)}, bf16[4,2,64,512]{3,2,1,0:T(8,128)(2,1)}, bf16[4,2,64,512]{3,2,1,0:T(8,128)(2,1)S(1)}, bf16[4,2,64,512...) custom-call(s32[1]{0:T(128)} %bitcast.1.odd, ...), custom_call_target="tpu_custom_call" | custom-call | flops 6442450944 | bytes 15728640 | tf_op jit(solution)/shard_map/density/pallas_call | solution.py:365
  261.8 2.2 collective-permute-start.38
  264.0 6.0 %collective-permute-done.40.recv_ref = bf16[4,2,64,512]{3,2,1,0:T(8,128)(2,1)S(1)} collective-permute-done((bf16[4,2,64,512]{3,2,1,0:T(8,128)(2,1)}, bf16[4,2,64,512]{3,2,1,0:T(8,128)(2,1)S(1)}, u32[]{:S(2)}, u32[]{:S(2)}) %collective-permute-start.40) | collective-permute-done | bytes 524320 | tf_op jit(solution)/shard_map/ppermute | solution.py:424
  270.1 2.9 collective-permute-start.39
  273.0 13.1 %rows.2.refs_17_ = bf16[16,2,2,128,512]{4,3,2,1,0:T(8,128)(2,1)} custom-call(s32[1]{0:T(128)} %bitcast.mine, s32[16,16]{1,0:T(8,128)} %copy-done.10, bf16[1,512,512]{2,1,0:T(8,128)(2,1)} %get-tuple-element.76.refs_0_.refs_16_, bf16[1,512,512]{2,1,0:T(8,128)(2,1)} %get-tuple-element.77.refs_1_.refs_17_, bf16[1,512,512]{2,1,0:T(8,128)(2,1)} %copy-done.22, ...), custom_call_target="tpu_custom_call" | custom-call | flops 67108864 | bytes 10485760 | tf_op jit(solution)/shard_map/rows/pallas_call | solution.py:283
  286.1 12.8 %rows.3 = bf16[16,2,2,128,512]{4,3,2,1,0:T(8,128)(2,1)} custom-call(s32[1]{0:T(128)} %bitcast.mine, s32[16,16]{1,0:T(8,128)} %copy-done.10, bf16[2,512,512]{2,1,0:T(8,128)(2,1)} %get-tuple-element.74.refs_0_.refs_8_, bf16[2,512,512]{2,1,0:T(8,128)(2,1)} %copy-done.14, ...), custom_call_target="tpu_custom_call", output_to_operand_aliasing={{}: (19, {})} | custom-call | flops 67108864 | bytes 10485760 | tf_op jit(solution)/shard_map/rows/pallas_call | solution.py:283
  299.3 1.7 collective-permute-start.42
  301.2 2.2 collective-permute-start.43
  305.5 1.9 collective-permute-done.41
  309.1 3.2 collective-permute-done.42
  312.3 2.2 collective-permute-start.49
  314.5 5.6 %collective-permute-start.50 = (bf16[2,64,512]{2,1,0:T(8,128)(2,1)S(1)}, bf16[2,64,512]{2,1,0:T(8,128)(2,1)S(1)}, u32[]{:S(2)}, u32[]{:S(2)}) collective-permute-start(bf16[2,64,512]{2,1,0:T(8,128)(2,1)S(1)} %get-tuple-element.108), channel_id=1, source_target_pairs={{0,16},{4,20},{8,24},{12,28},{16,0},{20,4},{24,8},{28,12},{1,17},{... | collective-permute-start | bytes 393224 | tf_op jit(solution)/shard_map/ppermute | solution.py:424
  320.2 3.6 %collective-permute-start.51 = (bf16[2,64,512]{2,1,0:T(8,128)(2,1)S(1)}, bf16[2,64,512]{2,1,0:T(8,128)(2,1)S(1)}, u32[]{:S(2)}, u32[]{:S(2)}) collective-permute-start(bf16[2,64,512]{2,1,0:T(8,128)(2,1)S(1)} %get-tuple-element.109), channel_id=1, source_target_pairs={{0,24},{4,28},{8,0},{12,4},{16,8},{20,12},{24,16},{28,20},{1,25},{... | collective-permute-start | bytes 393224 | tf_op jit(solution)/shard_map/ppermute | solution.py:424
  325.0 6.9 %collective-permute-done.50 = bf16[2,64,512]{2,1,0:T(8,128)(2,1)S(1)} collective-permute-done((bf16[2,64,512]{2,1,0:T(8,128)(2,1)S(1)}, bf16[2,64,512]{2,1,0:T(8,128)(2,1)S(1)}, u32[]{:S(2)}, u32[]{:S(2)}) %collective-permute-start.50) | collective-permute-done | bytes 131104 | tf_op jit(solution)/shard_map/ppermute | solution.py:424
  332.1 1.8 copy.20
  (160 shorter events, 39.2 us)
Async XLA Ops:
  4.8 19.2 %collective-permute-start.9 = (bf16[2,256,512]{2,1,0:T(8,128)(2,1)}, bf16[2,256,512]{2,1,0:T(8,128)(2,1)S(1)}, u32[]{:S(2)}, u32[]{:S(2)}) collective-permute-start(bf16[2,256,512]{2,1,0:T(8,128)(2,1)} %get-tuple-element.63), channel_id=1, source_target_pairs={{0,4},{4,0},{8,12},{12,8},{16,20},{20,16},{24,28},{28,24},{1,5},{5... | collective-permute-start | bytes 1572872 | tf_op jit(solution)/shard_map/ppermute | solution.py:424
  11.9 16.9 %collective-permute-start.10 = (bf16[2,256,512]{2,1,0:T(8,128)(2,1)}, bf16[2,256,512]{2,1,0:T(8,128)(2,1)S(1)}, u32[]{:S(2)}, u32[]{:S(2)}) collective-permute-start(bf16[2,256,512]{2,1,0:T(8,128)(2,1)} %get-tuple-element.62.keep), channel_id=1, source_target_pairs={{4,12},{8,0},{12,20},{16,8},{20,28},{24,16},{5,13},{9,1},{13,21},{... | collective-permute-start | bytes 1572872 | tf_op jit(solution)/shard_map/ppermute | solution.py:424
  13.2 19.1 %collective-permute-start.6 = (bf16[2,256,512]{2,1,0:T(8,128)(2,1)}, bf16[2,256,512]{2,1,0:T(8,128)(2,1)S(1)}, u32[]{:S(2)}, u32[]{:S(2)}) collective-permute-start(bf16[2,256,512]{2,1,0:T(8,128)(2,1)} %get-tuple-element.61), channel_id=1, source_target_pairs={{0,4},{4,0},{8,12},{12,8},{16,20},{20,16},{24,28},{28,24},{1,5},{5... | collective-permute-start | bytes 1572872 | tf_op jit(solution)/shard_map/ppermute | solution.py:424
  15.9 22.6 %collective-permute-start.7 = (bf16[2,256,512]{2,1,0:T(8,128)(2,1)}, bf16[2,256,512]{2,1,0:T(8,128)(2,1)S(1)}, u32[]{:S(2)}, u32[]{:S(2)}) collective-permute-start(bf16[2,256,512]{2,1,0:T(8,128)(2,1)} %get-tuple-element.60.keep), channel_id=1, source_target_pairs={{4,12},{8,0},{12,20},{16,8},{20,28},{24,16},{5,13},{9,1},{13,21},{... | collective-permute-start | bytes 1572872 | tf_op jit(solution)/shard_map/ppermute | solution.py:424
  21.4 22.9 %collective-permute-start.3 = (bf16[2,256,512]{2,1,0:T(8,128)(2,1)}, bf16[2,256,512]{2,1,0:T(8,128)(2,1)}, u32[]{:S(2)}, u32[]{:S(2)}) collective-permute-start(bf16[2,256,512]{2,1,0:T(8,128)(2,1)} %get-tuple-element.59), channel_id=1, source_target_pairs={{0,4},{4,0},{8,12},{12,8},{16,20},{20,16},{24,28},{28,24},{1,5},{5... | collective-permute-start | bytes 1572872 | tf_op jit(solution)/shard_map/ppermute | solution.py:424
  23.9 29.6 %collective-permute-start = (bf16[2,256,512]{2,1,0:T(8,128)(2,1)}, bf16[2,256,512]{2,1,0:T(8,128)(2,1)S(1)}, u32[]{:S(2)}, u32[]{:S(2)}) collective-permute-start(bf16[2,256,512]{2,1,0:T(8,128)(2,1)} %get-tuple-element.57), channel_id=1, source_target_pairs={{0,4},{4,0},{8,12},{12,8},{16,20},{20,16},{24,28},{28,24},{1,5},{5... | collective-permute-start | bytes 1572872 | tf_op jit(solution)/shard_map/ppermute | solution.py:424
  28.7 28.6 %collective-permute-start.11 = (bf16[2,256,512]{2,1,0:T(8,128)(2,1)S(1)}, bf16[2,256,512]{2,1,0:T(8,128)(2,1)S(1)}, u32[]{:S(2)}, u32[]{:S(2)}) collective-permute-start(bf16[2,256,512]{2,1,0:T(8,128)(2,1)S(1)} %collective-permute-done.9.recv), channel_id=1, source_target_pairs={{0,8},{8,16},{12,4},{16,24},{20,12},{28,20},{1,9},{9,17},{13,5},{1... | collective-permute-start | bytes 1572872 | tf_op jit(solution)/shard_map/ppermute | solution.py:424
  32.3 27.2 %collective-permute-start.8 = (bf16[2,256,512]{2,1,0:T(8,128)(2,1)S(1)}, bf16[2,256,512]{2,1,0:T(8,128)(2,1)}, u32[]{:S(2)}, u32[]{:S(2)}) collective-permute-start(bf16[2,256,512]{2,1,0:T(8,128)(2,1)S(1)} %collective-permute-done.6.recv), channel_id=1, source_target_pairs={{0,8},{8,16},{12,4},{16,24},{20,12},{28,20},{1,9},{9,17},{13,5},{1... | collective-permute-start | bytes 1572872 | tf_op jit(solution)/shard_map/ppermute | solution.py:424
  38.6 82.6 %collective-permute-start.33 = (bf16[16,128,512]{2,1,0:T(8,128)(2,1)}, bf16[16,128,512]{2,1,0:T(8,128)(2,1)}, u32[]{:S(2)}, u32[]{:S(2)}) collective-permute-start(bf16[16,128,512]{2,1,0:T(8,128)(2,1)} %refs_0_.1), channel_id=1, source_target_pairs={{0,2},{1,3},{2,0},{3,1},{4,6},{5,7},{6,4},{7,5},{8,10},{9,11},{10,... | collective-permute-start | bytes 6291464 | tf_op jit(solution)/shard_map/ppermute | solution.py:430
  44.3 26.6 %collective-permute-start.4 = (bf16[2,256,512]{2,1,0:T(8,128)(2,1)}, bf16[2,256,512]{2,1,0:T(8,128)(2,1)S(1)}, u32[]{:S(2)}, u32[]{:S(2)}) collective-permute-start(bf16[2,256,512]{2,1,0:T(8,128)(2,1)} %get-tuple-element.58.keep), channel_id=1, source_target_pairs={{4,12},{8,0},{12,20},{16,8},{20,28},{24,16},{5,13},{9,1},{13,21},{... | collective-permute-start | bytes 1572872 | tf_op jit(solution)/shard_map/ppermute | solution.py:424
  53.6 17.3 %collective-permute-start.5 = (bf16[2,256,512]{2,1,0:T(8,128)(2,1)}, bf16[2,256,512]{2,1,0:T(8,128)(2,1)S(1)}, u32[]{:S(2)}, u32[]{:S(2)}) collective-permute-start(bf16[2,256,512]{2,1,0:T(8,128)(2,1)} %collective-permute-done.3.recv), channel_id=1, source_target_pairs={{0,8},{8,16},{12,4},{16,24},{20,12},{28,20},{1,9},{9,17},{13,5},{1... | collective-permute-start | bytes 1572872 | tf_op jit(solution)/shard_map/ppermute | solution.py:424
  58.2 16.8 %collective-permute-start.1 = (bf16[2,256,512]{2,1,0:T(8,128)(2,1)}, bf16[2,256,512]{2,1,0:T(8,128)(2,1)S(1)}, u32[]{:S(2)}, u32[]{:S(2)}) collective-permute-start(bf16[2,256,512]{2,1,0:T(8,128)(2,1)} %get-tuple-element.56.keep), channel_id=1, source_target_pairs={{4,12},{8,0},{12,20},{16,8},{20,28},{24,16},{5,13},{9,1},{13,21},{... | collective-permute-start | bytes 1572872 | tf_op jit(solution)/shard_map/ppermute | solution.py:424
  59.5 19.7 %collective-permute-start.2 = (bf16[2,256,512]{2,1,0:T(8,128)(2,1)S(1)}, bf16[2,256,512]{2,1,0:T(8,128)(2,1)S(1)}, u32[]{:S(2)}, u32[]{:S(2)}) collective-permute-start(bf16[2,256,512]{2,1,0:T(8,128)(2,1)S(1)} %collective-permute-done.recv), channel_id=1, source_target_pairs={{0,8},{8,16},{12,4},{16,24},{20,12},{28,20},{1,9},{9,17},{13,5},{1... | collective-permute-start | bytes 1572872 | tf_op jit(solution)/shard_map/ppermute | solution.py:424
  83.3 15.4 %collective-permute-start.20 = (bf16[1,512,512]{2,1,0:T(8,128)(2,1)}, bf16[1,512,512]{2,1,0:T(8,128)(2,1)S(1)}, u32[]{:S(2)}, u32[]{:S(2)}) collective-permute-start(bf16[1,512,512]{2,1,0:T(8,128)(2,1)} %get-tuple-element.79), channel_id=1, source_target_pairs={{0,4},{4,0},{8,12},{12,8},{16,20},{20,16},{24,28},{28,24},{1,5},{5... | collective-permute-start | bytes 1572872 | tf_op jit(solution)/shard_map/ppermute | solution.py:424
  85.7 14.5 %collective-permute-start.22 = (bf16[1,512,512]{2,1,0:T(8,128)(2,1)}, bf16[1,512,512]{2,1,0:T(8,128)(2,1)S(1)}, u32[]{:S(2)}, u32[]{:S(2)}) collective-permute-start(bf16[1,512,512]{2,1,0:T(8,128)(2,1)} %get-tuple-element.77.refs_1_.refs_17_), channel_id=1, source_target_pairs={{0,2},{1,3},{2,0},{3,1},{4,6},{5,7},{6,4},{7,5},{8,10},{9,11},{10,... | collective-permute-start | bytes 1572872 | tf_op jit(solution)/shard_map/ppermute | solution.py:430
  87.2 13.0 %collective-permute-start.26 = (bf16[1,512,512]{2,1,0:T(8,128)(2,1)}, bf16[1,512,512]{2,1,0:T(8,128)(2,1)S(1)}, u32[]{:S(2)}, u32[]{:S(2)}) collective-permute-start(bf16[1,512,512]{2,1,0:T(8,128)(2,1)} %get-tuple-element.77.refs_1_.refs_17_), channel_id=1, source_target_pairs={{0,1},{1,0},{2,3},{3,2},{4,5},{5,4},{6,7},{7,6},{8,9},{9,8},{10,11... | collective-permute-start | bytes 1572872 | tf_op jit(solution)/shard_map/ppermute | solution.py:430
  87.2 20.4 %collective-permute-start.19 = (bf16[1,512,512]{2,1,0:T(8,128)(2,1)S(1)}, bf16[1,512,512]{2,1,0:T(8,128)(2,1)S(1)}, u32[]{:S(2)}, u32[]{:S(2)}) collective-permute-start(bf16[1,512,512]{2,1,0:T(8,128)(2,1)S(1)} %copy-done.35), channel_id=1, source_target_pairs={{0,4},{4,0},{8,12},{12,8},{16,20},{20,16},{24,28},{28,24},{1,5},{5... | collective-permute-start | bytes 1572872 | tf_op jit(solution)/shard_map/ppermute | solution.py:424
  98.7 14.8 %collective-permute-start.21 = (bf16[1,512,512]{2,1,0:T(8,128)(2,1)S(1)}, bf16[1,512,512]{2,1,0:T(8,128)(2,1)S(1)}, u32[]{:S(2)}, u32[]{:S(2)}) collective-permute-start(bf16[1,512,512]{2,1,0:T(8,128)(2,1)S(1)} %copy-done.2), channel_id=1, source_target_pairs={{0,2},{1,3},{2,0},{3,1},{4,6},{5,7},{6,4},{7,5},{8,10},{9,11},{10,... | collective-permute-start | bytes 1572872 | tf_op jit(solution)/shard_map/ppermute | solution.py:430
  100.1 13.3 %collective-permute-start.25 = (bf16[1,512,512]{2,1,0:T(8,128)(2,1)S(1)}, bf16[1,512,512]{2,1,0:T(8,128)(2,1)S(1)}, u32[]{:S(2)}, u32[]{:S(2)}) collective-permute-start(bf16[1,512,512]{2,1,0:T(8,128)(2,1)S(1)} %copy-done.2), channel_id=1, source_target_pairs={{0,1},{1,0},{2,3},{3,2},{4,5},{5,4},{6,7},{7,6},{8,9},{9,8},{10,11... | collective-permute-start | bytes 1572872 | tf_op jit(solution)/shard_map/ppermute | solution.py:430
  100.2 20.2 %collective-permute-start.24 = (bf16[1,512,512]{2,1,0:T(8,128)(2,1)S(1)}, bf16[1,512,512]{2,1,0:T(8,128)(2,1)}, u32[]{:S(2)}, u32[]{:S(2)}) collective-permute-start(bf16[1,512,512]{2,1,0:T(8,128)(2,1)S(1)} %collective-permute-done.20.refs_3_.refs_19_), channel_id=1, source_target_pairs={{0,2},{1,3},{2,0},{3,1},{4,6},{5,7},{6,4},{7,5},{8,10},{9,11},{10,... | collective-permute-start | bytes 1572872 | tf_op jit(solution)/shard_map/ppermute | solution.py:430
  107.5 35.3 %collective-permute-start.34 = (bf16[16,128,512]{2,1,0:T(8,128)(2,1)}, bf16[16,128,512]{2,1,0:T(8,128)(2,1)S(1)}, u32[]{:S(2)}, u32[]{:S(2)}) collective-permute-start(bf16[16,128,512]{2,1,0:T(8,128)(2,1)} %refs_0_.1), channel_id=1, source_target_pairs={{0,1},{1,0},{2,3},{3,2},{4,5},{5,4},{6,7},{7,6},{8,9},{9,8},{10,11... | collective-permute-start | bytes 6291464 | tf_op jit(solution)/shard_map/ppermute | solution.py:430
  120.3 20.9 %collective-permute-start.12 = (bf16[2,512,512]{2,1,0:T(8,128)(2,1)}, bf16[2,512,512]{2,1,0:T(8,128)(2,1)S(1)}, u32[]{:S(2)}, u32[]{:S(2)}) collective-permute-start(bf16[2,512,512]{2,1,0:T(8,128)(2,1)} %get-tuple-element.75), channel_id=1, source_target_pairs={{0,4},{4,0},{8,12},{12,8},{16,20},{20,16},{24,28},{28,24},{1,5},{5... | collective-permute-start | bytes 3145736 | tf_op jit(solution)/shard_map/ppermute | solution.py:424
  121.2 61.9 %collective-permute-start.35 = (bf16[16,128,512]{2,1,0:T(8,128)(2,1)}, bf16[16,128,512]{2,1,0:T(8,128)(2,1)}, u32[]{:S(2)}, u32[]{:S(2)}) collective-permute-start(bf16[16,128,512]{2,1,0:T(8,128)(2,1)} %collective-permute-done.33.refs_1_), channel_id=1, source_target_pairs={{0,1},{1,0},{2,3},{3,2},{4,5},{5,4},{6,7},{7,6},{8,9},{9,8},{10,11... | collective-permute-start | bytes 6291464 | tf_op jit(solution)/shard_map/ppermute | solution.py:430
  121.2 14.4 %collective-permute-start.23 = (bf16[1,512,512]{2,1,0:T(8,128)(2,1)S(1)}, bf16[1,512,512]{2,1,0:T(8,128)(2,1)}, u32[]{:S(2)}, u32[]{:S(2)}) collective-permute-start(bf16[1,512,512]{2,1,0:T(8,128)(2,1)S(1)} %collective-permute-done.19.refs_2_.refs_18_), channel_id=1, source_target_pairs={{0,2},{1,3},{2,0},{3,1},{4,6},{5,7},{6,4},{7,5},{8,10},{9,11},{10,... | collective-permute-start | bytes 1572872 | tf_op jit(solution)/shard_map/ppermute | solution.py:430
  122.8 14.4 %collective-permute-start.27 = (bf16[1,512,512]{2,1,0:T(8,128)(2,1)S(1)}, bf16[1,512,512]{2,1,0:T(8,128)(2,1)S(1)}, u32[]{:S(2)}, u32[]{:S(2)}) collective-permute-start(bf16[1,512,512]{2,1,0:T(8,128)(2,1)S(1)} %collective-permute-done.19.refs_2_.refs_18_), channel_id=1, source_target_pairs={{0,1},{1,0},{2,3},{3,2},{4,5},{5,4},{6,7},{7,6},{8,9},{9,8},{10,11... | collective-permute-start | bytes 1572872 | tf_op jit(solution)/shard_map/ppermute | solution.py:430
  135.7 26.3 %collective-permute-start.13 = (bf16[2,512,512]{2,1,0:T(8,128)(2,1)}, bf16[2,512,512]{2,1,0:T(8,128)(2,1)}, u32[]{:S(2)}, u32[]{:S(2)}) collective-permute-start(bf16[2,512,512]{2,1,0:T(8,128)(2,1)} %get-tuple-element.74.refs_0_.refs_8_), channel_id=1, source_target_pairs={{0,2},{1,3},{2,0},{3,1},{4,6},{5,7},{6,4},{7,5},{8,10},{9,11},{10,... | collective-permute-start | bytes 3145736 | tf_op jit(solution)/shard_map/ppermute | solution.py:430
  141.3 41.8 %collective-permute-start.14 = (bf16[2,512,512]{2,1,0:T(8,128)(2,1)S(1)}, bf16[2,512,512]{2,1,0:T(8,128)(2,1)}, u32[]{:S(2)}, u32[]{:S(2)}) collective-permute-start(bf16[2,512,512]{2,1,0:T(8,128)(2,1)S(1)} %collective-permute-done.12.refs_1_.refs_9_), channel_id=1, source_target_pairs={{0,2},{1,3},{2,0},{3,1},{4,6},{5,7},{6,4},{7,5},{8,10},{9,11},{10,... | collective-permute-start | bytes 3145736 | tf_op jit(solution)/shard_map/ppermute | solution.py:430
  142.8 19.2 %collective-permute-start.32 = (bf16[1,512,512]{2,1,0:T(8,128)(2,1)}, bf16[1,512,512]{2,1,0:T(8,128)(2,1)}, u32[]{:S(2)}, u32[]{:S(2)}) collective-permute-start(bf16[1,512,512]{2,1,0:T(8,128)(2,1)} %collective-permute-done.24.refs_7_.refs_23_), channel_id=1, source_target_pairs={{0,1},{1,0},{2,3},{3,2},{4,5},{5,4},{6,7},{7,6},{8,9},{9,8},{10,11... | collective-permute-start | bytes 1572872 | tf_op jit(solution)/shard_map/ppermute | solution.py:430
  144.9 51.3 %collective-permute-start.31 = (bf16[1,512,512]{2,1,0:T(8,128)(2,1)}, bf16[1,512,512]{2,1,0:T(8,128)(2,1)}, u32[]{:S(2)}, u32[]{:S(2)}) collective-permute-start(bf16[1,512,512]{2,1,0:T(8,128)(2,1)} %collective-permute-done.23.refs_6_.refs_22_), channel_id=1, source_target_pairs={{0,1},{1,0},{2,3},{3,2},{4,5},{5,4},{6,7},{7,6},{8,9},{9,8},{10,11... | collective-permute-start | bytes 1572872 | tf_op jit(solution)/shard_map/ppermute | solution.py:430
  162.0 59.9 %collective-permute-start.15 = (bf16[2,512,512]{2,1,0:T(8,128)(2,1)}, bf16[2,512,512]{2,1,0:T(8,128)(2,1)S(1)}, u32[]{:S(2)}, u32[]{:S(2)}) collective-permute-start(bf16[2,512,512]{2,1,0:T(8,128)(2,1)} %get-tuple-element.74.refs_0_.refs_8_), channel_id=1, source_target_pairs={{0,1},{1,0},{2,3},{3,2},{4,5},{5,4},{6,7},{7,6},{8,9},{9,8},{10,11... | collective-permute-start | bytes 3145736 | tf_op jit(solution)/shard_map/ppermute | solution.py:430
  162.0 59.9 %collective-permute-start.16 = (bf16[2,512,512]{2,1,0:T(8,128)(2,1)S(1)}, bf16[2,512,512]{2,1,0:T(8,128)(2,1)S(1)}, u32[]{:S(2)}, u32[]{:S(2)}) collective-permute-start(bf16[2,512,512]{2,1,0:T(8,128)(2,1)S(1)} %collective-permute-done.12.refs_1_.refs_9_), channel_id=1, source_target_pairs={{0,1},{1,0},{2,3},{3,2},{4,5},{5,4},{6,7},{7,6},{8,9},{9,8},{10,11... | collective-permute-start | bytes 3145736 | tf_op jit(solution)/shard_map/ppermute | solution.py:430
  183.1 38.8 %collective-permute-start.17 = (bf16[2,512,512]{2,1,0:T(8,128)(2,1)}, bf16[2,512,512]{2,1,0:T(8,128)(2,1)S(1)}, u32[]{:S(2)}, u32[]{:S(2)}) collective-permute-start(bf16[2,512,512]{2,1,0:T(8,128)(2,1)} %collective-permute-done.13.refs_2_.refs_10_), channel_id=1, source_target_pairs={{0,1},{1,0},{2,3},{3,2},{4,5},{5,4},{6,7},{7,6},{8,9},{9,8},{10,11... | collective-permute-start | bytes 3145736 | tf_op jit(solution)/shard_map/ppermute | solution.py:430
  183.1 38.9 %collective-permute-start.18 = (bf16[2,512,512]{2,1,0:T(8,128)(2,1)}, bf16[2,512,512]{2,1,0:T(8,128)(2,1)S(1)}, u32[]{:S(2)}, u32[]{:S(2)}) collective-permute-start(bf16[2,512,512]{2,1,0:T(8,128)(2,1)} %collective-permute-done.14.refs_3_.refs_11_), channel_id=1, source_target_pairs={{0,1},{1,0},{2,3},{3,2},{4,5},{5,4},{6,7},{7,6},{8,9},{9,8},{10,11... | collective-permute-start | bytes 3145736 | tf_op jit(solution)/shard_map/ppermute | solution.py:430
  242.9 15.0 %collective-permute-start.36 = (bf16[4,2,64,512]{3,2,1,0:T(8,128)(2,1)}, bf16[4,2,64,512]{3,2,1,0:T(8,128)(2,1)}, u32[]{:S(2)}, u32[]{:S(2)}) collective-permute-start(bf16[4,2,64,512]{3,2,1,0:T(8,128)(2,1)} %get-tuple-element.87), channel_id=1, source_target_pairs={{0,4},{4,0},{8,12},{12,8},{16,20},{20,16},{24,28},{28,24},{1,5},{5... | collective-permute-start | bytes 1572872 | tf_op jit(solution)/shard_map/ppermute | solution.py:424
  255.1 15.0 %collective-permute-start.40 = (bf16[4,2,64,512]{3,2,1,0:T(8,128)(2,1)}, bf16[4,2,64,512]{3,2,1,0:T(8,128)(2,1)S(1)}, u32[]{:S(2)}, u32[]{:S(2)}) collective-permute-start(bf16[4,2,64,512]{3,2,1,0:T(8,128)(2,1)} %get-tuple-element.93), channel_id=1, source_target_pairs={{0,4},{4,0},{8,12},{12,8},{16,20},{20,16},{24,28},{28,24},{1,5},{5... | collective-permute-start | bytes 1572872 | tf_op jit(solution)/shard_map/ppermute | solution.py:424
  255.9 43.2 %collective-permute-start.44 = (bf16[4,2,64,512]{3,2,1,0:T(8,128)(2,1)}, bf16[4,2,64,512]{3,2,1,0:T(8,128)(2,1)S(1)}, u32[]{:S(2)}, u32[]{:S(2)}) collective-permute-start(bf16[4,2,64,512]{3,2,1,0:T(8,128)(2,1)} %get-tuple-element.99), channel_id=1, source_target_pairs={{0,4},{4,0},{8,12},{12,8},{16,20},{20,16},{24,28},{28,24},{1,5},{5... | collective-permute-start | bytes 1572872 | tf_op jit(solution)/shard_map/ppermute | solution.py:424
  257.1 42.2 %collective-permute-start.48 = (bf16[4,2,64,512]{3,2,1,0:T(8,128)(2,1)}, bf16[4,2,64,512]{3,2,1,0:T(8,128)(2,1)S(1)}, u32[]{:S(2)}, u32[]{:S(2)}) collective-permute-start(bf16[4,2,64,512]{3,2,1,0:T(8,128)(2,1)} %get-tuple-element.105), channel_id=1, source_target_pairs={{0,4},{4,0},{8,12},{12,8},{16,20},{20,16},{24,28},{28,24},{1,5},{5... | collective-permute-start | bytes 1572872 | tf_op jit(solution)/shard_map/ppermute | solution.py:424
  260.2 41.0 %collective-permute-start.37 = (bf16[2,64,512]{2,1,0:T(8,128)(2,1)S(1)}, bf16[2,64,512]{2,1,0:T(8,128)(2,1)S(1)}, u32[]{:S(2)}, u32[]{:S(2)}) collective-permute-start(bf16[2,64,512]{2,1,0:T(8,128)(2,1)S(1)} %get-tuple-element.89), channel_id=1, source_target_pairs={{0,8},{4,12},{8,16},{12,20},{16,24},{20,28},{24,0},{28,4},{1,9},{5... | collective-permute-start | bytes 393224 | tf_op jit(solution)/shard_map/ppermute | solution.py:424
  261.8 41.6 %collective-permute-start.38 = (bf16[2,64,512]{2,1,0:T(8,128)(2,1)S(1)}, bf16[2,64,512]{2,1,0:T(8,128)(2,1)S(1)}, u32[]{:S(2)}, u32[]{:S(2)}) collective-permute-start(bf16[2,64,512]{2,1,0:T(8,128)(2,1)S(1)} %get-tuple-element.90), channel_id=1, source_target_pairs={{0,16},{4,20},{8,24},{12,28},{16,0},{20,4},{24,8},{28,12},{1,17},{... | collective-permute-start | bytes 393224 | tf_op jit(solution)/shard_map/ppermute | solution.py:424
  270.1 33.9 %collective-permute-start.39 = (bf16[2,64,512]{2,1,0:T(8,128)(2,1)S(1)}, bf16[2,64,512]{2,1,0:T(8,128)(2,1)S(1)}, u32[]{:S(2)}, u32[]{:S(2)}) collective-permute-start(bf16[2,64,512]{2,1,0:T(8,128)(2,1)S(1)} %get-tuple-element.91), channel_id=1, source_target_pairs={{0,24},{4,28},{8,0},{12,4},{16,8},{20,12},{24,16},{28,20},{1,25},{... | collective-permute-start | bytes 393224 | tf_op jit(solution)/shard_map/ppermute | solution.py:424
  299.3 12.9 %collective-permute-start.42 = (bf16[2,64,512]{2,1,0:T(8,128)(2,1)S(1)}, bf16[2,64,512]{2,1,0:T(8,128)(2,1)S(1)}, u32[]{:S(2)}, u32[]{:S(2)}) collective-permute-start(bf16[2,64,512]{2,1,0:T(8,128)(2,1)S(1)} %get-tuple-element.96), channel_id=1, source_target_pairs={{0,16},{4,20},{8,24},{12,28},{16,0},{20,4},{24,8},{28,12},{1,17},{... | collective-permute-start | bytes 393224 | tf_op jit(solution)/shard_map/ppermute | solution.py:424
  301.2 13.3 %collective-permute-start.43 = (bf16[2,64,512]{2,1,0:T(8,128)(2,1)S(1)}, bf16[2,64,512]{2,1,0:T(8,128)(2,1)S(1)}, u32[]{:S(2)}, u32[]{:S(2)}) collective-permute-start(bf16[2,64,512]{2,1,0:T(8,128)(2,1)S(1)} %get-tuple-element.97), channel_id=1, source_target_pairs={{0,24},{4,28},{8,0},{12,4},{16,8},{20,12},{24,16},{28,20},{1,25},{... | collective-permute-start | bytes 393224 | tf_op jit(solution)/shard_map/ppermute | solution.py:424
  303.4 16.8 %collective-permute-start.45 = (bf16[2,64,512]{2,1,0:T(8,128)(2,1)S(1)}, bf16[2,64,512]{2,1,0:T(8,128)(2,1)S(1)}, u32[]{:S(2)}, u32[]{:S(2)}) collective-permute-start(bf16[2,64,512]{2,1,0:T(8,128)(2,1)S(1)} %get-tuple-element.101), channel_id=1, source_target_pairs={{0,8},{4,12},{8,16},{12,20},{16,24},{20,28},{24,0},{28,4},{1,9},{5... | collective-permute-start | bytes 393224 | tf_op jit(solution)/shard_map/ppermute | solution.py:424
  304.0 20.9 %collective-permute-start.46 = (bf16[2,64,512]{2,1,0:T(8,128)(2,1)S(1)}, bf16[2,64,512]{2,1,0:T(8,128)(2,1)S(1)}, u32[]{:S(2)}, u32[]{:S(2)}) collective-permute-start(bf16[2,64,512]{2,1,0:T(8,128)(2,1)S(1)} %get-tuple-element.102), channel_id=1, source_target_pairs={{0,16},{4,20},{8,24},{12,28},{16,0},{20,4},{24,8},{28,12},{1,17},{... | collective-permute-start | bytes 393224 | tf_op jit(solution)/shard_map/ppermute | solution.py:424
  307.4 17.5 %collective-permute-start.47 = (bf16[2,64,512]{2,1,0:T(8,128)(2,1)S(1)}, bf16[2,64,512]{2,1,0:T(8,128)(2,1)S(1)}, u32[]{:S(2)}, u32[]{:S(2)}) collective-permute-start(bf16[2,64,512]{2,1,0:T(8,128)(2,1)S(1)} %get-tuple-element.103), channel_id=1, source_target_pairs={{0,24},{4,28},{8,0},{12,4},{16,8},{20,12},{24,16},{28,20},{1,25},{... | collective-permute-start | bytes 393224 | tf_op jit(solution)/shard_map/ppermute | solution.py:424
  312.3 12.7 %collective-permute-start.49 = (bf16[2,64,512]{2,1,0:T(8,128)(2,1)S(1)}, bf16[2,64,512]{2,1,0:T(8,128)(2,1)S(1)}, u32[]{:S(2)}, u32[]{:S(2)}) collective-permute-start(bf16[2,64,512]{2,1,0:T(8,128)(2,1)S(1)} %get-tuple-element.107), channel_id=1, source_target_pairs={{0,8},{4,12},{8,16},{12,20},{16,24},{20,28},{24,0},{28,4},{1,9},{5... | collective-permute-start | bytes 393224 | tf_op jit(solution)/shard_map/ppermute | solution.py:424
  314.5 17.4 %collective-permute-start.50 = (bf16[2,64,512]{2,1,0:T(8,128)(2,1)S(1)}, bf16[2,64,512]{2,1,0:T(8,128)(2,1)S(1)}, u32[]{:S(2)}, u32[]{:S(2)}) collective-permute-start(bf16[2,64,512]{2,1,0:T(8,128)(2,1)S(1)} %get-tuple-element.108), channel_id=1, source_target_pairs={{0,16},{4,20},{8,24},{12,28},{16,0},{20,4},{24,8},{28,12},{1,17},{... | collective-permute-start | bytes 393224 | tf_op jit(solution)/shard_map/ppermute | solution.py:424
  320.2 11.8 %collective-permute-start.51 = (bf16[2,64,512]{2,1,0:T(8,128)(2,1)S(1)}, bf16[2,64,512]{2,1,0:T(8,128)(2,1)S(1)}, u32[]{:S(2)}, u32[]{:S(2)}) collective-permute-start(bf16[2,64,512]{2,1,0:T(8,128)(2,1)S(1)} %get-tuple-element.109), channel_id=1, source_target_pairs={{0,24},{4,28},{8,0},{12,4},{16,8},{20,12},{24,16},{28,20},{1,25},{... | collective-permute-start | bytes 393224 | tf_op jit(solution)/shard_map/ppermute | solution.py:424
  (42 other events, 916.4 us)

commit v7 on v6

--- a/solution.py
+++ b/solution.py
@@ -81,21 +81,21 @@
     )(which[None], green, broadening)
 
 
-def place_kernel(where, *refs):
+def place_kernel(order, where, *refs):
     pieces, (full_ref, turned_ref) = refs[:-2], refs[-2:]
     rows = pieces[0].shape[1]
     for at, c_ref in enumerate(pieces):
-        start = pl.ds(pl.multiple_of(where[at] * rows, rows), rows)
+        start = pl.ds(pl.multiple_of((where[0] ^ order[at]) * rows, rows), rows)
         for q in range(c_ref.shape[0]):
             full_ref[q, start, :] = c_ref[q]
             turned_ref[q, :, start] = c_ref[q].T
 
 
-def place_coupling(where, pieces):
+def place_coupling(where, order, pieces):
     nk, rows, n = pieces[0].shape
     each = 2
     return pl.pallas_call(
-        place_kernel,
+        functools.partial(place_kernel, order),
         out_shape=[pltpu.HBM((nk, n, n), BF16)] * 2,
         grid_spec=pltpu.PrefetchScalarGridSpec(
             num_scalar_prefetch=1,
@@ -106,7 +106,7 @@
         compiler_params=params(56),
         cost_estimate=cost(nk * n * n * 4, nk * n * n * 6),
         name="place",
-    )(where, *pieces)
+    )(where[None], *pieces)
 
 
 def source_kernel(odd, steps, strength, boson, keep, recv, kz, rz, *refs):
@@ -339,32 +339,32 @@
     )(green, broadening, x, y, *alias)
 
 
-def last_density_kernel(scale, energy, odd, g_ref, gamma_ref, x_ref, y_ref, held_ref, *refs):
+def last_density_kernel(scale, energy, chunks, odd, g_ref, gamma_ref, x_ref, y_ref, held_ref, *refs):
     d_ref, outs = refs[-1], refs[:-1]
     groups, _, rows, _ = outs[0].shape
     for c, d in enumerate(density_terms(energy, g_ref, gamma_ref, x_ref, y_ref)):
         d_ref[c] = (d + held_ref[0, c]) * scale
-    for i in range(len(outs) // 2):
-        keep_ref, send_ref = outs[2 * i], outs[2 * i + 1]
+    for at, (i, low, parts) in enumerate(chunks):
+        keep_ref, send_ref = outs[2 * at], outs[2 * at + 1]
 
         @pl.when(pl.program_id(0) == i)
         def _():
-            for c in range(2):
+            for c in range(parts):
                 for g in range(groups):
                     mine = pl.multiple_of((2 * g + odd[0]) * rows, rows)
                     other = pl.multiple_of((2 * g + 1 - odd[0]) * rows, rows)
-                    keep_ref[g, c] = d_ref[c, pl.ds(mine, rows), :].astype(BF16)
-                    send_ref[g, c] = d_ref[c, pl.ds(other, rows), :].astype(BF16)
-
-
-def last_density(scale, energy, start, count, groups, odd, green, broadening, x, y, held):
+                    keep_ref[g, c] = d_ref[low + c, pl.ds(mine, rows), :].astype(BF16)
+                    send_ref[g, c] = d_ref[low + c, pl.ds(other, rows), :].astype(BF16)
+
+
+def last_density(scale, energy, start, count, chunks, groups, odd, green, broadening, x, y, held):
     _, le, _, n, _ = green.shape
     rows = n // (2 * groups)
     one = pl.BlockSpec((1, n, n), lambda i, odd: (start + i, 0, 0))
-    out = pl.BlockSpec((groups, 2, rows, n), lambda i, odd: (0, 0, 0, 0))
-    return pl.pallas_call(
-        functools.partial(last_density_kernel, scale, energy),
-        out_shape=[jax.ShapeDtypeStruct((groups, 2, rows, n), BF16)] * (2 * count),
+    shapes = [(groups, parts, rows, n) for _, _, parts in chunks for _ in range(2)]
+    return pl.pallas_call(
+        functools.partial(last_density_kernel, scale, energy, chunks),
+        out_shape=[jax.ShapeDtypeStruct(shape, BF16) for shape in shapes],
         grid_spec=pltpu.PrefetchScalarGridSpec(
             num_scalar_prefetch=1,
             grid=(count,),
@@ -375,7 +375,7 @@
                 one,
                 pl.BlockSpec((1, 2, n, n), lambda i, odd: (start + i, 0, 0, 0)),
             ],
-            out_specs=[out] * (2 * count),
+            out_specs=[pl.BlockSpec(shape, lambda i, odd: (0, 0, 0, 0)) for shape in shapes],
             scratch_shapes=[pltpu.VMEM((2, n, n), F32)],
         ),
         compiler_params=params(44),
@@ -464,7 +464,7 @@
                 odd, modes, j, h, hk, keep[j][h], recv[j][h], kz[j][h], rz[j][h], last)
         got.append(last)
 
-    full, turned = place_coupling(jnp.stack([mine ^ o for o in order]), coupling_pieces)
+    full, turned = place_coupling(mine, tuple(order), coupling_pieces)
 
     held_rows, held_density = None, None
     scale = 1.0 / (le * ne)
@@ -480,11 +480,13 @@
         else:
             shares = []
             x, y = home_blocks(mine, slots, pieces, full, turned, lk)
-            for first, count in ((0, 1), (1, lk - 1)):
+            whole = [(i, 0, 2) for i in range(lk - 2)]
+            calls = ((0, 1, ((0, 0, 2),)), (1, lk - 1, tuple(whole) + ((lk - 2, 0, 1), (lk - 2, 1, 1))))
+            for first, count, chunks in calls:
                 shares = shares + list(last_density(
-                    scale, e, first, count, groups, odd,
+                    scale, e, first, count, chunks, groups, odd,
                     green_ret, broadening, x, y, held_density))
-            for k in range(lk):
+            for k in range(len(shares) // 2):
                 kept, sent = shares[2 * k], shares[2 * k + 1]
                 other = permuted(sent, pairs)
                 parts = pair_sum(group, kept, other)
@@ -493,6 +495,7 @@
                     perm = [(i, (i + 2 * d) % ne) for i in range(ne)]
                     total = total + permuted(parts[d], perm).astype(F32)
                 late.append(total)
+            late = late[:-2] + [jnp.concatenate(late[-2:], axis=0)]
         held_rows = own_rows(mine, slots, pieces, coupling, e, le, held_rows)
     density = jnp.transpose(jnp.stack(late), (2, 0, 1, 3))
     return held_rows, density

time: 335 us -> 339 us (1.012)
  waiting for transfers between devices: 123 us -> 132 us
    ppermute x31 -> x35, waiting for transfers between devices: 60.1 us -> 67.4 us  [permuted(): return lax.ppermute(x, 'energy', perm)]
    unnamed x77 -> x79, local copies, waits for them, and re-layouts: 10 us -> 7.26 us
    ppermute x31 -> x35, starting transfers between devices: 63.5 us -> 64.1 us  [permuted(): return lax.ppermute(x, 'energy', perm)]
  transfers between devices with their start and end apart: 52 -> 56, of which waited for: 17 -> 19; matrix products, arithmetic and copies ran while one was open for 0% -> 0% of each run, Pallas kernels for 30% -> 29%
where the time goes in v7:
time: 339 us; the launch traced here: 338 us
  waiting for transfers between devices  132 us (39%)
  Pallas kernels  122 us (36%)
  starting transfers between devices  75.9 us (22%)
  local copies, waits for them, and re-layouts  7.26 us (2%)
    ppermute x35, waiting for transfers between devices, permuted(): return lax.ppermute(x, 'energy', perm)  67.4 us
    ppermute x21, waiting for transfers between devices, swap(): moved = lax.ppermute(x, 'mom', [(i, i ^ stride) for i in range(nm)])  64.2 us
    ppermute x35, starting transfers between devices, permuted(): return lax.ppermute(x, 'energy', perm)  64.1 us
    pallas_call x2, Pallas kernels, own_rows(): pl.pallas_call(functools.partial(rows_kernel, len(pieces)), out_shape=jax...  26.1 us
    pallas_call x2, Pallas kernels, home_blocks(): pl.pallas_call(functools.partial(home_kernel, lk, len(pieces)), out_shape...  25.9 us
    pallas_call x4, Pallas kernels, lesser_packed(): pl.pallas_call(lesser_kernel, out_shape=[pltpu.HBM((le, n // 2, n), BF16)...  16.6 us
    pallas_call x2, Pallas kernels, last_density(): pl.pallas_call(functools.partial(last_density_kernel, scale, energy, chun...  15.9 us
    pallas_call x4, Pallas kernels, sources(): pl.pallas_call(source_kernel, out_shape=[pltpu.HBM(shape, BF16) for shape...  13.2 us
  transfers between devices with their start and end apart: 56, of which 19 were waited for; matrix products, arithmetic and copies ran while one was open for 0% of the time, Pallas kernels for 29%

profile of v7, /device:TPU:0, one launch (start us, length us, event | category | flops | bytes accessed | tf_op | source)
XLA Modules:
  0.0 338.4 jit_solution(10917729817926841171)
XLA Ops:
  0.6 4.1 %lesser.7 = (bf16[2,256,512]{2,1,0:T(8,128)(2,1)}, bf16[2,256,512]{2,1,0:T(8,128)(2,1)}) custom-call(s32[1]{0:T(128)} %bitcast.5.sel, bf16[4,2,2,512,512]{4,3,2,1,0:T(8,128)(2,1)} %g_ref.13, f32[4,2,512]{2,1,0:T(2,128)} %gamma_ref.13), custom_call_target="tpu_custom_call" | custom-call | flops 1610612736 | bytes 3145728 | tf_op jit(solution)/shard_map/lesser/pallas_call | solution.py:66
  4.8 3.0 collective-permute-start.9
  7.8 4.1 %lesser.6 = (bf16[2,256,512]{2,1,0:T(8,128)(2,1)}, bf16[2,256,512]{2,1,0:T(8,128)(2,1)}) custom-call(s32[1]{0:T(128)} %bitcast.4.sel, bf16[4,2,2,512,512]{4,3,2,1,0:T(8,128)(2,1)} %g_ref.13, f32[4,2,512]{2,1,0:T(2,128)} %gamma_ref.13), custom_call_target="tpu_custom_call" | custom-call | flops 1610612736 | bytes 3145728 | tf_op jit(solution)/shard_map/lesser/pallas_call | solution.py:66
  13.2 2.8 collective-permute-start.6
  17.3 4.1 %lesser.5 = (bf16[2,256,512]{2,1,0:T(8,128)(2,1)}, bf16[2,256,512]{2,1,0:T(8,128)(2,1)}) custom-call(s32[1]{0:T(128)} %bitcast.3.sel, bf16[4,2,2,512,512]{4,3,2,1,0:T(8,128)(2,1)} %g_ref.13, f32[4,2,512]{2,1,0:T(2,128)} %gamma_ref.13), custom_call_target="tpu_custom_call" | custom-call | flops 1610612736 | bytes 3145728 | tf_op jit(solution)/shard_map/lesser/pallas_call | solution.py:66
  21.4 2.6 collective-permute-start.3
  24.0 4.7 %collective-permute-done.10.kz = bf16[2,256,512]{2,1,0:T(8,128)(2,1)S(1)} collective-permute-done((bf16[2,256,512]{2,1,0:T(8,128)(2,1)}, bf16[2,256,512]{2,1,0:T(8,128)(2,1)S(1)}, u32[]{:S(2)}, u32[]{:S(2)}) %collective-permute-start.10) | collective-permute-done | bytes 524320 | tf_op jit(solution)/shard_map/ppermute | solution.py:424
  28.8 3.5 %collective-permute-start.11 = (bf16[2,256,512]{2,1,0:T(8,128)(2,1)S(1)}, bf16[2,256,512]{2,1,0:T(8,128)(2,1)S(1)}, u32[]{:S(2)}, u32[]{:S(2)}) collective-permute-start(bf16[2,256,512]{2,1,0:T(8,128)(2,1)S(1)} %collective-permute-done.9.recv), channel_id=1, source_target_pairs={{0,8},{8,16},{12,4},{16,24},{20,12},{28,20},{1,9},{9,17},{13,5},{1... | collective-permute-start | bytes 1572872 | tf_op jit(solution)/shard_map/ppermute | solution.py:424
  32.3 4.5 %collective-permute-start.8 = (bf16[2,256,512]{2,1,0:T(8,128)(2,1)S(1)}, bf16[2,256,512]{2,1,0:T(8,128)(2,1)}, u32[]{:S(2)}, u32[]{:S(2)}) collective-permute-start(bf16[2,256,512]{2,1,0:T(8,128)(2,1)S(1)} %collective-permute-done.6.recv), channel_id=1, source_target_pairs={{0,8},{8,16},{12,4},{16,24},{20,12},{28,20},{1,9},{9,17},{13,5},{1... | collective-permute-start | bytes 1572872 | tf_op jit(solution)/shard_map/ppermute | solution.py:424
  36.8 1.8 collective-permute-done.7.kz
  40.1 4.2 %lesser.4 = (bf16[2,256,512]{2,1,0:T(8,128)(2,1)}, bf16[2,256,512]{2,1,0:T(8,128)(2,1)}) custom-call(s32[1]{0:T(128)} %bitcast.2.sel, bf16[4,2,2,512,512]{4,3,2,1,0:T(8,128)(2,1)} %g_ref.13, f32[4,2,512]{2,1,0:T(2,128)} %gamma_ref.13), custom_call_target="tpu_custom_call" | custom-call | flops 1610612736 | bytes 3145728 | tf_op jit(solution)/shard_map/lesser/pallas_call | solution.py:66
  45.8 7.8 %collective-permute-done.recv = bf16[2,256,512]{2,1,0:T(8,128)(2,1)S(1)} collective-permute-done((bf16[2,256,512]{2,1,0:T(8,128)(2,1)}, bf16[2,256,512]{2,1,0:T(8,128)(2,1)S(1)}, u32[]{:S(2)}, u32[]{:S(2)}) %collective-permute-start) | collective-permute-done | bytes 524320 | tf_op jit(solution)/shard_map/ppermute | solution.py:424
  53.6 3.7 %collective-permute-start.5 = (bf16[2,256,512]{2,1,0:T(8,128)(2,1)}, bf16[2,256,512]{2,1,0:T(8,128)(2,1)S(1)}, u32[]{:S(2)}, u32[]{:S(2)}) collective-permute-start(bf16[2,256,512]{2,1,0:T(8,128)(2,1)} %collective-permute-done.3.recv), channel_id=1, source_target_pairs={{0,8},{8,16},{12,4},{16,24},{20,12},{28,20},{1,9},{9,17},{13,5},{1... | collective-permute-start | bytes 1572872 | tf_op jit(solution)/shard_map/ppermute | solution.py:424
  59.5 4.8 %collective-permute-start.2 = (bf16[2,256,512]{2,1,0:T(8,128)(2,1)S(1)}, bf16[2,256,512]{2,1,0:T(8,128)(2,1)S(1)}, u32[]{:S(2)}, u32[]{:S(2)}) collective-permute-start(bf16[2,256,512]{2,1,0:T(8,128)(2,1)S(1)} %collective-permute-done.recv), channel_id=1, source_target_pairs={{0,8},{8,16},{12,4},{16,24},{20,12},{28,20},{1,9},{9,17},{13,5},{1... | collective-permute-start | bytes 1572872 | tf_op jit(solution)/shard_map/ppermute | solution.py:424
  64.3 3.3 source.4
  67.6 3.3 source.5
  71.7 3.3 source.6
  75.0 4.2 %collective-permute-done.2.rz = bf16[2,256,512]{2,1,0:T(8,128)(2,1)S(1)} collective-permute-done((bf16[2,256,512]{2,1,0:T(8,128)(2,1)S(1)}, bf16[2,256,512]{2,1,0:T(8,128)(2,1)S(1)}, u32[]{:S(2)}, u32[]{:S(2)}) %collective-permute-start.2) | collective-permute-done | bytes 524320 | tf_op jit(solution)/shard_map/ppermute | solution.py:424
  80.0 3.3 source.7
  83.3 2.4 collective-permute-start.20
  87.3 11.4 %collective-permute-done.20.refs_3_.refs_19_ = bf16[1,512,512]{2,1,0:T(8,128)(2,1)S(1)} collective-permute-done((bf16[1,512,512]{2,1,0:T(8,128)(2,1)}, bf16[1,512,512]{2,1,0:T(8,128)(2,1)S(1)}, u32[]{:S(2)}, u32[]{:S(2)}) %collective-permute-start.20) | collective-permute-done | bytes 524320 | tf_op jit(solution)/shard_map/ppermute | solution.py:424
  100.8 6.8 %collective-permute-done.19.refs_2_.refs_18_ = bf16[1,512,512]{2,1,0:T(8,128)(2,1)S(1)} collective-permute-done((bf16[1,512,512]{2,1,0:T(8,128)(2,1)S(1)}, bf16[1,512,512]{2,1,0:T(8,128)(2,1)S(1)}, u32[]{:S(2)}, u32[]{:S(2)}) %collective-permute-start.19) | collective-permute-done | bytes 524320 | tf_op jit(solution)/shard_map/ppermute | solution.py:424
  107.6 5.9 %collective-permute-done.21.refs_4_.refs_20_ = bf16[1,512,512]{2,1,0:T(8,128)(2,1)S(1)} collective-permute-done((bf16[1,512,512]{2,1,0:T(8,128)(2,1)S(1)}, bf16[1,512,512]{2,1,0:T(8,128)(2,1)S(1)}, u32[]{:S(2)}, u32[]{:S(2)}) %collective-permute-start.21) | collective-permute-done | bytes 524320 | tf_op jit(solution)/shard_map/ppermute | solution.py:430
  114.0 6.3 %collective-permute-done.24.refs_7_.refs_23_ = bf16[1,512,512]{2,1,0:T(8,128)(2,1)S(1)} collective-permute-done((bf16[1,512,512]{2,1,0:T(8,128)(2,1)S(1)}, bf16[1,512,512]{2,1,0:T(8,128)(2,1)S(1)}, u32[]{:S(2)}, u32[]{:S(2)}) %collective-permute-start.24) | collective-permute-done | bytes 524320 | tf_op jit(solution)/shard_map/ppermute | solution.py:430
  122.9 12.7 %collective-permute-done.23.refs_6_.refs_22_ = bf16[1,512,512]{2,1,0:T(8,128)(2,1)} collective-permute-done((bf16[1,512,512]{2,1,0:T(8,128)(2,1)S(1)}, bf16[1,512,512]{2,1,0:T(8,128)(2,1)}, u32[]{:S(2)}, u32[]{:S(2)}) %collective-permute-start.23) | collective-permute-done | bytes 524320 | tf_op jit(solution)/shard_map/ppermute | solution.py:430
  137.1 4.1 %collective-permute-done.12.refs_1_.refs_9_ = bf16[2,512,512]{2,1,0:T(8,128)(2,1)S(1)} collective-permute-done((bf16[2,512,512]{2,1,0:T(8,128)(2,1)}, bf16[2,512,512]{2,1,0:T(8,128)(2,1)S(1)}, u32[]{:S(2)}, u32[]{:S(2)}) %collective-permute-start.12) | collective-permute-done | bytes 1048608 | tf_op jit(solution)/shard_map/ppermute | solution.py:424
  143.2 18.7 %collective-permute-done.13.refs_2_.refs_10_ = bf16[2,512,512]{2,1,0:T(8,128)(2,1)} collective-permute-done((bf16[2,512,512]{2,1,0:T(8,128)(2,1)}, bf16[2,512,512]{2,1,0:T(8,128)(2,1)}, u32[]{:S(2)}, u32[]{:S(2)}) %collective-permute-start.13) | collective-permute-done | bytes 1048608 | tf_op jit(solution)/shard_map/ppermute | solution.py:430
  162.5 20.6 %collective-permute-done.14.refs_3_.refs_11_ = bf16[2,512,512]{2,1,0:T(8,128)(2,1)} collective-permute-done((bf16[2,512,512]{2,1,0:T(8,128)(2,1)S(1)}, bf16[2,512,512]{2,1,0:T(8,128)(2,1)}, u32[]{:S(2)}, u32[]{:S(2)}) %collective-permute-start.14) | collective-permute-done | bytes 1048608 | tf_op jit(solution)/shard_map/ppermute | solution.py:430
  185.0 11.1 %place.1 = (bf16[16,512,512]{2,1,0:T(8,128)(2,1)}, bf16[16,512,512]{2,1,0:T(8,128)(2,1)}) custom-call(s32[1]{0:T(128)} %bitcast.mine.where, bf16[16,128,512]{2,1,0:T(8,128)(2,1)} %refs_0_.1, bf16[16,128,512]{2,1,0:T(8,128)(2,1)} %collective-permute-done.33.refs_1_, bf16[16,128,512]{2,1,0:T(8,128)(2,1)} %copy-done.29, bf16[16,128,512]{2,1,0:T(8,128)(2,1)} %copy-done.30), custom_call_target="tpu_custom_call" | custom-call | flops 16777216 | bytes 25165824 | tf_op jit(solution)/shard_map/place/pallas_call | solution.py:97
  196.1 12.9 %home.3 = (bf16[4,512,512]{2,1,0:T(8,128)(2,1)S(1)}, bf16[4,512,512]{2,1,0:T(8,128)(2,1)S(1)}) custom-call(s32[1]{0:T(128)} %bitcast.mine.where, s32[16,16]{1,0:T(8,128)S(1)} %fusion.4.slots, bf16[1,512,512]{2,1,0:T(8,128)(2,1)S(1)} %copy-done.2, bf16[1,512,512]{2,1,0:T(8,128)(2,1)S(1)} %copy-done.1, bf16[1,512,512]{2,1,0:T(8,128)(2,1)} %copy-done.20, ...), custom_call_target="tpu_custom_call" | custom-call | flops 67108864 | bytes 29360128 | tf_op jit(solution)/shard_map/home/pallas_call | solution.py:215
  209.1 12.7 %density.3.held_ref = f32[4,2,512,512]{3,2,1,0:T(8,128)} custom-call(bf16[4,2,2,512,512]{4,3,2,1,0:T(8,128)(2,1)} %g_ref.13, f32[4,2,512]{2,1,0:T(2,128)S(1)} %copy-done.7, bf16[4,512,512]{2,1,0:T(8,128)(2,1)S(1)} %get-tuple-element.90.x_ref, bf16[4,512,512]{2,1,0:T(8,128)(2,1)S(1)} %get-tuple-element.91.y_ref), custom_call_target="tpu_custom_call" | custom-call | flops 8589934592 | bytes 20971520 | tf_op jit(solution)/shard_map/density/pallas_call | solution.py:325
  221.9 12.9 %home.2 = (bf16[4,512,512]{2,1,0:T(8,128)(2,1)S(1)}, bf16[4,512,512]{2,1,0:T(8,128)(2,1)S(1)}) custom-call(s32[1]{0:T(128)} %bitcast.mine.where, s32[16,16]{1,0:T(8,128)S(1)} %fusion.4.slots, bf16[2,512,512]{2,1,0:T(8,128)(2,1)S(1)} %copy-done, bf16[2,512,512]{2,1,0:T(8,128)(2,1)} %copy-done.16, ...), custom_call_target="tpu_custom_call" | custom-call | flops 67108864 | bytes 29360128 | tf_op jit(solution)/shard_map/home/pallas_call | solution.py:215
  234.8 5.3 %density.4 = (bf16[4,2,64,512]{3,2,1,0:T(8,128)(2,1)S(1)}, bf16[4,2,64,512]{3,2,1,0:T(8,128)(2,1)}) custom-call(s32[1]{0:T(128)} %bitcast.1.odd, bf16[4,2,2,512,512]{4,3,2,1,0:T(8,128)(2,1)} %g_ref.13, f32[4,2,512]{2,1,0:T(2,128)S(1)} %copy-done.7, bf16[4,512,512]{2,1,0:T(8,128)(2,1)S(1)} %get-tuple-element.88.x_ref, ...), custom_call_target="tpu_custom_call" | custom-call | flops 2147483648 | bytes 5242880 | tf_op jit(solution)/shard_map/density/pallas_call | solution.py:365
  241.3 10.5 %density.5 = (bf16[4,2,64,512]{3,2,1,0:T(8,128)(2,1)S(1)}, bf16[4,2,64,512]{3,2,1,0:T(8,128)(2,1)S(1)}, bf16[4,2,64,512]{3,2,1,0:T(8,128)(2,1)S(1)}, bf16[4,2,64...) custom-call(s32[1]{0:T(128)} %bitcast.1.odd, ...), custom_call_target="tpu_custom_call" | custom-call | flops 6442450944 | bytes 15728640 | tf_op jit(solution)/shard_map/density/pallas_call | solution.py:365
  255.5 7.4 %collective-permute-done.48.recv_ref = bf16[4,1,64,512]{3,2,1,0:T(8,128)(2,1)S(1)} collective-permute-done((bf16[4,1,64,512]{3,2,1,0:T(8,128)(2,1)}, bf16[4,1,64,512]{3,2,1,0:T(8,128)(2,1)S(1)}, u32[]{:S(2)}, u32[]{:S(2)}) %collective-permute-start.48) | collective-permute-done | bytes 262176 | tf_op jit(solution)/shard_map/ppermute | solution.py:424
  264.6 1.9 collective-permute-start.50
  266.5 2.0 collective-permute-start.51
  268.5 13.1 %rows.2.refs_17_ = bf16[16,2,2,128,512]{4,3,2,1,0:T(8,128)(2,1)} custom-call(s32[1]{0:T(128)} %bitcast.mine.where, s32[16,16]{1,0:T(8,128)} %copy-done.8, bf16[1,512,512]{2,1,0:T(8,128)(2,1)} %get-tuple-element.82.refs_0_.refs_16_, bf16[1,512,512]{2,1,0:T(8,128)(2,1)} %get-tuple-element.83.refs_1_.refs_17_, bf16[1,512,512]{2,1,0:T(8,128)(2,1)} %copy-done.20, ...), custom_call_target="tpu_custom_call" | custom-call | flops 67108864 | bytes 10485760 | tf_op jit(solution)/shard_map/rows/pallas_call | solution.py:283
  281.7 12.9 %rows.3 = bf16[16,2,2,128,512]{4,3,2,1,0:T(8,128)(2,1)} custom-call(s32[1]{0:T(128)} %bitcast.mine.where, s32[16,16]{1,0:T(8,128)} %copy-done.8, bf16[2,512,512]{2,1,0:T(8,128)(2,1)} %get-tuple-element.80.refs_0_.refs_8_, bf16[2,512,512]{2,1,0:T(8,128)(2,1)} %copy-done.16, ...), custom_call_target="tpu_custom_call", output_to_operand_aliasing={{}: (19, {})} | custom-call | flops 67108864 | bytes 10485760 | tf_op jit(solution)/shard_map/rows/pallas_call | solution.py:283
  297.9 2.9 collective-permute-start.55
  301.0 2.6 collective-permute-done.53
  303.6 2.0 collective-permute-done.54
  306.3 3.8 %collective-permute-start.39 = (bf16[2,64,512]{2,1,0:T(8,128)(2,1)S(1)}, bf16[2,64,512]{2,1,0:T(8,128)(2,1)S(1)}, u32[]{:S(2)}, u32[]{:S(2)}) collective-permute-start(bf16[2,64,512]{2,1,0:T(8,128)(2,1)S(1)} %get-tuple-element.97), channel_id=1, source_target_pairs={{0,24},{4,28},{8,0},{12,4},{16,8},{20,12},{24,16},{28,20},{1,25},{... | collective-permute-start | bytes 393224 | tf_op jit(solution)/shard_map/ppermute | solution.py:424
  310.9 5.7 %collective-permute-done.44.recv_ref = bf16[4,2,64,512]{3,2,1,0:T(8,128)(2,1)S(1)} collective-permute-done((bf16[4,2,64,512]{3,2,1,0:T(8,128)(2,1)S(1)}, bf16[4,2,64,512]{3,2,1,0:T(8,128)(2,1)S(1)}, u32[]{:S(2)}, u32[]{:S(2)}) %collective-permute-start.44) | collective-permute-done | bytes 524320 | tf_op jit(solution)/shard_map/ppermute | solution.py:424
  317.1 2.1 collective-permute-start.43
  319.2 5.4 %collective-permute-start.46 = (bf16[2,64,512]{2,1,0:T(8,128)(2,1)S(1)}, bf16[2,64,512]{2,1,0:T(8,128)(2,1)S(1)}, u32[]{:S(2)}, u32[]{:S(2)}) collective-permute-start(bf16[2,64,512]{2,1,0:T(8,128)(2,1)S(1)} %get-tuple-element.108), channel_id=1, source_target_pairs={{0,16},{4,20},{8,24},{12,28},{16,0},{20,4},{24,8},{28,12},{1,17},{... | collective-permute-start | bytes 393224 | tf_op jit(solution)/shard_map/ppermute | solution.py:424
  324.7 3.6 %collective-permute-start.47 = (bf16[2,64,512]{2,1,0:T(8,128)(2,1)S(1)}, bf16[2,64,512]{2,1,0:T(8,128)(2,1)S(1)}, u32[]{:S(2)}, u32[]{:S(2)}) collective-permute-start(bf16[2,64,512]{2,1,0:T(8,128)(2,1)S(1)} %get-tuple-element.109), channel_id=1, source_target_pairs={{0,24},{4,28},{8,0},{12,4},{16,8},{20,12},{24,16},{28,20},{1,25},{... | collective-permute-start | bytes 393224 | tf_op jit(solution)/shard_map/ppermute | solution.py:424
  329.5 6.9 %collective-permute-done.46 = bf16[2,64,512]{2,1,0:T(8,128)(2,1)S(1)} collective-permute-done((bf16[2,64,512]{2,1,0:T(8,128)(2,1)S(1)}, bf16[2,64,512]{2,1,0:T(8,128)(2,1)S(1)}, u32[]{:S(2)}, u32[]{:S(2)}) %collective-permute-start.46) | collective-permute-done | bytes 131104 | tf_op jit(solution)/shard_map/ppermute | solution.py:424
  (172 shorter events, 37.1 us)
Async XLA Ops:
  4.8 19.2 %collective-permute-start.9 = (bf16[2,256,512]{2,1,0:T(8,128)(2,1)}, bf16[2,256,512]{2,1,0:T(8,128)(2,1)S(1)}, u32[]{:S(2)}, u32[]{:S(2)}) collective-permute-start(bf16[2,256,512]{2,1,0:T(8,128)(2,1)} %get-tuple-element.69), channel_id=1, source_target_pairs={{0,4},{4,0},{8,12},{12,8},{16,20},{20,16},{24,28},{28,24},{1,5},{5... | collective-permute-start | bytes 1572872 | tf_op jit(solution)/shard_map/ppermute | solution.py:424
  11.9 16.9 %collective-permute-start.10 = (bf16[2,256,512]{2,1,0:T(8,128)(2,1)}, bf16[2,256,512]{2,1,0:T(8,128)(2,1)S(1)}, u32[]{:S(2)}, u32[]{:S(2)}) collective-permute-start(bf16[2,256,512]{2,1,0:T(8,128)(2,1)} %get-tuple-element.68.keep), channel_id=1, source_target_pairs={{4,12},{8,0},{12,20},{16,8},{20,28},{24,16},{5,13},{9,1},{13,21},{... | collective-permute-start | bytes 1572872 | tf_op jit(solution)/shard_map/ppermute | solution.py:424
  13.2 19.1 %collective-permute-start.6 = (bf16[2,256,512]{2,1,0:T(8,128)(2,1)}, bf16[2,256,512]{2,1,0:T(8,128)(2,1)S(1)}, u32[]{:S(2)}, u32[]{:S(2)}) collective-permute-start(bf16[2,256,512]{2,1,0:T(8,128)(2,1)} %get-tuple-element.67), channel_id=1, source_target_pairs={{0,4},{4,0},{8,12},{12,8},{16,20},{20,16},{24,28},{28,24},{1,5},{5... | collective-permute-start | bytes 1572872 | tf_op jit(solution)/shard_map/ppermute | solution.py:424
  16.0 22.6 %collective-permute-start.7 = (bf16[2,256,512]{2,1,0:T(8,128)(2,1)}, bf16[2,256,512]{2,1,0:T(8,128)(2,1)S(1)}, u32[]{:S(2)}, u32[]{:S(2)}) collective-permute-start(bf16[2,256,512]{2,1,0:T(8,128)(2,1)} %get-tuple-element.66.keep), channel_id=1, source_target_pairs={{4,12},{8,0},{12,20},{16,8},{20,28},{24,16},{5,13},{9,1},{13,21},{... | collective-permute-start | bytes 1572872 | tf_op jit(solution)/shard_map/ppermute | solution.py:424
  21.4 22.9 %collective-permute-start.3 = (bf16[2,256,512]{2,1,0:T(8,128)(2,1)}, bf16[2,256,512]{2,1,0:T(8,128)(2,1)}, u32[]{:S(2)}, u32[]{:S(2)}) collective-permute-start(bf16[2,256,512]{2,1,0:T(8,128)(2,1)} %get-tuple-element.65), channel_id=1, source_target_pairs={{0,4},{4,0},{8,12},{12,8},{16,20},{20,16},{24,28},{28,24},{1,5},{5... | collective-permute-start | bytes 1572872 | tf_op jit(solution)/shard_map/ppermute | solution.py:424
  23.9 29.7 %collective-permute-start = (bf16[2,256,512]{2,1,0:T(8,128)(2,1)}, bf16[2,256,512]{2,1,0:T(8,128)(2,1)S(1)}, u32[]{:S(2)}, u32[]{:S(2)}) collective-permute-start(bf16[2,256,512]{2,1,0:T(8,128)(2,1)} %get-tuple-element.63), channel_id=1, source_target_pairs={{0,4},{4,0},{8,12},{12,8},{16,20},{20,16},{24,28},{28,24},{1,5},{5... | collective-permute-start | bytes 1572872 | tf_op jit(solution)/shard_map/ppermute | solution.py:424
  28.8 28.6 %collective-permute-start.11 = (bf16[2,256,512]{2,1,0:T(8,128)(2,1)S(1)}, bf16[2,256,512]{2,1,0:T(8,128)(2,1)S(1)}, u32[]{:S(2)}, u32[]{:S(2)}) collective-permute-start(bf16[2,256,512]{2,1,0:T(8,128)(2,1)S(1)} %collective-permute-done.9.recv), channel_id=1, source_target_pairs={{0,8},{8,16},{12,4},{16,24},{20,12},{28,20},{1,9},{9,17},{13,5},{1... | collective-permute-start | bytes 1572872 | tf_op jit(solution)/shard_map/ppermute | solution.py:424
  32.3 27.2 %collective-permute-start.8 = (bf16[2,256,512]{2,1,0:T(8,128)(2,1)S(1)}, bf16[2,256,512]{2,1,0:T(8,128)(2,1)}, u32[]{:S(2)}, u32[]{:S(2)}) collective-permute-start(bf16[2,256,512]{2,1,0:T(8,128)(2,1)S(1)} %collective-permute-done.6.recv), channel_id=1, source_target_pairs={{0,8},{8,16},{12,4},{16,24},{20,12},{28,20},{1,9},{9,17},{13,5},{1... | collective-permute-start | bytes 1572872 | tf_op jit(solution)/shard_map/ppermute | solution.py:424
  38.6 82.6 %collective-permute-start.33 = (bf16[16,128,512]{2,1,0:T(8,128)(2,1)}, bf16[16,128,512]{2,1,0:T(8,128)(2,1)}, u32[]{:S(2)}, u32[]{:S(2)}) collective-permute-start(bf16[16,128,512]{2,1,0:T(8,128)(2,1)} %refs_0_.1), channel_id=1, source_target_pairs={{0,2},{1,3},{2,0},{3,1},{4,6},{5,7},{6,4},{7,5},{8,10},{9,11},{10,... | collective-permute-start | bytes 6291464 | tf_op jit(solution)/shard_map/ppermute | solution.py:430
  44.3 26.5 %collective-permute-start.4 = (bf16[2,256,512]{2,1,0:T(8,128)(2,1)}, bf16[2,256,512]{2,1,0:T(8,128)(2,1)S(1)}, u32[]{:S(2)}, u32[]{:S(2)}) collective-permute-start(bf16[2,256,512]{2,1,0:T(8,128)(2,1)} %get-tuple-element.64.keep), channel_id=1, source_target_pairs={{4,12},{8,0},{12,20},{16,8},{20,28},{24,16},{5,13},{9,1},{13,21},{... | collective-permute-start | bytes 1572872 | tf_op jit(solution)/shard_map/ppermute | solution.py:424
  53.6 17.3 %collective-permute-start.5 = (bf16[2,256,512]{2,1,0:T(8,128)(2,1)}, bf16[2,256,512]{2,1,0:T(8,128)(2,1)S(1)}, u32[]{:S(2)}, u32[]{:S(2)}) collective-permute-start(bf16[2,256,512]{2,1,0:T(8,128)(2,1)} %collective-permute-done.3.recv), channel_id=1, source_target_pairs={{0,8},{8,16},{12,4},{16,24},{20,12},{28,20},{1,9},{9,17},{13,5},{1... | collective-permute-start | bytes 1572872 | tf_op jit(solution)/shard_map/ppermute | solution.py:424
  58.2 16.8 %collective-permute-start.1 = (bf16[2,256,512]{2,1,0:T(8,128)(2,1)}, bf16[2,256,512]{2,1,0:T(8,128)(2,1)S(1)}, u32[]{:S(2)}, u32[]{:S(2)}) collective-permute-start(bf16[2,256,512]{2,1,0:T(8,128)(2,1)} %get-tuple-element.62.keep), channel_id=1, source_target_pairs={{4,12},{8,0},{12,20},{16,8},{20,28},{24,16},{5,13},{9,1},{13,21},{... | collective-permute-start | bytes 1572872 | tf_op jit(solution)/shard_map/ppermute | solution.py:424
  59.5 19.7 %collective-permute-start.2 = (bf16[2,256,512]{2,1,0:T(8,128)(2,1)S(1)}, bf16[2,256,512]{2,1,0:T(8,128)(2,1)S(1)}, u32[]{:S(2)}, u32[]{:S(2)}) collective-permute-start(bf16[2,256,512]{2,1,0:T(8,128)(2,1)S(1)} %collective-permute-done.recv), channel_id=1, source_target_pairs={{0,8},{8,16},{12,4},{16,24},{20,12},{28,20},{1,9},{9,17},{13,5},{1... | collective-permute-start | bytes 1572872 | tf_op jit(solution)/shard_map/ppermute | solution.py:424
  83.3 15.4 %collective-permute-start.20 = (bf16[1,512,512]{2,1,0:T(8,128)(2,1)}, bf16[1,512,512]{2,1,0:T(8,128)(2,1)S(1)}, u32[]{:S(2)}, u32[]{:S(2)}) collective-permute-start(bf16[1,512,512]{2,1,0:T(8,128)(2,1)} %get-tuple-element.85), channel_id=1, source_target_pairs={{0,4},{4,0},{8,12},{12,8},{16,20},{20,16},{24,28},{28,24},{1,5},{5... | collective-permute-start | bytes 1572872 | tf_op jit(solution)/shard_map/ppermute | solution.py:424
  85.7 14.5 %collective-permute-start.22 = (bf16[1,512,512]{2,1,0:T(8,128)(2,1)}, bf16[1,512,512]{2,1,0:T(8,128)(2,1)S(1)}, u32[]{:S(2)}, u32[]{:S(2)}) collective-permute-start(bf16[1,512,512]{2,1,0:T(8,128)(2,1)} %get-tuple-element.83.refs_1_.refs_17_), channel_id=1, source_target_pairs={{0,2},{1,3},{2,0},{3,1},{4,6},{5,7},{6,4},{7,5},{8,10},{9,11},{10,... | collective-permute-start | bytes 1572872 | tf_op jit(solution)/shard_map/ppermute | solution.py:430
  87.2 13.0 %collective-permute-start.26 = (bf16[1,512,512]{2,1,0:T(8,128)(2,1)}, bf16[1,512,512]{2,1,0:T(8,128)(2,1)S(1)}, u32[]{:S(2)}, u32[]{:S(2)}) collective-permute-start(bf16[1,512,512]{2,1,0:T(8,128)(2,1)} %get-tuple-element.83.refs_1_.refs_17_), channel_id=1, source_target_pairs={{0,1},{1,0},{2,3},{3,2},{4,5},{5,4},{6,7},{7,6},{8,9},{9,8},{10,11... | collective-permute-start | bytes 1572872 | tf_op jit(solution)/shard_map/ppermute | solution.py:430
  87.2 20.4 %collective-permute-start.19 = (bf16[1,512,512]{2,1,0:T(8,128)(2,1)S(1)}, bf16[1,512,512]{2,1,0:T(8,128)(2,1)S(1)}, u32[]{:S(2)}, u32[]{:S(2)}) collective-permute-start(bf16[1,512,512]{2,1,0:T(8,128)(2,1)S(1)} %copy-done.36), channel_id=1, source_target_pairs={{0,4},{4,0},{8,12},{12,8},{16,20},{20,16},{24,28},{28,24},{1,5},{5... | collective-permute-start | bytes 1572872 | tf_op jit(solution)/shard_map/ppermute | solution.py:424
  98.7 14.8 %collective-permute-start.21 = (bf16[1,512,512]{2,1,0:T(8,128)(2,1)S(1)}, bf16[1,512,512]{2,1,0:T(8,128)(2,1)S(1)}, u32[]{:S(2)}, u32[]{:S(2)}) collective-permute-start(bf16[1,512,512]{2,1,0:T(8,128)(2,1)S(1)} %copy-done.2), channel_id=1, source_target_pairs={{0,2},{1,3},{2,0},{3,1},{4,6},{5,7},{6,4},{7,5},{8,10},{9,11},{10,... | collective-permute-start | bytes 1572872 | tf_op jit(solution)/shard_map/ppermute | solution.py:430
  100.2 13.3 %collective-permute-start.25 = (bf16[1,512,512]{2,1,0:T(8,128)(2,1)S(1)}, bf16[1,512,512]{2,1,0:T(8,128)(2,1)S(1)}, u32[]{:S(2)}, u32[]{:S(2)}) collective-permute-start(bf16[1,512,512]{2,1,0:T(8,128)(2,1)S(1)} %copy-done.2), channel_id=1, source_target_pairs={{0,1},{1,0},{2,3},{3,2},{4,5},{5,4},{6,7},{7,6},{8,9},{9,8},{10,11... | collective-permute-start | bytes 1572872 | tf_op jit(solution)/shard_map/ppermute | solution.py:430
  100.2 20.1 %collective-permute-start.24 = (bf16[1,512,512]{2,1,0:T(8,128)(2,1)S(1)}, bf16[1,512,512]{2,1,0:T(8,128)(2,1)S(1)}, u32[]{:S(2)}, u32[]{:S(2)}) collective-permute-start(bf16[1,512,512]{2,1,0:T(8,128)(2,1)S(1)} %collective-permute-done.20.refs_3_.refs_19_), channel_id=1, source_target_pairs={{0,2},{1,3},{2,0},{3,1},{4,6},{5,7},{6,4},{7,5},{8,10},{9,11},{10,... | collective-permute-start | bytes 1572872 | tf_op jit(solution)/shard_map/ppermute | solution.py:430
  107.6 35.1 %collective-permute-start.34 = (bf16[16,128,512]{2,1,0:T(8,128)(2,1)}, bf16[16,128,512]{2,1,0:T(8,128)(2,1)S(1)}, u32[]{:S(2)}, u32[]{:S(2)}) collective-permute-start(bf16[16,128,512]{2,1,0:T(8,128)(2,1)} %refs_0_.1), channel_id=1, source_target_pairs={{0,1},{1,0},{2,3},{3,2},{4,5},{5,4},{6,7},{7,6},{8,9},{9,8},{10,11... | collective-permute-start | bytes 6291464 | tf_op jit(solution)/shard_map/ppermute | solution.py:430
  120.3 20.9 %collective-permute-start.12 = (bf16[2,512,512]{2,1,0:T(8,128)(2,1)}, bf16[2,512,512]{2,1,0:T(8,128)(2,1)S(1)}, u32[]{:S(2)}, u32[]{:S(2)}) collective-permute-start(bf16[2,512,512]{2,1,0:T(8,128)(2,1)} %get-tuple-element.81), channel_id=1, source_target_pairs={{0,4},{4,0},{8,12},{12,8},{16,20},{20,16},{24,28},{28,24},{1,5},{5... | collective-permute-start | bytes 3145736 | tf_op jit(solution)/shard_map/ppermute | solution.py:424
  121.2 61.9 %collective-permute-start.35 = (bf16[16,128,512]{2,1,0:T(8,128)(2,1)}, bf16[16,128,512]{2,1,0:T(8,128)(2,1)S(1)}, u32[]{:S(2)}, u32[]{:S(2)}) collective-permute-start(bf16[16,128,512]{2,1,0:T(8,128)(2,1)} %collective-permute-done.33.refs_1_), channel_id=1, source_target_pairs={{0,1},{1,0},{2,3},{3,2},{4,5},{5,4},{6,7},{7,6},{8,9},{9,8},{10,11... | collective-permute-start | bytes 6291464 | tf_op jit(solution)/shard_map/ppermute | solution.py:430
  121.2 14.4 %collective-permute-start.23 = (bf16[1,512,512]{2,1,0:T(8,128)(2,1)S(1)}, bf16[1,512,512]{2,1,0:T(8,128)(2,1)}, u32[]{:S(2)}, u32[]{:S(2)}) collective-permute-start(bf16[1,512,512]{2,1,0:T(8,128)(2,1)S(1)} %collective-permute-done.19.refs_2_.refs_18_), channel_id=1, source_target_pairs={{0,2},{1,3},{2,0},{3,1},{4,6},{5,7},{6,4},{7,5},{8,10},{9,11},{10,... | collective-permute-start | bytes 1572872 | tf_op jit(solution)/shard_map/ppermute | solution.py:430
  122.7 14.4 %collective-permute-start.29 = (bf16[1,512,512]{2,1,0:T(8,128)(2,1)S(1)}, bf16[1,512,512]{2,1,0:T(8,128)(2,1)S(1)}, u32[]{:S(2)}, u32[]{:S(2)}) collective-permute-start(bf16[1,512,512]{2,1,0:T(8,128)(2,1)S(1)} %collective-permute-done.21.refs_4_.refs_20_), channel_id=1, source_target_pairs={{0,1},{1,0},{2,3},{3,2},{4,5},{5,4},{6,7},{7,6},{8,9},{9,8},{10,11... | collective-permute-start | bytes 1572872 | tf_op jit(solution)/shard_map/ppermute | solution.py:430
  135.6 26.3 %collective-permute-start.13 = (bf16[2,512,512]{2,1,0:T(8,128)(2,1)}, bf16[2,512,512]{2,1,0:T(8,128)(2,1)}, u32[]{:S(2)}, u32[]{:S(2)}) collective-permute-start(bf16[2,512,512]{2,1,0:T(8,128)(2,1)} %get-tuple-element.80.refs_0_.refs_8_), channel_id=1, source_target_pairs={{0,2},{1,3},{2,0},{3,1},{4,6},{5,7},{6,4},{7,5},{8,10},{9,11},{10,... | collective-permute-start | bytes 3145736 | tf_op jit(solution)/shard_map/ppermute | solution.py:430
  141.2 41.8 %collective-permute-start.14 = (bf16[2,512,512]{2,1,0:T(8,128)(2,1)S(1)}, bf16[2,512,512]{2,1,0:T(8,128)(2,1)}, u32[]{:S(2)}, u32[]{:S(2)}) collective-permute-start(bf16[2,512,512]{2,1,0:T(8,128)(2,1)S(1)} %collective-permute-done.12.refs_1_.refs_9_), channel_id=1, source_target_pairs={{0,2},{1,3},{2,0},{3,1},{4,6},{5,7},{6,4},{7,5},{8,10},{9,11},{10,... | collective-permute-start | bytes 3145736 | tf_op jit(solution)/shard_map/ppermute | solution.py:430
  142.7 19.3 %collective-permute-start.32 = (bf16[1,512,512]{2,1,0:T(8,128)(2,1)S(1)}, bf16[1,512,512]{2,1,0:T(8,128)(2,1)S(1)}, u32[]{:S(2)}, u32[]{:S(2)}) collective-permute-start(bf16[1,512,512]{2,1,0:T(8,128)(2,1)S(1)} %collective-permute-done.24.refs_7_.refs_23_), channel_id=1, source_target_pairs={{0,1},{1,0},{2,3},{3,2},{4,5},{5,4},{6,7},{7,6},{8,9},{9,8},{10,11... | collective-permute-start | bytes 1572872 | tf_op jit(solution)/shard_map/ppermute | solution.py:430
  142.7 53.4 %collective-permute-start.31 = (bf16[1,512,512]{2,1,0:T(8,128)(2,1)}, bf16[1,512,512]{2,1,0:T(8,128)(2,1)}, u32[]{:S(2)}, u32[]{:S(2)}) collective-permute-start(bf16[1,512,512]{2,1,0:T(8,128)(2,1)} %collective-permute-done.23.refs_6_.refs_22_), channel_id=1, source_target_pairs={{0,1},{1,0},{2,3},{3,2},{4,5},{5,4},{6,7},{7,6},{8,9},{9,8},{10,11... | collective-permute-start | bytes 1572872 | tf_op jit(solution)/shard_map/ppermute | solution.py:430
  162.0 59.9 %collective-permute-start.15 = (bf16[2,512,512]{2,1,0:T(8,128)(2,1)}, bf16[2,512,512]{2,1,0:T(8,128)(2,1)}, u32[]{:S(2)}, u32[]{:S(2)}) collective-permute-start(bf16[2,512,512]{2,1,0:T(8,128)(2,1)} %get-tuple-element.80.refs_0_.refs_8_), channel_id=1, source_target_pairs={{0,1},{1,0},{2,3},{3,2},{4,5},{5,4},{6,7},{7,6},{8,9},{9,8},{10,11... | collective-permute-start | bytes 3145736 | tf_op jit(solution)/shard_map/ppermute | solution.py:430
  162.0 59.9 %collective-permute-start.16 = (bf16[2,512,512]{2,1,0:T(8,128)(2,1)S(1)}, bf16[2,512,512]{2,1,0:T(8,128)(2,1)}, u32[]{:S(2)}, u32[]{:S(2)}) collective-permute-start(bf16[2,512,512]{2,1,0:T(8,128)(2,1)S(1)} %collective-permute-done.12.refs_1_.refs_9_), channel_id=1, source_target_pairs={{0,1},{1,0},{2,3},{3,2},{4,5},{5,4},{6,7},{7,6},{8,9},{9,8},{10,11... | collective-permute-start | bytes 3145736 | tf_op jit(solution)/shard_map/ppermute | solution.py:430
  183.0 38.8 %collective-permute-start.17 = (bf16[2,512,512]{2,1,0:T(8,128)(2,1)}, bf16[2,512,512]{2,1,0:T(8,128)(2,1)}, u32[]{:S(2)}, u32[]{:S(2)}) collective-permute-start(bf16[2,512,512]{2,1,0:T(8,128)(2,1)} %collective-permute-done.13.refs_2_.refs_10_), channel_id=1, source_target_pairs={{0,1},{1,0},{2,3},{3,2},{4,5},{5,4},{6,7},{7,6},{8,9},{9,8},{10,11... | collective-permute-start | bytes 3145736 | tf_op jit(solution)/shard_map/ppermute | solution.py:430
  184.5 37.4 %collective-permute-start.18 = (bf16[2,512,512]{2,1,0:T(8,128)(2,1)}, bf16[2,512,512]{2,1,0:T(8,128)(2,1)}, u32[]{:S(2)}, u32[]{:S(2)}) collective-permute-start(bf16[2,512,512]{2,1,0:T(8,128)(2,1)} %collective-permute-done.14.refs_3_.refs_11_), channel_id=1, source_target_pairs={{0,1},{1,0},{2,3},{3,2},{4,5},{5,4},{6,7},{7,6},{8,9},{9,8},{10,11... | collective-permute-start | bytes 3145736 | tf_op jit(solution)/shard_map/ppermute | solution.py:430
  240.2 57.7 %collective-permute-start.36 = (bf16[4,2,64,512]{3,2,1,0:T(8,128)(2,1)}, bf16[4,2,64,512]{3,2,1,0:T(8,128)(2,1)S(1)}, u32[]{:S(2)}, u32[]{:S(2)}) collective-permute-start(bf16[4,2,64,512]{3,2,1,0:T(8,128)(2,1)} %get-tuple-element.93), channel_id=1, source_target_pairs={{0,4},{4,0},{8,12},{12,8},{16,20},{20,16},{24,28},{28,24},{1,5},{5... | collective-permute-start | bytes 1572872 | tf_op jit(solution)/shard_map/ppermute | solution.py:424
  254.3 40.3 %collective-permute-start.52 = (bf16[4,1,64,512]{3,2,1,0:T(8,128)(2,1)S(1)}, bf16[4,1,64,512]{3,2,1,0:T(8,128)(2,1)S(1)}, u32[]{:S(2)}, u32[]{:S(2)}) collective-permute-start(bf16[4,1,64,512]{3,2,1,0:T(8,128)(2,1)S(1)} %get-tuple-element.117), channel_id=1, source_target_pairs={{0,4},{4,0},{8,12},{12,8},{16,20},{20,16},{24,28},{28,24},{1,5},{5... | collective-permute-start | bytes 786440 | tf_op jit(solution)/shard_map/ppermute | solution.py:424
  262.9 32.7 %collective-permute-start.49 = (bf16[1,64,512]{2,1,0:T(8,128)(2,1)S(1)}, bf16[1,64,512]{2,1,0:T(8,128)(2,1)S(1)}, u32[]{:S(2)}, u32[]{:S(2)}) collective-permute-start(bf16[1,64,512]{2,1,0:T(8,128)(2,1)S(1)} %get-tuple-element.113), channel_id=1, source_target_pairs={{0,8},{4,12},{8,16},{12,20},{16,24},{20,28},{24,0},{28,4},{1,9},{5... | collective-permute-start | bytes 196616 | tf_op jit(solution)/shard_map/ppermute | solution.py:424
  264.6 32.3 %collective-permute-start.50 = (bf16[1,64,512]{2,1,0:T(8,128)(2,1)S(1)}, bf16[1,64,512]{2,1,0:T(8,128)(2,1)S(1)}, u32[]{:S(2)}, u32[]{:S(2)}) collective-permute-start(bf16[1,64,512]{2,1,0:T(8,128)(2,1)S(1)} %get-tuple-element.114), channel_id=1, source_target_pairs={{0,16},{4,20},{8,24},{12,28},{16,0},{20,4},{24,8},{28,12},{1,17},{... | collective-permute-start | bytes 196616 | tf_op jit(solution)/shard_map/ppermute | solution.py:424
  266.5 30.4 %collective-permute-start.51 = (bf16[1,64,512]{2,1,0:T(8,128)(2,1)S(1)}, bf16[1,64,512]{2,1,0:T(8,128)(2,1)S(1)}, u32[]{:S(2)}, u32[]{:S(2)}) collective-permute-start(bf16[1,64,512]{2,1,0:T(8,128)(2,1)S(1)} %get-tuple-element.115), channel_id=1, source_target_pairs={{0,24},{4,28},{8,0},{12,4},{16,8},{20,12},{24,16},{28,20},{1,25},{... | collective-permute-start | bytes 196616 | tf_op jit(solution)/shard_map/ppermute | solution.py:424
  294.6 15.5 %collective-permute-start.40 = (bf16[4,2,64,512]{3,2,1,0:T(8,128)(2,1)S(1)}, bf16[4,2,64,512]{3,2,1,0:T(8,128)(2,1)S(1)}, u32[]{:S(2)}, u32[]{:S(2)}) collective-permute-start(bf16[4,2,64,512]{3,2,1,0:T(8,128)(2,1)S(1)} %copy-done.15), channel_id=1, source_target_pairs={{0,4},{4,0},{8,12},{12,8},{16,20},{20,16},{24,28},{28,24},{1,5},{5... | collective-permute-start | bytes 1572872 | tf_op jit(solution)/shard_map/ppermute | solution.py:424
  295.7 20.9 %collective-permute-start.44 = (bf16[4,2,64,512]{3,2,1,0:T(8,128)(2,1)S(1)}, bf16[4,2,64,512]{3,2,1,0:T(8,128)(2,1)S(1)}, u32[]{:S(2)}, u32[]{:S(2)}) collective-permute-start(bf16[4,2,64,512]{3,2,1,0:T(8,128)(2,1)S(1)} %copy-done.13), channel_id=1, source_target_pairs={{0,4},{4,0},{8,12},{12,8},{16,20},{20,16},{24,28},{28,24},{1,5},{5... | collective-permute-start | bytes 1572872 | tf_op jit(solution)/shard_map/ppermute | solution.py:424
  303.6 13.5 %collective-permute-start.37 = (bf16[2,64,512]{2,1,0:T(8,128)(2,1)S(1)}, bf16[2,64,512]{2,1,0:T(8,128)(2,1)S(1)}, u32[]{:S(2)}, u32[]{:S(2)}) collective-permute-start(bf16[2,64,512]{2,1,0:T(8,128)(2,1)S(1)} %get-tuple-element.95), channel_id=1, source_target_pairs={{0,8},{4,12},{8,16},{12,20},{16,24},{20,28},{24,0},{28,4},{1,9},{5... | collective-permute-start | bytes 393224 | tf_op jit(solution)/shard_map/ppermute | solution.py:424
  305.6 13.6 %collective-permute-start.38 = (bf16[2,64,512]{2,1,0:T(8,128)(2,1)S(1)}, bf16[2,64,512]{2,1,0:T(8,128)(2,1)S(1)}, u32[]{:S(2)}, u32[]{:S(2)}) collective-permute-start(bf16[2,64,512]{2,1,0:T(8,128)(2,1)S(1)} %get-tuple-element.96), channel_id=1, source_target_pairs={{0,16},{4,20},{8,24},{12,28},{16,0},{20,4},{24,8},{28,12},{1,17},{... | collective-permute-start | bytes 393224 | tf_op jit(solution)/shard_map/ppermute | solution.py:424
  306.3 12.8 %collective-permute-start.39 = (bf16[2,64,512]{2,1,0:T(8,128)(2,1)S(1)}, bf16[2,64,512]{2,1,0:T(8,128)(2,1)S(1)}, u32[]{:S(2)}, u32[]{:S(2)}) collective-permute-start(bf16[2,64,512]{2,1,0:T(8,128)(2,1)S(1)} %get-tuple-element.97), channel_id=1, source_target_pairs={{0,24},{4,28},{8,0},{12,4},{16,8},{20,12},{24,16},{28,20},{1,25},{... | collective-permute-start | bytes 393224 | tf_op jit(solution)/shard_map/ppermute | solution.py:424
  310.3 14.3 %collective-permute-start.41 = (bf16[2,64,512]{2,1,0:T(8,128)(2,1)S(1)}, bf16[2,64,512]{2,1,0:T(8,128)(2,1)S(1)}, u32[]{:S(2)}, u32[]{:S(2)}) collective-permute-start(bf16[2,64,512]{2,1,0:T(8,128)(2,1)S(1)} %get-tuple-element.101), channel_id=1, source_target_pairs={{0,8},{4,12},{8,16},{12,20},{16,24},{20,28},{24,0},{28,4},{1,9},{5... | collective-permute-start | bytes 393224 | tf_op jit(solution)/shard_map/ppermute | solution.py:424
  316.6 12.8 %collective-permute-start.42 = (bf16[2,64,512]{2,1,0:T(8,128)(2,1)S(1)}, bf16[2,64,512]{2,1,0:T(8,128)(2,1)S(1)}, u32[]{:S(2)}, u32[]{:S(2)}) collective-permute-start(bf16[2,64,512]{2,1,0:T(8,128)(2,1)S(1)} %get-tuple-element.102), channel_id=1, source_target_pairs={{0,16},{4,20},{8,24},{12,28},{16,0},{20,4},{24,8},{28,12},{1,17},{... | collective-permute-start | bytes 393224 | tf_op jit(solution)/shard_map/ppermute | solution.py:424
  317.1 12.3 %collective-permute-start.43 = (bf16[2,64,512]{2,1,0:T(8,128)(2,1)S(1)}, bf16[2,64,512]{2,1,0:T(8,128)(2,1)S(1)}, u32[]{:S(2)}, u32[]{:S(2)}) collective-permute-start(bf16[2,64,512]{2,1,0:T(8,128)(2,1)S(1)} %get-tuple-element.103), channel_id=1, source_target_pairs={{0,24},{4,28},{8,0},{12,4},{16,8},{20,12},{24,16},{28,20},{1,25},{... | collective-permute-start | bytes 393224 | tf_op jit(solution)/shard_map/ppermute | solution.py:424
  319.2 17.2 %collective-permute-start.46 = (bf16[2,64,512]{2,1,0:T(8,128)(2,1)S(1)}, bf16[2,64,512]{2,1,0:T(8,128)(2,1)S(1)}, u32[]{:S(2)}, u32[]{:S(2)}) collective-permute-start(bf16[2,64,512]{2,1,0:T(8,128)(2,1)S(1)} %get-tuple-element.108), channel_id=1, source_target_pairs={{0,16},{4,20},{8,24},{12,28},{16,0},{20,4},{24,8},{28,12},{1,17},{... | collective-permute-start | bytes 393224 | tf_op jit(solution)/shard_map/ppermute | solution.py:424
  324.7 11.8 %collective-permute-start.47 = (bf16[2,64,512]{2,1,0:T(8,128)(2,1)S(1)}, bf16[2,64,512]{2,1,0:T(8,128)(2,1)S(1)}, u32[]{:S(2)}, u32[]{:S(2)}) collective-permute-start(bf16[2,64,512]{2,1,0:T(8,128)(2,1)S(1)} %get-tuple-element.109), channel_id=1, source_target_pairs={{0,24},{4,28},{8,0},{12,4},{16,8},{20,12},{24,16},{28,20},{1,25},{... | collective-permute-start | bytes 393224 | tf_op jit(solution)/shard_map/ppermute | solution.py:424
  (47 other events, 1365.5 us)

commit v8 on v6

--- a/solution.py
+++ b/solution.py
@@ -81,21 +81,21 @@
     )(which[None], green, broadening)
 
 
-def place_kernel(where, *refs):
+def place_kernel(order, where, *refs):
     pieces, (full_ref, turned_ref) = refs[:-2], refs[-2:]
     rows = pieces[0].shape[1]
     for at, c_ref in enumerate(pieces):
-        start = pl.ds(pl.multiple_of(where[at] * rows, rows), rows)
+        start = pl.ds(pl.multiple_of((where[0] ^ order[at]) * rows, rows), rows)
         for q in range(c_ref.shape[0]):
             full_ref[q, start, :] = c_ref[q]
             turned_ref[q, :, start] = c_ref[q].T
 
 
-def place_coupling(where, pieces):
+def place_coupling(where, order, pieces):
     nk, rows, n = pieces[0].shape
     each = 2
     return pl.pallas_call(
-        place_kernel,
+        functools.partial(place_kernel, order),
         out_shape=[pltpu.HBM((nk, n, n), BF16)] * 2,
         grid_spec=pltpu.PrefetchScalarGridSpec(
             num_scalar_prefetch=1,
@@ -106,7 +106,7 @@
         compiler_params=params(56),
         cost_estimate=cost(nk * n * n * 4, nk * n * n * 6),
         name="place",
-    )(where, *pieces)
+    )(where[None], *pieces)
 
 
 def source_kernel(odd, steps, strength, boson, keep, recv, kz, rz, *refs):
@@ -228,13 +228,13 @@
     )(mine[None], slots, *pieces, full, turned)
 
 
-def rows_kernel(pieces, mine, slots, *refs):
+def rows_kernel(pieces, base, mine, slots, *refs):
     a_refs, b_refs, refs = refs[:pieces], refs[pieces:2 * pieces], refs[2 * pieces:]
     c_ref, out_ref, d_ref = (refs[0],) + refs[-2:]
     each, rows, cols = a_refs[0].shape
     count = pieces * each
     row, col = row_col(rows, cols)
-    above = (col - row) + (pl.program_id(0) * cols - mine[0] * rows)
+    above = (col - row) + ((base + pl.program_id(0)) * cols - mine[0] * rows)
     for s in range(pieces):
         for j in range(each):
             a, b = a_refs[s][j].astype(F32), b_refs[s][j].astype(F32).T
@@ -269,25 +269,25 @@
     lax.fori_loop(0, wide * (rows // tr) * (count // kg), tile, 0)
 
 
-def own_rows(mine, slots, pieces, coupling, energy, le, held):
+def own_rows(mine, slots, pieces, coupling, energy, le, base, steps, held):
     each, n, _ = pieces[0].shape
     count, rows, _ = coupling.shape
     cols = n // 2
     alias = [] if held is None else [held]
     in_specs = (
-        [pl.BlockSpec((each, rows, cols), lambda t, mine, slots: (0, mine[0], t))] * len(pieces)
-        + [pl.BlockSpec((each, cols, rows), lambda t, mine, slots: (0, t, mine[0]))] * len(pieces)
-        + [pl.BlockSpec((count, rows, cols), lambda t, mine, slots: (0, 0, t))]
+        [pl.BlockSpec((each, rows, cols), lambda t, mine, slots: (0, mine[0], base + t))] * len(pieces)
+        + [pl.BlockSpec((each, cols, rows), lambda t, mine, slots: (0, base + t, mine[0]))] * len(pieces)
+        + [pl.BlockSpec((count, rows, cols), lambda t, mine, slots: (0, 0, base + t))]
         + [pl.BlockSpec(memory_space=pl.ANY)] * len(alias)
     )
     return pl.pallas_call(
-        functools.partial(rows_kernel, len(pieces)),
+        functools.partial(rows_kernel, len(pieces), base),
         out_shape=jax.ShapeDtypeStruct((count, le, 2, rows, n), BF16),
         grid_spec=pltpu.PrefetchScalarGridSpec(
             num_scalar_prefetch=2,
-            grid=(n // cols,),
+            grid=(steps,),
             in_specs=in_specs,
-            out_specs=pl.BlockSpec((count, 1, 2, rows, cols), lambda t, mine, slots: (0, energy, 0, 0, t)),
+            out_specs=pl.BlockSpec((count, 1, 2, rows, cols), lambda t, mine, slots: (0, energy, 0, 0, base + t)),
             scratch_shapes=[pltpu.VMEM((count, 2, rows, cols), BF16)],
         ),
         input_output_aliases={2 + len(in_specs) - 1: 0} if alias else {},
@@ -464,7 +464,7 @@
                 odd, modes, j, h, hk, keep[j][h], recv[j][h], kz[j][h], rz[j][h], last)
         got.append(last)
 
-    full, turned = place_coupling(jnp.stack([mine ^ o for o in order]), coupling_pieces)
+    full, turned = place_coupling(mine, tuple(order), coupling_pieces)
 
     held_rows, held_density = None, None
     scale = 1.0 / (le * ne)
@@ -480,7 +480,7 @@
         else:
             shares = []
             x, y = home_blocks(mine, slots, pieces, full, turned, lk)
-            for first, count in ((0, 1), (1, lk - 1)):
+            for first, count in ((0, 1), (1, 1), (2, lk - 2)):
                 shares = shares + list(last_density(
                     scale, e, first, count, groups, odd,
                     green_ret, broadening, x, y, held_density))
@@ -493,7 +493,9 @@
                     perm = [(i, (i + 2 * d) % ne) for i in range(ne)]
                     total = total + permuted(parts[d], perm).astype(F32)
                 late.append(total)
-        held_rows = own_rows(mine, slots, pieces, coupling, e, le, held_rows)
+        for base, steps in (((0, 2),) if e < le - 1 else ((0, 1), (1, 1))):
+            held_rows = own_rows(
+                mine, slots, pieces, coupling, e, le, base, steps, held_rows)
     density = jnp.transpose(jnp.stack(late), (2, 0, 1, 3))
     return held_rows, density
 

time: 335 us -> 342 us (1.021)
  Pallas kernels: 124 us -> 130 us
    unnamed x77 -> x75, local copies, waits for them, and re-layouts: 10 us -> 6.69 us
    pallas_call x3 -> x4, Pallas kernels: 37.8 us -> 41 us  [the longest x3 29.9 us: own_rows(): pl.pallas_call(functools.partial(rows_kernel, len(pieces), base), out_sha...]
    pallas_call x2 -> x3, Pallas kernels: 16.3 us -> 18.9 us  [last_density(): pl.pallas_call(functools.partial(last_density_kernel, scale, energy), out...]
where the time goes in v8:
time: 342 us; the launch traced here: 341 us
  Pallas kernels  130 us (38%)
  waiting for transfers between devices  126 us (37%)
  starting transfers between devices  76.4 us (22%)
  local copies, waits for them, and re-layouts  6.69 us (2%)
    ppermute x31, starting transfers between devices, permuted(): return lax.ppermute(x, 'energy', perm)  64.6 us
    ppermute x21, waiting for transfers between devices, swap(): moved = lax.ppermute(x, 'mom', [(i, i ^ stride) for i in range(nm)])  64.2 us
    ppermute x31, waiting for transfers between devices, permuted(): return lax.ppermute(x, 'energy', perm)  61.8 us
    pallas_call x3, Pallas kernels, own_rows(): pl.pallas_call(functools.partial(rows_kernel, len(pieces), base), out_sha...  29.9 us
    pallas_call x2, Pallas kernels, home_blocks(): pl.pallas_call(functools.partial(home_kernel, lk, len(pieces)), out_shape...  26.1 us
    pallas_call x3, Pallas kernels, last_density(): pl.pallas_call(functools.partial(last_density_kernel, scale, energy), out...  18.9 us
    pallas_call x4, Pallas kernels, lesser_packed(): pl.pallas_call(lesser_kernel, out_shape=[pltpu.HBM((le, n // 2, n), BF16)...  16.5 us
    pallas_call x4, Pallas kernels, sources(): pl.pallas_call(source_kernel, out_shape=[pltpu.HBM(shape, BF16) for shape...  13.2 us
  transfers between devices with their start and end apart: 52, of which 17 were waited for; matrix products, arithmetic and copies ran while one was open for 0% of the time, Pallas kernels for 30%

profile of v8, /device:TPU:0, one launch (start us, length us, event | category | flops | bytes accessed | tf_op | source)
XLA Modules:
  0.0 340.7 jit_solution(6707349360762270460)
XLA Ops:
  0.6 4.1 %lesser.7 = (bf16[2,256,512]{2,1,0:T(8,128)(2,1)}, bf16[2,256,512]{2,1,0:T(8,128)(2,1)}) custom-call(s32[1]{0:T(128)} %bitcast.5.sel, bf16[4,2,2,512,512]{4,3,2,1,0:T(8,128)(2,1)} %g_ref.15, f32[4,2,512]{2,1,0:T(2,128)} %gamma_ref.15), custom_call_target="tpu_custom_call" | custom-call | flops 1610612736 | bytes 3145728 | tf_op jit(solution)/shard_map/lesser/pallas_call | solution.py:66
  4.8 3.0 collective-permute-start.9
  7.8 4.1 %lesser.6 = (bf16[2,256,512]{2,1,0:T(8,128)(2,1)}, bf16[2,256,512]{2,1,0:T(8,128)(2,1)}) custom-call(s32[1]{0:T(128)} %bitcast.4.sel, bf16[4,2,2,512,512]{4,3,2,1,0:T(8,128)(2,1)} %g_ref.15, f32[4,2,512]{2,1,0:T(2,128)} %gamma_ref.15), custom_call_target="tpu_custom_call" | custom-call | flops 1610612736 | bytes 3145728 | tf_op jit(solution)/shard_map/lesser/pallas_call | solution.py:66
  13.2 2.8 collective-permute-start.6
  17.2 4.1 %lesser.5 = (bf16[2,256,512]{2,1,0:T(8,128)(2,1)}, bf16[2,256,512]{2,1,0:T(8,128)(2,1)}) custom-call(s32[1]{0:T(128)} %bitcast.3.sel, bf16[4,2,2,512,512]{4,3,2,1,0:T(8,128)(2,1)} %g_ref.15, f32[4,2,512]{2,1,0:T(2,128)} %gamma_ref.15), custom_call_target="tpu_custom_call" | custom-call | flops 1610612736 | bytes 3145728 | tf_op jit(solution)/shard_map/lesser/pallas_call | solution.py:66
  21.4 2.6 collective-permute-start.3
  24.0 4.7 %collective-permute-done.10.kz = bf16[2,256,512]{2,1,0:T(8,128)(2,1)S(1)} collective-permute-done((bf16[2,256,512]{2,1,0:T(8,128)(2,1)}, bf16[2,256,512]{2,1,0:T(8,128)(2,1)S(1)}, u32[]{:S(2)}, u32[]{:S(2)}) %collective-permute-start.10) | collective-permute-done | bytes 524320 | tf_op jit(solution)/shard_map/ppermute | solution.py:424
  28.7 3.5 %collective-permute-start.11 = (bf16[2,256,512]{2,1,0:T(8,128)(2,1)S(1)}, bf16[2,256,512]{2,1,0:T(8,128)(2,1)S(1)}, u32[]{:S(2)}, u32[]{:S(2)}) collective-permute-start(bf16[2,256,512]{2,1,0:T(8,128)(2,1)S(1)} %collective-permute-done.9.recv), channel_id=1, source_target_pairs={{0,8},{8,16},{12,4},{16,24},{20,12},{28,20},{1,9},{9,17},{13,5},{1... | collective-permute-start | bytes 1572872 | tf_op jit(solution)/shard_map/ppermute | solution.py:424
  32.3 4.5 %collective-permute-start.8 = (bf16[2,256,512]{2,1,0:T(8,128)(2,1)S(1)}, bf16[2,256,512]{2,1,0:T(8,128)(2,1)}, u32[]{:S(2)}, u32[]{:S(2)}) collective-permute-start(bf16[2,256,512]{2,1,0:T(8,128)(2,1)S(1)} %collective-permute-done.6.recv), channel_id=1, source_target_pairs={{0,8},{8,16},{12,4},{16,24},{20,12},{28,20},{1,9},{9,17},{13,5},{1... | collective-permute-start | bytes 1572872 | tf_op jit(solution)/shard_map/ppermute | solution.py:424
  40.1 4.2 %lesser.4 = (bf16[2,256,512]{2,1,0:T(8,128)(2,1)}, bf16[2,256,512]{2,1,0:T(8,128)(2,1)}) custom-call(s32[1]{0:T(128)} %bitcast.2.sel, bf16[4,2,2,512,512]{4,3,2,1,0:T(8,128)(2,1)} %g_ref.15, f32[4,2,512]{2,1,0:T(2,128)} %gamma_ref.15), custom_call_target="tpu_custom_call" | custom-call | flops 1610612736 | bytes 3145728 | tf_op jit(solution)/shard_map/lesser/pallas_call | solution.py:66
  45.7 7.9 %collective-permute-done.recv = bf16[2,256,512]{2,1,0:T(8,128)(2,1)S(1)} collective-permute-done((bf16[2,256,512]{2,1,0:T(8,128)(2,1)}, bf16[2,256,512]{2,1,0:T(8,128)(2,1)S(1)}, u32[]{:S(2)}, u32[]{:S(2)}) %collective-permute-start) | collective-permute-done | bytes 524320 | tf_op jit(solution)/shard_map/ppermute | solution.py:424
  53.6 3.7 %collective-permute-start.5 = (bf16[2,256,512]{2,1,0:T(8,128)(2,1)}, bf16[2,256,512]{2,1,0:T(8,128)(2,1)S(1)}, u32[]{:S(2)}, u32[]{:S(2)}) collective-permute-start(bf16[2,256,512]{2,1,0:T(8,128)(2,1)} %collective-permute-done.3.recv), channel_id=1, source_target_pairs={{0,8},{8,16},{12,4},{16,24},{20,12},{28,20},{1,9},{9,17},{13,5},{1... | collective-permute-start | bytes 1572872 | tf_op jit(solution)/shard_map/ppermute | solution.py:424
  59.5 4.8 %collective-permute-start.2 = (bf16[2,256,512]{2,1,0:T(8,128)(2,1)S(1)}, bf16[2,256,512]{2,1,0:T(8,128)(2,1)S(1)}, u32[]{:S(2)}, u32[]{:S(2)}) collective-permute-start(bf16[2,256,512]{2,1,0:T(8,128)(2,1)S(1)} %collective-permute-done.recv), channel_id=1, source_target_pairs={{0,8},{8,16},{12,4},{16,24},{20,12},{28,20},{1,9},{9,17},{13,5},{1... | collective-permute-start | bytes 1572872 | tf_op jit(solution)/shard_map/ppermute | solution.py:424
  64.3 3.3 source.4
  67.6 3.3 source.5
  71.7 3.3 source.6
  75.0 4.2 %collective-permute-done.2.rz = bf16[2,256,512]{2,1,0:T(8,128)(2,1)S(1)} collective-permute-done((bf16[2,256,512]{2,1,0:T(8,128)(2,1)S(1)}, bf16[2,256,512]{2,1,0:T(8,128)(2,1)S(1)}, u32[]{:S(2)}, u32[]{:S(2)}) %collective-permute-start.2) | collective-permute-done | bytes 524320 | tf_op jit(solution)/shard_map/ppermute | solution.py:424
  80.0 3.3 source.7
  83.3 2.4 collective-permute-start.20
  87.2 11.4 %collective-permute-done.20.refs_3_.refs_19_ = bf16[1,512,512]{2,1,0:T(8,128)(2,1)S(1)} collective-permute-done((bf16[1,512,512]{2,1,0:T(8,128)(2,1)}, bf16[1,512,512]{2,1,0:T(8,128)(2,1)S(1)}, u32[]{:S(2)}, u32[]{:S(2)}) %collective-permute-start.20) | collective-permute-done | bytes 524320 | tf_op jit(solution)/shard_map/ppermute | solution.py:424
  100.8 6.8 %collective-permute-done.19.refs_2_.refs_18_ = bf16[1,512,512]{2,1,0:T(8,128)(2,1)S(1)} collective-permute-done((bf16[1,512,512]{2,1,0:T(8,128)(2,1)S(1)}, bf16[1,512,512]{2,1,0:T(8,128)(2,1)S(1)}, u32[]{:S(2)}, u32[]{:S(2)}) %collective-permute-start.19) | collective-permute-done | bytes 524320 | tf_op jit(solution)/shard_map/ppermute | solution.py:424
  107.5 5.9 %collective-permute-done.21.refs_4_.refs_20_ = bf16[1,512,512]{2,1,0:T(8,128)(2,1)S(1)} collective-permute-done((bf16[1,512,512]{2,1,0:T(8,128)(2,1)S(1)}, bf16[1,512,512]{2,1,0:T(8,128)(2,1)S(1)}, u32[]{:S(2)}, u32[]{:S(2)}) %collective-permute-start.21) | collective-permute-done | bytes 524320 | tf_op jit(solution)/shard_map/ppermute | solution.py:430
  114.0 6.3 %collective-permute-done.24.refs_7_.refs_23_ = bf16[1,512,512]{2,1,0:T(8,128)(2,1)S(1)} collective-permute-done((bf16[1,512,512]{2,1,0:T(8,128)(2,1)S(1)}, bf16[1,512,512]{2,1,0:T(8,128)(2,1)S(1)}, u32[]{:S(2)}, u32[]{:S(2)}) %collective-permute-start.24) | collective-permute-done | bytes 524320 | tf_op jit(solution)/shard_map/ppermute | solution.py:430
  122.8 12.7 %collective-permute-done.23.refs_6_.refs_22_ = bf16[1,512,512]{2,1,0:T(8,128)(2,1)} collective-permute-done((bf16[1,512,512]{2,1,0:T(8,128)(2,1)S(1)}, bf16[1,512,512]{2,1,0:T(8,128)(2,1)}, u32[]{:S(2)}, u32[]{:S(2)}) %collective-permute-start.23) | collective-permute-done | bytes 524320 | tf_op jit(solution)/shard_map/ppermute | solution.py:430
  137.1 4.1 %collective-permute-done.12.refs_1_.refs_9_ = bf16[2,512,512]{2,1,0:T(8,128)(2,1)S(1)} collective-permute-done((bf16[2,512,512]{2,1,0:T(8,128)(2,1)}, bf16[2,512,512]{2,1,0:T(8,128)(2,1)S(1)}, u32[]{:S(2)}, u32[]{:S(2)}) %collective-permute-start.12) | collective-permute-done | bytes 1048608 | tf_op jit(solution)/shard_map/ppermute | solution.py:424
  143.2 18.7 %collective-permute-done.13.refs_2_.refs_10_ = bf16[2,512,512]{2,1,0:T(8,128)(2,1)} collective-permute-done((bf16[2,512,512]{2,1,0:T(8,128)(2,1)}, bf16[2,512,512]{2,1,0:T(8,128)(2,1)}, u32[]{:S(2)}, u32[]{:S(2)}) %collective-permute-start.13) | collective-permute-done | bytes 1048608 | tf_op jit(solution)/shard_map/ppermute | solution.py:430
  162.4 20.6 %collective-permute-done.14.refs_3_.refs_11_ = bf16[2,512,512]{2,1,0:T(8,128)(2,1)} collective-permute-done((bf16[2,512,512]{2,1,0:T(8,128)(2,1)S(1)}, bf16[2,512,512]{2,1,0:T(8,128)(2,1)}, u32[]{:S(2)}, u32[]{:S(2)}) %collective-permute-start.14) | collective-permute-done | bytes 1048608 | tf_op jit(solution)/shard_map/ppermute | solution.py:430
  185.0 11.1 %place.1 = (bf16[16,512,512]{2,1,0:T(8,128)(2,1)}, bf16[16,512,512]{2,1,0:T(8,128)(2,1)}) custom-call(s32[1]{0:T(128)} %bitcast.mine.where, bf16[16,128,512]{2,1,0:T(8,128)(2,1)} %refs_0_.1, bf16[16,128,512]{2,1,0:T(8,128)(2,1)} %collective-permute-done.33.refs_1_, bf16[16,128,512]{2,1,0:T(8,128)(2,1)} %copy-done.27, bf16[16,128,512]{2,1,0:T(8,128)(2,1)} %copy-done.28), custom_call_target="tpu_custom_call" | custom-call | flops 16777216 | bytes 25165824 | tf_op jit(solution)/shard_map/place/pallas_call | solution.py:97
  196.1 12.9 %home.3 = (bf16[4,512,512]{2,1,0:T(8,128)(2,1)S(1)}, bf16[4,512,512]{2,1,0:T(8,128)(2,1)S(1)}) custom-call(s32[1]{0:T(128)} %bitcast.mine.where, s32[16,16]{1,0:T(8,128)S(1)} %fusion.4.slots, bf16[1,512,512]{2,1,0:T(8,128)(2,1)S(1)} %copy-done.2, bf16[1,512,512]{2,1,0:T(8,128)(2,1)S(1)} %copy-done.1, bf16[1,512,512]{2,1,0:T(8,128)(2,1)} %copy-done.18, ...), custom_call_target="tpu_custom_call" | custom-call | flops 67108864 | bytes 29360128 | tf_op jit(solution)/shard_map/home/pallas_call | solution.py:215
  209.1 12.7 %density.4.held_ref = f32[4,2,512,512]{3,2,1,0:T(8,128)} custom-call(bf16[4,2,2,512,512]{4,3,2,1,0:T(8,128)(2,1)} %g_ref.15, f32[4,2,512]{2,1,0:T(2,128)S(1)} %copy-done.3, bf16[4,512,512]{2,1,0:T(8,128)(2,1)S(1)} %get-tuple-element.84.x_ref, bf16[4,512,512]{2,1,0:T(8,128)(2,1)S(1)} %get-tuple-element.85.y_ref), custom_call_target="tpu_custom_call" | custom-call | flops 8589934592 | bytes 20971520 | tf_op jit(solution)/shard_map/density/pallas_call | solution.py:325
  221.9 13.2 %home.2 = (bf16[4,512,512]{2,1,0:T(8,128)(2,1)S(1)}, bf16[4,512,512]{2,1,0:T(8,128)(2,1)S(1)}) custom-call(s32[1]{0:T(128)} %bitcast.mine.where, s32[16,16]{1,0:T(8,128)S(1)} %fusion.4.slots, bf16[2,512,512]{2,1,0:T(8,128)(2,1)S(1)} %copy-done, bf16[2,512,512]{2,1,0:T(8,128)(2,1)} %copy-done.14, ...), custom_call_target="tpu_custom_call" | custom-call | flops 67108864 | bytes 29360128 | tf_op jit(solution)/shard_map/home/pallas_call | solution.py:215
  235.0 5.3 %density.5 = (bf16[4,2,64,512]{3,2,1,0:T(8,128)(2,1)S(1)}, bf16[4,2,64,512]{3,2,1,0:T(8,128)(2,1)}) custom-call(s32[1]{0:T(128)} %bitcast.1.odd, bf16[4,2,2,512,512]{4,3,2,1,0:T(8,128)(2,1)} %g_ref.15, f32[4,2,512]{2,1,0:T(2,128)S(1)} %copy-done.3, bf16[4,512,512]{2,1,0:T(8,128)(2,1)S(1)} %get-tuple-element.82.x_ref, ...), custom_call_target="tpu_custom_call" | custom-call | flops 2147483648 | bytes 5242880 | tf_op jit(solution)/shard_map/density/pallas_call | solution.py:365
  240.4 5.5 %density.6 = (bf16[4,2,64,512]{3,2,1,0:T(8,128)(2,1)S(1)}, bf16[4,2,64,512]{3,2,1,0:T(8,128)(2,1)}) custom-call(s32[1]{0:T(128)} %bitcast.1.odd, bf16[4,2,2,512,512]{4,3,2,1,0:T(8,128)(2,1)} %g_ref.15, f32[4,2,512]{2,1,0:T(2,128)S(1)} %copy-done.3, bf16[4,512,512]{2,1,0:T(8,128)(2,1)S(1)} %get-tuple-element.82.x_ref, ...), custom_call_target="tpu_custom_call" | custom-call | flops 2147483648 | bytes 5242880 | tf_op jit(solution)/shard_map/density/pallas_call | solution.py:365
  247.9 8.1 %density.7 = (bf16[4,2,64,512]{3,2,1,0:T(8,128)(2,1)S(1)}, bf16[4,2,64,512]{3,2,1,0:T(8,128)(2,1)}, bf16[4,2,64,512]{3,2,1,0:T(8,128)(2,1)S(1)}, bf16[4,2,64,512]{3,2,1,0:T(8,128)(2,1)}) custom-call(s32[1]{0:T(128)} %bitcast.1.odd, bf16[4,2,2,512,512]{4,3,2,1,0:T(8,128)(2,1)} %g_ref.15, f32[4,2,512]{2,1,0:T(2,128)S(1)} %copy-done.3, ...), custom_call_target="tpu_custom_call" | custom-call | flops 4294967296 | bytes 10485760 | tf_op jit(solution)/shard_map/density/pallas_call | solution.py:365
  258.0 2.9 collective-permute-done.36.recv_ref
  264.8 2.2 collective-permute-start.38
  267.0 5.1 %collective-permute-done.40.recv_ref = bf16[4,2,64,512]{3,2,1,0:T(8,128)(2,1)S(1)} collective-permute-done((bf16[4,2,64,512]{3,2,1,0:T(8,128)(2,1)}, bf16[4,2,64,512]{3,2,1,0:T(8,128)(2,1)S(1)}, u32[]{:S(2)}, u32[]{:S(2)}) %collective-permute-start.40) | collective-permute-done | bytes 524320 | tf_op jit(solution)/shard_map/ppermute | solution.py:424
  272.1 3.3 collective-permute-start.39
  275.3 13.1 %rows.3.refs_17_ = bf16[16,2,2,128,512]{4,3,2,1,0:T(8,128)(2,1)} custom-call(s32[1]{0:T(128)} %bitcast.mine.where, s32[16,16]{1,0:T(8,128)} %copy-done.10, bf16[1,512,512]{2,1,0:T(8,128)(2,1)} %get-tuple-element.76.refs_0_.refs_16_, bf16[1,512,512]{2,1,0:T(8,128)(2,1)} %get-tuple-element.77.refs_1_.refs_17_, bf16[1,512,512]{2,1,0:T(8,128)(2,1)} %copy-done.18, ...), custom_call_target="tpu_custom_call" | custom-call | flops 67108864 | bytes 10485760 | tf_op jit(solution)/shard_map/rows/pallas_call | solution.py:283
  288.5 8.4 %rows.4.refs_17_ = bf16[16,2,2,128,512]{4,3,2,1,0:T(8,128)(2,1)} custom-call(s32[1]{0:T(128)} %bitcast.mine.where, s32[16,16]{1,0:T(8,128)} %copy-done.10, bf16[2,512,512]{2,1,0:T(8,128)(2,1)} %get-tuple-element.74.refs_0_.refs_8_, bf16[2,512,512]{2,1,0:T(8,128)(2,1)} %copy-done.14, ...), custom_call_target="tpu_custom_call", output_to_operand_aliasing={{}: (19, {})} | custom-call | flops 67108864 | bytes 10485760 | tf_op jit(solution)/shard_map/rows/pallas_call | solution.py:283
  296.9 8.4 %rows.5 = bf16[16,2,2,128,512]{4,3,2,1,0:T(8,128)(2,1)} custom-call(s32[1]{0:T(128)} %bitcast.mine.where, s32[16,16]{1,0:T(8,128)} %copy-done.10, bf16[2,512,512]{2,1,0:T(8,128)(2,1)} %get-tuple-element.74.refs_0_.refs_8_, bf16[2,512,512]{2,1,0:T(8,128)(2,1)} %copy-done.14, ...), custom_call_target="tpu_custom_call", output_to_operand_aliasing={{}: (19, {})} | custom-call | flops 67108864 | bytes 10485760 | tf_op jit(solution)/shard_map/rows/pallas_call | solution.py:283
  307.2 2.5 collective-permute-start.43
  311.9 1.8 collective-permute-done.41
  314.8 4.3 %collective-permute-done.42 = bf16[2,64,512]{2,1,0:T(8,128)(2,1)S(1)} collective-permute-done((bf16[2,64,512]{2,1,0:T(8,128)(2,1)S(1)}, bf16[2,64,512]{2,1,0:T(8,128)(2,1)S(1)}, u32[]{:S(2)}, u32[]{:S(2)}) %collective-permute-start.42) | collective-permute-done | bytes 131104 | tf_op jit(solution)/shard_map/ppermute | solution.py:424
  319.1 3.1 collective-permute-start.49
  322.3 4.0 %collective-permute-start.50 = (bf16[2,64,512]{2,1,0:T(8,128)(2,1)S(1)}, bf16[2,64,512]{2,1,0:T(8,128)(2,1)S(1)}, u32[]{:S(2)}, u32[]{:S(2)}) collective-permute-start(bf16[2,64,512]{2,1,0:T(8,128)(2,1)S(1)} %get-tuple-element.108), channel_id=1, source_target_pairs={{0,16},{4,20},{8,24},{12,28},{16,0},{20,4},{24,8},{28,12},{1,17},{... | collective-permute-start | bytes 393224 | tf_op jit(solution)/shard_map/ppermute | solution.py:424
  326.3 5.7 %collective-permute-start.51 = (bf16[2,64,512]{2,1,0:T(8,128)(2,1)S(1)}, bf16[2,64,512]{2,1,0:T(8,128)(2,1)S(1)}, u32[]{:S(2)}, u32[]{:S(2)}) collective-permute-start(bf16[2,64,512]{2,1,0:T(8,128)(2,1)S(1)} %get-tuple-element.109), channel_id=1, source_target_pairs={{0,24},{4,28},{8,0},{12,4},{16,8},{20,12},{24,16},{28,20},{1,25},{... | collective-permute-start | bytes 393224 | tf_op jit(solution)/shard_map/ppermute | solution.py:424
  332.1 6.7 %collective-permute-done.50 = bf16[2,64,512]{2,1,0:T(8,128)(2,1)S(1)} collective-permute-done((bf16[2,64,512]{2,1,0:T(8,128)(2,1)S(1)}, bf16[2,64,512]{2,1,0:T(8,128)(2,1)S(1)}, u32[]{:S(2)}, u32[]{:S(2)}) %collective-permute-start.50) | collective-permute-done | bytes 131104 | tf_op jit(solution)/shard_map/ppermute | solution.py:424
  (159 shorter events, 38.8 us)
Async XLA Ops:
  4.8 19.2 %collective-permute-start.9 = (bf16[2,256,512]{2,1,0:T(8,128)(2,1)}, bf16[2,256,512]{2,1,0:T(8,128)(2,1)S(1)}, u32[]{:S(2)}, u32[]{:S(2)}) collective-permute-start(bf16[2,256,512]{2,1,0:T(8,128)(2,1)} %get-tuple-element.63), channel_id=1, source_target_pairs={{0,4},{4,0},{8,12},{12,8},{16,20},{20,16},{24,28},{28,24},{1,5},{5... | collective-permute-start | bytes 1572872 | tf_op jit(solution)/shard_map/ppermute | solution.py:424
  11.9 16.9 %collective-permute-start.10 = (bf16[2,256,512]{2,1,0:T(8,128)(2,1)}, bf16[2,256,512]{2,1,0:T(8,128)(2,1)S(1)}, u32[]{:S(2)}, u32[]{:S(2)}) collective-permute-start(bf16[2,256,512]{2,1,0:T(8,128)(2,1)} %get-tuple-element.62.keep), channel_id=1, source_target_pairs={{4,12},{8,0},{12,20},{16,8},{20,28},{24,16},{5,13},{9,1},{13,21},{... | collective-permute-start | bytes 1572872 | tf_op jit(solution)/shard_map/ppermute | solution.py:424
  13.2 19.1 %collective-permute-start.6 = (bf16[2,256,512]{2,1,0:T(8,128)(2,1)}, bf16[2,256,512]{2,1,0:T(8,128)(2,1)S(1)}, u32[]{:S(2)}, u32[]{:S(2)}) collective-permute-start(bf16[2,256,512]{2,1,0:T(8,128)(2,1)} %get-tuple-element.61), channel_id=1, source_target_pairs={{0,4},{4,0},{8,12},{12,8},{16,20},{20,16},{24,28},{28,24},{1,5},{5... | collective-permute-start | bytes 1572872 | tf_op jit(solution)/shard_map/ppermute | solution.py:424
  15.9 22.6 %collective-permute-start.7 = (bf16[2,256,512]{2,1,0:T(8,128)(2,1)}, bf16[2,256,512]{2,1,0:T(8,128)(2,1)S(1)}, u32[]{:S(2)}, u32[]{:S(2)}) collective-permute-start(bf16[2,256,512]{2,1,0:T(8,128)(2,1)} %get-tuple-element.60.keep), channel_id=1, source_target_pairs={{4,12},{8,0},{12,20},{16,8},{20,28},{24,16},{5,13},{9,1},{13,21},{... | collective-permute-start | bytes 1572872 | tf_op jit(solution)/shard_map/ppermute | solution.py:424
  21.4 22.9 %collective-permute-start.3 = (bf16[2,256,512]{2,1,0:T(8,128)(2,1)}, bf16[2,256,512]{2,1,0:T(8,128)(2,1)}, u32[]{:S(2)}, u32[]{:S(2)}) collective-permute-start(bf16[2,256,512]{2,1,0:T(8,128)(2,1)} %get-tuple-element.59), channel_id=1, source_target_pairs={{0,4},{4,0},{8,12},{12,8},{16,20},{20,16},{24,28},{28,24},{1,5},{5... | collective-permute-start | bytes 1572872 | tf_op jit(solution)/shard_map/ppermute | solution.py:424
  23.9 29.6 %collective-permute-start = (bf16[2,256,512]{2,1,0:T(8,128)(2,1)}, bf16[2,256,512]{2,1,0:T(8,128)(2,1)S(1)}, u32[]{:S(2)}, u32[]{:S(2)}) collective-permute-start(bf16[2,256,512]{2,1,0:T(8,128)(2,1)} %get-tuple-element.57), channel_id=1, source_target_pairs={{0,4},{4,0},{8,12},{12,8},{16,20},{20,16},{24,28},{28,24},{1,5},{5... | collective-permute-start | bytes 1572872 | tf_op jit(solution)/shard_map/ppermute | solution.py:424
  28.7 28.6 %collective-permute-start.11 = (bf16[2,256,512]{2,1,0:T(8,128)(2,1)S(1)}, bf16[2,256,512]{2,1,0:T(8,128)(2,1)S(1)}, u32[]{:S(2)}, u32[]{:S(2)}) collective-permute-start(bf16[2,256,512]{2,1,0:T(8,128)(2,1)S(1)} %collective-permute-done.9.recv), channel_id=1, source_target_pairs={{0,8},{8,16},{12,4},{16,24},{20,12},{28,20},{1,9},{9,17},{13,5},{1... | collective-permute-start | bytes 1572872 | tf_op jit(solution)/shard_map/ppermute | solution.py:424
  32.3 27.2 %collective-permute-start.8 = (bf16[2,256,512]{2,1,0:T(8,128)(2,1)S(1)}, bf16[2,256,512]{2,1,0:T(8,128)(2,1)}, u32[]{:S(2)}, u32[]{:S(2)}) collective-permute-start(bf16[2,256,512]{2,1,0:T(8,128)(2,1)S(1)} %collective-permute-done.6.recv), channel_id=1, source_target_pairs={{0,8},{8,16},{12,4},{16,24},{20,12},{28,20},{1,9},{9,17},{13,5},{1... | collective-permute-start | bytes 1572872 | tf_op jit(solution)/shard_map/ppermute | solution.py:424
  38.6 82.5 %collective-permute-start.33 = (bf16[16,128,512]{2,1,0:T(8,128)(2,1)}, bf16[16,128,512]{2,1,0:T(8,128)(2,1)}, u32[]{:S(2)}, u32[]{:S(2)}) collective-permute-start(bf16[16,128,512]{2,1,0:T(8,128)(2,1)} %refs_0_.1), channel_id=1, source_target_pairs={{0,2},{1,3},{2,0},{3,1},{4,6},{5,7},{6,4},{7,5},{8,10},{9,11},{10,... | collective-permute-start | bytes 6291464 | tf_op jit(solution)/shard_map/ppermute | solution.py:430
  44.3 26.6 %collective-permute-start.4 = (bf16[2,256,512]{2,1,0:T(8,128)(2,1)}, bf16[2,256,512]{2,1,0:T(8,128)(2,1)S(1)}, u32[]{:S(2)}, u32[]{:S(2)}) collective-permute-start(bf16[2,256,512]{2,1,0:T(8,128)(2,1)} %get-tuple-element.58.keep), channel_id=1, source_target_pairs={{4,12},{8,0},{12,20},{16,8},{20,28},{24,16},{5,13},{9,1},{13,21},{... | collective-permute-start | bytes 1572872 | tf_op jit(solution)/shard_map/ppermute | solution.py:424
  53.6 17.3 %collective-permute-start.5 = (bf16[2,256,512]{2,1,0:T(8,128)(2,1)}, bf16[2,256,512]{2,1,0:T(8,128)(2,1)S(1)}, u32[]{:S(2)}, u32[]{:S(2)}) collective-permute-start(bf16[2,256,512]{2,1,0:T(8,128)(2,1)} %collective-permute-done.3.recv), channel_id=1, source_target_pairs={{0,8},{8,16},{12,4},{16,24},{20,12},{28,20},{1,9},{9,17},{13,5},{1... | collective-permute-start | bytes 1572872 | tf_op jit(solution)/shard_map/ppermute | solution.py:424
  58.2 16.8 %collective-permute-start.1 = (bf16[2,256,512]{2,1,0:T(8,128)(2,1)}, bf16[2,256,512]{2,1,0:T(8,128)(2,1)S(1)}, u32[]{:S(2)}, u32[]{:S(2)}) collective-permute-start(bf16[2,256,512]{2,1,0:T(8,128)(2,1)} %get-tuple-element.56.keep), channel_id=1, source_target_pairs={{4,12},{8,0},{12,20},{16,8},{20,28},{24,16},{5,13},{9,1},{13,21},{... | collective-permute-start | bytes 1572872 | tf_op jit(solution)/shard_map/ppermute | solution.py:424
  59.5 19.7 %collective-permute-start.2 = (bf16[2,256,512]{2,1,0:T(8,128)(2,1)S(1)}, bf16[2,256,512]{2,1,0:T(8,128)(2,1)S(1)}, u32[]{:S(2)}, u32[]{:S(2)}) collective-permute-start(bf16[2,256,512]{2,1,0:T(8,128)(2,1)S(1)} %collective-permute-done.recv), channel_id=1, source_target_pairs={{0,8},{8,16},{12,4},{16,24},{20,12},{28,20},{1,9},{9,17},{13,5},{1... | collective-permute-start | bytes 1572872 | tf_op jit(solution)/shard_map/ppermute | solution.py:424
  83.3 15.4 %collective-permute-start.20 = (bf16[1,512,512]{2,1,0:T(8,128)(2,1)}, bf16[1,512,512]{2,1,0:T(8,128)(2,1)S(1)}, u32[]{:S(2)}, u32[]{:S(2)}) collective-permute-start(bf16[1,512,512]{2,1,0:T(8,128)(2,1)} %get-tuple-element.79), channel_id=1, source_target_pairs={{0,4},{4,0},{8,12},{12,8},{16,20},{20,16},{24,28},{28,24},{1,5},{5... | collective-permute-start | bytes 1572872 | tf_op jit(solution)/shard_map/ppermute | solution.py:424
  85.7 14.5 %collective-permute-start.22 = (bf16[1,512,512]{2,1,0:T(8,128)(2,1)}, bf16[1,512,512]{2,1,0:T(8,128)(2,1)S(1)}, u32[]{:S(2)}, u32[]{:S(2)}) collective-permute-start(bf16[1,512,512]{2,1,0:T(8,128)(2,1)} %get-tuple-element.77.refs_1_.refs_17_), channel_id=1, source_target_pairs={{0,2},{1,3},{2,0},{3,1},{4,6},{5,7},{6,4},{7,5},{8,10},{9,11},{10,... | collective-permute-start | bytes 1572872 | tf_op jit(solution)/shard_map/ppermute | solution.py:430
  87.2 13.0 %collective-permute-start.26 = (bf16[1,512,512]{2,1,0:T(8,128)(2,1)}, bf16[1,512,512]{2,1,0:T(8,128)(2,1)S(1)}, u32[]{:S(2)}, u32[]{:S(2)}) collective-permute-start(bf16[1,512,512]{2,1,0:T(8,128)(2,1)} %get-tuple-element.77.refs_1_.refs_17_), channel_id=1, source_target_pairs={{0,1},{1,0},{2,3},{3,2},{4,5},{5,4},{6,7},{7,6},{8,9},{9,8},{10,11... | collective-permute-start | bytes 1572872 | tf_op jit(solution)/shard_map/ppermute | solution.py:430
  87.2 20.4 %collective-permute-start.19 = (bf16[1,512,512]{2,1,0:T(8,128)(2,1)S(1)}, bf16[1,512,512]{2,1,0:T(8,128)(2,1)S(1)}, u32[]{:S(2)}, u32[]{:S(2)}) collective-permute-start(bf16[1,512,512]{2,1,0:T(8,128)(2,1)S(1)} %copy-done.34), channel_id=1, source_target_pairs={{0,4},{4,0},{8,12},{12,8},{16,20},{20,16},{24,28},{28,24},{1,5},{5... | collective-permute-start | bytes 1572872 | tf_op jit(solution)/shard_map/ppermute | solution.py:424
  98.7 14.8 %collective-permute-start.21 = (bf16[1,512,512]{2,1,0:T(8,128)(2,1)S(1)}, bf16[1,512,512]{2,1,0:T(8,128)(2,1)S(1)}, u32[]{:S(2)}, u32[]{:S(2)}) collective-permute-start(bf16[1,512,512]{2,1,0:T(8,128)(2,1)S(1)} %copy-done.2), channel_id=1, source_target_pairs={{0,2},{1,3},{2,0},{3,1},{4,6},{5,7},{6,4},{7,5},{8,10},{9,11},{10,... | collective-permute-start | bytes 1572872 | tf_op jit(solution)/shard_map/ppermute | solution.py:430
  100.1 13.3 %collective-permute-start.25 = (bf16[1,512,512]{2,1,0:T(8,128)(2,1)S(1)}, bf16[1,512,512]{2,1,0:T(8,128)(2,1)S(1)}, u32[]{:S(2)}, u32[]{:S(2)}) collective-permute-start(bf16[1,512,512]{2,1,0:T(8,128)(2,1)S(1)} %copy-done.2), channel_id=1, source_target_pairs={{0,1},{1,0},{2,3},{3,2},{4,5},{5,4},{6,7},{7,6},{8,9},{9,8},{10,11... | collective-permute-start | bytes 1572872 | tf_op jit(solution)/shard_map/ppermute | solution.py:430
  100.2 20.1 %collective-permute-start.24 = (bf16[1,512,512]{2,1,0:T(8,128)(2,1)S(1)}, bf16[1,512,512]{2,1,0:T(8,128)(2,1)S(1)}, u32[]{:S(2)}, u32[]{:S(2)}) collective-permute-start(bf16[1,512,512]{2,1,0:T(8,128)(2,1)S(1)} %collective-permute-done.20.refs_3_.refs_19_), channel_id=1, source_target_pairs={{0,2},{1,3},{2,0},{3,1},{4,6},{5,7},{6,4},{7,5},{8,10},{9,11},{10,... | collective-permute-start | bytes 1572872 | tf_op jit(solution)/shard_map/ppermute | solution.py:430
  107.5 35.1 %collective-permute-start.34 = (bf16[16,128,512]{2,1,0:T(8,128)(2,1)}, bf16[16,128,512]{2,1,0:T(8,128)(2,1)S(1)}, u32[]{:S(2)}, u32[]{:S(2)}) collective-permute-start(bf16[16,128,512]{2,1,0:T(8,128)(2,1)} %refs_0_.1), channel_id=1, source_target_pairs={{0,1},{1,0},{2,3},{3,2},{4,5},{5,4},{6,7},{7,6},{8,9},{9,8},{10,11... | collective-permute-start | bytes 6291464 | tf_op jit(solution)/shard_map/ppermute | solution.py:430
  120.2 20.9 %collective-permute-start.12 = (bf16[2,512,512]{2,1,0:T(8,128)(2,1)}, bf16[2,512,512]{2,1,0:T(8,128)(2,1)S(1)}, u32[]{:S(2)}, u32[]{:S(2)}) collective-permute-start(bf16[2,512,512]{2,1,0:T(8,128)(2,1)} %get-tuple-element.75), channel_id=1, source_target_pairs={{0,4},{4,0},{8,12},{12,8},{16,20},{20,16},{24,28},{28,24},{1,5},{5... | collective-permute-start | bytes 3145736 | tf_op jit(solution)/shard_map/ppermute | solution.py:424
  121.1 61.9 %collective-permute-start.35 = (bf16[16,128,512]{2,1,0:T(8,128)(2,1)}, bf16[16,128,512]{2,1,0:T(8,128)(2,1)S(1)}, u32[]{:S(2)}, u32[]{:S(2)}) collective-permute-start(bf16[16,128,512]{2,1,0:T(8,128)(2,1)} %collective-permute-done.33.refs_1_), channel_id=1, source_target_pairs={{0,1},{1,0},{2,3},{3,2},{4,5},{5,4},{6,7},{7,6},{8,9},{9,8},{10,11... | collective-permute-start | bytes 6291464 | tf_op jit(solution)/shard_map/ppermute | solution.py:430
  121.1 14.4 %collective-permute-start.23 = (bf16[1,512,512]{2,1,0:T(8,128)(2,1)S(1)}, bf16[1,512,512]{2,1,0:T(8,128)(2,1)}, u32[]{:S(2)}, u32[]{:S(2)}) collective-permute-start(bf16[1,512,512]{2,1,0:T(8,128)(2,1)S(1)} %collective-permute-done.19.refs_2_.refs_18_), channel_id=1, source_target_pairs={{0,2},{1,3},{2,0},{3,1},{4,6},{5,7},{6,4},{7,5},{8,10},{9,11},{10,... | collective-permute-start | bytes 1572872 | tf_op jit(solution)/shard_map/ppermute | solution.py:430
  122.7 14.4 %collective-permute-start.27 = (bf16[1,512,512]{2,1,0:T(8,128)(2,1)S(1)}, bf16[1,512,512]{2,1,0:T(8,128)(2,1)S(1)}, u32[]{:S(2)}, u32[]{:S(2)}) collective-permute-start(bf16[1,512,512]{2,1,0:T(8,128)(2,1)S(1)} %collective-permute-done.19.refs_2_.refs_18_), channel_id=1, source_target_pairs={{0,1},{1,0},{2,3},{3,2},{4,5},{5,4},{6,7},{7,6},{8,9},{9,8},{10,11... | collective-permute-start | bytes 1572872 | tf_op jit(solution)/shard_map/ppermute | solution.py:430
  135.6 26.3 %collective-permute-start.13 = (bf16[2,512,512]{2,1,0:T(8,128)(2,1)}, bf16[2,512,512]{2,1,0:T(8,128)(2,1)}, u32[]{:S(2)}, u32[]{:S(2)}) collective-permute-start(bf16[2,512,512]{2,1,0:T(8,128)(2,1)} %get-tuple-element.74.refs_0_.refs_8_), channel_id=1, source_target_pairs={{0,2},{1,3},{2,0},{3,1},{4,6},{5,7},{6,4},{7,5},{8,10},{9,11},{10,... | collective-permute-start | bytes 3145736 | tf_op jit(solution)/shard_map/ppermute | solution.py:430
  141.2 41.8 %collective-permute-start.14 = (bf16[2,512,512]{2,1,0:T(8,128)(2,1)S(1)}, bf16[2,512,512]{2,1,0:T(8,128)(2,1)}, u32[]{:S(2)}, u32[]{:S(2)}) collective-permute-start(bf16[2,512,512]{2,1,0:T(8,128)(2,1)S(1)} %collective-permute-done.12.refs_1_.refs_9_), channel_id=1, source_target_pairs={{0,2},{1,3},{2,0},{3,1},{4,6},{5,7},{6,4},{7,5},{8,10},{9,11},{10,... | collective-permute-start | bytes 3145736 | tf_op jit(solution)/shard_map/ppermute | solution.py:430
  142.6 19.3 %collective-permute-start.32 = (bf16[1,512,512]{2,1,0:T(8,128)(2,1)S(1)}, bf16[1,512,512]{2,1,0:T(8,128)(2,1)S(1)}, u32[]{:S(2)}, u32[]{:S(2)}) collective-permute-start(bf16[1,512,512]{2,1,0:T(8,128)(2,1)S(1)} %collective-permute-done.24.refs_7_.refs_23_), channel_id=1, source_target_pairs={{0,1},{1,0},{2,3},{3,2},{4,5},{5,4},{6,7},{7,6},{8,9},{9,8},{10,11... | collective-permute-start | bytes 1572872 | tf_op jit(solution)/shard_map/ppermute | solution.py:430
  142.7 53.4 %collective-permute-start.31 = (bf16[1,512,512]{2,1,0:T(8,128)(2,1)}, bf16[1,512,512]{2,1,0:T(8,128)(2,1)}, u32[]{:S(2)}, u32[]{:S(2)}) collective-permute-start(bf16[1,512,512]{2,1,0:T(8,128)(2,1)} %collective-permute-done.23.refs_6_.refs_22_), channel_id=1, source_target_pairs={{0,1},{1,0},{2,3},{3,2},{4,5},{5,4},{6,7},{7,6},{8,9},{9,8},{10,11... | collective-permute-start | bytes 1572872 | tf_op jit(solution)/shard_map/ppermute | solution.py:430
  161.9 59.9 %collective-permute-start.15 = (bf16[2,512,512]{2,1,0:T(8,128)(2,1)}, bf16[2,512,512]{2,1,0:T(8,128)(2,1)}, u32[]{:S(2)}, u32[]{:S(2)}) collective-permute-start(bf16[2,512,512]{2,1,0:T(8,128)(2,1)} %get-tuple-element.74.refs_0_.refs_8_), channel_id=1, source_target_pairs={{0,1},{1,0},{2,3},{3,2},{4,5},{5,4},{6,7},{7,6},{8,9},{9,8},{10,11... | collective-permute-start | bytes 3145736 | tf_op jit(solution)/shard_map/ppermute | solution.py:430
  161.9 59.9 %collective-permute-start.16 = (bf16[2,512,512]{2,1,0:T(8,128)(2,1)S(1)}, bf16[2,512,512]{2,1,0:T(8,128)(2,1)}, u32[]{:S(2)}, u32[]{:S(2)}) collective-permute-start(bf16[2,512,512]{2,1,0:T(8,128)(2,1)S(1)} %collective-permute-done.12.refs_1_.refs_9_), channel_id=1, source_target_pairs={{0,1},{1,0},{2,3},{3,2},{4,5},{5,4},{6,7},{7,6},{8,9},{9,8},{10,11... | collective-permute-start | bytes 3145736 | tf_op jit(solution)/shard_map/ppermute | solution.py:430
  183.0 38.9 %collective-permute-start.17 = (bf16[2,512,512]{2,1,0:T(8,128)(2,1)}, bf16[2,512,512]{2,1,0:T(8,128)(2,1)}, u32[]{:S(2)}, u32[]{:S(2)}) collective-permute-start(bf16[2,512,512]{2,1,0:T(8,128)(2,1)} %collective-permute-done.13.refs_2_.refs_10_), channel_id=1, source_target_pairs={{0,1},{1,0},{2,3},{3,2},{4,5},{5,4},{6,7},{7,6},{8,9},{9,8},{10,11... | collective-permute-start | bytes 3145736 | tf_op jit(solution)/shard_map/ppermute | solution.py:430
  184.4 37.4 %collective-permute-start.18 = (bf16[2,512,512]{2,1,0:T(8,128)(2,1)}, bf16[2,512,512]{2,1,0:T(8,128)(2,1)}, u32[]{:S(2)}, u32[]{:S(2)}) collective-permute-start(bf16[2,512,512]{2,1,0:T(8,128)(2,1)} %collective-permute-done.14.refs_3_.refs_11_), channel_id=1, source_target_pairs={{0,1},{1,0},{2,3},{3,2},{4,5},{5,4},{6,7},{7,6},{8,9},{9,8},{10,11... | collective-permute-start | bytes 3145736 | tf_op jit(solution)/shard_map/ppermute | solution.py:430
  245.8 15.1 %collective-permute-start.36 = (bf16[4,2,64,512]{3,2,1,0:T(8,128)(2,1)}, bf16[4,2,64,512]{3,2,1,0:T(8,128)(2,1)}, u32[]{:S(2)}, u32[]{:S(2)}) collective-permute-start(bf16[4,2,64,512]{3,2,1,0:T(8,128)(2,1)} %get-tuple-element.87), channel_id=1, source_target_pairs={{0,4},{4,0},{8,12},{12,8},{16,20},{20,16},{24,28},{28,24},{1,5},{5... | collective-permute-start | bytes 1572872 | tf_op jit(solution)/shard_map/ppermute | solution.py:424
  247.0 25.1 %collective-permute-start.40 = (bf16[4,2,64,512]{3,2,1,0:T(8,128)(2,1)}, bf16[4,2,64,512]{3,2,1,0:T(8,128)(2,1)S(1)}, u32[]{:S(2)}, u32[]{:S(2)}) collective-permute-start(bf16[4,2,64,512]{3,2,1,0:T(8,128)(2,1)} %get-tuple-element.93), channel_id=1, source_target_pairs={{0,4},{4,0},{8,12},{12,8},{16,20},{20,16},{24,28},{28,24},{1,5},{5... | collective-permute-start | bytes 1572872 | tf_op jit(solution)/shard_map/ppermute | solution.py:424
  256.0 49.4 %collective-permute-start.44 = (bf16[4,2,64,512]{3,2,1,0:T(8,128)(2,1)}, bf16[4,2,64,512]{3,2,1,0:T(8,128)(2,1)S(1)}, u32[]{:S(2)}, u32[]{:S(2)}) collective-permute-start(bf16[4,2,64,512]{3,2,1,0:T(8,128)(2,1)} %get-tuple-element.99), channel_id=1, source_target_pairs={{0,4},{4,0},{8,12},{12,8},{16,20},{20,16},{24,28},{28,24},{1,5},{5... | collective-permute-start | bytes 1572872 | tf_op jit(solution)/shard_map/ppermute | solution.py:424
  257.2 48.4 %collective-permute-start.48 = (bf16[4,2,64,512]{3,2,1,0:T(8,128)(2,1)}, bf16[4,2,64,512]{3,2,1,0:T(8,128)(2,1)S(1)}, u32[]{:S(2)}, u32[]{:S(2)}) collective-permute-start(bf16[4,2,64,512]{3,2,1,0:T(8,128)(2,1)} %get-tuple-element.105), channel_id=1, source_target_pairs={{0,4},{4,0},{8,12},{12,8},{16,20},{20,16},{24,28},{28,24},{1,5},{5... | collective-permute-start | bytes 1572872 | tf_op jit(solution)/shard_map/ppermute | solution.py:424
  263.2 44.0 %collective-permute-start.37 = (bf16[2,64,512]{2,1,0:T(8,128)(2,1)S(1)}, bf16[2,64,512]{2,1,0:T(8,128)(2,1)S(1)}, u32[]{:S(2)}, u32[]{:S(2)}) collective-permute-start(bf16[2,64,512]{2,1,0:T(8,128)(2,1)S(1)} %get-tuple-element.89), channel_id=1, source_target_pairs={{0,8},{4,12},{8,16},{12,20},{16,24},{20,28},{24,0},{28,4},{1,9},{5... | collective-permute-start | bytes 393224 | tf_op jit(solution)/shard_map/ppermute | solution.py:424
  264.8 44.9 %collective-permute-start.38 = (bf16[2,64,512]{2,1,0:T(8,128)(2,1)S(1)}, bf16[2,64,512]{2,1,0:T(8,128)(2,1)S(1)}, u32[]{:S(2)}, u32[]{:S(2)}) collective-permute-start(bf16[2,64,512]{2,1,0:T(8,128)(2,1)S(1)} %get-tuple-element.90), channel_id=1, source_target_pairs={{0,16},{4,20},{8,24},{12,28},{16,0},{20,4},{24,8},{28,12},{1,17},{... | collective-permute-start | bytes 393224 | tf_op jit(solution)/shard_map/ppermute | solution.py:424
  272.1 38.2 %collective-permute-start.39 = (bf16[2,64,512]{2,1,0:T(8,128)(2,1)S(1)}, bf16[2,64,512]{2,1,0:T(8,128)(2,1)S(1)}, u32[]{:S(2)}, u32[]{:S(2)}) collective-permute-start(bf16[2,64,512]{2,1,0:T(8,128)(2,1)S(1)} %get-tuple-element.91), channel_id=1, source_target_pairs={{0,24},{4,28},{8,0},{12,4},{16,8},{20,12},{24,16},{28,20},{1,25},{... | collective-permute-start | bytes 393224 | tf_op jit(solution)/shard_map/ppermute | solution.py:424
  305.6 13.5 %collective-permute-start.42 = (bf16[2,64,512]{2,1,0:T(8,128)(2,1)S(1)}, bf16[2,64,512]{2,1,0:T(8,128)(2,1)S(1)}, u32[]{:S(2)}, u32[]{:S(2)}) collective-permute-start(bf16[2,64,512]{2,1,0:T(8,128)(2,1)S(1)} %get-tuple-element.96), channel_id=1, source_target_pairs={{0,16},{4,20},{8,24},{12,28},{16,0},{20,4},{24,8},{28,12},{1,17},{... | collective-permute-start | bytes 393224 | tf_op jit(solution)/shard_map/ppermute | solution.py:424
  307.2 15.1 %collective-permute-start.43 = (bf16[2,64,512]{2,1,0:T(8,128)(2,1)S(1)}, bf16[2,64,512]{2,1,0:T(8,128)(2,1)S(1)}, u32[]{:S(2)}, u32[]{:S(2)}) collective-permute-start(bf16[2,64,512]{2,1,0:T(8,128)(2,1)S(1)} %get-tuple-element.97), channel_id=1, source_target_pairs={{0,24},{4,28},{8,0},{12,4},{16,8},{20,12},{24,16},{28,20},{1,25},{... | collective-permute-start | bytes 393224 | tf_op jit(solution)/shard_map/ppermute | solution.py:424
  309.7 16.6 %collective-permute-start.45 = (bf16[2,64,512]{2,1,0:T(8,128)(2,1)S(1)}, bf16[2,64,512]{2,1,0:T(8,128)(2,1)S(1)}, u32[]{:S(2)}, u32[]{:S(2)}) collective-permute-start(bf16[2,64,512]{2,1,0:T(8,128)(2,1)S(1)} %get-tuple-element.101), channel_id=1, source_target_pairs={{0,8},{4,12},{8,16},{12,20},{16,24},{20,28},{24,0},{28,4},{1,9},{5... | collective-permute-start | bytes 393224 | tf_op jit(solution)/shard_map/ppermute | solution.py:424
  310.3 21.7 %collective-permute-start.46 = (bf16[2,64,512]{2,1,0:T(8,128)(2,1)S(1)}, bf16[2,64,512]{2,1,0:T(8,128)(2,1)S(1)}, u32[]{:S(2)}, u32[]{:S(2)}) collective-permute-start(bf16[2,64,512]{2,1,0:T(8,128)(2,1)S(1)} %get-tuple-element.102), channel_id=1, source_target_pairs={{0,16},{4,20},{8,24},{12,28},{16,0},{20,4},{24,8},{28,12},{1,17},{... | collective-permute-start | bytes 393224 | tf_op jit(solution)/shard_map/ppermute | solution.py:424
  313.7 18.3 %collective-permute-start.47 = (bf16[2,64,512]{2,1,0:T(8,128)(2,1)S(1)}, bf16[2,64,512]{2,1,0:T(8,128)(2,1)S(1)}, u32[]{:S(2)}, u32[]{:S(2)}) collective-permute-start(bf16[2,64,512]{2,1,0:T(8,128)(2,1)S(1)} %get-tuple-element.103), channel_id=1, source_target_pairs={{0,24},{4,28},{8,0},{12,4},{16,8},{20,12},{24,16},{28,20},{1,25},{... | collective-permute-start | bytes 393224 | tf_op jit(solution)/shard_map/ppermute | solution.py:424
  319.1 13.0 %collective-permute-start.49 = (bf16[2,64,512]{2,1,0:T(8,128)(2,1)S(1)}, bf16[2,64,512]{2,1,0:T(8,128)(2,1)S(1)}, u32[]{:S(2)}, u32[]{:S(2)}) collective-permute-start(bf16[2,64,512]{2,1,0:T(8,128)(2,1)S(1)} %get-tuple-element.107), channel_id=1, source_target_pairs={{0,8},{4,12},{8,16},{12,20},{16,24},{20,28},{24,0},{28,4},{1,9},{5... | collective-permute-start | bytes 393224 | tf_op jit(solution)/shard_map/ppermute | solution.py:424
  322.3 16.5 %collective-permute-start.50 = (bf16[2,64,512]{2,1,0:T(8,128)(2,1)S(1)}, bf16[2,64,512]{2,1,0:T(8,128)(2,1)S(1)}, u32[]{:S(2)}, u32[]{:S(2)}) collective-permute-start(bf16[2,64,512]{2,1,0:T(8,128)(2,1)S(1)} %get-tuple-element.108), channel_id=1, source_target_pairs={{0,16},{4,20},{8,24},{12,28},{16,0},{20,4},{24,8},{28,12},{1,17},{... | collective-permute-start | bytes 393224 | tf_op jit(solution)/shard_map/ppermute | solution.py:424
  326.3 12.5 %collective-permute-start.51 = (bf16[2,64,512]{2,1,0:T(8,128)(2,1)S(1)}, bf16[2,64,512]{2,1,0:T(8,128)(2,1)S(1)}, u32[]{:S(2)}, u32[]{:S(2)}) collective-permute-start(bf16[2,64,512]{2,1,0:T(8,128)(2,1)S(1)} %get-tuple-element.109), channel_id=1, source_target_pairs={{0,24},{4,28},{8,0},{12,4},{16,8},{20,12},{24,16},{28,20},{1,25},{... | collective-permute-start | bytes 393224 | tf_op jit(solution)/shard_map/ppermute | solution.py:424
  (41 other events, 1308.4 us)

commit v9 on v8

--- a/solution.py
+++ b/solution.py
@@ -427,13 +427,16 @@
         return hbm(permuted(x, perm))
 
     def swap(x, stride):
-        moved = lax.ppermute(x, "mom", [(i, i ^ stride) for i in range(nm)])
-        return hbm(moved)
-
-    def spread(x):
+        return lax.ppermute(x, "mom", [(i, i ^ stride) for i in range(nm)])
+
+    def spread(x, last=False):
         held = [x]
-        for s in strides:
-            held = held + [swap(piece, s) for piece in held]
+        for at, s in enumerate(strides):
+            moved = [swap(piece, s) for piece in held]
+            held = held + [
+                piece if last and at == len(strides) - 1 and i == len(held) - 1 else hbm(piece)
+                for i, piece in enumerate(moved)
+            ]
         return held
 
     order = [0]
@@ -472,7 +475,7 @@
     for e in range(le):
         use = [got[j] for j in range(hk)] if e == 0 else [last]
         fresh = [spread(part[e]) for part in use]
-        back = [spread(over_energy(part[le + e], pairs)) for part in use]
+        back = [spread(over_energy(part[le + e], pairs), e == le - 1) for part in use]
         pieces = [part[at] for at in range(nm) for part in fresh + back]
         if e < le - 1:
             x, y = home_blocks(mine, slots, pieces, full, turned, lk)

time: 342 us -> 342 us (level)
  no operation moved by 1% of the time
where the time goes in v9:
time: 342 us; the launch traced here: 341 us
  Pallas kernels  130 us (38%)
  waiting for transfers between devices  126 us (37%)
  starting transfers between devices  76.4 us (22%)
  local copies, waits for them, and re-layouts  6.69 us (2%)
    ppermute x31, starting transfers between devices, permuted(): return lax.ppermute(x, 'energy', perm)  64.6 us
    ppermute x21, waiting for transfers between devices, swap(): return lax.ppermute(x, 'mom', [(i, i ^ stride) for i in range(nm)])  64.2 us
    ppermute x31, waiting for transfers between devices, permuted(): return lax.ppermute(x, 'energy', perm)  61.8 us
    pallas_call x3, Pallas kernels, own_rows(): pl.pallas_call(functools.partial(rows_kernel, len(pieces), base), out_sha...  29.9 us
    pallas_call x2, Pallas kernels, home_blocks(): pl.pallas_call(functools.partial(home_kernel, lk, len(pieces)), out_shape...  26.1 us
    pallas_call x3, Pallas kernels, last_density(): pl.pallas_call(functools.partial(last_density_kernel, scale, energy), out...  18.9 us
    pallas_call x4, Pallas kernels, lesser_packed(): pl.pallas_call(lesser_kernel, out_shape=[pltpu.HBM((le, n // 2, n), BF16)...  16.5 us
    pallas_call x4, Pallas kernels, sources(): pl.pallas_call(source_kernel, out_shape=[pltpu.HBM(shape, BF16) for shape...  13.2 us
  transfers between devices with their start and end apart: 52, of which 17 were waited for; matrix products, arithmetic and copies ran while one was open for 0% of the time, Pallas kernels for 30%

profile of v9, /device:TPU:0, one launch (start us, length us, event | category | flops | bytes accessed | tf_op | source)
XLA Modules:
  0.0 340.7 jit_solution(6707349360762270460)
XLA Ops:
  0.6 4.1 %lesser.7 = (bf16[2,256,512]{2,1,0:T(8,128)(2,1)}, bf16[2,256,512]{2,1,0:T(8,128)(2,1)}) custom-call(s32[1]{0:T(128)} %bitcast.5.sel, bf16[4,2,2,512,512]{4,3,2,1,0:T(8,128)(2,1)} %g_ref.15, f32[4,2,512]{2,1,0:T(2,128)} %gamma_ref.15), custom_call_target="tpu_custom_call" | custom-call | flops 1610612736 | bytes 3145728 | tf_op jit(solution)/shard_map/lesser/pallas_call | solution.py:66
  4.8 3.0 collective-permute-start.9
  7.8 4.1 %lesser.6 = (bf16[2,256,512]{2,1,0:T(8,128)(2,1)}, bf16[2,256,512]{2,1,0:T(8,128)(2,1)}) custom-call(s32[1]{0:T(128)} %bitcast.4.sel, bf16[4,2,2,512,512]{4,3,2,1,0:T(8,128)(2,1)} %g_ref.15, f32[4,2,512]{2,1,0:T(2,128)} %gamma_ref.15), custom_call_target="tpu_custom_call" | custom-call | flops 1610612736 | bytes 3145728 | tf_op jit(solution)/shard_map/lesser/pallas_call | solution.py:66
  13.2 2.8 collective-permute-start.6
  17.2 4.1 %lesser.5 = (bf16[2,256,512]{2,1,0:T(8,128)(2,1)}, bf16[2,256,512]{2,1,0:T(8,128)(2,1)}) custom-call(s32[1]{0:T(128)} %bitcast.3.sel, bf16[4,2,2,512,512]{4,3,2,1,0:T(8,128)(2,1)} %g_ref.15, f32[4,2,512]{2,1,0:T(2,128)} %gamma_ref.15), custom_call_target="tpu_custom_call" | custom-call | flops 1610612736 | bytes 3145728 | tf_op jit(solution)/shard_map/lesser/pallas_call | solution.py:66
  21.4 2.6 collective-permute-start.3
  24.0 4.7 %collective-permute-done.10.kz = bf16[2,256,512]{2,1,0:T(8,128)(2,1)S(1)} collective-permute-done((bf16[2,256,512]{2,1,0:T(8,128)(2,1)}, bf16[2,256,512]{2,1,0:T(8,128)(2,1)S(1)}, u32[]{:S(2)}, u32[]{:S(2)}) %collective-permute-start.10) | collective-permute-done | bytes 524320 | tf_op jit(solution)/shard_map/ppermute | solution.py:424
  28.7 3.5 %collective-permute-start.11 = (bf16[2,256,512]{2,1,0:T(8,128)(2,1)S(1)}, bf16[2,256,512]{2,1,0:T(8,128)(2,1)S(1)}, u32[]{:S(2)}, u32[]{:S(2)}) collective-permute-start(bf16[2,256,512]{2,1,0:T(8,128)(2,1)S(1)} %collective-permute-done.9.recv), channel_id=1, source_target_pairs={{0,8},{8,16},{12,4},{16,24},{20,12},{28,20},{1,9},{9,17},{13,5},{1... | collective-permute-start | bytes 1572872 | tf_op jit(solution)/shard_map/ppermute | solution.py:424
  32.3 4.5 %collective-permute-start.8 = (bf16[2,256,512]{2,1,0:T(8,128)(2,1)S(1)}, bf16[2,256,512]{2,1,0:T(8,128)(2,1)}, u32[]{:S(2)}, u32[]{:S(2)}) collective-permute-start(bf16[2,256,512]{2,1,0:T(8,128)(2,1)S(1)} %collective-permute-done.6.recv), channel_id=1, source_target_pairs={{0,8},{8,16},{12,4},{16,24},{20,12},{28,20},{1,9},{9,17},{13,5},{1... | collective-permute-start | bytes 1572872 | tf_op jit(solution)/shard_map/ppermute | solution.py:424
  40.1 4.2 %lesser.4 = (bf16[2,256,512]{2,1,0:T(8,128)(2,1)}, bf16[2,256,512]{2,1,0:T(8,128)(2,1)}) custom-call(s32[1]{0:T(128)} %bitcast.2.sel, bf16[4,2,2,512,512]{4,3,2,1,0:T(8,128)(2,1)} %g_ref.15, f32[4,2,512]{2,1,0:T(2,128)} %gamma_ref.15), custom_call_target="tpu_custom_call" | custom-call | flops 1610612736 | bytes 3145728 | tf_op jit(solution)/shard_map/lesser/pallas_call | solution.py:66
  45.7 7.9 %collective-permute-done.recv = bf16[2,256,512]{2,1,0:T(8,128)(2,1)S(1)} collective-permute-done((bf16[2,256,512]{2,1,0:T(8,128)(2,1)}, bf16[2,256,512]{2,1,0:T(8,128)(2,1)S(1)}, u32[]{:S(2)}, u32[]{:S(2)}) %collective-permute-start) | collective-permute-done | bytes 524320 | tf_op jit(solution)/shard_map/ppermute | solution.py:424
  53.6 3.7 %collective-permute-start.5 = (bf16[2,256,512]{2,1,0:T(8,128)(2,1)}, bf16[2,256,512]{2,1,0:T(8,128)(2,1)S(1)}, u32[]{:S(2)}, u32[]{:S(2)}) collective-permute-start(bf16[2,256,512]{2,1,0:T(8,128)(2,1)} %collective-permute-done.3.recv), channel_id=1, source_target_pairs={{0,8},{8,16},{12,4},{16,24},{20,12},{28,20},{1,9},{9,17},{13,5},{1... | collective-permute-start | bytes 1572872 | tf_op jit(solution)/shard_map/ppermute | solution.py:424
  59.5 4.8 %collective-permute-start.2 = (bf16[2,256,512]{2,1,0:T(8,128)(2,1)S(1)}, bf16[2,256,512]{2,1,0:T(8,128)(2,1)S(1)}, u32[]{:S(2)}, u32[]{:S(2)}) collective-permute-start(bf16[2,256,512]{2,1,0:T(8,128)(2,1)S(1)} %collective-permute-done.recv), channel_id=1, source_target_pairs={{0,8},{8,16},{12,4},{16,24},{20,12},{28,20},{1,9},{9,17},{13,5},{1... | collective-permute-start | bytes 1572872 | tf_op jit(solution)/shard_map/ppermute | solution.py:424
  64.3 3.3 source.4
  67.6 3.3 source.5
  71.7 3.3 source.6
  75.0 4.2 %collective-permute-done.2.rz = bf16[2,256,512]{2,1,0:T(8,128)(2,1)S(1)} collective-permute-done((bf16[2,256,512]{2,1,0:T(8,128)(2,1)S(1)}, bf16[2,256,512]{2,1,0:T(8,128)(2,1)S(1)}, u32[]{:S(2)}, u32[]{:S(2)}) %collective-permute-start.2) | collective-permute-done | bytes 524320 | tf_op jit(solution)/shard_map/ppermute | solution.py:424
  80.0 3.3 source.7
  83.3 2.4 collective-permute-start.20
  87.2 11.4 %collective-permute-done.20.refs_3_.refs_19_ = bf16[1,512,512]{2,1,0:T(8,128)(2,1)S(1)} collective-permute-done((bf16[1,512,512]{2,1,0:T(8,128)(2,1)}, bf16[1,512,512]{2,1,0:T(8,128)(2,1)S(1)}, u32[]{:S(2)}, u32[]{:S(2)}) %collective-permute-start.20) | collective-permute-done | bytes 524320 | tf_op jit(solution)/shard_map/ppermute | solution.py:424
  100.8 6.8 %collective-permute-done.19.refs_2_.refs_18_ = bf16[1,512,512]{2,1,0:T(8,128)(2,1)S(1)} collective-permute-done((bf16[1,512,512]{2,1,0:T(8,128)(2,1)S(1)}, bf16[1,512,512]{2,1,0:T(8,128)(2,1)S(1)}, u32[]{:S(2)}, u32[]{:S(2)}) %collective-permute-start.19) | collective-permute-done | bytes 524320 | tf_op jit(solution)/shard_map/ppermute | solution.py:424
  107.5 5.9 %collective-permute-done.21.refs_4_.refs_20_ = bf16[1,512,512]{2,1,0:T(8,128)(2,1)S(1)} collective-permute-done((bf16[1,512,512]{2,1,0:T(8,128)(2,1)S(1)}, bf16[1,512,512]{2,1,0:T(8,128)(2,1)S(1)}, u32[]{:S(2)}, u32[]{:S(2)}) %collective-permute-start.21) | collective-permute-done | bytes 524320 | tf_op jit(solution)/shard_map/ppermute | solution.py:430
  114.0 6.3 %collective-permute-done.24.refs_7_.refs_23_ = bf16[1,512,512]{2,1,0:T(8,128)(2,1)S(1)} collective-permute-done((bf16[1,512,512]{2,1,0:T(8,128)(2,1)S(1)}, bf16[1,512,512]{2,1,0:T(8,128)(2,1)S(1)}, u32[]{:S(2)}, u32[]{:S(2)}) %collective-permute-start.24) | collective-permute-done | bytes 524320 | tf_op jit(solution)/shard_map/ppermute | solution.py:430
  122.8 12.7 %collective-permute-done.23.refs_6_.refs_22_ = bf16[1,512,512]{2,1,0:T(8,128)(2,1)} collective-permute-done((bf16[1,512,512]{2,1,0:T(8,128)(2,1)S(1)}, bf16[1,512,512]{2,1,0:T(8,128)(2,1)}, u32[]{:S(2)}, u32[]{:S(2)}) %collective-permute-start.23) | collective-permute-done | bytes 524320 | tf_op jit(solution)/shard_map/ppermute | solution.py:430
  137.1 4.1 %collective-permute-done.12.refs_1_.refs_9_ = bf16[2,512,512]{2,1,0:T(8,128)(2,1)S(1)} collective-permute-done((bf16[2,512,512]{2,1,0:T(8,128)(2,1)}, bf16[2,512,512]{2,1,0:T(8,128)(2,1)S(1)}, u32[]{:S(2)}, u32[]{:S(2)}) %collective-permute-start.12) | collective-permute-done | bytes 1048608 | tf_op jit(solution)/shard_map/ppermute | solution.py:424
  143.2 18.7 %collective-permute-done.13.refs_2_.refs_10_ = bf16[2,512,512]{2,1,0:T(8,128)(2,1)} collective-permute-done((bf16[2,512,512]{2,1,0:T(8,128)(2,1)}, bf16[2,512,512]{2,1,0:T(8,128)(2,1)}, u32[]{:S(2)}, u32[]{:S(2)}) %collective-permute-start.13) | collective-permute-done | bytes 1048608 | tf_op jit(solution)/shard_map/ppermute | solution.py:430
  162.4 20.6 %collective-permute-done.14.refs_3_.refs_11_ = bf16[2,512,512]{2,1,0:T(8,128)(2,1)} collective-permute-done((bf16[2,512,512]{2,1,0:T(8,128)(2,1)S(1)}, bf16[2,512,512]{2,1,0:T(8,128)(2,1)}, u32[]{:S(2)}, u32[]{:S(2)}) %collective-permute-start.14) | collective-permute-done | bytes 1048608 | tf_op jit(solution)/shard_map/ppermute | solution.py:430
  185.0 11.1 %place.1 = (bf16[16,512,512]{2,1,0:T(8,128)(2,1)}, bf16[16,512,512]{2,1,0:T(8,128)(2,1)}) custom-call(s32[1]{0:T(128)} %bitcast.mine.where, bf16[16,128,512]{2,1,0:T(8,128)(2,1)} %refs_0_.1, bf16[16,128,512]{2,1,0:T(8,128)(2,1)} %collective-permute-done.33.refs_1_, bf16[16,128,512]{2,1,0:T(8,128)(2,1)} %copy-done.27, bf16[16,128,512]{2,1,0:T(8,128)(2,1)} %copy-done.28), custom_call_target="tpu_custom_call" | custom-call | flops 16777216 | bytes 25165824 | tf_op jit(solution)/shard_map/place/pallas_call | solution.py:97
  196.1 12.9 %home.3 = (bf16[4,512,512]{2,1,0:T(8,128)(2,1)S(1)}, bf16[4,512,512]{2,1,0:T(8,128)(2,1)S(1)}) custom-call(s32[1]{0:T(128)} %bitcast.mine.where, s32[16,16]{1,0:T(8,128)S(1)} %fusion.4.slots, bf16[1,512,512]{2,1,0:T(8,128)(2,1)S(1)} %copy-done.2, bf16[1,512,512]{2,1,0:T(8,128)(2,1)S(1)} %copy-done.1, bf16[1,512,512]{2,1,0:T(8,128)(2,1)} %copy-done.18, ...), custom_call_target="tpu_custom_call" | custom-call | flops 67108864 | bytes 29360128 | tf_op jit(solution)/shard_map/home/pallas_call | solution.py:215
  209.1 12.7 %density.4.held_ref = f32[4,2,512,512]{3,2,1,0:T(8,128)} custom-call(bf16[4,2,2,512,512]{4,3,2,1,0:T(8,128)(2,1)} %g_ref.15, f32[4,2,512]{2,1,0:T(2,128)S(1)} %copy-done.3, bf16[4,512,512]{2,1,0:T(8,128)(2,1)S(1)} %get-tuple-element.84.x_ref, bf16[4,512,512]{2,1,0:T(8,128)(2,1)S(1)} %get-tuple-element.85.y_ref), custom_call_target="tpu_custom_call" | custom-call | flops 8589934592 | bytes 20971520 | tf_op jit(solution)/shard_map/density/pallas_call | solution.py:325
  221.9 13.2 %home.2 = (bf16[4,512,512]{2,1,0:T(8,128)(2,1)S(1)}, bf16[4,512,512]{2,1,0:T(8,128)(2,1)S(1)}) custom-call(s32[1]{0:T(128)} %bitcast.mine.where, s32[16,16]{1,0:T(8,128)S(1)} %fusion.4.slots, bf16[2,512,512]{2,1,0:T(8,128)(2,1)S(1)} %copy-done, bf16[2,512,512]{2,1,0:T(8,128)(2,1)} %copy-done.14, ...), custom_call_target="tpu_custom_call" | custom-call | flops 67108864 | bytes 29360128 | tf_op jit(solution)/shard_map/home/pallas_call | solution.py:215
  235.0 5.3 %density.5 = (bf16[4,2,64,512]{3,2,1,0:T(8,128)(2,1)S(1)}, bf16[4,2,64,512]{3,2,1,0:T(8,128)(2,1)}) custom-call(s32[1]{0:T(128)} %bitcast.1.odd, bf16[4,2,2,512,512]{4,3,2,1,0:T(8,128)(2,1)} %g_ref.15, f32[4,2,512]{2,1,0:T(2,128)S(1)} %copy-done.3, bf16[4,512,512]{2,1,0:T(8,128)(2,1)S(1)} %get-tuple-element.82.x_ref, ...), custom_call_target="tpu_custom_call" | custom-call | flops 2147483648 | bytes 5242880 | tf_op jit(solution)/shard_map/density/pallas_call | solution.py:365
  240.4 5.5 %density.6 = (bf16[4,2,64,512]{3,2,1,0:T(8,128)(2,1)S(1)}, bf16[4,2,64,512]{3,2,1,0:T(8,128)(2,1)}) custom-call(s32[1]{0:T(128)} %bitcast.1.odd, bf16[4,2,2,512,512]{4,3,2,1,0:T(8,128)(2,1)} %g_ref.15, f32[4,2,512]{2,1,0:T(2,128)S(1)} %copy-done.3, bf16[4,512,512]{2,1,0:T(8,128)(2,1)S(1)} %get-tuple-element.82.x_ref, ...), custom_call_target="tpu_custom_call" | custom-call | flops 2147483648 | bytes 5242880 | tf_op jit(solution)/shard_map/density/pallas_call | solution.py:365
  247.9 8.1 %density.7 = (bf16[4,2,64,512]{3,2,1,0:T(8,128)(2,1)S(1)}, bf16[4,2,64,512]{3,2,1,0:T(8,128)(2,1)}, bf16[4,2,64,512]{3,2,1,0:T(8,128)(2,1)S(1)}, bf16[4,2,64,512]{3,2,1,0:T(8,128)(2,1)}) custom-call(s32[1]{0:T(128)} %bitcast.1.odd, bf16[4,2,2,512,512]{4,3,2,1,0:T(8,128)(2,1)} %g_ref.15, f32[4,2,512]{2,1,0:T(2,128)S(1)} %copy-done.3, ...), custom_call_target="tpu_custom_call" | custom-call | flops 4294967296 | bytes 10485760 | tf_op jit(solution)/shard_map/density/pallas_call | solution.py:365
  258.0 2.9 collective-permute-done.36.recv_ref
  264.8 2.2 collective-permute-start.38
  267.0 5.1 %collective-permute-done.40.recv_ref = bf16[4,2,64,512]{3,2,1,0:T(8,128)(2,1)S(1)} collective-permute-done((bf16[4,2,64,512]{3,2,1,0:T(8,128)(2,1)}, bf16[4,2,64,512]{3,2,1,0:T(8,128)(2,1)S(1)}, u32[]{:S(2)}, u32[]{:S(2)}) %collective-permute-start.40) | collective-permute-done | bytes 524320 | tf_op jit(solution)/shard_map/ppermute | solution.py:424
  272.1 3.3 collective-permute-start.39
  275.3 13.1 %rows.3.refs_17_ = bf16[16,2,2,128,512]{4,3,2,1,0:T(8,128)(2,1)} custom-call(s32[1]{0:T(128)} %bitcast.mine.where, s32[16,16]{1,0:T(8,128)} %copy-done.10, bf16[1,512,512]{2,1,0:T(8,128)(2,1)} %get-tuple-element.76.refs_0_.refs_16_, bf16[1,512,512]{2,1,0:T(8,128)(2,1)} %get-tuple-element.77.refs_1_.refs_17_, bf16[1,512,512]{2,1,0:T(8,128)(2,1)} %copy-done.18, ...), custom_call_target="tpu_custom_call" | custom-call | flops 67108864 | bytes 10485760 | tf_op jit(solution)/shard_map/rows/pallas_call | solution.py:283
  288.5 8.4 %rows.4.refs_17_ = bf16[16,2,2,128,512]{4,3,2,1,0:T(8,128)(2,1)} custom-call(s32[1]{0:T(128)} %bitcast.mine.where, s32[16,16]{1,0:T(8,128)} %copy-done.10, bf16[2,512,512]{2,1,0:T(8,128)(2,1)} %get-tuple-element.74.refs_0_.refs_8_, bf16[2,512,512]{2,1,0:T(8,128)(2,1)} %copy-done.14, ...), custom_call_target="tpu_custom_call", output_to_operand_aliasing={{}: (19, {})} | custom-call | flops 67108864 | bytes 10485760 | tf_op jit(solution)/shard_map/rows/pallas_call | solution.py:283
  296.9 8.4 %rows.5 = bf16[16,2,2,128,512]{4,3,2,1,0:T(8,128)(2,1)} custom-call(s32[1]{0:T(128)} %bitcast.mine.where, s32[16,16]{1,0:T(8,128)} %copy-done.10, bf16[2,512,512]{2,1,0:T(8,128)(2,1)} %get-tuple-element.74.refs_0_.refs_8_, bf16[2,512,512]{2,1,0:T(8,128)(2,1)} %copy-done.14, ...), custom_call_target="tpu_custom_call", output_to_operand_aliasing={{}: (19, {})} | custom-call | flops 67108864 | bytes 10485760 | tf_op jit(solution)/shard_map/rows/pallas_call | solution.py:283
  307.2 2.5 collective-permute-start.43
  311.9 1.8 collective-permute-done.41
  314.8 4.3 %collective-permute-done.42 = bf16[2,64,512]{2,1,0:T(8,128)(2,1)S(1)} collective-permute-done((bf16[2,64,512]{2,1,0:T(8,128)(2,1)S(1)}, bf16[2,64,512]{2,1,0:T(8,128)(2,1)S(1)}, u32[]{:S(2)}, u32[]{:S(2)}) %collective-permute-start.42) | collective-permute-done | bytes 131104 | tf_op jit(solution)/shard_map/ppermute | solution.py:424
  319.1 3.1 collective-permute-start.49
  322.3 4.0 %collective-permute-start.50 = (bf16[2,64,512]{2,1,0:T(8,128)(2,1)S(1)}, bf16[2,64,512]{2,1,0:T(8,128)(2,1)S(1)}, u32[]{:S(2)}, u32[]{:S(2)}) collective-permute-start(bf16[2,64,512]{2,1,0:T(8,128)(2,1)S(1)} %get-tuple-element.108), channel_id=1, source_target_pairs={{0,16},{4,20},{8,24},{12,28},{16,0},{20,4},{24,8},{28,12},{1,17},{... | collective-permute-start | bytes 393224 | tf_op jit(solution)/shard_map/ppermute | solution.py:424
  326.3 5.7 %collective-permute-start.51 = (bf16[2,64,512]{2,1,0:T(8,128)(2,1)S(1)}, bf16[2,64,512]{2,1,0:T(8,128)(2,1)S(1)}, u32[]{:S(2)}, u32[]{:S(2)}) collective-permute-start(bf16[2,64,512]{2,1,0:T(8,128)(2,1)S(1)} %get-tuple-element.109), channel_id=1, source_target_pairs={{0,24},{4,28},{8,0},{12,4},{16,8},{20,12},{24,16},{28,20},{1,25},{... | collective-permute-start | bytes 393224 | tf_op jit(solution)/shard_map/ppermute | solution.py:424
  332.1 6.7 %collective-permute-done.50 = bf16[2,64,512]{2,1,0:T(8,128)(2,1)S(1)} collective-permute-done((bf16[2,64,512]{2,1,0:T(8,128)(2,1)S(1)}, bf16[2,64,512]{2,1,0:T(8,128)(2,1)S(1)}, u32[]{:S(2)}, u32[]{:S(2)}) %collective-permute-start.50) | collective-permute-done | bytes 131104 | tf_op jit(solution)/shard_map/ppermute | solution.py:424
  (159 shorter events, 38.8 us)
Async XLA Ops:
  4.8 19.2 %collective-permute-start.9 = (bf16[2,256,512]{2,1,0:T(8,128)(2,1)}, bf16[2,256,512]{2,1,0:T(8,128)(2,1)S(1)}, u32[]{:S(2)}, u32[]{:S(2)}) collective-permute-start(bf16[2,256,512]{2,1,0:T(8,128)(2,1)} %get-tuple-element.63), channel_id=1, source_target_pairs={{0,4},{4,0},{8,12},{12,8},{16,20},{20,16},{24,28},{28,24},{1,5},{5... | collective-permute-start | bytes 1572872 | tf_op jit(solution)/shard_map/ppermute | solution.py:424
  11.9 16.9 %collective-permute-start.10 = (bf16[2,256,512]{2,1,0:T(8,128)(2,1)}, bf16[2,256,512]{2,1,0:T(8,128)(2,1)S(1)}, u32[]{:S(2)}, u32[]{:S(2)}) collective-permute-start(bf16[2,256,512]{2,1,0:T(8,128)(2,1)} %get-tuple-element.62.keep), channel_id=1, source_target_pairs={{4,12},{8,0},{12,20},{16,8},{20,28},{24,16},{5,13},{9,1},{13,21},{... | collective-permute-start | bytes 1572872 | tf_op jit(solution)/shard_map/ppermute | solution.py:424
  13.2 19.1 %collective-permute-start.6 = (bf16[2,256,512]{2,1,0:T(8,128)(2,1)}, bf16[2,256,512]{2,1,0:T(8,128)(2,1)S(1)}, u32[]{:S(2)}, u32[]{:S(2)}) collective-permute-start(bf16[2,256,512]{2,1,0:T(8,128)(2,1)} %get-tuple-element.61), channel_id=1, source_target_pairs={{0,4},{4,0},{8,12},{12,8},{16,20},{20,16},{24,28},{28,24},{1,5},{5... | collective-permute-start | bytes 1572872 | tf_op jit(solution)/shard_map/ppermute | solution.py:424
  15.9 22.6 %collective-permute-start.7 = (bf16[2,256,512]{2,1,0:T(8,128)(2,1)}, bf16[2,256,512]{2,1,0:T(8,128)(2,1)S(1)}, u32[]{:S(2)}, u32[]{:S(2)}) collective-permute-start(bf16[2,256,512]{2,1,0:T(8,128)(2,1)} %get-tuple-element.60.keep), channel_id=1, source_target_pairs={{4,12},{8,0},{12,20},{16,8},{20,28},{24,16},{5,13},{9,1},{13,21},{... | collective-permute-start | bytes 1572872 | tf_op jit(solution)/shard_map/ppermute | solution.py:424
  21.4 22.9 %collective-permute-start.3 = (bf16[2,256,512]{2,1,0:T(8,128)(2,1)}, bf16[2,256,512]{2,1,0:T(8,128)(2,1)}, u32[]{:S(2)}, u32[]{:S(2)}) collective-permute-start(bf16[2,256,512]{2,1,0:T(8,128)(2,1)} %get-tuple-element.59), channel_id=1, source_target_pairs={{0,4},{4,0},{8,12},{12,8},{16,20},{20,16},{24,28},{28,24},{1,5},{5... | collective-permute-start | bytes 1572872 | tf_op jit(solution)/shard_map/ppermute | solution.py:424
  23.9 29.6 %collective-permute-start = (bf16[2,256,512]{2,1,0:T(8,128)(2,1)}, bf16[2,256,512]{2,1,0:T(8,128)(2,1)S(1)}, u32[]{:S(2)}, u32[]{:S(2)}) collective-permute-start(bf16[2,256,512]{2,1,0:T(8,128)(2,1)} %get-tuple-element.57), channel_id=1, source_target_pairs={{0,4},{4,0},{8,12},{12,8},{16,20},{20,16},{24,28},{28,24},{1,5},{5... | collective-permute-start | bytes 1572872 | tf_op jit(solution)/shard_map/ppermute | solution.py:424
  28.7 28.6 %collective-permute-start.11 = (bf16[2,256,512]{2,1,0:T(8,128)(2,1)S(1)}, bf16[2,256,512]{2,1,0:T(8,128)(2,1)S(1)}, u32[]{:S(2)}, u32[]{:S(2)}) collective-permute-start(bf16[2,256,512]{2,1,0:T(8,128)(2,1)S(1)} %collective-permute-done.9.recv), channel_id=1, source_target_pairs={{0,8},{8,16},{12,4},{16,24},{20,12},{28,20},{1,9},{9,17},{13,5},{1... | collective-permute-start | bytes 1572872 | tf_op jit(solution)/shard_map/ppermute | solution.py:424
  32.3 27.2 %collective-permute-start.8 = (bf16[2,256,512]{2,1,0:T(8,128)(2,1)S(1)}, bf16[2,256,512]{2,1,0:T(8,128)(2,1)}, u32[]{:S(2)}, u32[]{:S(2)}) collective-permute-start(bf16[2,256,512]{2,1,0:T(8,128)(2,1)S(1)} %collective-permute-done.6.recv), channel_id=1, source_target_pairs={{0,8},{8,16},{12,4},{16,24},{20,12},{28,20},{1,9},{9,17},{13,5},{1... | collective-permute-start | bytes 1572872 | tf_op jit(solution)/shard_map/ppermute | solution.py:424
  38.6 82.5 %collective-permute-start.33 = (bf16[16,128,512]{2,1,0:T(8,128)(2,1)}, bf16[16,128,512]{2,1,0:T(8,128)(2,1)}, u32[]{:S(2)}, u32[]{:S(2)}) collective-permute-start(bf16[16,128,512]{2,1,0:T(8,128)(2,1)} %refs_0_.1), channel_id=1, source_target_pairs={{0,2},{1,3},{2,0},{3,1},{4,6},{5,7},{6,4},{7,5},{8,10},{9,11},{10,... | collective-permute-start | bytes 6291464 | tf_op jit(solution)/shard_map/ppermute | solution.py:430
  44.3 26.6 %collective-permute-start.4 = (bf16[2,256,512]{2,1,0:T(8,128)(2,1)}, bf16[2,256,512]{2,1,0:T(8,128)(2,1)S(1)}, u32[]{:S(2)}, u32[]{:S(2)}) collective-permute-start(bf16[2,256,512]{2,1,0:T(8,128)(2,1)} %get-tuple-element.58.keep), channel_id=1, source_target_pairs={{4,12},{8,0},{12,20},{16,8},{20,28},{24,16},{5,13},{9,1},{13,21},{... | collective-permute-start | bytes 1572872 | tf_op jit(solution)/shard_map/ppermute | solution.py:424
  53.6 17.3 %collective-permute-start.5 = (bf16[2,256,512]{2,1,0:T(8,128)(2,1)}, bf16[2,256,512]{2,1,0:T(8,128)(2,1)S(1)}, u32[]{:S(2)}, u32[]{:S(2)}) collective-permute-start(bf16[2,256,512]{2,1,0:T(8,128)(2,1)} %collective-permute-done.3.recv), channel_id=1, source_target_pairs={{0,8},{8,16},{12,4},{16,24},{20,12},{28,20},{1,9},{9,17},{13,5},{1... | collective-permute-start | bytes 1572872 | tf_op jit(solution)/shard_map/ppermute | solution.py:424
  58.2 16.8 %collective-permute-start.1 = (bf16[2,256,512]{2,1,0:T(8,128)(2,1)}, bf16[2,256,512]{2,1,0:T(8,128)(2,1)S(1)}, u32[]{:S(2)}, u32[]{:S(2)}) collective-permute-start(bf16[2,256,512]{2,1,0:T(8,128)(2,1)} %get-tuple-element.56.keep), channel_id=1, source_target_pairs={{4,12},{8,0},{12,20},{16,8},{20,28},{24,16},{5,13},{9,1},{13,21},{... | collective-permute-start | bytes 1572872 | tf_op jit(solution)/shard_map/ppermute | solution.py:424
  59.5 19.7 %collective-permute-start.2 = (bf16[2,256,512]{2,1,0:T(8,128)(2,1)S(1)}, bf16[2,256,512]{2,1,0:T(8,128)(2,1)S(1)}, u32[]{:S(2)}, u32[]{:S(2)}) collective-permute-start(bf16[2,256,512]{2,1,0:T(8,128)(2,1)S(1)} %collective-permute-done.recv), channel_id=1, source_target_pairs={{0,8},{8,16},{12,4},{16,24},{20,12},{28,20},{1,9},{9,17},{13,5},{1... | collective-permute-start | bytes 1572872 | tf_op jit(solution)/shard_map/ppermute | solution.py:424
  83.3 15.4 %collective-permute-start.20 = (bf16[1,512,512]{2,1,0:T(8,128)(2,1)}, bf16[1,512,512]{2,1,0:T(8,128)(2,1)S(1)}, u32[]{:S(2)}, u32[]{:S(2)}) collective-permute-start(bf16[1,512,512]{2,1,0:T(8,128)(2,1)} %get-tuple-element.79), channel_id=1, source_target_pairs={{0,4},{4,0},{8,12},{12,8},{16,20},{20,16},{24,28},{28,24},{1,5},{5... | collective-permute-start | bytes 1572872 | tf_op jit(solution)/shard_map/ppermute | solution.py:424
  85.7 14.5 %collective-permute-start.22 = (bf16[1,512,512]{2,1,0:T(8,128)(2,1)}, bf16[1,512,512]{2,1,0:T(8,128)(2,1)S(1)}, u32[]{:S(2)}, u32[]{:S(2)}) collective-permute-start(bf16[1,512,512]{2,1,0:T(8,128)(2,1)} %get-tuple-element.77.refs_1_.refs_17_), channel_id=1, source_target_pairs={{0,2},{1,3},{2,0},{3,1},{4,6},{5,7},{6,4},{7,5},{8,10},{9,11},{10,... | collective-permute-start | bytes 1572872 | tf_op jit(solution)/shard_map/ppermute | solution.py:430
  87.2 13.0 %collective-permute-start.26 = (bf16[1,512,512]{2,1,0:T(8,128)(2,1)}, bf16[1,512,512]{2,1,0:T(8,128)(2,1)S(1)}, u32[]{:S(2)}, u32[]{:S(2)}) collective-permute-start(bf16[1,512,512]{2,1,0:T(8,128)(2,1)} %get-tuple-element.77.refs_1_.refs_17_), channel_id=1, source_target_pairs={{0,1},{1,0},{2,3},{3,2},{4,5},{5,4},{6,7},{7,6},{8,9},{9,8},{10,11... | collective-permute-start | bytes 1572872 | tf_op jit(solution)/shard_map/ppermute | solution.py:430
  87.2 20.4 %collective-permute-start.19 = (bf16[1,512,512]{2,1,0:T(8,128)(2,1)S(1)}, bf16[1,512,512]{2,1,0:T(8,128)(2,1)S(1)}, u32[]{:S(2)}, u32[]{:S(2)}) collective-permute-start(bf16[1,512,512]{2,1,0:T(8,128)(2,1)S(1)} %copy-done.34), channel_id=1, source_target_pairs={{0,4},{4,0},{8,12},{12,8},{16,20},{20,16},{24,28},{28,24},{1,5},{5... | collective-permute-start | bytes 1572872 | tf_op jit(solution)/shard_map/ppermute | solution.py:424
  98.7 14.8 %collective-permute-start.21 = (bf16[1,512,512]{2,1,0:T(8,128)(2,1)S(1)}, bf16[1,512,512]{2,1,0:T(8,128)(2,1)S(1)}, u32[]{:S(2)}, u32[]{:S(2)}) collective-permute-start(bf16[1,512,512]{2,1,0:T(8,128)(2,1)S(1)} %copy-done.2), channel_id=1, source_target_pairs={{0,2},{1,3},{2,0},{3,1},{4,6},{5,7},{6,4},{7,5},{8,10},{9,11},{10,... | collective-permute-start | bytes 1572872 | tf_op jit(solution)/shard_map/ppermute | solution.py:430
  100.1 13.3 %collective-permute-start.25 = (bf16[1,512,512]{2,1,0:T(8,128)(2,1)S(1)}, bf16[1,512,512]{2,1,0:T(8,128)(2,1)S(1)}, u32[]{:S(2)}, u32[]{:S(2)}) collective-permute-start(bf16[1,512,512]{2,1,0:T(8,128)(2,1)S(1)} %copy-done.2), channel_id=1, source_target_pairs={{0,1},{1,0},{2,3},{3,2},{4,5},{5,4},{6,7},{7,6},{8,9},{9,8},{10,11... | collective-permute-start | bytes 1572872 | tf_op jit(solution)/shard_map/ppermute | solution.py:430
  100.2 20.1 %collective-permute-start.24 = (bf16[1,512,512]{2,1,0:T(8,128)(2,1)S(1)}, bf16[1,512,512]{2,1,0:T(8,128)(2,1)S(1)}, u32[]{:S(2)}, u32[]{:S(2)}) collective-permute-start(bf16[1,512,512]{2,1,0:T(8,128)(2,1)S(1)} %collective-permute-done.20.refs_3_.refs_19_), channel_id=1, source_target_pairs={{0,2},{1,3},{2,0},{3,1},{4,6},{5,7},{6,4},{7,5},{8,10},{9,11},{10,... | collective-permute-start | bytes 1572872 | tf_op jit(solution)/shard_map/ppermute | solution.py:430
  107.5 35.1 %collective-permute-start.34 = (bf16[16,128,512]{2,1,0:T(8,128)(2,1)}, bf16[16,128,512]{2,1,0:T(8,128)(2,1)S(1)}, u32[]{:S(2)}, u32[]{:S(2)}) collective-permute-start(bf16[16,128,512]{2,1,0:T(8,128)(2,1)} %refs_0_.1), channel_id=1, source_target_pairs={{0,1},{1,0},{2,3},{3,2},{4,5},{5,4},{6,7},{7,6},{8,9},{9,8},{10,11... | collective-permute-start | bytes 6291464 | tf_op jit(solution)/shard_map/ppermute | solution.py:430
  120.2 20.9 %collective-permute-start.12 = (bf16[2,512,512]{2,1,0:T(8,128)(2,1)}, bf16[2,512,512]{2,1,0:T(8,128)(2,1)S(1)}, u32[]{:S(2)}, u32[]{:S(2)}) collective-permute-start(bf16[2,512,512]{2,1,0:T(8,128)(2,1)} %get-tuple-element.75), channel_id=1, source_target_pairs={{0,4},{4,0},{8,12},{12,8},{16,20},{20,16},{24,28},{28,24},{1,5},{5... | collective-permute-start | bytes 3145736 | tf_op jit(solution)/shard_map/ppermute | solution.py:424
  121.1 61.9 %collective-permute-start.35 = (bf16[16,128,512]{2,1,0:T(8,128)(2,1)}, bf16[16,128,512]{2,1,0:T(8,128)(2,1)S(1)}, u32[]{:S(2)}, u32[]{:S(2)}) collective-permute-start(bf16[16,128,512]{2,1,0:T(8,128)(2,1)} %collective-permute-done.33.refs_1_), channel_id=1, source_target_pairs={{0,1},{1,0},{2,3},{3,2},{4,5},{5,4},{6,7},{7,6},{8,9},{9,8},{10,11... | collective-permute-start | bytes 6291464 | tf_op jit(solution)/shard_map/ppermute | solution.py:430
  121.1 14.4 %collective-permute-start.23 = (bf16[1,512,512]{2,1,0:T(8,128)(2,1)S(1)}, bf16[1,512,512]{2,1,0:T(8,128)(2,1)}, u32[]{:S(2)}, u32[]{:S(2)}) collective-permute-start(bf16[1,512,512]{2,1,0:T(8,128)(2,1)S(1)} %collective-permute-done.19.refs_2_.refs_18_), channel_id=1, source_target_pairs={{0,2},{1,3},{2,0},{3,1},{4,6},{5,7},{6,4},{7,5},{8,10},{9,11},{10,... | collective-permute-start | bytes 1572872 | tf_op jit(solution)/shard_map/ppermute | solution.py:430
  122.7 14.4 %collective-permute-start.27 = (bf16[1,512,512]{2,1,0:T(8,128)(2,1)S(1)}, bf16[1,512,512]{2,1,0:T(8,128)(2,1)S(1)}, u32[]{:S(2)}, u32[]{:S(2)}) collective-permute-start(bf16[1,512,512]{2,1,0:T(8,128)(2,1)S(1)} %collective-permute-done.19.refs_2_.refs_18_), channel_id=1, source_target_pairs={{0,1},{1,0},{2,3},{3,2},{4,5},{5,4},{6,7},{7,6},{8,9},{9,8},{10,11... | collective-permute-start | bytes 1572872 | tf_op jit(solution)/shard_map/ppermute | solution.py:430
  135.6 26.3 %collective-permute-start.13 = (bf16[2,512,512]{2,1,0:T(8,128)(2,1)}, bf16[2,512,512]{2,1,0:T(8,128)(2,1)}, u32[]{:S(2)}, u32[]{:S(2)}) collective-permute-start(bf16[2,512,512]{2,1,0:T(8,128)(2,1)} %get-tuple-element.74.refs_0_.refs_8_), channel_id=1, source_target_pairs={{0,2},{1,3},{2,0},{3,1},{4,6},{5,7},{6,4},{7,5},{8,10},{9,11},{10,... | collective-permute-start | bytes 3145736 | tf_op jit(solution)/shard_map/ppermute | solution.py:430
  141.2 41.8 %collective-permute-start.14 = (bf16[2,512,512]{2,1,0:T(8,128)(2,1)S(1)}, bf16[2,512,512]{2,1,0:T(8,128)(2,1)}, u32[]{:S(2)}, u32[]{:S(2)}) collective-permute-start(bf16[2,512,512]{2,1,0:T(8,128)(2,1)S(1)} %collective-permute-done.12.refs_1_.refs_9_), channel_id=1, source_target_pairs={{0,2},{1,3},{2,0},{3,1},{4,6},{5,7},{6,4},{7,5},{8,10},{9,11},{10,... | collective-permute-start | bytes 3145736 | tf_op jit(solution)/shard_map/ppermute | solution.py:430
  142.6 19.3 %collective-permute-start.32 = (bf16[1,512,512]{2,1,0:T(8,128)(2,1)S(1)}, bf16[1,512,512]{2,1,0:T(8,128)(2,1)S(1)}, u32[]{:S(2)}, u32[]{:S(2)}) collective-permute-start(bf16[1,512,512]{2,1,0:T(8,128)(2,1)S(1)} %collective-permute-done.24.refs_7_.refs_23_), channel_id=1, source_target_pairs={{0,1},{1,0},{2,3},{3,2},{4,5},{5,4},{6,7},{7,6},{8,9},{9,8},{10,11... | collective-permute-start | bytes 1572872 | tf_op jit(solution)/shard_map/ppermute | solution.py:430
  142.7 53.4 %collective-permute-start.31 = (bf16[1,512,512]{2,1,0:T(8,128)(2,1)}, bf16[1,512,512]{2,1,0:T(8,128)(2,1)}, u32[]{:S(2)}, u32[]{:S(2)}) collective-permute-start(bf16[1,512,512]{2,1,0:T(8,128)(2,1)} %collective-permute-done.23.refs_6_.refs_22_), channel_id=1, source_target_pairs={{0,1},{1,0},{2,3},{3,2},{4,5},{5,4},{6,7},{7,6},{8,9},{9,8},{10,11... | collective-permute-start | bytes 1572872 | tf_op jit(solution)/shard_map/ppermute | solution.py:430
  161.9 59.9 %collective-permute-start.15 = (bf16[2,512,512]{2,1,0:T(8,128)(2,1)}, bf16[2,512,512]{2,1,0:T(8,128)(2,1)}, u32[]{:S(2)}, u32[]{:S(2)}) collective-permute-start(bf16[2,512,512]{2,1,0:T(8,128)(2,1)} %get-tuple-element.74.refs_0_.refs_8_), channel_id=1, source_target_pairs={{0,1},{1,0},{2,3},{3,2},{4,5},{5,4},{6,7},{7,6},{8,9},{9,8},{10,11... | collective-permute-start | bytes 3145736 | tf_op jit(solution)/shard_map/ppermute | solution.py:430
  161.9 59.9 %collective-permute-start.16 = (bf16[2,512,512]{2,1,0:T(8,128)(2,1)S(1)}, bf16[2,512,512]{2,1,0:T(8,128)(2,1)}, u32[]{:S(2)}, u32[]{:S(2)}) collective-permute-start(bf16[2,512,512]{2,1,0:T(8,128)(2,1)S(1)} %collective-permute-done.12.refs_1_.refs_9_), channel_id=1, source_target_pairs={{0,1},{1,0},{2,3},{3,2},{4,5},{5,4},{6,7},{7,6},{8,9},{9,8},{10,11... | collective-permute-start | bytes 3145736 | tf_op jit(solution)/shard_map/ppermute | solution.py:430
  183.0 38.9 %collective-permute-start.17 = (bf16[2,512,512]{2,1,0:T(8,128)(2,1)}, bf16[2,512,512]{2,1,0:T(8,128)(2,1)}, u32[]{:S(2)}, u32[]{:S(2)}) collective-permute-start(bf16[2,512,512]{2,1,0:T(8,128)(2,1)} %collective-permute-done.13.refs_2_.refs_10_), channel_id=1, source_target_pairs={{0,1},{1,0},{2,3},{3,2},{4,5},{5,4},{6,7},{7,6},{8,9},{9,8},{10,11... | collective-permute-start | bytes 3145736 | tf_op jit(solution)/shard_map/ppermute | solution.py:430
  184.4 37.4 %collective-permute-start.18 = (bf16[2,512,512]{2,1,0:T(8,128)(2,1)}, bf16[2,512,512]{2,1,0:T(8,128)(2,1)}, u32[]{:S(2)}, u32[]{:S(2)}) collective-permute-start(bf16[2,512,512]{2,1,0:T(8,128)(2,1)} %collective-permute-done.14.refs_3_.refs_11_), channel_id=1, source_target_pairs={{0,1},{1,0},{2,3},{3,2},{4,5},{5,4},{6,7},{7,6},{8,9},{9,8},{10,11... | collective-permute-start | bytes 3145736 | tf_op jit(solution)/shard_map/ppermute | solution.py:430
  245.8 15.1 %collective-permute-start.36 = (bf16[4,2,64,512]{3,2,1,0:T(8,128)(2,1)}, bf16[4,2,64,512]{3,2,1,0:T(8,128)(2,1)}, u32[]{:S(2)}, u32[]{:S(2)}) collective-permute-start(bf16[4,2,64,512]{3,2,1,0:T(8,128)(2,1)} %get-tuple-element.87), channel_id=1, source_target_pairs={{0,4},{4,0},{8,12},{12,8},{16,20},{20,16},{24,28},{28,24},{1,5},{5... | collective-permute-start | bytes 1572872 | tf_op jit(solution)/shard_map/ppermute | solution.py:424
  247.0 25.1 %collective-permute-start.40 = (bf16[4,2,64,512]{3,2,1,0:T(8,128)(2,1)}, bf16[4,2,64,512]{3,2,1,0:T(8,128)(2,1)S(1)}, u32[]{:S(2)}, u32[]{:S(2)}) collective-permute-start(bf16[4,2,64,512]{3,2,1,0:T(8,128)(2,1)} %get-tuple-element.93), channel_id=1, source_target_pairs={{0,4},{4,0},{8,12},{12,8},{16,20},{20,16},{24,28},{28,24},{1,5},{5... | collective-permute-start | bytes 1572872 | tf_op jit(solution)/shard_map/ppermute | solution.py:424
  256.0 49.4 %collective-permute-start.44 = (bf16[4,2,64,512]{3,2,1,0:T(8,128)(2,1)}, bf16[4,2,64,512]{3,2,1,0:T(8,128)(2,1)S(1)}, u32[]{:S(2)}, u32[]{:S(2)}) collective-permute-start(bf16[4,2,64,512]{3,2,1,0:T(8,128)(2,1)} %get-tuple-element.99), channel_id=1, source_target_pairs={{0,4},{4,0},{8,12},{12,8},{16,20},{20,16},{24,28},{28,24},{1,5},{5... | collective-permute-start | bytes 1572872 | tf_op jit(solution)/shard_map/ppermute | solution.py:424
  257.2 48.4 %collective-permute-start.48 = (bf16[4,2,64,512]{3,2,1,0:T(8,128)(2,1)}, bf16[4,2,64,512]{3,2,1,0:T(8,128)(2,1)S(1)}, u32[]{:S(2)}, u32[]{:S(2)}) collective-permute-start(bf16[4,2,64,512]{3,2,1,0:T(8,128)(2,1)} %get-tuple-element.105), channel_id=1, source_target_pairs={{0,4},{4,0},{8,12},{12,8},{16,20},{20,16},{24,28},{28,24},{1,5},{5... | collective-permute-start | bytes 1572872 | tf_op jit(solution)/shard_map/ppermute | solution.py:424
  263.2 44.0 %collective-permute-start.37 = (bf16[2,64,512]{2,1,0:T(8,128)(2,1)S(1)}, bf16[2,64,512]{2,1,0:T(8,128)(2,1)S(1)}, u32[]{:S(2)}, u32[]{:S(2)}) collective-permute-start(bf16[2,64,512]{2,1,0:T(8,128)(2,1)S(1)} %get-tuple-element.89), channel_id=1, source_target_pairs={{0,8},{4,12},{8,16},{12,20},{16,24},{20,28},{24,0},{28,4},{1,9},{5... | collective-permute-start | bytes 393224 | tf_op jit(solution)/shard_map/ppermute | solution.py:424
  264.8 44.9 %collective-permute-start.38 = (bf16[2,64,512]{2,1,0:T(8,128)(2,1)S(1)}, bf16[2,64,512]{2,1,0:T(8,128)(2,1)S(1)}, u32[]{:S(2)}, u32[]{:S(2)}) collective-permute-start(bf16[2,64,512]{2,1,0:T(8,128)(2,1)S(1)} %get-tuple-element.90), channel_id=1, source_target_pairs={{0,16},{4,20},{8,24},{12,28},{16,0},{20,4},{24,8},{28,12},{1,17},{... | collective-permute-start | bytes 393224 | tf_op jit(solution)/shard_map/ppermute | solution.py:424
  272.1 38.2 %collective-permute-start.39 = (bf16[2,64,512]{2,1,0:T(8,128)(2,1)S(1)}, bf16[2,64,512]{2,1,0:T(8,128)(2,1)S(1)}, u32[]{:S(2)}, u32[]{:S(2)}) collective-permute-start(bf16[2,64,512]{2,1,0:T(8,128)(2,1)S(1)} %get-tuple-element.91), channel_id=1, source_target_pairs={{0,24},{4,28},{8,0},{12,4},{16,8},{20,12},{24,16},{28,20},{1,25},{... | collective-permute-start | bytes 393224 | tf_op jit(solution)/shard_map/ppermute | solution.py:424
  305.6 13.5 %collective-permute-start.42 = (bf16[2,64,512]{2,1,0:T(8,128)(2,1)S(1)}, bf16[2,64,512]{2,1,0:T(8,128)(2,1)S(1)}, u32[]{:S(2)}, u32[]{:S(2)}) collective-permute-start(bf16[2,64,512]{2,1,0:T(8,128)(2,1)S(1)} %get-tuple-element.96), channel_id=1, source_target_pairs={{0,16},{4,20},{8,24},{12,28},{16,0},{20,4},{24,8},{28,12},{1,17},{... | collective-permute-start | bytes 393224 | tf_op jit(solution)/shard_map/ppermute | solution.py:424
  307.2 15.1 %collective-permute-start.43 = (bf16[2,64,512]{2,1,0:T(8,128)(2,1)S(1)}, bf16[2,64,512]{2,1,0:T(8,128)(2,1)S(1)}, u32[]{:S(2)}, u32[]{:S(2)}) collective-permute-start(bf16[2,64,512]{2,1,0:T(8,128)(2,1)S(1)} %get-tuple-element.97), channel_id=1, source_target_pairs={{0,24},{4,28},{8,0},{12,4},{16,8},{20,12},{24,16},{28,20},{1,25},{... | collective-permute-start | bytes 393224 | tf_op jit(solution)/shard_map/ppermute | solution.py:424
  309.7 16.6 %collective-permute-start.45 = (bf16[2,64,512]{2,1,0:T(8,128)(2,1)S(1)}, bf16[2,64,512]{2,1,0:T(8,128)(2,1)S(1)}, u32[]{:S(2)}, u32[]{:S(2)}) collective-permute-start(bf16[2,64,512]{2,1,0:T(8,128)(2,1)S(1)} %get-tuple-element.101), channel_id=1, source_target_pairs={{0,8},{4,12},{8,16},{12,20},{16,24},{20,28},{24,0},{28,4},{1,9},{5... | collective-permute-start | bytes 393224 | tf_op jit(solution)/shard_map/ppermute | solution.py:424
  310.3 21.7 %collective-permute-start.46 = (bf16[2,64,512]{2,1,0:T(8,128)(2,1)S(1)}, bf16[2,64,512]{2,1,0:T(8,128)(2,1)S(1)}, u32[]{:S(2)}, u32[]{:S(2)}) collective-permute-start(bf16[2,64,512]{2,1,0:T(8,128)(2,1)S(1)} %get-tuple-element.102), channel_id=1, source_target_pairs={{0,16},{4,20},{8,24},{12,28},{16,0},{20,4},{24,8},{28,12},{1,17},{... | collective-permute-start | bytes 393224 | tf_op jit(solution)/shard_map/ppermute | solution.py:424
  313.7 18.3 %collective-permute-start.47 = (bf16[2,64,512]{2,1,0:T(8,128)(2,1)S(1)}, bf16[2,64,512]{2,1,0:T(8,128)(2,1)S(1)}, u32[]{:S(2)}, u32[]{:S(2)}) collective-permute-start(bf16[2,64,512]{2,1,0:T(8,128)(2,1)S(1)} %get-tuple-element.103), channel_id=1, source_target_pairs={{0,24},{4,28},{8,0},{12,4},{16,8},{20,12},{24,16},{28,20},{1,25},{... | collective-permute-start | bytes 393224 | tf_op jit(solution)/shard_map/ppermute | solution.py:424
  319.1 13.0 %collective-permute-start.49 = (bf16[2,64,512]{2,1,0:T(8,128)(2,1)S(1)}, bf16[2,64,512]{2,1,0:T(8,128)(2,1)S(1)}, u32[]{:S(2)}, u32[]{:S(2)}) collective-permute-start(bf16[2,64,512]{2,1,0:T(8,128)(2,1)S(1)} %get-tuple-element.107), channel_id=1, source_target_pairs={{0,8},{4,12},{8,16},{12,20},{16,24},{20,28},{24,0},{28,4},{1,9},{5... | collective-permute-start | bytes 393224 | tf_op jit(solution)/shard_map/ppermute | solution.py:424
  322.3 16.5 %collective-permute-start.50 = (bf16[2,64,512]{2,1,0:T(8,128)(2,1)S(1)}, bf16[2,64,512]{2,1,0:T(8,128)(2,1)S(1)}, u32[]{:S(2)}, u32[]{:S(2)}) collective-permute-start(bf16[2,64,512]{2,1,0:T(8,128)(2,1)S(1)} %get-tuple-element.108), channel_id=1, source_target_pairs={{0,16},{4,20},{8,24},{12,28},{16,0},{20,4},{24,8},{28,12},{1,17},{... | collective-permute-start | bytes 393224 | tf_op jit(solution)/shard_map/ppermute | solution.py:424
  326.3 12.5 %collective-permute-start.51 = (bf16[2,64,512]{2,1,0:T(8,128)(2,1)S(1)}, bf16[2,64,512]{2,1,0:T(8,128)(2,1)S(1)}, u32[]{:S(2)}, u32[]{:S(2)}) collective-permute-start(bf16[2,64,512]{2,1,0:T(8,128)(2,1)S(1)} %get-tuple-element.109), channel_id=1, source_target_pairs={{0,24},{4,28},{8,0},{12,4},{16,8},{20,12},{24,16},{28,20},{1,25},{... | collective-permute-start | bytes 393224 | tf_op jit(solution)/shard_map/ppermute | solution.py:424
  (41 other events, 1308.4 us)
